TPU v7x, 32 devices: a whole 2x2x4 slice. The times are simulated.
32 devices in a mesh: dp: 4 (over x, core), fsdp: 8 (over z, y).
Axes of the slice: x: 2, y: 2, z: 4, core: 2. Of those that a mesh axis runs over, the one named last changes fastest.
Arguments:
- patches: bfloat16 [25600, 1024], P(('dp', 'fsdp')), may hold values from -6 to 6
- cotangent: bfloat16 [25600, 1024], P(('dp', 'fsdp')), may hold values from -6 to 6
- window_rows: int32 [25600], P(('dp', 'fsdp')), may hold values from 0 to 799, as said below
- rel_index: int32 [100, 100], replicated, may hold values from 0 to 360, as said below
- params: float32 [12619776], P(('dp', 'fsdp')), as said below
- first_moment: float32 [12619776], P(('dp', 'fsdp')), may hold values from -6 to 6
- second_moment: float32 [12619776], P(('dp', 'fsdp')), may hold values from 0.001 to 0.05
- learn_rate: float32 [], replicated, may hold values from 0.05 to 0.5
- step_count: int32 [], replicated, may hold values from 10 to 1999
Outputs:
- activations: bfloat16 [25600, 1024], P(('dp', 'fsdp'))
- input_grad: bfloat16 [25600, 1024], P(('dp', 'fsdp'))
- group_rms: float32 [13], replicated
- params_new: float32 [12619776], P(('dp', 'fsdp'))
- first_new: float32 [12619776], P(('dp', 'fsdp'))
- second_new: float32 [12619776], P(('dp', 'fsdp'))
Inputs may be any that keep to these rules, and one draw needn't show every extreme that they name: `window_rows`: each aligned block of 800 entries is a permutation of 0 to 799. rel_index[i, j] depends only on the difference of the positions of patches i and j in a 10 x 10 window (row-major), and distinct differences have distinct rows. `params`: finite parameters in the layout of the steps.
All inputs are finite; a program needn't handle non-finite values.
Results may differ from a plain program's by a relative error of at most 0.014.
The roundings to bfloat16 on the way count: a program that leaves them out, or rounds other values in their place, can miss the bound.
Values may be sent and summed in bfloat16 or wider, within the bound.
No kernel may reach another device: no remote copies, remote signals or barrier semaphores. Data moves between devices by JAX's collectives and lax.ppermute only.
A program may use at most 384 MiB of HBM per device.

v0:
```python
from functools import partial
import math

import jax
import jax.numpy as jnp
from jax import lax
from jax.sharding import PartitionSpec as P

D = 1024
HEADS = 32
HEAD_DIM = 32
FF = 4096
WT = 100
TABLE_ROWS = 361
RAW = 12607776


def tensor_shapes():
    return [
        (D,),
        (D,),
        (D, 3 * D),
        (3 * D,),
        (TABLE_ROWS, HEADS),
        (D, D),
        (D,),
        (D,),
        (D,),
        (D, FF),
        (FF,),
        (FF, D),
        (D,),
    ]


def unpack(flat_vector):
    pieces = []
    offset = 0
    for layout in tensor_shapes():
        entries = math.prod(layout)
        pieces.append(flat_vector[offset : offset + entries].reshape(layout))
        offset += entries
    return pieces


def norm_forward(inputs, norm_gain, norm_shift):
    center = inputs - jnp.mean(inputs, axis=-1, keepdims=True)
    spread = jnp.mean(center * center, axis=-1, keepdims=True)
    return center * lax.rsqrt(spread + 1e-05) * norm_gain + norm_shift


def contract_rows(left_side, right_side):
    return lax.dot_general(
        left_side, right_side, (((0,), (0,)), ((), ())), preferred_element_type=jnp.float32
    )


def contract_last(left_side, right_side):
    return lax.dot_general(
        left_side, right_side, (((1,), (1,)), ((), ())), preferred_element_type=jnp.float32
    )


def gather_params(shard_low):
    return lax.all_gather(shard_low, ("dp", "fsdp"), axis=0, tiled=True)


def prepare(gathered, rel_index):
    pieces = unpack(gathered)
    flat_ids = rel_index.reshape(-1)
    picker = (flat_ids[:, None] == jnp.arange(TABLE_ROWS, dtype=jnp.int32)[None, :]).astype(
        jnp.bfloat16
    )
    bias_rows = jnp.dot(picker, pieces[4], preferred_element_type=jnp.float32)
    table_bias = bias_rows.T.reshape(HEADS, WT, WT)
    return (pieces, table_bias)


def attention_scores(queries, keys_low, table_bias):
    raw_scores = jnp.einsum(
        "nqhd,nkhd->nhqk", queries, keys_low, preferred_element_type=jnp.float32
    )
    return raw_scores + table_bias[None]


def scatter_third(flat_view, column_start, column_count):
    block_cols = flat_view[:, column_start : column_start + column_count]
    return lax.psum_scatter(block_cols, ("dp", "fsdp"), scatter_dimension=0, tiled=True)


def local(
    patches,
    cotangent,
    window_rows,
    rel_index,
    params,
    first_moment,
    second_moment,
    learn_rate,
    step_count,
):
    tok_rows = patches.shape[0]
    windows = tok_rows // WT
    devices_all = lax.axis_size(("dp", "fsdp"))
    rows_in = patches[window_rows].astype(jnp.float32)
    cot_rows = cotangent[window_rows].astype(jnp.float32)
    shard_low = params.astype(jnp.bfloat16)
    pieces, table_bias = prepare(gather_params(shard_low), rel_index)
    (
        attn_gain,
        attn_shift,
        mix_weight,
        mix_bias,
        bias_table,
        out_weight,
        out_bias,
        mlp_gain,
        mlp_shift,
        expand_weight,
        expand_bias,
        shrink_weight,
        shrink_bias,
    ) = pieces
    normed_f, first_pull = jax.vjp(
        norm_forward, rows_in, attn_gain.astype(jnp.float32), attn_shift.astype(jnp.float32)
    )
    normed = normed_f.astype(jnp.bfloat16)
    mixed_rows = jnp.dot(normed, mix_weight, preferred_element_type=jnp.float32) + mix_bias.astype(
        jnp.float32
    )
    queries = (
        (mixed_rows[:, :D] * HEAD_DIM ** (-0.5))
        .astype(jnp.bfloat16)
        .reshape(windows, WT, HEADS, HEAD_DIM)
    )
    keys_low = mixed_rows[:, D : 2 * D].astype(jnp.bfloat16).reshape(windows, WT, HEADS, HEAD_DIM)
    values_low = mixed_rows[:, 2 * D :].astype(jnp.bfloat16).reshape(windows, WT, HEADS, HEAD_DIM)
    scores = attention_scores(queries, keys_low, table_bias)
    row_max = jnp.max(scores, axis=-1, keepdims=True)
    exponent = jnp.exp(scores - row_max)
    row_total = jnp.sum(exponent, axis=-1, keepdims=True)
    attn_probs = exponent / row_total
    log_total = row_max + jnp.log(row_total)
    context = jnp.einsum(
        "nhqk,nkhd->nqhd",
        attn_probs.astype(jnp.bfloat16),
        values_low,
        preferred_element_type=jnp.float32,
    )
    attended = context.reshape(tok_rows, D).astype(jnp.bfloat16)
    middle = (
        rows_in
        + jnp.dot(attended, out_weight, preferred_element_type=jnp.float32)
        + out_bias.astype(jnp.float32)
    )
    second_f, second_pull = jax.vjp(
        norm_forward, middle, mlp_gain.astype(jnp.float32), mlp_shift.astype(jnp.float32)
    )
    second = second_f.astype(jnp.bfloat16)
    hidden_pre = jnp.dot(
        second, expand_weight, preferred_element_type=jnp.float32
    ) + expand_bias.astype(jnp.float32)
    hidden = jax.nn.gelu(hidden_pre, approximate=False).astype(jnp.bfloat16)
    result = (
        middle
        + jnp.dot(hidden, shrink_weight, preferred_element_type=jnp.float32)
        + shrink_bias.astype(jnp.float32)
    )
    activations = (
        jnp.zeros((tok_rows, D), jnp.bfloat16).at[window_rows].set(result.astype(jnp.bfloat16))
    )
    back_pieces, back_bias = prepare(gather_params(shard_low), rel_index)
    back_mix = back_pieces[2]
    back_out = back_pieces[5]
    back_expand = back_pieces[9]
    back_shrink = back_pieces[11]
    grad_out = cot_rows.astype(jnp.bfloat16)
    shrink_grad = contract_rows(hidden, grad_out)
    shrink_bias_grad = jnp.sum(grad_out.astype(jnp.float32), axis=0)
    hidden_grad = contract_last(grad_out, back_shrink)
    gelu_pull = jax.vjp(partial(jax.nn.gelu, approximate=False), hidden_pre)[1]
    pre_grad = gelu_pull(hidden_grad)[0].astype(jnp.bfloat16)
    expand_grad = contract_rows(second, pre_grad)
    expand_bias_grad = jnp.sum(pre_grad.astype(jnp.float32), axis=0)
    second_grad = contract_last(pre_grad, back_expand)
    middle_part, mlp_gain_grad, mlp_shift_grad = second_pull(second_grad)
    middle_grad = cot_rows + middle_part
    branch_grad = middle_grad.astype(jnp.bfloat16)
    out_grad = contract_rows(attended, branch_grad)
    out_bias_grad = jnp.sum(branch_grad.astype(jnp.float32), axis=0)
    context_grad = (
        contract_last(branch_grad, back_out)
        .astype(jnp.bfloat16)
        .reshape(windows, WT, HEADS, HEAD_DIM)
    )
    again_scores = attention_scores(queries, keys_low, back_bias)
    again_probs = jnp.exp(again_scores - log_total)
    probs_low = again_probs.astype(jnp.bfloat16)
    values_grad = jnp.einsum(
        "nhqk,nqhd->nkhd", probs_low, context_grad, preferred_element_type=jnp.float32
    )
    probs_grad = jnp.einsum(
        "nqhd,nkhd->nhqk", context_grad, values_low, preferred_element_type=jnp.float32
    )
    scores_grad = (
        again_probs * (probs_grad - jnp.sum(again_probs * probs_grad, axis=-1, keepdims=True))
    ).astype(jnp.bfloat16)
    query_grad = jnp.einsum(
        "nhqk,nkhd->nqhd", scores_grad, keys_low, preferred_element_type=jnp.float32
    ) * HEAD_DIM ** (-0.5)
    key_grad = jnp.einsum(
        "nhqk,nqhd->nkhd", scores_grad, queries, preferred_element_type=jnp.float32
    )
    mixed_grad = jnp.concatenate(
        [
            query_grad.reshape(tok_rows, D),
            key_grad.reshape(tok_rows, D),
            values_grad.reshape(tok_rows, D),
        ],
        axis=1,
    ).astype(jnp.bfloat16)
    bias_sum = jnp.sum(scores_grad.astype(jnp.float32), axis=0).reshape(HEADS, WT * WT)
    flat_ids = rel_index.reshape(-1)
    picker_full = (flat_ids[:, None] == jnp.arange(TABLE_ROWS, dtype=jnp.int32)[None, :]).astype(
        jnp.float32
    )
    table_grad = lax.dot_general(
        picker_full,
        bias_sum,
        (((0,), (1,)), ((), ())),
        precision=lax.Precision.HIGHEST,
        preferred_element_type=jnp.float32,
    )
    mix_grad = contract_rows(normed, mixed_grad)
    mix_bias_grad = jnp.sum(mixed_grad.astype(jnp.float32), axis=0)
    normed_grad = contract_last(mixed_grad, back_mix)
    input_part, attn_gain_grad, attn_shift_grad = first_pull(normed_grad)
    input_rows = (middle_grad + input_part).astype(jnp.bfloat16)
    input_grad = jnp.zeros((tok_rows, D), jnp.bfloat16).at[window_rows].set(input_rows)
    grad_list = [
        attn_gain_grad,
        attn_shift_grad,
        mix_grad,
        mix_bias_grad,
        table_grad,
        out_grad,
        out_bias_grad,
        mlp_gain_grad,
        mlp_shift_grad,
        expand_grad,
        expand_bias_grad,
        shrink_grad,
        shrink_bias_grad,
    ]
    shard_len = params.shape[0]
    tail_len = shard_len * devices_all - RAW
    flat_grad = jnp.concatenate(
        [piece_grad.reshape(-1) for piece_grad in grad_list] + [jnp.zeros((tail_len,), jnp.float32)]
    )
    flat_view = flat_grad.reshape(devices_all, shard_len)
    third_len = shard_len // 3
    owned_parts = [
        scatter_third(flat_view, part_index * third_len, third_len) for part_index in range(3)
    ]
    owned_grad = jnp.concatenate(owned_parts, axis=1).reshape(shard_len)
    scaled = owned_grad / jnp.sqrt(jnp.float32(tok_rows * devices_all))
    bounds = [0]
    for layout in tensor_shapes():
        bounds.append(bounds[-1] + math.prod(layout))
    entry_counts = jnp.array(
        [bounds[index + 1] - bounds[index] for index in range(len(bounds) - 1)], jnp.float32
    )
    lower_edge = jnp.array(bounds[:-1], jnp.int32)
    upper_edge = jnp.array(bounds[1:], jnp.int32)
    positions = lax.axis_index(("dp", "fsdp")) * shard_len + jnp.arange(shard_len, dtype=jnp.int32)
    member = (
        (positions[None, :] >= lower_edge[:, None]) & (positions[None, :] < upper_edge[:, None])
    ).astype(jnp.float32)
    local_sums = jnp.sum(member * (scaled * scaled)[None, :], axis=1)
    group_total = lax.psum(local_sums, ("dp", "fsdp"))
    group_rms = jnp.sqrt(group_total / entry_counts)
    first_new = 0.9 * first_moment + 0.1 * scaled
    second_new = 0.999 * second_moment + 0.001 * scaled * scaled
    step_float = step_count.astype(jnp.float32)
    first_fix = 1.0 - jnp.power(jnp.float32(0.9), step_float)
    second_fix = 1.0 - jnp.power(jnp.float32(0.999), step_float)
    update = first_new / first_fix / (jnp.sqrt(second_new / second_fix) + 1e-08) + 0.05 * params
    params_new = params - learn_rate * update
    return (activations, input_grad, group_rms, params_new, first_new, second_new)


def solution(mesh):
    placed = (
        P(("dp", "fsdp"), None),
        P(("dp", "fsdp"), None),
        P(("dp", "fsdp")),
        P(),
        P(("dp", "fsdp")),
        P(("dp", "fsdp")),
        P(("dp", "fsdp")),
        P(),
        P(),
    )
    return jax.shard_map(
        local,
        mesh=mesh,
        in_specs=placed,
        out_specs=(
            P(("dp", "fsdp"), None),
            P(("dp", "fsdp"), None),
            P(),
            P(("dp", "fsdp")),
            P(("dp", "fsdp")),
            P(("dp", "fsdp")),
        ),
        check_vma=False,
    )
```

profile of v0, /device:TPU:0, one launch (start us, length us, event | category | flops | bytes accessed | tf_op | source)
XLA Modules:
  0.0 2321.4 jit_solution(15224172397560249245)
XLA Ops:
  28.6 269.1 %all-gather.3.cloned.1.call-done = bf16[32,1,394368]{2,1,0:T(2,128)(2,1)} async-done(((bf16[1,1,394368]{2,1,0:T(2,128)(2,1)}), bf16[32,1,394368]{2,1,0:T(2,128)(2,1)}) %all-gather.3.cloned.1.call-update) | async-done | bytes 25239568 | tf_op jit(solution)/shard_map/all_gather | solution.py:65
  297.8 155.1 %reduce = bf16[32,394368]{1,0:T(8,128)(2,1)} reduce(bf16[32,1,394368]{2,1,0:T(2,128)(2,1)} %all-gather.3.cloned.1.call-done, bf16[]{:T(256)} %constant.141), dimensions={1}, to_apply=%all-gather.reduce_sub_computation | reduce | bytes 50479104 | tf_op jit(solution)/shard_map/all_gather | solution.py:65
  452.9 59.5 %reshape.253 = bf16[12619776]{0:T(1024)(128)(2,1)} reshape(bf16[32,394368]{1,0:T(8,128)(2,1)} %reduce) | data formatting | bytes 50479104
  525.8 16.0 fusion.71
  606.3 10.9 add_reduce_fusion
  647.4 13.3 reshape.203
  666.8 13.3 reshape.204
  690.9 42.6 %convert_reduce_fusion.1 = (f32[4096]{0:T(1024)}, bf16[800,4096]{1,0:T(8,128)(2,1)}, f32[800,4096]{1,0:T(8,128)}) fusion(f32[800,4096]{1,0:T(8,128)S(1)} %fusion.62, f32[4096]{0:T(1024)S(1)} %slice_convert_fusion, bf16[800,1024]{1,0:T(8,128)(2,1)S(1)} %copy-done.14, bf16[4096,1024]{1,0:T(8,128)(2,1)} %reshape.204), kind=kOutput, calls=%fused_computation.16 | convolution fusion | flops 6956642304 | bytes 42827776 | tf_op jit(solution)/shard_map/dot_general | solution.py:59
  733.5 12.2 multiply_reduce_fusion.1
  762.0 15.6 multiply_reduce_fusion
  777.6 12.4 convert_reduce_fusion
  837.8 12.0 fusion.63
  866.7 12.5 convolution_bitcast_fusion.1
  888.5 12.1 copy.104
  904.0 11.4 fusion.11
  920.8 14.4 copy.106
  954.3 413.5 %concatenate.22 = f32[12619776]{0:T(1024)} concatenate(f32[1024]{0:T(1024)S(1)} %get-tuple-element.8, f32[1024]{0:T(1024)S(1)} %get-tuple-element.11, f32[3145728]{0:T(1024)} %bitcast.72, f32[3072]{0:T(1024)S(1)} %convert_reduce_fusion.2, f32[11552]{0:T(1024)S(1)} %reshape.211, f32[1048576]{0:T(1024)} %bitcast.73, f32[1024]{0:T(1024)S(1)} %get-tuple-element.30, ...), dimensions={0} | concatenate | bytes 100958208 | tf_op jit(solution)/shard_map/concatenate | solution.py:257
  1367.7 50.7 %reshape.215 = f32[32,394368]{1,0:T(8,128)} reshape(f32[12619776]{0:T(1024)} %concatenate.22) | data formatting | bytes 100958208 | tf_op jit(solution)/shard_map/reshape | solution.py:260
  1418.4 33.6 %fusion.70 = (f32[32,131456]{1,0:T(8,128)}, f32[32,131456]{1,0:T(8,128)}, f32[32,131456]{1,0:T(8,128)}) fusion(f32[32,394368]{1,0:T(8,128)} %reshape.215), kind=kLoop, calls=%fused_computation.145 | loop fusion | bytes 100958208 | tf_op jit(solution)/shard_map/slice | solution.py:87
  1454.7 11.6 scatter_custom_fusion.1
  1466.2 13.0 fusion.75
  1479.3 714.2 %all-reduce.6.cloned.1.call-done = (f32[32,131456]{1,0:T(8,128)}, f32[32,131456]{1,0:T(8,128)}, f32[32,131456]{1,0:T(8,128)}) async-done(((f32[32,131456]{1,0:T(8,128)}, f32[32,131456]{1,0:T(8,128)}, f32[32,131456]{1,0:T(8,128)}), (f32[32,131456]{1,0:T(8,128)}, f32[32,131456]{1,0:T(8,128)}, f32[32,131456]{1,0:T(8,128)})) %all-reduce.6.cloned.1.call-update) | async-done | bytes 50479120
  2229.0 39.5 %psum.7 = f32[13]{0:T(128)S(1)} all-reduce(f32[13]{0:T(128)S(1)} %select_reduce_fusion), channel_id=1, replica_groups=mesh['dp'=4,'fsdp'=8] {'dp','fsdp'}, use_global_device_ids=true, to_apply=%region_26.0 | all-reduce | flops 13 | bytes 104 | tf_op jit(solution)/shard_map/psum | solution.py:280
  2269.1 42.5 %multiply_reduce_fusion.4 = (f32[394368]{0:T(1024)S(1)}, f32[394368]{0:T(1024)S(1)}) fusion(f32[1,131456]{1,0:T(1,128)S(1)} %copy-done.24, f32[1,131456]{1,0:T(1,128)S(1)} %copy-done.26, f32[1,131456]{1,0:T(1,128)S(1)} %copy-done.25), kind=kLoop, calls=%fused_computation.106 | loop fusion | flops 2366208 | bytes 4732416 | tf_op jit(solution)/shard_map/mul | solution.py:283
  (228 shorter events, 303.9 us)
Async XLA Ops:
  7.2 290.6 %all-gather.3.cloned.1.call-start = ((), (), s32[]{:S(2)}) async-start(), calls=%async_computation | async-start | bytes 52056576 | tf_op jit(solution)/shard_map/all_gather | solution.py:65
  18.6 2174.9 %all-reduce.6.cloned.1.call-start = ((), (), s32[]{:S(2)}) async-start(), calls=%async_computation.1 | async-start | bytes 100958208
  18.8 523.9 %copy-start.38 = (s32[10000]{0:T(1024)}, s32[10000]{0:T(1024)S(1)}, u32[]{:S(2)}) copy-start(s32[10000]{0:T(1024)S(1)} %eq.8) | copy-start | bytes 120004
  28.0 535.6 %copy-start.35 = (f32[800]{0:T(1024)}, f32[800]{0:T(1024)S(1)}, u32[]{:S(2)}) copy-start(f32[800]{0:T(1024)S(1)} %broadcast_multiply_fusion.1) | copy-start | bytes 9604
  28.6 424.3 %copy-start.46 = (f32[800]{0:T(1024)}, f32[800]{0:T(1024)S(1)}, u32[]{:S(2)}) copy-start(f32[800]{0:T(1024)S(1)} %fusion.29) | copy-start | bytes 9604
  28.6 535.0 %copy-start.42 = (f32[800]{0:T(1024)}, f32[800]{0:T(1024)S(1)}, u32[]{:S(2)}) copy-start(f32[800]{0:T(1024)S(1)} %fusion.57) | copy-start | bytes 9604
  513.9 49.8 %copy-start.40 = (f32[1024]{0:T(1024)}, f32[1024]{0:T(1024)S(1)}, u32[]{:S(2)}) copy-start(f32[1024]{0:T(1024)S(1)} %get-tuple-element.44) | copy-start | bytes 12292
  513.9 49.8 %copy-start.55 = (f32[1024]{0:T(1024)}, f32[1024]{0:T(1024)S(1)}, u32[]{:S(2)}) copy-start(f32[1024]{0:T(1024)S(1)} %get-tuple-element.43) | copy-start | bytes 12292
  513.9 166.2 %copy-start.53 = (f32[1024]{0:T(1024)}, f32[1024]{0:T(1024)S(1)}, u32[]{:S(2)}) copy-start(f32[1024]{0:T(1024)S(1)} %get-tuple-element.40) | copy-start | bytes 12292
  553.0 74.1 %copy-start.3 = (f32[32,100,100]{1,2,0:T(8,128)}, f32[32,100,100]{1,2,0:T(8,128)S(1)}, u32[]{:S(2)}) copy-start(f32[32,100,100]{1,2,0:T(8,128)S(1)} %copy.81) | copy-start | bytes 3840004
  642.8 17.9 copy-start.29
  690.8 42.6 %copy-start.16 = (f32[800,4096]{1,0:T(8,128)}, f32[800,4096]{1,0:T(8,128)S(1)}, u32[]{:S(2)}) copy-start(f32[800,4096]{1,0:T(8,128)S(1)} %fusion.62) | copy-start | bytes 39321604
  690.9 42.6 %copy-start.10 = (f32[800,1024]{1,0:T(8,128)S(1)}, f32[800,1024]{1,0:T(8,128)}, u32[]{:S(2)}) copy-start(f32[800,1024]{1,0:T(8,128)} %copy-done.9) | copy-start | bytes 9830404
  837.8 28.9 %slice-start.6 = ((s8[6553600]{0:T(1024)(128)(4,1)}), s8[4194304]{0:T(1024)(128)(4,1)S(1)}, s32[]{:S(2)}) async-start(s8[6553600]{0:T(1024)(128)(4,1)} %bitcast.78), calls=%async_computation.8 | async-start | bytes 8388608
  862.2 17.0 slice-start
  862.2 17.0 slice-start.1
  915.5 19.8 slice-start.4
  2219.9 48.7 %copy-start.60 = (f32[13]{0:T(128)S(1)}, f32[13]{0:T(128)}, u32[]{:S(2)}) copy-start(f32[13]{0:T(128)} %constant.131) | copy-start | bytes 160
  2219.9 49.2 %copy-start.24 = (f32[1,131456]{1,0:T(1,128)S(1)}, f32[1,131456]{1,0:T(1,128)}, u32[]{:S(2)}) copy-start(f32[1,131456]{1,0:T(1,128)} %get-tuple-element.26) | copy-start | bytes 1577476
  2219.9 49.2 %copy-start.25 = (f32[1,131456]{1,0:T(1,128)S(1)}, f32[1,131456]{1,0:T(1,128)}, u32[]{:S(2)}) copy-start(f32[1,131456]{1,0:T(1,128)} %get-tuple-element.22) | copy-start | bytes 1577476
  2219.9 49.1 %copy-start.26 = (f32[1,131456]{1,0:T(1,128)S(1)}, f32[1,131456]{1,0:T(1,128)}, u32[]{:S(2)}) copy-start(f32[1,131456]{1,0:T(1,128)} %get-tuple-element.61) | copy-start | bytes 1577476
  2229.0 82.6 %copy-start.22 = (f32[394368]{0:T(1024)S(1)}, f32[394368]{0:T(1024)}, u32[]{:S(2)}) copy-start(f32[394368]{0:T(1024)} %param.16) | copy-start | bytes 4732420
  2268.5 43.1 %copy-start.33 = (f32[394368]{0:T(1024)S(1)}, f32[394368]{0:T(1024)}, u32[]{:S(2)}) copy-start(f32[394368]{0:T(1024)} %param.18) | copy-start | bytes 4732420
  2268.5 43.1 %copy-start.34 = (f32[394368]{0:T(1024)S(1)}, f32[394368]{0:T(1024)}, u32[]{:S(2)}) copy-start(f32[394368]{0:T(1024)} %param.17) | copy-start | bytes 4732420
  (47 other events, 339.8 us)
Sparse Core Ops, SparseCore 0:
  18.7 278.9 all-gather.2
  1452.1 741.3 all-reduce.5
where the time goes:
time: 2360 us; the launch traced here: 2320 us
  waiting for transfers between devices  983 us (42%)
  local copies, waits for them, and re-layouts  790 us (33%)
  other arithmetic  277 us (12%)
  matrix products  214 us (9%)
  blocking collectives  39.5 us (2%)
    unnamed x3, waiting for transfers between devices  714 us
    concatenate x1, local copies, waits for them, and re-layouts, local(): jnp.concatenate([piece_grad.reshape(-1) for piece_grad in grad_list] + [j...  413 us
    all_gather x1, waiting for transfers between devices, gather_params(): return lax.all_gather(shard_low, ('dp', 'fsdp'), axis=0, tiled=True)  269 us
    all_gather x1, other arithmetic, gather_params(): return lax.all_gather(shard_low, ('dp', 'fsdp'), axis=0, tiled=True)  155 us
    unnamed x146, local copies, waits for them, and re-layouts  120 us
    dot_general x4, matrix products, contract_last(): lax.dot_general(left_side, right_side, (((1,), (1,)), ((), ())), preferre...  69.9 us
    reshape x1, local copies, waits for them, and re-layouts, local(): flat_view = flat_grad.reshape(devices_all, shard_len)  50.7 us
  transfers between devices with their start and end apart: 2, of which 2 were waited for; matrix products, arithmetic and copies ran while one was open for 2% of the time, Pallas kernels for 0%

commit v1 on v0

v1 whole, which is shorter than its diff:
```python
from functools import partial
import math

import jax
import jax.numpy as jnp
from jax import lax
from jax.experimental import pallas as pl
from jax.experimental.pallas import tpu as pltpu
from jax.sharding import PartitionSpec as P

D = 1024
HEADS = 32
HEAD_DIM = 32
FF = 4096
WT = 100
TABLE_ROWS = 361
RAW = 12607776
LANES = 128
AXES = ("dp", "fsdp")
BF16 = jnp.bfloat16
F32 = jnp.float32
VMEM_LIMIT = 60 << 20

SHAPES = [
    (D,),
    (D,),
    (D, 3 * D),
    (3 * D,),
    (TABLE_ROWS, HEADS),
    (D, D),
    (D,),
    (D,),
    (D,),
    (D, FF),
    (FF,),
    (FF, D),
    (D,),
]
STARTS = [0]
for _shape in SHAPES:
    STARTS.append(STARTS[-1] + math.prod(_shape))

SPLIT = STARTS[5]
LIFT = (-SPLIT) % LANES


def p_row(position):
    lifted = position + (LIFT if position >= SPLIT else 0)
    assert lifted % LANES == 0
    return lifted // LANES


SPLIT_ROW = p_row(SPLIT)
END_ROW = p_row(RAW)


def round_up(value, step):
    return -(-value // step) * step


class Geometry:
    def __init__(self, dp, fsdp, shard_len):
        assert dp == 4 and shard_len % LANES == 0 and fsdp % 2 == 0
        self.dp, self.fsdp = dp, fsdp
        self.devices = dp * fsdp
        self.line = fsdp // 2
        assert self.line & (self.line - 1) == 0
        self.rows = shard_len // LANES
        first, last = p_row(STARTS[3]) // self.rows, (SPLIT_ROW - 1) // self.rows
        table_first = (STARTS[4] // LANES) // self.rows
        assert last - table_first in (0, 1) and first >= 0
        self.spill_from, self.spill_to = last, table_first
        self.spill = SPLIT_ROW - self.rows * last if last != table_first else 0
        self.spill_pad = round_up(self.spill, 8)
        self.half = round_up(-(-(self.rows + 1 + self.spill) // 2), 16)
        self.slot = 2 * self.half
        tiles = self.slot // 16
        self.step = 16 * max(t for t in range(1, 13) if tiles % t == 0)
        self.bit_x, self.bit_core, self.bit_y = 2 * fsdp, fsdp, 1

    def permute(self, value, mask_core0, mask_core1):
        pairs = []
        for index in range(self.devices):
            core = (index // self.fsdp) % 2
            pairs.append((index, index ^ (mask_core1 if core else mask_core0)))
        return lax.ppermute(value, AXES, pairs)

    def core_swap(self, value):
        return self.permute(value, self.bit_core, self.bit_core)


def prepare_kernel(geo, me_ref, shard_ref, spill_ref, out_ref, pad_ref):
    rows = geo.rows
    base = me_ref[0] * rows
    pad_ref[0:8, :] = jnp.zeros((8, LANES), F32)
    pad_ref[8 : 8 + rows, :] = shard_ref[...]
    tail = geo.slot + 16 - (8 + rows)
    pad_ref[8 + rows : geo.slot + 16, :] = jnp.zeros((tail, LANES), F32)
    step = geo.step

    def body(i, _):
        r0 = pl.multiple_of(i * step, 8)
        here = pad_ref[pl.ds(r0 + 8, step), :]
        above = pad_ref[pl.ds(r0 + 7, step), :]
        lane = lax.broadcasted_iota(jnp.int32, (step, LANES), 1)
        row = lax.broadcasted_iota(jnp.int32, (step, LANES), 0)
        flat = (base + r0 + row) * LANES + lane
        moved = jnp.where(
            lane >= LIFT, pltpu.roll(here, LIFT, 1), pltpu.roll(above, LIFT, 1)
        )
        value = jnp.where(flat < SPLIT, here, jnp.where(flat >= SPLIT + LIFT, moved, 0.0))
        out_ref[pl.ds(r0, step), :] = value.astype(BF16)
        return 0

    lax.fori_loop(0, geo.slot // step, body, 0)
    if geo.spill:

        @pl.when(me_ref[0] == geo.spill_to)
        def _():
            lane = lax.broadcasted_iota(jnp.int32, (geo.spill_pad, LANES), 1)
            row = lax.broadcasted_iota(jnp.int32, (geo.spill_pad, LANES), 0)
            flat = (geo.rows * geo.spill_from + row) * LANES + lane
            pad_ref[0 : geo.spill_pad, :] = jnp.where(flat < SPLIT, spill_ref[...], 0.0)
            top = (rows // 16) * 16
            over = rows - top
            span = round_up(over + geo.spill_pad, 16)
            pad_ref[geo.spill_pad : geo.spill_pad + 16, :] = jnp.zeros((16, LANES), F32)
            lower = out_ref[top : top + 16, :].astype(F32)
            head = lax.broadcasted_iota(jnp.int32, (16, LANES), 0)
            for r in range(0, span, 16):
                if r == 0:
                    shifted = pltpu.roll(pad_ref[0:16, :], over, 0)
                    block = jnp.where(head < over, lower, shifted)
                else:
                    block = pad_ref[r - over : r - over + 16, :]
                if top + r + 16 <= geo.slot:
                    out_ref[top + r : top + r + 16, :] = block.astype(BF16)


def prepare(geo, me, shard, spill):
    spec = pl.BlockSpec(memory_space=pltpu.VMEM)
    return pl.pallas_call(
        partial(prepare_kernel, geo),
        out_shape=jax.ShapeDtypeStruct((geo.slot, LANES), BF16),
        in_specs=[pl.BlockSpec(memory_space=pltpu.SMEM), spec, spec],
        out_specs=spec,
        scratch_shapes=[pltpu.VMEM((geo.slot + 16, LANES), F32)],
        compiler_params=pltpu.CompilerParams(vmem_limit_bytes=VMEM_LIMIT),
        name="prepare_share",
    )(me, shard, spill)


def place(geo, me_ref, device, half):
    y = device % 2
    z = (device // 2) % geo.line
    x = device // (2 * geo.fsdp)
    rel_x = x ^ me_ref[1]
    rel_z = z ^ me_ref[3]
    rel_y = y ^ me_ref[4]
    mine = half == me_ref[2]
    first, second = (rel_x, rel_y) if half == 0 else (rel_y, rel_x)
    return mine, second, first * geo.line + rel_z


def on_arrays(geo, me_ref, phases, device, half, action):
    mine, second, at = place(geo, me_ref, device, half)
    phase = (device // geo.fsdp) % 2
    for slot_index, group in enumerate(phases):
        for own in range(2):
            for late in range(2):
                number = slot_index * 4 + (1 - own) * 2 + late
                cond = (mine if own else jnp.logical_not(mine)) & (second == late)
                if len(phases) > 1:
                    cond = cond & (phase == group)

                @pl.when(cond)
                def _(number=number):
                    action(number, at)


class Region:
    def __init__(self, geo, row0, count, parts, full_end=False):
        self.row0, self.count, self.parts = row0, count, parts
        self.low = max(row0 - 1, 0) // geo.rows
        last = row0 + count - 1
        self.high = last // geo.rows
        if row0 == 0:
            self.high = geo.spill_to if geo.spill else self.high
        if full_end:
            self.high = geo.devices - 1
        self.slots = self.high - self.low + 1
        self.offset = row0 - geo.rows * self.low
        self.scratch_rows = round_up(geo.rows * (self.slots - 1) + geo.slot, 16)
        groups = sorted({(d // geo.fsdp) % 2 for d in range(self.low, self.high + 1)})
        self.phases = groups


def regions(geo):
    def mat(index):
        depth, width = SHAPES[index]
        return ("mat", p_row(STARTS[index]), depth, width // LANES)

    def vec(first, last):
        start, stop = p_row(STARTS[first]), -(-(STARTS[last]) // LANES)
        if STARTS[last] > SPLIT:
            stop = p_row(STARTS[last])
        return ("vec", start, stop - start)

    table = ("vec", STARTS[4] // LANES, SPLIT_ROW - STARTS[4] // LANES)
    r_mix, r_out, r_exp, r_shr = (p_row(STARTS[i]) for i in (2, 5, 9, 11))
    return [
        Region(geo, 0, r_out, [vec(0, 2), mat(2), vec(3, 4), table]),
        Region(geo, r_out, r_exp - r_out, [mat(5), vec(6, 9)]),
        Region(geo, r_exp, r_shr - r_exp, [mat(9), vec(10, 11)]),
        Region(geo, r_shr, END_ROW - r_shr, [mat(11), vec(12, 13)], full_end=True),
    ]


def unpack_kernel(geo, region, me_ref, *refs):
    arrays = 4 * len(region.phases)
    srcs = refs[:arrays]
    outs = refs[arrays : arrays + len(region.parts)]
    flat_ref, slot_ref, sems = refs[arrays + len(region.parts) :]

    def fetch(step):
        device = region.low + step
        buf = lax.rem(step, 2)
        for half in range(2):

            def start(number, at, half=half):
                pltpu.make_async_copy(
                    srcs[number].at[at],
                    slot_ref.at[buf, pl.ds(half * geo.half, geo.half)],
                    sems.at[buf, half],
                ).start()

            on_arrays(geo, me_ref, region.phases, device, half, start)

    fetch(0)

    def slot_body(step, carry):
        @pl.when(step + 1 < region.slots)
        def _():
            fetch(step + 1)

        buf = lax.rem(step, 2)
        for half in range(2):
            pltpu.make_async_copy(
                srcs[0].at[0],
                slot_ref.at[buf, pl.ds(half * geo.half, geo.half)],
                sems.at[buf, half],
            ).wait()
        base = step * geo.rows

        def rows_body(i, _):
            r0 = pl.multiple_of(i * geo.step, 16)
            flat_ref[pl.ds(base + r0, geo.step), :] = slot_ref[buf, pl.ds(r0, geo.step), :].astype(F32)
            return 0

        lax.fori_loop(0, geo.slot // geo.step, rows_body, 0)
        flat_ref[pl.ds(base, 1), :] = flat_ref[pl.ds(base, 1), :] + carry
        return flat_ref[pl.ds(base + geo.rows, 1), :]

    lax.fori_loop(0, region.slots, slot_body, jnp.zeros((1, LANES), F32))

    for part, out_ref in zip(region.parts, outs):
        at = region.offset + part[1] - region.row0
        if part[0] == "vec":
            out_ref[...] = flat_ref[at : at + part[2], :]
        else:
            _, _, depth, cols = part
            block = 16 if cols > 8 else 64

            def mat_body(i, _, at=at, cols=cols, block=block, out_ref=out_ref):
                i0 = pl.multiple_of(i * block, block)
                for c in range(cols):
                    out_ref[pl.ds(i0, block), c * LANES : (c + 1) * LANES] = flat_ref[
                        pl.ds(at + i0 * cols + c, block, stride=cols), :
                    ].astype(BF16)
                return 0

            lax.fori_loop(0, depth // block, mat_body, 0)


def part_shape(part):
    if part[0] == "vec":
        return jax.ShapeDtypeStruct((part[2], LANES), F32)
    return jax.ShapeDtypeStruct((part[2], part[3] * LANES), BF16)


def unpack(geo, region, me, gathered):
    vmem = pl.BlockSpec(memory_space=pltpu.VMEM)
    operands = [array for group in region.phases for array in gathered[group]]
    return pl.pallas_call(
        partial(unpack_kernel, geo, region),
        out_shape=[part_shape(part) for part in region.parts],
        in_specs=[pl.BlockSpec(memory_space=pltpu.SMEM)]
        + [pl.BlockSpec(memory_space=pl.ANY)] * len(operands),
        out_specs=[vmem] * len(region.parts),
        scratch_shapes=[
            pltpu.VMEM((region.scratch_rows, LANES), F32),
            pltpu.VMEM((2, geo.slot, LANES), BF16),
            pltpu.SemaphoreType.DMA((2, 2)),
        ],
        compiler_params=pltpu.CompilerParams(vmem_limit_bytes=VMEM_LIMIT),
        cost_estimate=pl.CostEstimate(
            flops=0, bytes_accessed=4 * LANES * region.count, transcendentals=0
        ),
        name="unpack_weights",
    )(me, *operands)


def pack_kernel(geo, region, shared, grid_steps, kb, cols, fresh, me_ref, a_ref, b_ref, *refs):
    vecs = sum(part[0] == "vec" for part in region.parts)
    arrays = 4 * len(region.phases)
    vec_refs = refs[:vecs]
    refs = refs[vecs:]
    if not fresh:
        refs = refs[arrays:]
    outs = refs[:arrays]
    flat_ref, left_ref, slot_ref, old_ref, sems, old_sem = refs[arrays:]
    step = pl.program_id(0)

    @pl.when(step == 0)
    def _():
        def clear(start, stop):
            span = 64
            while start < stop:
                size = min(span, stop - start)
                flat_ref[start : start + size, :] = jnp.zeros((size, LANES), F32)
                start += size

        clear(0, region.offset)
        clear(region.offset + region.count, region.scratch_rows)
        numbers = iter(range(vecs))
        for part in region.parts:
            if part[0] == "vec":
                at = region.offset + part[1] - region.row0
                flat_ref[at : at + part[2], :] = vec_refs[next(numbers)][...]

    mat = [part for part in region.parts if part[0] == "mat"][0]
    at = region.offset + mat[1] - region.row0
    left_ref[...] = a_ref[...].T
    chunk = 4

    def panel(j, _):
        c0 = j * chunk
        res = jnp.dot(
            left_ref[...],
            b_ref[:, pl.ds(pl.multiple_of(c0 * LANES, LANES), chunk * LANES)],
            preferred_element_type=F32,
        )
        for c in range(chunk):
            flat_ref[pl.ds(at + step * (kb * cols) + c0 + c, kb, stride=cols), :] = res[
                :, c * LANES : (c + 1) * LANES
            ]
        return 0

    lax.fori_loop(0, cols // chunk, panel, 0)

    @pl.when(step == grid_steps - 1)
    def _():
        def send(index, half, parity, start):
            def action(number, at_slot):
                copy = pltpu.make_async_copy(
                    slot_ref.at[parity, half], outs[number].at[at_slot], sems.at[parity, half]
                )
                copy.start()

            if start:
                on_arrays(geo, me_ref, region.phases, region.low + index, half, action)
            else:
                pltpu.make_async_copy(
                    slot_ref.at[parity, half], outs[0].at[0], sems.at[parity, half]
                ).wait()

        if shared:
            for half in range(2):

                def action(number, at_slot, half=half):
                    pltpu.make_async_copy(
                        outs[number].at[at_slot], old_ref.at[half], old_sem.at[half]
                    ).start()

                on_arrays(geo, me_ref, region.phases, region.high, half, action)
            for half in range(2):
                pltpu.make_async_copy(outs[0].at[0], old_ref.at[half], old_sem.at[half]).wait()

        def slot_body(index, _):
            parity = lax.rem(index, 2)
            for half in range(2):

                @pl.when(index >= 2)
                def _(half=half):
                    send(index, half, parity, False)

                base = index * geo.rows + half * geo.half
                stride = geo.step if geo.half % geo.step == 0 else 16
                is_last = index == region.slots - 1

                def rows_body(i, _, half=half, base=base):
                    r0 = pl.multiple_of(i * stride, 16)
                    value = flat_ref[pl.ds(base + r0, stride), :]
                    slot_ref[parity, half, pl.ds(r0, stride), :] = value.astype(BF16)
                    return 0

                def rows_add(i, _, half=half, base=base):
                    r0 = pl.multiple_of(i * stride, 16)
                    value = flat_ref[pl.ds(base + r0, stride), :]
                    value = value + old_ref[half, pl.ds(r0, stride), :].astype(F32)
                    slot_ref[parity, half, pl.ds(r0, stride), :] = value.astype(BF16)
                    return 0

                if shared:

                    @pl.when(is_last)
                    def _(rows_add=rows_add):
                        lax.fori_loop(0, geo.half // stride, rows_add, 0)

                    @pl.when(jnp.logical_not(is_last))
                    def _(rows_body=rows_body):
                        lax.fori_loop(0, geo.half // stride, rows_body, 0)
                else:
                    lax.fori_loop(0, geo.half // stride, rows_body, 0)
                send(index, half, parity, True)
            return 0

        lax.fori_loop(0, region.slots, slot_body, 0)
        for index in range(max(0, region.slots - 2), region.slots):
            for half in range(2):
                send(index, half, index % 2, False)


def pack(geo, region, me, left, right, vectors, previous, shared):
    tokens, depth = left.shape
    width = right.shape[1]
    cols = width // LANES
    kb = 256
    steps = depth // kb
    arrays = [previous.get(group) for group in region.phases]
    fresh_groups = [entry is None for entry in arrays]
    slot_shape = jax.ShapeDtypeStruct((2 * geo.line, geo.half, LANES), BF16)
    count = 4 * len(region.phases)
    operands = [me, left, right] + vectors
    specs = [
        pl.BlockSpec(memory_space=pltpu.SMEM),
        pl.BlockSpec((tokens, kb), lambda k: (0, k)),
        pl.BlockSpec((tokens, width), lambda k: (0, 0), pipeline_mode=pl.Buffered(1)),
    ] + [pl.BlockSpec(vector.shape, lambda k: (0, 0)) for vector in vectors]
    aliases = {}
    fresh = all(fresh_groups)
    if not fresh:
        for position, entry in enumerate(arrays):
            for number in range(4):
                if entry is None:
                    operands.append(jnp.zeros(slot_shape.shape, BF16))
                else:
                    operands.append(entry[number])
                specs.append(pl.BlockSpec(memory_space=pl.ANY))
                aliases[len(operands) - 1] = position * 4 + number
    results = pl.pallas_call(
        partial(pack_kernel, geo, region, shared, steps, kb, cols, fresh),
        grid=(steps,),
        out_shape=[slot_shape] * count,
        in_specs=specs,
        out_specs=[pl.BlockSpec(memory_space=pl.ANY)] * count,
        scratch_shapes=[
            pltpu.VMEM((region.scratch_rows, LANES), F32),
            pltpu.VMEM((kb, tokens), BF16),
            pltpu.VMEM((2, 2, geo.half, LANES), BF16),
            pltpu.VMEM((2, geo.half, LANES), BF16),
            pltpu.SemaphoreType.DMA((2, 2)),
            pltpu.SemaphoreType.DMA((2,)),
        ],
        input_output_aliases=aliases,
        compiler_params=pltpu.CompilerParams(vmem_limit_bytes=VMEM_LIMIT),
        cost_estimate=pl.CostEstimate(
            flops=2 * tokens * depth * width,
            bytes_accessed=2 * depth * width,
            transcendentals=0,
        ),
        name="weight_grad_pack",
    )(*operands)
    updated = dict(previous)
    for position, group in enumerate(region.phases):
        updated[group] = results[position * 4 : position * 4 + 4]
    return updated


def line_masks(geo):
    if geo.line == 4:
        return [[2, 4, 6]]
    return [[2 << bit] for bit in range(geo.line.bit_length() - 1)]


def gather_group(geo, half_share):
    held = half_share[None]
    for masks in line_masks(geo):
        held = jnp.concatenate([held] + [geo.permute(held, mask, mask) for mask in masks], axis=0)
    across = geo.permute(held, geo.bit_x, geo.bit_y)
    near = jnp.concatenate([held, across], axis=0)
    far = geo.permute(near, geo.bit_y, geo.bit_x)
    return [near, far, geo.core_swap(near), geo.core_swap(far)]


def reduce_group(geo, keep_near, keep_far, send_near, send_far):
    got_far = geo.core_swap(send_far)
    got_near = geo.core_swap(send_near)
    far = (keep_far.astype(F32) + got_far.astype(F32)).astype(BF16)
    from_far = geo.permute(far, geo.bit_y, geo.bit_x)
    near = keep_near.astype(F32) + got_near.astype(F32) + from_far.astype(F32)
    count = geo.line
    from_across = geo.permute(near[count:].astype(BF16), geo.bit_x, geo.bit_y)
    held = near[:count] + from_across.astype(F32)
    for masks in reversed(line_masks(geo)):
        block = held.shape[0] // (len(masks) + 1)
        total = held[:block]
        for number, mask in enumerate(masks):
            part = held[(number + 1) * block : (number + 2) * block].astype(BF16)
            total = total + geo.permute(part, mask, mask).astype(F32)
        held = total
    return held[0]


def update_kernel(geo, me_ref, coef_ref, grad_ref, params_ref, first_ref, second_ref, *outs):
    params_out, first_out, second_out, sums_ref = outs
    rows = geo.rows
    base = me_ref[0] * rows
    span = 64
    steps = -(-rows // span)
    tensors = len(SHAPES)
    scale, first_fix, second_fix, rate = (coef_ref[i] for i in range(4))
    sums_ref[...] = jnp.zeros((16, LANES), F32)

    def body(i, _):
        r0 = jnp.minimum(i * span, rows - span)
        skip = i * span - r0
        here = grad_ref[pl.ds(r0, span), :]
        below = grad_ref[pl.ds(r0 + 1, span), :]
        lane = lax.broadcasted_iota(jnp.int32, (span, LANES), 1)
        row = lax.broadcasted_iota(jnp.int32, (span, LANES), 0)
        flat = (base + r0 + row) * LANES + lane
        moved = jnp.where(
            lane < LANES - LIFT,
            pltpu.roll(here, LANES - LIFT, 1),
            pltpu.roll(below, LANES - LIFT, 1),
        )
        grad = jnp.where(flat < SPLIT, here, moved)
        scaled = grad * scale
        first_new = 0.9 * first_ref[pl.ds(r0, span), :] + 0.1 * scaled
        second_new = 0.999 * second_ref[pl.ds(r0, span), :] + 0.001 * scaled * scaled
        params = params_ref[pl.ds(r0, span), :]
        update = first_new / first_fix / (jnp.sqrt(second_new / second_fix) + 1e-08) + 0.05 * params
        params_out[pl.ds(r0, span), :] = params - rate * update
        first_out[pl.ds(r0, span), :] = first_new
        second_out[pl.ds(r0, span), :] = second_new
        squares = jnp.where(row >= skip, scaled * scaled, 0.0)
        low = (base + r0) * LANES
        high = (base + r0 + span) * LANES
        for t in range(tensors):

            @pl.when((low < STARTS[t + 1]) & (high > STARTS[t]))
            def _(t=t):
                inside = (flat >= STARTS[t]) & (flat < STARTS[t + 1])
                part = jnp.where(inside, squares, 0.0)
                sums_ref[t : t + 1, :] += jnp.sum(part, axis=0, keepdims=True)

        return 0

    lax.fori_loop(0, steps, body, 0)


def update_step(geo, me, coef, grad, params, first, second):
    vmem = pl.BlockSpec(memory_space=pltpu.VMEM)
    smem = pl.BlockSpec(memory_space=pltpu.SMEM)
    rows = jax.ShapeDtypeStruct((geo.rows, LANES), F32)
    return pl.pallas_call(
        partial(update_kernel, geo),
        out_shape=[rows, rows, rows, jax.ShapeDtypeStruct((16, LANES), F32)],
        in_specs=[smem, smem, vmem, vmem, vmem, vmem],
        out_specs=[vmem] * 4,
        compiler_params=pltpu.CompilerParams(vmem_limit_bytes=VMEM_LIMIT),
        name="moments_update",
    )(me, coef, grad, params, first, second)


def norm_forward(inputs, norm_gain, norm_shift):
    center = inputs - jnp.mean(inputs, axis=-1, keepdims=True)
    spread = jnp.mean(center * center, axis=-1, keepdims=True)
    return center * lax.rsqrt(spread + 1e-05) * norm_gain + norm_shift


def contract_last(left_side, right_side):
    return lax.dot_general(
        left_side, right_side, (((1,), (1,)), ((), ())), preferred_element_type=F32
    )


def attention_scores(queries, keys_low, table_bias):
    raw_scores = jnp.einsum("nqhd,nkhd->nhqk", queries, keys_low, preferred_element_type=F32)
    return raw_scores + table_bias[None]


def local(
    patches,
    cotangent,
    window_rows,
    rel_index,
    params,
    first_moment,
    second_moment,
    learn_rate,
    step_count,
):
    tok_rows = patches.shape[0]
    windows = tok_rows // WT
    geo = Geometry(lax.axis_size("dp"), lax.axis_size("fsdp"), params.shape[0])
    me_flat = lax.axis_index(AXES)
    core = lax.axis_index("dp") % 2
    me = jnp.stack(
        [
            me_flat,
            lax.axis_index("dp") // 2,
            core,
            lax.axis_index("fsdp") // 2,
            lax.axis_index("fsdp") % 2,
        ]
    ).astype(jnp.int32)
    shard = params.reshape(geo.rows, LANES)
    if geo.spill:
        spill = lax.ppermute(shard[: geo.spill_pad], AXES, [(geo.spill_from, geo.spill_to)])
    else:
        spill = jnp.zeros((8, LANES), F32)
    share = prepare(geo, me, shard, spill).reshape(2, geo.half, LANES)
    mine = lax.dynamic_index_in_dim(share, core, 0, keepdims=False)
    other = geo.core_swap(lax.dynamic_index_in_dim(share, 1 - core, 0, keepdims=False))
    gathered = {
        0: gather_group(geo, jnp.where(core == 0, mine, other)),
        1: gather_group(geo, jnp.where(core == 0, other, mine)),
    }
    region_list = regions(geo)
    vec1, mix_weight, mix_rows, table_rows = unpack(geo, region_list[0], me, gathered)
    out_weight, vec3 = unpack(geo, region_list[1], me, gathered)
    expand_weight, expand_rows = unpack(geo, region_list[2], me, gathered)
    shrink_weight, shrink_rows = unpack(geo, region_list[3], me, gathered)
    attn_gain = vec1[:8].reshape(D)
    attn_shift = vec1[8:].reshape(D)
    mix_bias = mix_rows.reshape(3 * D)
    bias_table = table_rows.reshape(-1)[: TABLE_ROWS * HEADS].reshape(TABLE_ROWS, HEADS)
    out_bias, mlp_gain, mlp_shift = (vec3[8 * i : 8 * i + 8].reshape(D) for i in range(3))
    expand_bias = expand_rows.reshape(FF)
    shrink_bias = shrink_rows.reshape(D)

    rows_in = patches[window_rows].astype(F32)
    cot_rows = cotangent[window_rows].astype(F32)
    flat_ids = rel_index.reshape(-1)
    picker = (flat_ids[:, None] == jnp.arange(TABLE_ROWS, dtype=jnp.int32)[None, :]).astype(BF16)
    bias_rows = jnp.dot(picker, bias_table.astype(BF16), preferred_element_type=F32)
    table_bias = bias_rows.T.reshape(HEADS, WT, WT)
    normed_f, first_pull = jax.vjp(norm_forward, rows_in, attn_gain, attn_shift)
    normed = normed_f.astype(BF16)
    mixed_rows = jnp.dot(normed, mix_weight, preferred_element_type=F32) + mix_bias
    queries = (
        (mixed_rows[:, :D] * HEAD_DIM ** (-0.5))
        .astype(BF16)
        .reshape(windows, WT, HEADS, HEAD_DIM)
    )
    keys_low = mixed_rows[:, D : 2 * D].astype(BF16).reshape(windows, WT, HEADS, HEAD_DIM)
    values_low = mixed_rows[:, 2 * D :].astype(BF16).reshape(windows, WT, HEADS, HEAD_DIM)
    scores = attention_scores(queries, keys_low, table_bias)
    row_max = jnp.max(scores, axis=-1, keepdims=True)
    exponent = jnp.exp(scores - row_max)
    row_total = jnp.sum(exponent, axis=-1, keepdims=True)
    attn_probs = exponent / row_total
    log_total = row_max + jnp.log(row_total)
    context = jnp.einsum(
        "nhqk,nkhd->nqhd", attn_probs.astype(BF16), values_low, preferred_element_type=F32
    )
    attended = context.reshape(tok_rows, D).astype(BF16)
    middle = rows_in + jnp.dot(attended, out_weight, preferred_element_type=F32) + out_bias
    second_f, second_pull = jax.vjp(norm_forward, middle, mlp_gain, mlp_shift)
    second = second_f.astype(BF16)
    hidden_pre = jnp.dot(second, expand_weight, preferred_element_type=F32) + expand_bias
    hidden = jax.nn.gelu(hidden_pre, approximate=False).astype(BF16)
    result = middle + jnp.dot(hidden, shrink_weight, preferred_element_type=F32) + shrink_bias
    activations = jnp.zeros((tok_rows, D), BF16).at[window_rows].set(result.astype(BF16))

    slots = {}
    grad_out = cot_rows.astype(BF16)
    shrink_bias_grad = jnp.sum(grad_out.astype(F32), axis=0)
    slots = pack(
        geo, region_list[3], me, hidden, grad_out, [shrink_bias_grad.reshape(-1, LANES)], slots, False
    )
    hidden_grad = contract_last(grad_out, shrink_weight)
    gelu_pull = jax.vjp(partial(jax.nn.gelu, approximate=False), hidden_pre)[1]
    pre_grad = gelu_pull(hidden_grad)[0].astype(BF16)
    expand_bias_grad = jnp.sum(pre_grad.astype(F32), axis=0)
    slots = pack(
        geo,
        region_list[2],
        me,
        second,
        pre_grad,
        [expand_bias_grad.reshape(-1, LANES)],
        slots,
        region_list[2].high == region_list[3].low,
    )
    second_grad = contract_last(pre_grad, expand_weight)
    middle_part, mlp_gain_grad, mlp_shift_grad = second_pull(second_grad)
    middle_grad = cot_rows + middle_part
    branch_grad = middle_grad.astype(BF16)
    out_bias_grad = jnp.sum(branch_grad.astype(F32), axis=0)
    vec3_grad = jnp.concatenate([out_bias_grad, mlp_gain_grad, mlp_shift_grad]).reshape(-1, LANES)
    slots = pack(
        geo,
        region_list[1],
        me,
        attended,
        branch_grad,
        [vec3_grad],
        slots,
        region_list[1].high == region_list[2].low,
    )
    context_grad = (
        contract_last(branch_grad, out_weight).astype(BF16).reshape(windows, WT, HEADS, HEAD_DIM)
    )
    again_scores = attention_scores(queries, keys_low, table_bias)
    again_probs = jnp.exp(again_scores - log_total)
    probs_low = again_probs.astype(BF16)
    values_grad = jnp.einsum(
        "nhqk,nqhd->nkhd", probs_low, context_grad, preferred_element_type=F32
    )
    probs_grad = jnp.einsum(
        "nqhd,nkhd->nhqk", context_grad, values_low, preferred_element_type=F32
    )
    scores_grad = (
        again_probs * (probs_grad - jnp.sum(again_probs * probs_grad, axis=-1, keepdims=True))
    ).astype(BF16)
    query_grad = jnp.einsum(
        "nhqk,nkhd->nqhd", scores_grad, keys_low, preferred_element_type=F32
    ) * HEAD_DIM ** (-0.5)
    key_grad = jnp.einsum("nhqk,nqhd->nkhd", scores_grad, queries, preferred_element_type=F32)
    mixed_grad = jnp.concatenate(
        [
            query_grad.reshape(tok_rows, D),
            key_grad.reshape(tok_rows, D),
            values_grad.reshape(tok_rows, D),
        ],
        axis=1,
    ).astype(BF16)
    bias_sum = jnp.sum(scores_grad.astype(F32), axis=0).reshape(HEADS, WT * WT)
    picker_full = (flat_ids[:, None] == jnp.arange(TABLE_ROWS, dtype=jnp.int32)[None, :]).astype(F32)
    table_grad = lax.dot_general(
        picker_full,
        bias_sum,
        (((0,), (1,)), ((), ())),
        precision=lax.Precision.HIGHEST,
        preferred_element_type=F32,
    )
    mix_bias_grad = jnp.sum(mixed_grad.astype(F32), axis=0)
    normed_grad = contract_last(mixed_grad, mix_weight)
    input_part, attn_gain_grad, attn_shift_grad = first_pull(normed_grad)
    input_rows = (middle_grad + input_part).astype(BF16)
    input_grad = jnp.zeros((tok_rows, D), BF16).at[window_rows].set(input_rows)
    vec1_grad = jnp.concatenate([attn_gain_grad, attn_shift_grad]).reshape(-1, LANES)
    table_pad = region_list[0].parts[3][2] * LANES - TABLE_ROWS * HEADS
    table_vec = jnp.pad(table_grad.reshape(-1), (0, table_pad)).reshape(-1, LANES)
    slots = pack(
        geo,
        region_list[0],
        me,
        normed,
        mixed_grad,
        [vec1_grad, mix_bias_grad.reshape(-1, LANES), table_vec],
        slots,
        region_list[0].high == region_list[1].low,
    )

    sums = [reduce_group(geo, *slots[group]) for group in range(2)]
    stay = jnp.where(core == 0, sums[0], sums[1])
    leave = geo.core_swap(jnp.where(core == 0, sums[1], sums[0]))
    owned = jnp.where(
        core == 0,
        jnp.concatenate([stay, leave], axis=0),
        jnp.concatenate([leave, stay], axis=0),
    )
    if geo.spill:
        extra = lax.ppermute(
            owned[geo.rows : geo.rows + geo.spill], AXES, [(geo.spill_to, geo.spill_from)]
        )
        owned = owned + jnp.pad(extra, ((0, geo.slot - geo.spill), (0, 0)))
    step_float = step_count.astype(F32)
    coef = jnp.stack(
        [
            1.0 / jnp.sqrt(F32(tok_rows * geo.devices)),
            1.0 - jnp.power(F32(0.9), step_float),
            1.0 - jnp.power(F32(0.999), step_float),
            learn_rate,
        ]
    )
    params_new, first_new, second_new, squares = update_step(
        geo,
        me,
        coef,
        owned,
        shard,
        first_moment.reshape(geo.rows, LANES),
        second_moment.reshape(geo.rows, LANES),
    )
    group_total = lax.psum(jnp.sum(squares, axis=1)[: len(SHAPES)], AXES)
    entry_counts = jnp.array([math.prod(shape) for shape in SHAPES], F32)
    group_rms = jnp.sqrt(group_total / entry_counts)
    return (
        activations,
        input_grad,
        group_rms,
        params_new.reshape(-1),
        first_new.reshape(-1),
        second_new.reshape(-1),
    )


def solution(mesh):
    placed = (
        P(AXES, None),
        P(AXES, None),
        P(AXES),
        P(),
        P(AXES),
        P(AXES),
        P(AXES),
        P(),
        P(),
    )
    return jax.shard_map(
        local,
        mesh=mesh,
        in_specs=placed,
        out_specs=(P(AXES, None), P(AXES, None), P(), P(AXES), P(AXES), P(AXES)),
        check_vma=False,
    )
```

time: 2360 us -> 902 us (0.38); the launches traced: 2320 us -> 897 us
  waiting for transfers between devices: 983 us -> 264 us
  local copies, waits for them, and re-layouts: 790 us -> 116 us
  other arithmetic: 277 us -> 95.1 us
  Pallas kernels: 0 us -> 161 us
  starting transfers between devices: 0.08 us -> 51.7 us
  matrix products: 214 us -> 165 us
    unnamed x3 -> x0, waiting for transfers between devices: 714 us -> none
    concatenate x4 -> x2, local copies, waits for them, and re-layouts: 432 us -> 2.57 us  [gather_group(): near = jnp.concatenate([held, across], axis=0)]
    all_gather x1 -> x0, waiting for transfers between devices: 269 us -> none  [gather_params(): return lax.all_gather(shard_low, ('dp', 'fsdp'), axis=0, tiled=True)]
    ppermute x0 -> x32, waiting for transfers between devices: none -> 264 us  [the longest x30 264 us: permute(): return lax.ppermute(value, AXES, pairs)]
    pallas_call x0 -> x10, Pallas kernels: none -> 161 us  [the longest x4 86.2 us: pack(): pl.pallas_call(partial(pack_kernel, geo, region, shared, steps, kb, cols,...]
    all_gather x1 -> x0, other arithmetic: 155 us -> none  [gather_params(): return lax.all_gather(shard_low, ('dp', 'fsdp'), axis=0, tiled=True)]
    unnamed x146 -> x122, local copies, waits for them, and re-layouts: 120 us -> 12 us
    reshape x11 -> x7, local copies, waits for them, and re-layouts: 114 us -> 21.8 us  [the longest x1 5.4 us: local(): mixed_rows[:, D:2 * D].astype(BF16).reshape(windows, WT, HEADS, HEAD_DIM)]
  transfers between devices with their start and end apart: 2 -> 32, of which waited for: 2 -> 13; matrix products, arithmetic and copies ran while one was open for 2% -> 8% of each run, Pallas kernels for 0% -> 2%
where the time goes in v1:
time: 902 us; the launch traced here: 897 us
  waiting for transfers between devices  264 us (29%)
  matrix products  165 us (18%)
  Pallas kernels  161 us (18%)
  local copies, waits for them, and re-layouts  116 us (13%)
  other arithmetic  95.1 us (11%)
  starting transfers between devices  51.7 us (6%)
  blocking collectives  40 us (4%)
    ppermute x30, waiting for transfers between devices, permute(): return lax.ppermute(value, AXES, pairs)  264 us
    pallas_call x4, Pallas kernels, pack(): pl.pallas_call(partial(pack_kernel, geo, region, shared, steps, kb, cols,...  86.2 us
    dot_general x4, matrix products, contract_last(): lax.dot_general(left_side, right_side, (((1,), (1,)), ((), ())), preferre...  61.7 us
    pallas_call x4, Pallas kernels, unpack(): pl.pallas_call(partial(unpack_kernel, geo, region), out_shape=[part_shape...  56.1 us
    ppermute x30, starting transfers between devices, permute(): return lax.ppermute(value, AXES, pairs)  50.4 us
    psum x1, blocking collectives, local(): group_total = lax.psum(jnp.sum(squares, axis=1)[:len(SHAPES)], AXES)  40 us
  transfers between devices with their start and end apart: 32, of which 13 were waited for; matrix products, arithmetic and copies ran while one was open for 8% of the time, Pallas kernels for 2%

profile of v1, /device:TPU:0, one launch (start us, length us, event | category | flops | bytes accessed | tf_op | source)
XLA Modules:
  0.0 897.0 jit_solution(15597412665729738578)
XLA Ops:
  34.1 11.1 %collective-permute-start.2 = (bf16[1,1584,128]{2,1,0:T(8,128)(2,1)S(1)}, bf16[1,1584,128]{2,1,0:T(8,128)(2,1)S(1)}, u32[]{:S(2)}, u32[]{:S(2)}) collective-permute-start(bf16[1,1584,128]{2,1,0:T(8,128)(2,1)S(1)} %get-tuple-element.108), channel_id=1, source_target_pairs={{0,2},{1,3},{2,0},{3,1},{4,6},{5,7},{6,4},{7,5},{8,10},{9,11},{10,... | collective-permute-start | bytes 1216520 | tf_op jit(solution)/shard_map/ppermute | solution.py:86
  45.2 25.6 %collective-permute-done.10 = bf16[1,1584,128]{2,1,0:T(8,128)(2,1)S(1)} collective-permute-done((bf16[1,1584,128]{2,1,0:T(8,128)(2,1)S(1)}, bf16[1,1584,128]{2,1,0:T(8,128)(2,1)S(1)}, u32[]{:S(2)}, u32[]{:S(2)}) %collective-permute-start.10) | collective-permute-done | bytes 405536 | tf_op jit(solution)/shard_map/ppermute | solution.py:86
  72.5 14.9 %collective-permute-done.3 = bf16[1,1584,128]{2,1,0:T(8,128)(2,1)S(1)} collective-permute-done((bf16[1,1584,128]{2,1,0:T(8,128)(2,1)S(1)}, bf16[1,1584,128]{2,1,0:T(8,128)(2,1)S(1)}, u32[]{:S(2)}, u32[]{:S(2)}) %collective-permute-start.3) | collective-permute-done | bytes 405536 | tf_op jit(solution)/shard_map/ppermute | solution.py:86
  96.6 25.0 %collective-permute-done.5 = bf16[4,1584,128]{2,1,0:T(8,128)(2,1)S(1)} collective-permute-done((bf16[4,1584,128]{2,1,0:T(8,128)(2,1)S(1)}, bf16[4,1584,128]{2,1,0:T(8,128)(2,1)S(1)}, u32[]{:S(2)}, u32[]{:S(2)}) %collective-permute-start.5) | collective-permute-done | bytes 1622048 | tf_op jit(solution)/shard_map/ppermute | solution.py:86
  125.5 16.3 %collective-permute-done.13.refs_1_.refs_5_ = bf16[8,1584,128]{2,1,0:T(8,128)(2,1)} collective-permute-done((bf16[8,1584,128]{2,1,0:T(8,128)(2,1)}, bf16[8,1584,128]{2,1,0:T(8,128)(2,1)}, u32[]{:S(2)}, u32[]{:S(2)}) %collective-permute-start.13) | collective-permute-done | bytes 3244064 | tf_op jit(solution)/shard_map/ppermute | solution.py:86
  144.4 32.2 %collective-permute-done.6.refs_1_ = bf16[8,1584,128]{2,1,0:T(8,128)(2,1)} collective-permute-done((bf16[8,1584,128]{2,1,0:T(8,128)(2,1)}, bf16[8,1584,128]{2,1,0:T(8,128)(2,1)}, u32[]{:S(2)}, u32[]{:S(2)}) %collective-permute-start.6) | collective-permute-done | bytes 3244064 | tf_op jit(solution)/shard_map/ppermute | solution.py:86
  195.9 11.8 %unpack_weights.4 = (f32[16,128]{1,0:T(8,128)}, bf16[1024,3072]{1,0:T(8,128)(2,1)}, f32[24,128]{1,0:T(8,128)}, f32[91,128]{1,0:T(8,128)}) custom-call(s32[5]{0:T(128)} %stack.35.me_ref, bf16[8,1584,128]{2,1,0:T(8,128)(2,1)} %constant_dynamic-update-slice_fusion.refs_0_, bf16[8,1584,128]{2,1,0:T(8,128)(2,1)} %collective-permute-done.6.refs_1_, ...), custom_call_target="tpu_custom_call" | custom-call | bytes 12649984 | tf_op jit(solution)/shard_map/unpack_weights/pallas_call | solution.py:294
  303.6 22.9 %unpack_weights.6 = (bf16[1024,4096]{1,0:T(8,128)(2,1)}, f32[32,128]{1,0:T(8,128)}) custom-call(s32[5]{0:T(128)} %stack.35.me_ref, bf16[8,1584,128]{2,1,0:T(8,128)(2,1)} %constant_dynamic-update-slice_fusion.refs_0_, bf16[8,1584,128]{2,1,0:T(8,128)(2,1)} %collective-permute-done.6.refs_1_, bf16[8,1584,128]{2,1,0:T(8,128)(2,1)} %collective-permute-done.7.refs_2_, ...), custom_call_target="tpu_custom_call" | custom-call | bytes 16793600 | tf_op jit(solution)/shard_map/unpack_weights/pallas_call | solution.py:294
  326.5 13.2 %fusion.77 = f32[800,4096]{1,0:T(8,128)} fusion(bf16[800,1024]{1,0:T(8,128)(2,1)S(1)} %add_convert_fusion.5.a_ref, bf16[1024,4096]{1,0:T(8,128)(2,1)} %get-tuple-element.50), kind=kOutput, calls=%fused_computation.166 | convolution fusion | flops 6710886400 | bytes 23134208 | tf_op jit(solution)/shard_map/dot_general | solution.py:683
  339.7 15.9 %unpack_weights.7 = (bf16[4096,1024]{1,0:T(8,128)(2,1)}, f32[8,128]{1,0:T(8,128)}) custom-call(s32[5]{0:T(128)} %stack.35.me_ref, bf16[8,1584,128]{2,1,0:T(8,128)(2,1)} %constant_dynamic-update-slice_fusion.refs_0_, bf16[8,1584,128]{2,1,0:T(8,128)(2,1)} %collective-permute-done.6.refs_1_, bf16[8,1584,128]{2,1,0:T(8,128)(2,1)} %collective-permute-done.7.refs_2_, ...), custom_call_target="tpu_custom_call" | custom-call | bytes 16781312 | tf_op jit(solution)/shard_map/unpack_weights/pallas_call | solution.py:294
  355.7 41.6 %convert_reduce_fusion.1 = (f32[4096]{0:T(1024)}, bf16[800,4096]{1,0:T(8,128)(2,1)S(1)}, f32[800,4096]{1,0:T(8,128)}) fusion(f32[800,4096]{1,0:T(8,128)} %fusion.77, f32[4096]{0:T(1024)S(1)} %bitcast.127, bf16[800,1024]{1,0:T(8,128)(2,1)S(1)} %copy-done.17, bf16[4096,1024]{1,0:T(8,128)(2,1)} %get-tuple-element.52), kind=kOutput, calls=%fused_computation.16 | convolution fusion | flops 6956642304 | bytes 42827776 | tf_op jit(solution)/shard_map/dot_general | solution.py:594
  441.5 12.4 %convert_reduce_fusion = (f32[32,100,100]{1,2,0:T(8,128)}, bf16[8,32,100,100]{2,3,1,0:T(8,128)(2,1)S(1)}) fusion(f32[8,32,100,100]{2,3,1,0:T(8,128)} %get-tuple-element.133, f32[8,32,100]{2,1,0:T(8,128)S(1)} %get-tuple-element.132, f32[8,32,100]{2,1,0:T(8,128)S(1)} %copy-done.30, f32[8,32,100,100]{2,3,1,0:T(8,128)} %get-tuple-element.130, ...), kind=kLoop, calls=%fused_computation.9 | loop fusion | flops 17600000 | bytes 28364800 | tf_op jit(solution)/shard_map/reduce_sum | solution.py:751
  462.0 12.5 %multiply_convert_fusion.1.a_ref = bf16[800,4096]{1,0:T(8,128)(2,1)} fusion(f32[800,4096]{1,0:T(8,128)} %get-tuple-element.96, f32[800,4096]{1,0:T(8,128)} %fusion.77, f32[4096]{0:T(1024)S(1)} %bitcast.128), kind=kLoop, calls=%fused_computation.18 | loop fusion | flops 13107200 | bytes 32784384 | tf_op jit(solution)/shard_map/convert_element_type | solution.py:684
  538.0 25.0 %weight_grad_pack.4 = (bf16[8,1584,128]{2,1,0:T(8,128)(2,1)}, bf16[8,1584,128]{2,1,0:T(8,128)(2,1)}, bf16[8,1584,128]{2,1,0:T(8,128)(2,1)}, bf16[8,1584,128]{2,1...) custom-call(s32[5]{0:T(128)} %stack.35.me_ref, ...), custom_call_target="tpu_custom_call" | custom-call | flops 6710886400 | bytes 8388608 | tf_op jit(solution)/shard_map/weight_grad_pack/pallas_call | solution.py:461
  563.0 33.4 %weight_grad_pack.5 = (bf16[8,1584,128]{2,1,0:T(8,128)(2,1)}, bf16[8,1584,128]{2,1,0:T(8,128)(2,1)}, bf16[8,1584,128]{2,1,0:T(8,128)(2,1)}, bf16[8,1584,128]{2,1...) custom-call(s32[5]{0:T(128)} %stack.35.me_ref, ...), custom_call_target="tpu_custom_call", output_to_operand_aliasing={{0}: (4, {}), {1}: (5, {}), {2}: (6, {}), {3}: (7, {}), {4}... | custom-call | flops 6710886400 | bytes 8388608 | tf_op jit(solution)/shard_map/weight_grad_pack/pallas_call | solution.py:461
  596.4 18.5 %weight_grad_pack.6 = (bf16[8,1584,128]{2,1,0:T(8,128)(2,1)}, bf16[8,1584,128]{2,1,0:T(8,128)(2,1)}, bf16[8,1584,128]{2,1,0:T(8,128)(2,1)}, bf16[8,1584,128]{2,1,0:T(8,128)(2,1)}) custom-call(s32[5]{0:T(128)} %stack.35.me_ref, bf16[800,1024]{1,0:T(8,128)(2,1)} %copy-done.26, ...), custom_call_target="tpu_custom_call", output_to_operand_aliasing={{0}: (6, {}), {1}: (7, {}), {2}: (8, {}), {3}: (9, {})} | custom-call | flops 5033164800 | bytes 6291456 | tf_op jit(solution)/shard_map/weight_grad_pack/pallas_call | solution.py:461
  639.8 30.6 %collective-permute-done.18 = bf16[8,1584,128]{2,1,0:T(8,128)(2,1)} collective-permute-done((bf16[8,1584,128]{2,1,0:T(8,128)(2,1)S(1)}, bf16[8,1584,128]{2,1,0:T(8,128)(2,1)}, u32[]{:S(2)}, u32[]{:S(2)}) %collective-permute-start.18) | collective-permute-done | bytes 3244064 | tf_op jit(solution)/shard_map/ppermute | solution.py:86
  677.2 45.3 %collective-permute-done.25 = bf16[8,1584,128]{2,1,0:T(8,128)(2,1)} collective-permute-done((bf16[8,1584,128]{2,1,0:T(8,128)(2,1)S(1)}, bf16[8,1584,128]{2,1,0:T(8,128)(2,1)}, u32[]{:S(2)}, u32[]{:S(2)}) %collective-permute-start.25) | collective-permute-done | bytes 3244064 | tf_op jit(solution)/shard_map/ppermute | solution.py:86
  733.7 13.1 %collective-permute-done.26 = bf16[4,1584,128]{2,1,0:T(8,128)(2,1)S(1)} collective-permute-done((bf16[4,1584,128]{2,1,0:T(8,128)(2,1)S(1)}, bf16[4,1584,128]{2,1,0:T(8,128)(2,1)S(1)}, u32[]{:S(2)}, u32[]{:S(2)}) %collective-permute-start.26) | collective-permute-done | bytes 1622048 | tf_op jit(solution)/shard_map/ppermute | solution.py:86
  755.5 32.2 %collective-permute-done.21 = bf16[1,1584,128]{2,1,0:T(8,128)(2,1)S(1)} collective-permute-done((bf16[1,1584,128]{2,1,0:T(8,128)(2,1)S(1)}, bf16[1,1584,128]{2,1,0:T(8,128)(2,1)S(1)}, u32[]{:S(2)}, u32[]{:S(2)}) %collective-permute-start.21) | collective-permute-done | bytes 405536 | tf_op jit(solution)/shard_map/ppermute | solution.py:86
  787.6 15.5 %collective-permute-done.28 = bf16[1,1584,128]{2,1,0:T(8,128)(2,1)} collective-permute-done((bf16[1,1584,128]{2,1,0:T(8,128)(2,1)}, bf16[1,1584,128]{2,1,0:T(8,128)(2,1)}, u32[]{:S(2)}, u32[]{:S(2)}) %collective-permute-start.28) | collective-permute-done | bytes 405536 | tf_op jit(solution)/shard_map/ppermute | solution.py:86
  805.3 12.5 %fusion.78 = f32[800,1024]{1,0:T(8,128)} fusion(bf16[800,4096]{1,0:T(8,128)(2,1)} %multiply_convert_fusion.1.a_ref, bf16[4096,1024]{1,0:T(8,128)(2,1)} %get-tuple-element.52), kind=kOutput, calls=%fused_computation.167 | convolution fusion | flops 6710886400 | bytes 18219008 | tf_op jit(solution)/shard_map/dot_general | solution.py:685
  840.8 14.5 %moments_update.1 = (f32[3081,128]{1,0:T(8,128)}, f32[3081,128]{1,0:T(8,128)}, f32[3081,128]{1,0:T(8,128)}, f32[16,128]{1,0:T(8,128)}) custom-call(s32[5]{0:T(128)} %stack.35.me_ref, f32[4]{0:T(128)} %pad_maximum_fusion.5.coef_ref, f32[3168,128]{1,0:T(8,128)} %pad_add_fusion.grad_ref, f32[3081,128]{1,0:T(8,128)} %bitcast.121, f32[3081,128]{1,0:T(8,128)} %bitcast.124, ...), custom_call_target="tpu_custom_call" | custom-call | tf_op jit(solution)/shard_map/moments_update/pallas_call | solution.py:577
  856.2 40.0 %psum.7 = f32[13]{0:T(128)S(1)} all-reduce(f32[13]{0:T(128)S(1)} %bitcast.137), channel_id=1, replica_groups=mesh['dp'=4,'fsdp'=8] {'dp','fsdp'}, use_global_device_ids=true, to_apply=%region_23.24 | all-reduce | flops 13 | bytes 104 | tf_op jit(solution)/shard_map/psum | solution.py:810
  (275 shorter events, 358.1 us)
Async XLA Ops:
  20.0 50.8 %collective-permute-start.10 = (bf16[1,1584,128]{2,1,0:T(8,128)(2,1)S(1)}, bf16[1,1584,128]{2,1,0:T(8,128)(2,1)S(1)}, u32[]{:S(2)}, u32[]{:S(2)}) collective-permute-start(bf16[1,1584,128]{2,1,0:T(8,128)(2,1)S(1)} %get-tuple-element.121), channel_id=1, source_target_pairs={{0,4},{1,5},{2,6},{3,7},{4,0},{5,1},{6,2},{7,3},{8,12},{9,13},{10,... | collective-permute-start | bytes 1216520 | tf_op jit(solution)/shard_map/ppermute | solution.py:86
  20.0 50.8 %collective-permute-start.9 = (bf16[1,1584,128]{2,1,0:T(8,128)(2,1)S(1)}, bf16[1,1584,128]{2,1,0:T(8,128)(2,1)S(1)}, u32[]{:S(2)}, u32[]{:S(2)}) collective-permute-start(bf16[1,1584,128]{2,1,0:T(8,128)(2,1)S(1)} %get-tuple-element.121), channel_id=1, source_target_pairs={{0,2},{1,3},{2,0},{3,1},{4,6},{5,7},{6,4},{7,5},{8,10},{9,11},{10,... | collective-permute-start | bytes 1216520 | tf_op jit(solution)/shard_map/ppermute | solution.py:86
  24.4 48.1 %collective-permute-start.4 = (bf16[1,1584,128]{2,1,0:T(8,128)(2,1)S(1)}, bf16[1,1584,128]{2,1,0:T(8,128)(2,1)S(1)}, u32[]{:S(2)}, u32[]{:S(2)}) collective-permute-start(bf16[1,1584,128]{2,1,0:T(8,128)(2,1)S(1)} %get-tuple-element.108), channel_id=1, source_target_pairs={{0,6},{1,7},{2,4},{3,5},{4,2},{5,3},{6,0},{7,1},{8,14},{9,15},{10,... | collective-permute-start | bytes 1216520 | tf_op jit(solution)/shard_map/ppermute | solution.py:86
  24.4 63.0 %collective-permute-start.3 = (bf16[1,1584,128]{2,1,0:T(8,128)(2,1)S(1)}, bf16[1,1584,128]{2,1,0:T(8,128)(2,1)S(1)}, u32[]{:S(2)}, u32[]{:S(2)}) collective-permute-start(bf16[1,1584,128]{2,1,0:T(8,128)(2,1)S(1)} %get-tuple-element.108), channel_id=1, source_target_pairs={{0,4},{1,5},{2,6},{3,7},{4,0},{5,1},{6,2},{7,3},{8,12},{9,13},{10,... | collective-permute-start | bytes 1216520 | tf_op jit(solution)/shard_map/ppermute | solution.py:86
  34.1 53.2 %collective-permute-start.2 = (bf16[1,1584,128]{2,1,0:T(8,128)(2,1)S(1)}, bf16[1,1584,128]{2,1,0:T(8,128)(2,1)S(1)}, u32[]{:S(2)}, u32[]{:S(2)}) collective-permute-start(bf16[1,1584,128]{2,1,0:T(8,128)(2,1)S(1)} %get-tuple-element.108), channel_id=1, source_target_pairs={{0,2},{1,3},{2,0},{3,1},{4,6},{5,7},{6,4},{7,5},{8,10},{9,11},{10,... | collective-permute-start | bytes 1216520 | tf_op jit(solution)/shard_map/ppermute | solution.py:86
  71.0 22.8 %collective-permute-start.12 = (bf16[4,1584,128]{2,1,0:T(8,128)(2,1)S(1)}, bf16[4,1584,128]{2,1,0:T(8,128)(2,1)S(1)}, u32[]{:S(2)}, u32[]{:S(2)}) collective-permute-start(bf16[4,1584,128]{2,1,0:T(8,128)(2,1)S(1)} %pad_maximum_fusion.2), channel_id=1, source_target_pairs={{0,16},{1,17},{2,18},{3,19},{4,20},{5,21},{6,22},{7,23},{8,9},{9,8... | collective-permute-start | bytes 4866056 | tf_op jit(solution)/shard_map/ppermute | solution.py:86
  87.6 34.1 %collective-permute-start.5 = (bf16[4,1584,128]{2,1,0:T(8,128)(2,1)S(1)}, bf16[4,1584,128]{2,1,0:T(8,128)(2,1)S(1)}, u32[]{:S(2)}, u32[]{:S(2)}) collective-permute-start(bf16[4,1584,128]{2,1,0:T(8,128)(2,1)S(1)} %pad_maximum_fusion.1), channel_id=1, source_target_pairs={{0,16},{1,17},{2,18},{3,19},{4,20},{5,21},{6,22},{7,23},{8,9},{9,8... | collective-permute-start | bytes 4866056 | tf_op jit(solution)/shard_map/ppermute | solution.py:86
  95.1 46.7 %collective-permute-start.13 = (bf16[8,1584,128]{2,1,0:T(8,128)(2,1)}, bf16[8,1584,128]{2,1,0:T(8,128)(2,1)}, u32[]{:S(2)}, u32[]{:S(2)}) collective-permute-start(bf16[8,1584,128]{2,1,0:T(8,128)(2,1)} %constant_dynamic-update-slice_fusion.5.refs_0_.refs_4_), channel_id=1, source_target_pairs={{0,1},{1,0},{2,3},{3,2},{4,5},{5,4},{6,7},{7,6},{8,24},{9,25},{10,... | collective-permute-start | bytes 9732104 | tf_op jit(solution)/shard_map/ppermute | solution.py:86
  123.0 53.6 %collective-permute-start.6 = (bf16[8,1584,128]{2,1,0:T(8,128)(2,1)}, bf16[8,1584,128]{2,1,0:T(8,128)(2,1)}, u32[]{:S(2)}, u32[]{:S(2)}) collective-permute-start(bf16[8,1584,128]{2,1,0:T(8,128)(2,1)} %constant_dynamic-update-slice_fusion.refs_0_), channel_id=1, source_target_pairs={{0,1},{1,0},{2,3},{3,2},{4,5},{5,4},{6,7},{7,6},{8,24},{9,25},{10,... | collective-permute-start | bytes 9732104 | tf_op jit(solution)/shard_map/ppermute | solution.py:86
  125.5 64.1 %collective-permute-start.14 = (bf16[8,1584,128]{2,1,0:T(8,128)(2,1)}, bf16[8,1584,128]{2,1,0:T(8,128)(2,1)}, u32[]{:S(2)}, u32[]{:S(2)}) collective-permute-start(bf16[8,1584,128]{2,1,0:T(8,128)(2,1)} %constant_dynamic-update-slice_fusion.5.refs_0_.refs_4_), channel_id=1, source_target_pairs={{0,8},{1,9},{2,10},{3,11},{4,12},{5,13},{6,14},{7,15},{8,0},{9,1},... | collective-permute-start | bytes 9732104 | tf_op jit(solution)/shard_map/ppermute | solution.py:86
  141.8 47.8 %collective-permute-start.15 = (bf16[8,1584,128]{2,1,0:T(8,128)(2,1)}, bf16[8,1584,128]{2,1,0:T(8,128)(2,1)}, u32[]{:S(2)}, u32[]{:S(2)}) collective-permute-start(bf16[8,1584,128]{2,1,0:T(8,128)(2,1)} %collective-permute-done.13.refs_1_.refs_5_), channel_id=1, source_target_pairs={{0,8},{1,9},{2,10},{3,11},{4,12},{5,13},{6,14},{7,15},{8,0},{9,1},... | collective-permute-start | bytes 9732104 | tf_op jit(solution)/shard_map/ppermute | solution.py:86
  144.4 51.6 %collective-permute-start.7 = (bf16[8,1584,128]{2,1,0:T(8,128)(2,1)}, bf16[8,1584,128]{2,1,0:T(8,128)(2,1)}, u32[]{:S(2)}, u32[]{:S(2)}) collective-permute-start(bf16[8,1584,128]{2,1,0:T(8,128)(2,1)} %constant_dynamic-update-slice_fusion.refs_0_), channel_id=1, source_target_pairs={{0,8},{1,9},{2,10},{3,11},{4,12},{5,13},{6,14},{7,15},{8,0},{9,1},... | collective-permute-start | bytes 9732104 | tf_op jit(solution)/shard_map/ppermute | solution.py:86
  631.9 38.5 %collective-permute-start.18 = (bf16[8,1584,128]{2,1,0:T(8,128)(2,1)S(1)}, bf16[8,1584,128]{2,1,0:T(8,128)(2,1)}, u32[]{:S(2)}, u32[]{:S(2)}) collective-permute-start(bf16[8,1584,128]{2,1,0:T(8,128)(2,1)S(1)} %add_convert_fusion.2), channel_id=1, source_target_pairs={{0,1},{1,0},{2,3},{3,2},{4,5},{5,4},{6,7},{7,6},{8,24},{9,25},{10,... | collective-permute-start | bytes 9732104 | tf_op jit(solution)/shard_map/ppermute | solution.py:86
  633.4 43.8 %collective-permute-start.23 = (bf16[8,1584,128]{2,1,0:T(8,128)(2,1)S(1)}, bf16[8,1584,128]{2,1,0:T(8,128)(2,1)S(1)}, u32[]{:S(2)}, u32[]{:S(2)}) collective-permute-start(bf16[8,1584,128]{2,1,0:T(8,128)(2,1)S(1)} %copy-done.20), channel_id=1, source_target_pairs={{0,8},{1,9},{2,10},{3,11},{4,12},{5,13},{6,14},{7,15},{8,0},{9,1},... | collective-permute-start | bytes 9732104 | tf_op jit(solution)/shard_map/ppermute | solution.py:86
  638.3 84.2 %collective-permute-start.25 = (bf16[8,1584,128]{2,1,0:T(8,128)(2,1)S(1)}, bf16[8,1584,128]{2,1,0:T(8,128)(2,1)}, u32[]{:S(2)}, u32[]{:S(2)}) collective-permute-start(bf16[8,1584,128]{2,1,0:T(8,128)(2,1)S(1)} %add_convert_fusion.1), channel_id=1, source_target_pairs={{0,1},{1,0},{2,3},{3,2},{4,5},{5,4},{6,7},{7,6},{8,24},{9,25},{10,... | collective-permute-start | bytes 9732104 | tf_op jit(solution)/shard_map/ppermute | solution.py:86
  675.8 51.5 %collective-permute-start.19 = (bf16[4,1584,128]{2,1,0:T(8,128)(2,1)}, bf16[4,1584,128]{2,1,0:T(8,128)(2,1)S(1)}, u32[]{:S(2)}, u32[]{:S(2)}) collective-permute-start(bf16[4,1584,128]{2,1,0:T(8,128)(2,1)} %slice.178), channel_id=1, source_target_pairs={{0,16},{1,17},{2,18},{3,19},{4,20},{5,21},{6,22},{7,23},{8,9},{9,8... | collective-permute-start | bytes 4866056 | tf_op jit(solution)/shard_map/ppermute | solution.py:86
  725.8 21.0 %collective-permute-start.26 = (bf16[4,1584,128]{2,1,0:T(8,128)(2,1)S(1)}, bf16[4,1584,128]{2,1,0:T(8,128)(2,1)S(1)}, u32[]{:S(2)}, u32[]{:S(2)}) collective-permute-start(bf16[4,1584,128]{2,1,0:T(8,128)(2,1)S(1)} %slice.177), channel_id=1, source_target_pairs={{0,16},{1,17},{2,18},{3,19},{4,20},{5,21},{6,22},{7,23},{8,9},{9,8... | collective-permute-start | bytes 4866056 | tf_op jit(solution)/shard_map/ppermute | solution.py:86
  730.2 22.1 %collective-permute-start.20 = (bf16[1,1584,128]{2,1,0:T(8,128)(2,1)S(1)}, bf16[1,1584,128]{2,1,0:T(8,128)(2,1)S(1)}, u32[]{:S(2)}, u32[]{:S(2)}) collective-permute-start(bf16[1,1584,128]{2,1,0:T(8,128)(2,1)S(1)} %get-tuple-element.117), channel_id=1, source_target_pairs={{0,2},{1,3},{2,0},{3,1},{4,6},{5,7},{6,4},{7,5},{8,10},{9,11},{10,... | collective-permute-start | bytes 1216520 | tf_op jit(solution)/shard_map/ppermute | solution.py:86
  730.2 25.3 %collective-permute-start.22 = (bf16[1,1584,128]{2,1,0:T(8,128)(2,1)}, bf16[1,1584,128]{2,1,0:T(8,128)(2,1)S(1)}, u32[]{:S(2)}, u32[]{:S(2)}) collective-permute-start(bf16[1,1584,128]{2,1,0:T(8,128)(2,1)} %get-tuple-element.118), channel_id=1, source_target_pairs={{0,6},{1,7},{2,4},{3,5},{4,2},{5,3},{6,0},{7,1},{8,14},{9,15},{10,... | collective-permute-start | bytes 1216520 | tf_op jit(solution)/shard_map/ppermute | solution.py:86
  732.7 55.0 %collective-permute-start.21 = (bf16[1,1584,128]{2,1,0:T(8,128)(2,1)S(1)}, bf16[1,1584,128]{2,1,0:T(8,128)(2,1)S(1)}, u32[]{:S(2)}, u32[]{:S(2)}) collective-permute-start(bf16[1,1584,128]{2,1,0:T(8,128)(2,1)S(1)} %get-tuple-element.119), channel_id=1, source_target_pairs={{0,4},{1,5},{2,6},{3,7},{4,0},{5,1},{6,2},{7,3},{8,12},{9,13},{10,... | collective-permute-start | bytes 1216520 | tf_op jit(solution)/shard_map/ppermute | solution.py:86
  749.9 37.7 %collective-permute-start.27 = (bf16[1,1584,128]{2,1,0:T(8,128)(2,1)}, bf16[1,1584,128]{2,1,0:T(8,128)(2,1)}, u32[]{:S(2)}, u32[]{:S(2)}) collective-permute-start(bf16[1,1584,128]{2,1,0:T(8,128)(2,1)} %get-tuple-element.114), channel_id=1, source_target_pairs={{0,2},{1,3},{2,0},{3,1},{4,6},{5,7},{6,4},{7,5},{8,10},{9,11},{10,... | collective-permute-start | bytes 1216520 | tf_op jit(solution)/shard_map/ppermute | solution.py:86
  749.9 37.7 %collective-permute-start.29 = (bf16[1,1584,128]{2,1,0:T(8,128)(2,1)}, bf16[1,1584,128]{2,1,0:T(8,128)(2,1)}, u32[]{:S(2)}, u32[]{:S(2)}) collective-permute-start(bf16[1,1584,128]{2,1,0:T(8,128)(2,1)} %get-tuple-element.115), channel_id=1, source_target_pairs={{0,6},{1,7},{2,4},{3,5},{4,2},{5,3},{6,0},{7,1},{8,14},{9,15},{10,... | collective-permute-start | bytes 1216520 | tf_op jit(solution)/shard_map/ppermute | solution.py:86
  752.3 50.8 %collective-permute-start.28 = (bf16[1,1584,128]{2,1,0:T(8,128)(2,1)}, bf16[1,1584,128]{2,1,0:T(8,128)(2,1)}, u32[]{:S(2)}, u32[]{:S(2)}) collective-permute-start(bf16[1,1584,128]{2,1,0:T(8,128)(2,1)} %get-tuple-element.116), channel_id=1, source_target_pairs={{0,4},{1,5},{2,6},{3,7},{4,0},{5,1},{6,2},{7,3},{8,12},{9,13},{10,... | collective-permute-start | bytes 1216520 | tf_op jit(solution)/shard_map/ppermute | solution.py:86
  819.2 20.3 %collective-permute-start.31 = (f32[59,128]{1,0:T(8,128)S(1)}, f32[59,128]{1,0:T(8,128)S(1)}, u32[]{:S(2)}, u32[]{:S(2)}) collective-permute-start(f32[59,128]{1,0:T(8,128)S(1)} %slice.143), channel_id=1, source_target_pairs={{7,8}} | collective-permute-start | bytes 90632 | tf_op jit(solution)/shard_map/ppermute | solution.py:788
  (66 other events, 1351.8 us)

commit v2 on v0

v2 whole, which is shorter than its diff:
```python
from functools import partial
import math

import jax
import jax.numpy as jnp
from jax import lax
from jax.experimental import pallas as pl
from jax.experimental.pallas import tpu as pltpu
from jax.sharding import PartitionSpec as P

D = 1024
HEADS = 32
HEAD_DIM = 32
FF = 4096
WT = 100
WP = 104
TABLE_ROWS = 361
RAW = 12607776
LANES = 128
QUAD = LANES // HEAD_DIM
AXES = ("dp", "fsdp")
BF16 = jnp.bfloat16
F32 = jnp.float32
VMEM_LIMIT = 62 << 20

SHAPES = [
    (D,),
    (D,),
    (D, 3 * D),
    (3 * D,),
    (TABLE_ROWS, HEADS),
    (D, D),
    (D,),
    (D,),
    (D,),
    (D, FF),
    (FF,),
    (FF, D),
    (D,),
]
STARTS = [0]
for _shape in SHAPES:
    STARTS.append(STARTS[-1] + math.prod(_shape))

SPLIT = STARTS[5]
LIFT = (-SPLIT) % LANES


def p_row(position):
    lifted = position + (LIFT if position >= SPLIT else 0)
    assert lifted % LANES == 0
    return lifted // LANES


MIX_ROW, OUT_ROW, EXPAND_ROW, SHRINK_ROW = (p_row(STARTS[i]) for i in (2, 5, 9, 11))
SPLIT_ROW = p_row(SPLIT)
TAIL_ROW = p_row(STARTS[3])
TABLE_ROW = STARTS[4] // LANES
END_ROW = p_row(RAW)
HEAD_ROWS = MIX_ROW
LATE_TAIL = SPLIT_ROW - TAIL_ROW
LATE_ROWS = -(-(HEAD_ROWS + LATE_TAIL) // 8) * 8


def round_up(value, step):
    return -(-value // step) * step


def vmem():
    return pl.BlockSpec(memory_space=pltpu.VMEM)


def smem():
    return pl.BlockSpec(memory_space=pltpu.SMEM)


def anywhere():
    return pl.BlockSpec(memory_space=pl.ANY)


def params_of(**more):
    return pltpu.CompilerParams(vmem_limit_bytes=VMEM_LIMIT, **more)


def cost(flops, bytes_accessed, transcendentals=0):
    return pl.CostEstimate(
        flops=int(flops), bytes_accessed=int(bytes_accessed), transcendentals=int(transcendentals)
    )


def nn(left, right):
    return jnp.dot(left, right, preferred_element_type=F32)


def nt(left, right):
    return lax.dot_general(left, right, (((1,), (1,)), ((), ())), preferred_element_type=F32)


class Geometry:
    def __init__(self, dp, fsdp, shard_len):
        assert dp == 4 and shard_len % LANES == 0 and fsdp % 2 == 0
        self.fsdp = fsdp
        self.devices = dp * fsdp
        self.line = fsdp // 2
        assert self.line & (self.line - 1) == 0
        self.rows = shard_len // LANES
        first, last = TABLE_ROW // self.rows, (SPLIT_ROW - 1) // self.rows
        assert last - first in (0, 1)
        self.spill_from, self.spill_to = last, first
        self.spill = SPLIT_ROW - self.rows * last if last != first else 0
        self.quarter = round_up(-(-(self.rows + 16 + self.spill) // 4), 8)
        self.slot = 4 * self.quarter
        assert self.slot % 16 == 0
        tiles = self.slot // 16
        self.chunk = max(t for t in range(1, 13) if tiles % t == 0)
        self.bit_x, self.bit_core, self.bit_y = 2 * fsdp, fsdp, 1

    def base(self, device):
        return (device * self.rows) // 16 * 16

    def permute(self, value, mask_core0, mask_core1):
        pairs = []
        for index in range(self.devices):
            core = (index // self.fsdp) % 2
            pairs.append((index, index ^ (mask_core1 if core else mask_core0)))
        return lax.ppermute(value, AXES, pairs)

    def core_swap(self, value):
        return self.permute(value, self.bit_core, self.bit_core)


def prepare_kernel(geo, me_ref, shard_ref, spill_ref, out_ref, pad_ref):
    rows, slot = geo.rows, geo.slot
    base = me_ref[0] * rows
    shift = lax.rem(base, 16)
    pad_ref[0:32, :] = jnp.zeros((32, LANES), F32)
    pad_ref[16 + rows : slot + 32, :] = jnp.zeros((slot + 16 - rows, LANES), F32)
    whole = rows // 64

    def place_body(i, _):
        r0 = i * 64
        pad_ref[pl.ds(16 + shift + r0, 64), :] = shard_ref[pl.ds(pl.multiple_of(r0, 64), 64), :]
        return 0

    lax.fori_loop(0, whole, place_body, 0)
    rest = rows - whole * 64
    if rest:
        pad_ref[pl.ds(16 + shift + whole * 64, rest), :] = shard_ref[whole * 64 : rows, :]
    if geo.spill:
        count = geo.spill

        @pl.when(me_ref[0] == geo.spill_to)
        def _():
            lane = lax.broadcasted_iota(jnp.int32, (count, LANES), 1)
            row = lax.broadcasted_iota(jnp.int32, (count, LANES), 0)
            flat = (rows * geo.spill_from + row) * LANES + lane
            at = 16 + rows * geo.spill_from - geo.base(geo.spill_to)
            pad_ref[at : at + count, :] = jnp.where(flat < SPLIT, spill_ref[0:count, :], 0.0)

    step = 16 * geo.chunk

    def body(i, _):
        r0 = pl.multiple_of(i * step, 16)
        here = pad_ref[pl.ds(r0 + 16, step), :]
        above = pad_ref[pl.ds(r0 + 15, step), :]
        lane = lax.broadcasted_iota(jnp.int32, (step, LANES), 1)
        row = lax.broadcasted_iota(jnp.int32, (step, LANES), 0)
        flat = (base - shift + r0 + row) * LANES + lane
        moved = jnp.where(lane >= LIFT, pltpu.roll(here, LIFT, 1), pltpu.roll(above, LIFT, 1))
        value = jnp.where(flat < SPLIT, here, jnp.where(flat >= SPLIT + LIFT, moved, 0.0))
        out_ref[pl.ds(r0, step), :] = value.astype(BF16)
        return 0

    lax.fori_loop(0, slot // step, body, 0)


def prepare(geo, me, shard, spill):
    return pl.pallas_call(
        partial(prepare_kernel, geo),
        out_shape=jax.ShapeDtypeStruct((geo.slot, LANES), BF16),
        in_specs=[smem(), vmem(), vmem()],
        out_specs=vmem(),
        scratch_shapes=[pltpu.VMEM((geo.slot + 32, LANES), F32)],
        compiler_params=params_of(),
        name="prepare_share",
    )(me, shard, spill)


def on_arrays(geo, me_ref, groups, device, quarter, action):
    quarter_x, quarter_core = quarter // 2, quarter % 2
    rel_x = quarter_x ^ me_ref[1]
    rel_z = (lax.rem(device, geo.fsdp) // 2) ^ me_ref[3]
    rel_y = lax.rem(device, 2) ^ me_ref[4]
    mine = me_ref[2] == quarter_core
    first, last = (rel_x, rel_y) if quarter_core == 0 else (rel_y, rel_x)
    at = first * geo.line + rel_z
    for position, group in enumerate(groups):
        for own in range(2):
            for late in range(2):
                number = position * 4 + (1 - own) * 2 + late
                cond = (mine if own else jnp.logical_not(mine)) & (last == late)
                if len(groups) > 1:
                    cond = cond & (device // geo.fsdp == group)

                @pl.when(cond)
                def _(number=number):
                    action(number, at)


class Region:
    def __init__(self, geo, row0, row1, matrix, vectors, span=None, high=None):
        self.row0, self.row1 = row0, row1
        self.mat_row, self.depth, self.cols = matrix
        self.start, self.stop = span or (0, self.depth)
        self.vectors = vectors
        self.low = max(row0 - 1, 0) // geo.rows
        self.high = (row1 - 1) // geo.rows if high is None else high
        self.slots = self.high - self.low + 1
        self.origin = geo.base(self.low)
        self.pitch = 17 if self.cols % 32 == 0 else 16
        self.stride = self.cols * self.pitch // 16
        self.scratch_tiles = (geo.base(self.high) + geo.slot - self.origin) // 16
        self.groups = sorted({d // geo.fsdp for d in range(self.low, self.high + 1)})

    def address(self, row):
        rel = row - self.origin
        return rel if self.pitch == 16 else rel + rel // 16

    def scratch(self):
        return pltpu.VMEM((self.scratch_tiles * self.pitch, LANES), F32)


def copy_rows(region, ref, row, count, move):
    done = 0
    while done < count:
        size = min(count - done, 16 - (row + done - region.origin) % 16)
        if region.pitch == 16:
            size = count - done
        move(region.address(row + done), done, size)
        done += size


def unpack_kernel(geo, region, block, aliased, me_ref, *refs):
    arrays = 4 * len(region.groups)
    srcs, refs = refs[:arrays], refs[arrays:]
    if aliased:
        refs = refs[1:]
    weight_ref, refs = refs[0], refs[1:]
    vec_refs, refs = refs[: len(region.vectors)], refs[len(region.vectors) :]
    flat_ref, slot_ref, stage_ref, sems, out_sem = refs
    quarter, pitch, cols = geo.quarter, region.pitch, region.cols
    total = (region.stop - region.start) // block

    def fetch(step):
        device = region.low + step
        buf = lax.rem(step, 2)
        for q in range(4):

            def start(number, at, q=q):
                pltpu.make_async_copy(
                    srcs[number].at[at],
                    slot_ref.at[buf, pl.ds(q * quarter, quarter)],
                    sems.at[buf, q],
                ).start()

            on_arrays(geo, me_ref, region.groups, device, q, start)

    fetch(0)

    def slot_body(step, carry):
        tile_carry, done = carry

        @pl.when(step + 1 < region.slots)
        def _():
            fetch(step + 1)

        buf = lax.rem(step, 2)
        for q in range(4):
            pltpu.make_async_copy(
                srcs[0].at[0], slot_ref.at[buf, pl.ds(q * quarter, quarter)], sems.at[buf, q]
            ).wait()
        device = region.low + step
        first_tile = geo.base(device) // 16 - region.origin // 16
        next_row = (device + 1) * geo.rows // 16 * 16
        next_tile = next_row // 16 - region.origin // 16

        def rows_body(i, _):
            t0 = i * geo.chunk
            r0 = pl.multiple_of(t0 * 16, 16)
            if pitch == 16:
                to = pl.multiple_of((first_tile + t0) * 16, 16)
                flat_ref[pl.ds(to, geo.chunk * 16), :] = slot_ref[
                    buf, pl.ds(r0, geo.chunk * 16), :
                ].astype(F32)
            else:
                for t in range(geo.chunk):
                    flat_ref[pl.ds((first_tile + t0 + t) * pitch, 16), :] = slot_ref[
                        buf, pl.ds(r0 + t * 16, 16), :
                    ].astype(F32)
            return 0

        lax.fori_loop(0, geo.slot // 16 // geo.chunk, rows_body, 0)
        seam = pl.ds(first_tile * pitch, 16)
        flat_ref[seam, :] = flat_ref[seam, :] + tile_carry
        complete = jnp.maximum(next_row - region.mat_row - region.start * cols, 0) // (block * cols)
        complete = jnp.where(step == region.slots - 1, total, jnp.minimum(complete, total))

        def mat_body(i, _):
            to = pl.multiple_of(i * block, block)
            row = i * (block * region.stride)
            for c in range(cols):
                at = region.address(region.mat_row + region.start * cols + c)
                stage_ref[pl.ds(to, block), c * LANES : (c + 1) * LANES] = flat_ref[
                    pl.ds(at + row, block, stride=region.stride), :
                ].astype(BF16)
            pltpu.make_async_copy(
                stage_ref.at[pl.ds(to, block)],
                weight_ref.at[pl.ds(region.start + to, block)],
                out_sem,
            ).start()
            return 0

        lax.fori_loop(done, complete, mat_body, 0)
        return flat_ref[pl.ds(next_tile * pitch, 16), :], complete

    lax.fori_loop(0, region.slots, slot_body, (jnp.zeros((16, LANES), F32), jnp.int32(0)))
    for (row, count), out_ref in zip(region.vectors, vec_refs):

        def move(at, done, size, out_ref=out_ref):
            out_ref[done : done + size, :] = flat_ref[at : at + size, :]

        copy_rows(region, flat_ref, row, count, move)
    pltpu.make_async_copy(
        stage_ref, weight_ref.at[pl.ds(region.start, region.stop - region.start)], out_sem
    ).wait()


def unpack(geo, region, me, gathered, weight=None):
    operands = [me] + [array for group in region.groups for array in gathered[group]]
    specs = [smem()] + [anywhere()] * (len(operands) - 1)
    aliases = {}
    if weight is not None:
        operands.append(weight)
        specs.append(anywhere())
        aliases = {len(operands) - 1: 0}
    height = region.stop - region.start
    return pl.pallas_call(
        partial(unpack_kernel, geo, region, 64 if region.cols <= 8 else 16, weight is not None),
        out_shape=[jax.ShapeDtypeStruct((region.depth, region.cols * LANES), BF16)]
        + [jax.ShapeDtypeStruct((count, LANES), F32) for _, count in region.vectors],
        in_specs=specs,
        out_specs=[anywhere()] + [vmem()] * len(region.vectors),
        scratch_shapes=[
            region.scratch(),
            pltpu.VMEM((2, geo.slot, LANES), BF16),
            pltpu.VMEM((height, region.cols * LANES), BF16),
            pltpu.SemaphoreType.DMA((2, 4)),
            pltpu.SemaphoreType.DMA(()),
        ],
        input_output_aliases=aliases,
        compiler_params=params_of(),
        cost_estimate=cost(0, 8 * LANES * height * region.cols),
        name="unpack_weights",
    )(*operands)


def clear_rows(region, flat_ref):
    filled = sorted(
        [(region.mat_row, region.mat_row + region.depth * region.cols)]
        + [(row, row + count) for row, count in region.vectors]
    )
    edges = [region.origin] + [edge for run in filled for edge in run]
    edges.append(region.origin + 16 * region.scratch_tiles)
    for start, stop in zip(edges[::2], edges[1::2]):
        if stop > start:

            def move(at, done, size):
                for r in range(0, size, 64):
                    span = min(64, size - r)
                    flat_ref[at + r : at + r + span, :] = jnp.zeros((span, LANES), F32)

            copy_rows(region, flat_ref, start, stop - start, move)


def emit_slots(geo, region, shared, me_ref, flat_ref, slot_ref, old_ref, sems, old_sem, outs):
    quarter, pitch = geo.quarter, region.pitch

    def send(index, parity, start):
        for q in range(4):

            def action(number, at, q=q):
                pltpu.make_async_copy(
                    slot_ref.at[parity, pl.ds(q * quarter, quarter)],
                    outs[number].at[at],
                    sems.at[parity, q],
                ).start()

            if start:
                on_arrays(geo, me_ref, region.groups, region.low + index, q, action)
            else:
                pltpu.make_async_copy(
                    slot_ref.at[parity, pl.ds(q * quarter, quarter)],
                    outs[0].at[0],
                    sems.at[parity, q],
                ).wait()

    if shared:
        for q in range(4):

            def action(number, at, q=q):
                pltpu.make_async_copy(
                    outs[number].at[at], old_ref.at[pl.ds(q * quarter, quarter)], old_sem.at[q]
                ).start()

            on_arrays(geo, me_ref, region.groups, region.high, q, action)
        for q in range(4):
            pltpu.make_async_copy(
                outs[0].at[0], old_ref.at[pl.ds(q * quarter, quarter)], old_sem.at[q]
            ).wait()

    def slot_body(index, _):
        parity = lax.rem(index, 2)

        @pl.when(index >= 2)
        def _():
            send(index, parity, False)

        first_tile = geo.base(region.low + index) // 16 - region.origin // 16

        def convert(add):
            def rows_body(i, _):
                t0 = i * geo.chunk
                r0 = pl.multiple_of(t0 * 16, 16)
                for t in range(geo.chunk):
                    value = flat_ref[pl.ds((first_tile + t0 + t) * pitch, 16), :]
                    here = pl.ds(r0 + t * 16, 16)
                    if add:
                        value = value + old_ref[here, :].astype(F32)
                    slot_ref[parity, here, :] = value.astype(BF16)
                return 0

            lax.fori_loop(0, geo.slot // 16 // geo.chunk, rows_body, 0)

        if shared:
            last = index == region.slots - 1
            pl.when(last)(lambda: convert(True))
            pl.when(jnp.logical_not(last))(lambda: convert(False))
        else:
            convert(False)
        send(index, parity, True)
        return 0

    lax.fori_loop(0, region.slots, slot_body, 0)
    for index in range(max(0, region.slots - 2), region.slots):
        send(index, index % 2, False)


def emit_scratch(geo, region):
    return [
        region.scratch(),
        pltpu.VMEM((2, geo.slot, LANES), BF16),
        pltpu.VMEM((geo.slot, LANES), BF16),
        pltpu.SemaphoreType.DMA((2, 4)),
        pltpu.SemaphoreType.DMA((4,)),
    ]


def store_columns(region, flat_ref, row0, first_col, values):
    height = values.shape[0]
    for c in range(values.shape[1] // LANES):
        at = region.address(region.mat_row + first_col + c) + row0 * region.stride
        flat_ref[pl.ds(at, height, stride=region.stride), :] = values[
            :, c * LANES : (c + 1) * LANES
        ]


def with_slots(geo, region, slots, operands, specs):
    shape = jax.ShapeDtypeStruct((2 * geo.line, geo.quarter, LANES), BF16)
    aliases = {}
    count = 0
    for position, group in enumerate(region.groups):
        for number in range(4):
            if group in slots:
                operands.append(slots[group][number])
                specs.append(anywhere())
                aliases[len(operands) - 1] = position * 4 + number
                count += 1
    return [shape] * (4 * len(region.groups)), aliases, count


def updated_slots(region, slots, results):
    merged = dict(slots)
    for position, group in enumerate(region.groups):
        merged[group] = results[position * 4 : position * 4 + 4]
    return merged


def pack_kernel(geo, region, shared, grid_steps, height, skip, me_ref, a_ref, b_ref, *refs):
    vec_refs, refs = refs[: len(region.vectors)], refs[len(region.vectors) + skip :]
    arrays = 4 * len(region.groups)
    outs = refs[:arrays]
    flat_ref, slot_ref, old_ref, sems, old_sem, left_ref = refs[arrays:]
    step = pl.program_id(0)

    @pl.when(step == 0)
    def _():
        clear_rows(region, flat_ref)
        for (row, count), vec_ref in zip(region.vectors, vec_refs):

            def move(at, done, size, vec_ref=vec_ref):
                flat_ref[at : at + size, :] = vec_ref[done : done + size, :]

            copy_rows(region, flat_ref, row, count, move)

    left_ref[...] = a_ref[...].T

    def panel(j, _):
        lanes = pl.ds(pl.multiple_of(j * 512, 512), 512)
        store_columns(region, flat_ref, step * height, j * 4, nn(left_ref[...], b_ref[:, lanes]))
        return 0

    lax.fori_loop(0, region.cols // 4, panel, 0)

    @pl.when(step == grid_steps - 1)
    def _():
        emit_slots(
            geo, region, shared, me_ref, flat_ref, slot_ref, old_ref, sems, old_sem, outs
        )


def pack(geo, region, me, left, right, vectors, slots, shared):
    tokens = left.shape[0]
    height = 256
    steps = region.depth // height
    width = region.cols * LANES
    operands = [me, left, right] + vectors
    specs = [
        smem(),
        pl.BlockSpec((tokens, height), lambda k: (0, k)),
        pl.BlockSpec((tokens, width), lambda k: (0, 0), pipeline_mode=pl.Buffered(1)),
    ] + [pl.BlockSpec(vector.shape, lambda k: (0, 0)) for vector in vectors]
    shapes, aliases, skip = with_slots(geo, region, slots, operands, specs)
    results = pl.pallas_call(
        partial(pack_kernel, geo, region, shared, steps, height, skip),
        grid=(steps,),
        out_shape=shapes,
        in_specs=specs,
        out_specs=[anywhere()] * len(shapes),
        scratch_shapes=emit_scratch(geo, region) + [pltpu.VMEM((height, tokens), BF16)],
        input_output_aliases=aliases,
        compiler_params=params_of(),
        cost_estimate=cost(2 * tokens * region.depth * width, 2 * region.depth * width),
        name="weight_grad_pack",
    )(*operands)
    return updated_slots(region, slots, results)


def line_masks(geo):
    if geo.line == 4:
        return [[2, 4, 6]]
    return [[2 << bit] for bit in range(geo.line.bit_length() - 1)]


def spread_quarters(geo, share, dp_index):
    pieces = [lax.dynamic_index_in_dim(share, dp_index, 0, keepdims=False)]
    for offset in (1, 2, 3):
        piece = lax.dynamic_index_in_dim(share, dp_index ^ offset, 0, keepdims=False)
        mask = offset * geo.fsdp
        pieces.append(geo.permute(piece, mask, mask))
    stacked = jnp.stack(pieces)
    return [
        lax.dynamic_index_in_dim(stacked, dp_index ^ group, 0, keepdims=False)
        for group in range(4)
    ]


def gather_group(geo, piece):
    held = piece[None]
    for masks in line_masks(geo):
        held = jnp.concatenate([held] + [geo.permute(held, mask, mask) for mask in masks], axis=0)
    across = geo.permute(held, geo.bit_x, geo.bit_y)
    near = jnp.concatenate([held, across], axis=0)
    far = geo.permute(near, geo.bit_y, geo.bit_x)
    return [near, far, geo.core_swap(near), geo.core_swap(far)]


def reduce_group(geo, keep_near, keep_far, send_near, send_far):
    got_far = geo.core_swap(send_far)
    got_near = geo.core_swap(send_near)
    far = (keep_far.astype(F32) + got_far.astype(F32)).astype(BF16)
    from_far = geo.permute(far, geo.bit_y, geo.bit_x)
    near = keep_near.astype(F32) + got_near.astype(F32) + from_far.astype(F32)
    count = geo.line
    from_across = geo.permute(near[count:].astype(BF16), geo.bit_x, geo.bit_y)
    held = near[:count] + from_across.astype(F32)
    for masks in reversed(line_masks(geo)):
        block = held.shape[0] // (len(masks) + 1)
        total = held[:block]
        for number, mask in enumerate(masks):
            part = held[(number + 1) * block : (number + 2) * block].astype(BF16)
            total = total + geo.permute(part, mask, mask).astype(F32)
        held = total
    return held[0]


def collect_quarters(geo, sums, dp_index):
    stacked = jnp.stack(sums)
    pieces = [lax.dynamic_index_in_dim(stacked, dp_index, 0, keepdims=False)]
    for offset in (1, 2, 3):
        piece = lax.dynamic_index_in_dim(stacked, dp_index ^ offset, 0, keepdims=False)
        mask = offset * geo.fsdp
        pieces.append(geo.permute(piece, mask, mask))
    return pieces


def sum_everywhere(geo, value):
    mask = 1
    while mask < geo.devices:
        value = value + geo.permute(value, mask, mask)
        mask *= 2
    return value


def tensor_sums(sums_ref, squares, flat, low, high, tensors):
    for t in tensors:

        @pl.when((low < STARTS[t + 1]) & (high > STARTS[t]))
        def _(t=t):
            inside = (flat >= STARTS[t]) & (flat < STARTS[t + 1])
            part = jnp.where(inside, squares, 0.0)
            sums_ref[t : t + 1, :] += jnp.sum(part, axis=0, keepdims=True)


def squares_kernel(geo, me_ref, *refs):
    sums_ref = refs[-1]
    sums_ref[...] = jnp.zeros((16, LANES), F32)
    span = 8 * max(t for t in range(1, 13) if geo.quarter // 8 % t == 0)
    dp_index = me_ref[1] * 2 + me_ref[2]
    for group in range(4):
        device = group * geo.fsdp + me_ref[3] * 2 + me_ref[4]
        share = geo.rows * LANES
        base = device * geo.rows
        first = base - lax.rem(base, 16) + dp_index * geo.quarter

        def body(i, _, group=group, base=base, first=first):
            r0 = pl.multiple_of(i * span, 8)
            value = refs[group][pl.ds(r0, span), :]
            lane = lax.broadcasted_iota(jnp.int32, (span, LANES), 1)
            row = lax.broadcasted_iota(jnp.int32, (span, LANES), 0)
            lifted = (first + r0 + row) * LANES + lane
            flat = jnp.where(lifted < SPLIT, lifted, lifted - LIFT)
            owned = (flat >= base * LANES) & (flat < base * LANES + share)
            low = (first + r0) * LANES - LIFT
            high = (first + r0 + span) * LANES
            squares = jnp.where(owned, value * value, 0.0)
            tensor_sums(sums_ref, squares, flat, low, high, (2,) + tuple(range(5, 13)))
            return 0

        lax.fori_loop(0, geo.quarter // span, body, 0)


def square_sums(geo, me, sums):
    return pl.pallas_call(
        partial(squares_kernel, geo),
        out_shape=jax.ShapeDtypeStruct((16, LANES), F32),
        in_specs=[smem()] + [vmem()] * 4,
        out_specs=vmem(),
        compiler_params=params_of(),
        name="square_sums",
    )(me, *sums)


def update_kernel(geo, me_ref, coef_ref, q0, q1, q2, q3, late_ref, p_ref, m_ref, v_ref, *outs):
    params_out, first_out, second_out, grad_ref = outs
    rows, quarter = geo.rows, geo.quarter
    base = me_ref[0] * rows
    shift = lax.rem(base, 16)
    dp_index = me_ref[1] * 2 + me_ref[2]
    margin = 128
    for offset, ref in enumerate((q0, q1, q2, q3)):
        to = pl.multiple_of(margin + (dp_index ^ offset) * quarter, 8)
        grad_ref[pl.ds(to, quarter), :] = ref[...]
    for row, count, at in ((0, HEAD_ROWS, 0), (TAIL_ROW, LATE_TAIL, HEAD_ROWS)):

        @pl.when((base < row + count) & (base + rows > row))
        def _(row=row, count=count, at=at):
            lane = lax.broadcasted_iota(jnp.int32, (count, LANES), 1)
            p_rows = lax.broadcasted_iota(jnp.int32, (count, LANES), 0) + row
            before = p_rows * LANES + lane < SPLIT
            to = jnp.clip(margin + shift + row - base, 0, margin + geo.slot)
            here = pl.ds(to, count)
            late = late_ref[at : at + count, :]
            grad_ref[here, :] = jnp.where(before, late, grad_ref[here, :])

    span = 64
    scale, first_fix, second_fix, rate = (coef_ref[i] for i in range(4))

    def body(i, _):
        r0 = jnp.minimum(i * span, rows - span)
        here = grad_ref[pl.ds(margin + shift + r0, span), :]
        below = grad_ref[pl.ds(margin + shift + r0 + 1, span), :]
        lane = lax.broadcasted_iota(jnp.int32, (span, LANES), 1)
        row = lax.broadcasted_iota(jnp.int32, (span, LANES), 0)
        flat = (base + r0 + row) * LANES + lane
        back = LANES - LIFT
        moved = jnp.where(lane < back, pltpu.roll(here, back, 1), pltpu.roll(below, back, 1))
        scaled = jnp.where(flat < SPLIT, here, moved) * scale
        at = pl.ds(r0, span)
        first_new = 0.9 * m_ref[at, :] + 0.1 * scaled
        second_new = 0.999 * v_ref[at, :] + 0.001 * scaled * scaled
        params = p_ref[at, :]
        update = first_new / first_fix / (jnp.sqrt(second_new / second_fix) + 1e-08) + 0.05 * params
        params_out[at, :] = params - rate * update
        first_out[at, :] = first_new
        second_out[at, :] = second_new
        return 0

    lax.fori_loop(0, -(-rows // span), body, 0)


def update_step(geo, me, coef, quarters, late, params, first, second):
    rows = jax.ShapeDtypeStruct((geo.rows, LANES), F32)
    return pl.pallas_call(
        partial(update_kernel, geo),
        out_shape=[rows, rows, rows],
        in_specs=[smem(), smem()] + [vmem()] * 8,
        out_specs=[vmem()] * 3,
        scratch_shapes=[pltpu.VMEM((geo.slot + 384, LANES), F32)],
        compiler_params=params_of(),
        name="moments_update",
    )(me, coef, *quarters, late, params, first, second)


def row_blocks(tokens):
    return tokens // 4 if tokens % 64 == 0 else tokens


def permute_in_kernel(rows_ref, patches_ref, cot_ref, x_ref, g_ref):
    arrivals = patches_ref.shape[0]
    lane = lax.broadcasted_iota(jnp.int32, (WP, arrivals), 1)
    pick = jnp.where(rows_ref[...] == lane, 1.0, 0.0).astype(BF16)
    x_ref[...] = nn(pick, patches_ref[...]).astype(BF16)
    g_ref[...] = nn(pick, cot_ref[...]).astype(BF16)


def permute_in(row_ids, patches, cotangent):
    tokens = row_ids.shape[0]
    whole = pl.BlockSpec(patches.shape, lambda i: (0, 0))
    part = pl.BlockSpec((WP, D), lambda i: (i, 0))
    shape = jax.ShapeDtypeStruct((tokens, D), BF16)
    return pl.pallas_call(
        permute_in_kernel,
        grid=(tokens // WP,),
        out_shape=[shape, shape],
        in_specs=[pl.BlockSpec((WP, 1), lambda i: (i, 0)), whole, whole],
        out_specs=[part, part],
        compiler_params=params_of(),
        cost_estimate=cost(4 * tokens * tokens * D, 8 * tokens * D),
        name="window_order",
    )(row_ids, patches, cotangent)


def permute_out_kernel(rows_ref, x_ref, out_ref):
    count = out_ref.shape[0]
    arrival = lax.broadcasted_iota(jnp.int32, (count, rows_ref.shape[1]), 0)
    pick = jnp.where(rows_ref[...] == arrival + pl.program_id(0) * count, 1.0, 0.0).astype(BF16)
    out_ref[...] = nn(pick, x_ref[...]).astype(BF16)


def permute_out(row_ids, values, arrivals):
    tokens = values.shape[0]
    block = 160 if arrivals % 160 == 0 else arrivals
    return pl.pallas_call(
        permute_out_kernel,
        grid=(arrivals // block,),
        out_shape=jax.ShapeDtypeStruct((arrivals, D), BF16),
        in_specs=[
            pl.BlockSpec((1, tokens), lambda i: (0, 0)),
            pl.BlockSpec((tokens, D), lambda i: (0, 0)),
        ],
        out_specs=pl.BlockSpec((block, D), lambda i: (i, 0)),
        compiler_params=params_of(),
        cost_estimate=cost(2 * tokens * arrivals * D, 4 * tokens * D),
        name="arrival_order",
    )(row_ids, values)


def normalized(x):
    center = x - jnp.mean(x, axis=-1, keepdims=True)
    spread = jnp.mean(center * center, axis=-1, keepdims=True)
    inverse = lax.rsqrt(spread + 1e-05)
    return center * inverse, inverse


def normalized_back(e, xhat, inverse):
    mean = jnp.mean(e, axis=-1, keepdims=True)
    along = jnp.mean(e * xhat, axis=-1, keepdims=True)
    return (e - mean - xhat * along) * inverse


def mix_kernel(x_ref, gain_ref, shift_ref, w_ref, b_ref, normed_ref, mixed_ref):
    step = pl.program_id(0)
    tokens = x_ref.shape[0]

    @pl.when(step == 0)
    def _():
        def body(i, _):
            rows = pl.ds(pl.multiple_of(i * 16, 16), 16)
            xhat, _ = normalized(x_ref[rows, :].astype(F32))
            normed_ref[rows, :] = (xhat * gain_ref[...] + shift_ref[...]).astype(BF16)
            return 0

        lax.fori_loop(0, tokens // 16, body, 0, unroll=4)

    mixed = nn(normed_ref[...], w_ref[...]) + b_ref[...]
    scale = jnp.where(step < D // w_ref.shape[1], F32(HEAD_DIM ** (-0.5)), F32(1.0))
    mixed_ref[...] = (mixed * scale).astype(BF16)


def mix(x, gain, shift, weight, bias):
    tokens = x.shape[0]
    width = 512
    rows = pl.BlockSpec((tokens, D), lambda j: (0, 0))
    vec = pl.BlockSpec((1, D), lambda j: (0, 0))
    return pl.pallas_call(
        mix_kernel,
        grid=(3 * D // width,),
        out_shape=[
            jax.ShapeDtypeStruct((tokens, D), BF16),
            jax.ShapeDtypeStruct((tokens, 3 * D), BF16),
        ],
        in_specs=[
            rows,
            vec,
            vec,
            pl.BlockSpec((D, width), lambda j: (0, j)),
            pl.BlockSpec((1, width), lambda j: (0, j)),
        ],
        out_specs=[rows, pl.BlockSpec((tokens, width), lambda j: (0, j))],
        compiler_params=params_of(),
        cost_estimate=cost(6 * tokens * D * D, 6 * D * D + 8 * tokens * D),
        name="mix_rows",
    )(x, gain, shift, weight, bias)


def bias_kernel(ids_ref, table_ref, out_ref):
    entries = table_ref.shape[1]

    def body(j, _):
        entry = lax.broadcasted_iota(jnp.int32, (entries, LANES), 0)
        pick = jnp.where(ids_ref[pl.ds(j, 1), :] == entry, 1.0, 0.0).astype(BF16)
        out_ref[:, pl.ds(j, 1), :] = nn(table_ref[...], pick).reshape(HEADS, 1, LANES)
        return 0

    lax.fori_loop(0, WT, body, 0, unroll=4)
    for j in range(WT, WP):
        out_ref[:, j : j + 1, :] = jnp.full((HEADS, 1, LANES), -1e30, F32)


def score_bias(ids, table):
    return pl.pallas_call(
        bias_kernel,
        out_shape=jax.ShapeDtypeStruct((HEADS, WP, LANES), F32),
        in_specs=[vmem(), vmem()],
        out_specs=vmem(),
        compiler_params=params_of(),
        cost_estimate=cost(2 * HEADS * WP * LANES * 384, 4 * HEADS * WP * LANES),
        name="score_bias",
    )(ids, table)


def bias_back_kernel(ids_ref, sums_ref, out_ref):
    entries = out_ref.shape[0]
    out_ref[...] = jnp.zeros(out_ref.shape, F32)

    def body(j, _):
        lane = lax.broadcasted_iota(jnp.int32, (HEADS, LANES), 1)
        row = jnp.where(lane < WT, sums_ref[:, pl.ds(j, 1), :].reshape(HEADS, LANES), 0.0)
        high = row.astype(BF16)
        rest = row - high.astype(F32)
        middle = rest.astype(BF16)
        low = (rest - middle.astype(F32)).astype(BF16)
        parts = jnp.concatenate([high, middle, low], axis=0)
        entry = lax.broadcasted_iota(jnp.int32, (entries, LANES), 0)
        pick = jnp.where(ids_ref[pl.ds(j, 1), :] == entry, 1.0, 0.0).astype(BF16)
        out_ref[...] += nt(pick, parts)
        return 0

    lax.fori_loop(0, WT, body, 0, unroll=4)


def score_bias_back(ids, sums, entries):
    parts = pl.pallas_call(
        bias_back_kernel,
        out_shape=jax.ShapeDtypeStruct((entries, 3 * HEADS), F32),
        in_specs=[vmem(), vmem()],
        out_specs=vmem(),
        compiler_params=params_of(),
        cost_estimate=cost(6 * HEADS * WP * LANES * 384, 4 * HEADS * WP * LANES),
        name="score_bias_back",
    )(ids, sums)
    return parts[:, :HEADS] + parts[:, HEADS : 2 * HEADS] + parts[:, 2 * HEADS :]


def pad_rows(x, rows):
    return jnp.concatenate([x, jnp.zeros((rows - x.shape[0], x.shape[1]), x.dtype)], axis=0)


def one_head(x, head):
    lane = lax.broadcasted_iota(jnp.int32, x.shape, 1)
    return jnp.where(lane // HEAD_DIM == head, x, jnp.zeros_like(x))


def by_head(x):
    return jnp.concatenate([one_head(x, head) for head in range(QUAD)], axis=0)


def attention_kernel(q_ref, k_ref, v_ref, bias_ref, out_ref, log_ref):
    def block(b, _):
        lanes = pl.ds(pl.multiple_of(b * LANES, LANES), LANES)
        queries = pad_rows(q_ref[:, lanes], LANES)
        scores = nt(by_head(k_ref[:, lanes]), queries)
        values = v_ref[:, lanes].astype(F32).T.astype(BF16)
        parts = []
        for head in range(QUAD):
            s = scores[head * WP : (head + 1) * WP] + bias_ref[b * QUAD + head]
            top = jnp.max(s, axis=0, keepdims=True)
            e = jnp.exp(s - top)
            total = jnp.sum(e, axis=0, keepdims=True)
            probs = (e * (1.0 / total)).astype(BF16)
            log_ref[0, pl.ds(b * QUAD + head, 1), :] = top + jnp.log(total)
            parts.append(nn(values[head * HEAD_DIM : (head + 1) * HEAD_DIM], probs))
        context = jnp.concatenate(parts, axis=0).T
        out_ref[:, lanes] = context[:WP].astype(BF16)
        return 0

    lax.fori_loop(0, HEADS // QUAD, block, 0, unroll=4)


def attention(mixed, bias):
    windows = mixed.shape[0] // WP

    def third(c):
        return pl.BlockSpec((WP, D), lambda i, c=c: (i, c))

    return pl.pallas_call(
        attention_kernel,
        grid=(windows,),
        out_shape=[
            jax.ShapeDtypeStruct((windows * WP, D), BF16),
            jax.ShapeDtypeStruct((windows, HEADS, LANES), F32),
        ],
        in_specs=[third(0), third(1), third(2), pl.BlockSpec(bias.shape, lambda i: (0, 0, 0))],
        out_specs=[third(0), pl.BlockSpec((1, HEADS, LANES), lambda i: (i, 0, 0))],
        compiler_params=params_of(),
        cost_estimate=cost(12e9, 8 * windows * WP * D, windows * HEADS * WP * LANES),
        name="attention",
    )(mixed, mixed, mixed, bias)


def attention_back_kernel(
    q_ref, k_ref, v_ref, g_ref, bias_ref, log_ref, out_ref, acc_ref, column_ref
):
    @pl.when(pl.program_id(0) == 0)
    def _():
        acc_ref[...] = jnp.zeros(acc_ref.shape, F32)
        column_ref[...] = jnp.zeros(column_ref.shape, F32)

    def put(third, b, value):
        lanes = pl.ds(pl.multiple_of(third * D + b * LANES, LANES), LANES)
        low = value.astype(BF16)
        out_ref[:, lanes] = low
        column_ref[0:1, lanes] += jnp.sum(low.astype(F32), axis=0, keepdims=True)

    def block(b, _):
        lanes = pl.ds(pl.multiple_of(b * LANES, LANES), LANES)
        queries = pad_rows(q_ref[:, lanes], LANES)
        grads = pad_rows(g_ref[:, lanes], LANES)
        keys = k_ref[:, lanes]
        scores = nt(by_head(keys), queries)
        probs_grads = nt(by_head(v_ref[:, lanes]), grads)
        keys_t = keys.astype(F32).T.astype(BF16)
        query_parts, probs_parts, score_parts = [], [], []
        for head in range(QUAD):
            span = slice(head * WP, (head + 1) * WP)
            s = scores[span] + bias_ref[b * QUAD + head]
            probs = jnp.exp(s - log_ref[0, pl.ds(b * QUAD + head, 1), :])
            probs_grad = probs_grads[span]
            along = jnp.sum(probs * probs_grad, axis=0, keepdims=True)
            score_grad = (probs * (probs_grad - along)).astype(BF16)
            acc_ref[b * QUAD + head] += score_grad.astype(F32)
            probs_parts.append(probs.astype(BF16))
            score_parts.append(score_grad)
            query_parts.append(nn(keys_t[head * HEAD_DIM : (head + 1) * HEAD_DIM], score_grad))
        put(2, b, nn(jnp.concatenate(probs_parts, axis=1), by_head(grads)))
        put(1, b, nn(jnp.concatenate(score_parts, axis=1), by_head(queries)))
        put(0, b, jnp.concatenate(query_parts, axis=0).T[:WP] * HEAD_DIM ** (-0.5))
        return 0

    lax.fori_loop(0, HEADS // QUAD, block, 0, unroll=4)


def attention_back(mixed, grads, bias, logs):
    windows = mixed.shape[0] // WP

    def third(c):
        return pl.BlockSpec((WP, D), lambda i, c=c: (i, c))

    fixed = pl.BlockSpec(bias.shape, lambda i: (0, 0, 0))
    return pl.pallas_call(
        attention_back_kernel,
        grid=(windows,),
        out_shape=[
            jax.ShapeDtypeStruct((windows * WP, 3 * D), BF16),
            jax.ShapeDtypeStruct(bias.shape, F32),
            jax.ShapeDtypeStruct((8, 3 * D), F32),
        ],
        in_specs=[
            third(0),
            third(1),
            third(2),
            third(0),
            fixed,
            pl.BlockSpec((1, HEADS, LANES), lambda i: (i, 0, 0)),
        ],
        out_specs=[
            pl.BlockSpec((WP, 3 * D), lambda i: (i, 0)),
            fixed,
            pl.BlockSpec((8, 3 * D), lambda i: (0, 0)),
        ],
        compiler_params=params_of(),
        cost_estimate=cost(25e9, 16 * windows * WP * D, windows * HEADS * WP * LANES),
        name="attention_back",
    )(mixed, mixed, mixed, grads, bias, logs)


def middle_kernel(x_ref, a_ref, w_ref, b_ref, gain_ref, shift_ref, middle_ref, second_ref):
    middle = x_ref[...].astype(F32) + nn(a_ref[...], w_ref[...]) + b_ref[...]
    middle_ref[...] = middle
    xhat, _ = normalized(middle)
    second_ref[...] = (xhat * gain_ref[...] + shift_ref[...]).astype(BF16)


def middle_rows(x, attended, weight, bias, gain, shift):
    tokens = x.shape[0]
    block = row_blocks(tokens)
    rows = pl.BlockSpec((block, D), lambda i: (i, 0))
    vec = pl.BlockSpec((1, D), lambda i: (0, 0))
    return pl.pallas_call(
        middle_kernel,
        grid=(tokens // block,),
        out_shape=[
            jax.ShapeDtypeStruct((tokens, D), F32),
            jax.ShapeDtypeStruct((tokens, D), BF16),
        ],
        in_specs=[rows, rows, pl.BlockSpec((D, D), lambda i: (0, 0)), vec, vec, vec],
        out_specs=[rows, rows],
        compiler_params=params_of(),
        cost_estimate=cost(2 * tokens * D * D, 10 * tokens * D),
        name="middle_rows",
    )(x, attended, weight, bias, gain, shift)


def mlp_up_kernel(geo, region, shared, steps, skip, me_ref, s_ref, g_ref, w_ref, b_ref, *refs):
    vec_ref, refs = refs[0], refs[1 + skip :]
    hidden_ref, slope_ref, refs = refs[0], refs[1], refs[2:]
    arrays = 4 * len(region.groups)
    outs = refs[:arrays]
    flat_ref, slot_ref, old_ref, sems, old_sem = refs[arrays:]
    step = pl.program_id(0)
    height = w_ref.shape[1]

    @pl.when(step == 0)
    def _():
        clear_rows(region, flat_ref)
        ((row, count),) = region.vectors

        def move(at, done, size):
            flat_ref[at : at + size, :] = vec_ref[done : done + size, :]

        copy_rows(region, flat_ref, row, count, move)

    tokens = s_ref.shape[0]
    block = row_blocks(tokens)
    for r in range(0, tokens, block):
        rows = slice(r, r + block)
        u = nn(s_ref[rows, :], w_ref[...]) + b_ref[...]
        below = 0.5 * (1.0 + lax.erf(u * F32(math.sqrt(0.5))))
        density = jnp.exp(-0.5 * u * u) * F32(1.0 / math.sqrt(2.0 * math.pi))
        hidden_ref[rows, :] = (u * below).astype(BF16)
        slope_ref[rows, :] = below + u * density
    left = hidden_ref[...].T
    for j in range(0, D, 512):
        store_columns(
            region, flat_ref, step * height, j // LANES, nn(left, g_ref[:, j : j + 512])
        )

    @pl.when(step == steps - 1)
    def _():
        emit_slots(
            geo, region, shared, me_ref, flat_ref, slot_ref, old_ref, sems, old_sem, outs
        )


def mlp_up(geo, region, me, second, grad_out, weight, bias, vector, slots, shared):
    tokens = second.shape[0]
    height = 256
    steps = FF // height
    rows = pl.BlockSpec((tokens, D), lambda k: (0, 0), pipeline_mode=pl.Buffered(1))
    columns = pl.BlockSpec((tokens, height), lambda k: (0, k))
    operands = [me, second, grad_out, weight, bias, vector]
    specs = [
        smem(),
        rows,
        rows,
        pl.BlockSpec((D, height), lambda k: (0, k)),
        pl.BlockSpec((1, height), lambda k: (0, k)),
        pl.BlockSpec(vector.shape, lambda k: (0, 0)),
    ]
    shapes, aliases, skip = with_slots(geo, region, slots, operands, specs)
    results = pl.pallas_call(
        partial(mlp_up_kernel, geo, region, shared, steps, skip),
        grid=(steps,),
        out_shape=[
            jax.ShapeDtypeStruct((tokens, FF), BF16),
            jax.ShapeDtypeStruct((tokens, FF), F32),
        ]
        + shapes,
        in_specs=specs,
        out_specs=[columns, columns] + [anywhere()] * len(shapes),
        scratch_shapes=emit_scratch(geo, region),
        input_output_aliases={key: value + 2 for key, value in aliases.items()},
        compiler_params=params_of(),
        cost_estimate=cost(4 * tokens * D * FF, 4 * D * FF + 6 * tokens * FF),
        name="mlp_up",
    )(*operands)
    return results[0], results[1], updated_slots(region, slots, results[2:])


def mlp_down_kernel(geo, region, shared, steps, skip, me_ref, *refs):
    (h_ref, slope_ref, s_ref, g_ref, up_ref, down_ref, m_ref, b_ref) = refs[:8]
    refs = refs[8 + skip :]
    result_ref, grad_ref, refs = refs[0], refs[1], refs[2:]
    arrays = 4 * len(region.groups)
    outs = refs[:arrays]
    flat_ref, slot_ref, old_ref, sems, old_sem, left_ref, sum_ref, pre_ref = refs[arrays:]
    step = pl.program_id(0)
    tokens = s_ref.shape[0]
    block = row_blocks(tokens)
    width = h_ref.shape[1]

    @pl.when(step == 0)
    def _():
        clear_rows(region, flat_ref)
        left_ref[...] = s_ref[...].T
        sum_ref[...] = jnp.zeros(sum_ref.shape, F32)
        grad_ref[...] = jnp.zeros(grad_ref.shape, F32)

    column = jnp.zeros((1, width), F32)
    for r in range(0, tokens, block):
        rows = slice(r, r + block)
        pre = (nt(g_ref[rows, :], down_ref[...]) * slope_ref[rows, :]).astype(BF16)
        pre_ref[rows, :] = pre
        column = column + jnp.sum(pre.astype(F32), axis=0, keepdims=True)
        sum_ref[rows, :] += nn(h_ref[rows, :], down_ref[...])
        grad_ref[rows, :] += nt(pre, up_ref[...])
    cols = width // LANES
    ((vec_row, _),) = region.vectors
    for c in range(cols):
        at = region.address(vec_row + step * cols + c)
        flat_ref[pl.ds(at, 1), :] = column[:, c * LANES : (c + 1) * LANES]
    for r in range(0, D, 256):
        store_columns(
            region, flat_ref, r, step * cols, nn(left_ref[r : r + 256, :], pre_ref[...])
        )

    @pl.when(step == steps - 1)
    def _():
        for r in range(0, tokens, block):
            rows = slice(r, r + block)
            result_ref[rows, :] = (sum_ref[rows, :] + m_ref[rows, :] + b_ref[...]).astype(BF16)
        emit_slots(
            geo, region, shared, me_ref, flat_ref, slot_ref, old_ref, sems, old_sem, outs
        )


def mlp_down(geo, region, me, hidden, slope, second, grad_out, up, down, middle, bias, slots, shared):
    tokens = second.shape[0]
    width = 256
    steps = FF // width
    rows = pl.BlockSpec((tokens, D), lambda k: (0, 0), pipeline_mode=pl.Buffered(1))
    columns = pl.BlockSpec((tokens, width), lambda k: (0, k))
    operands = [me, hidden, slope, second, grad_out, up, down, middle, bias]
    specs = [
        smem(),
        columns,
        columns,
        rows,
        rows,
        pl.BlockSpec((D, width), lambda k: (0, k)),
        pl.BlockSpec((width, D), lambda k: (k, 0)),
        rows,
        pl.BlockSpec((1, D), lambda k: (0, 0)),
    ]
    shapes, aliases, skip = with_slots(geo, region, slots, operands, specs)
    whole = pl.BlockSpec((tokens, D), lambda k: (0, 0))
    results = pl.pallas_call(
        partial(mlp_down_kernel, geo, region, shared, steps, skip),
        grid=(steps,),
        out_shape=[
            jax.ShapeDtypeStruct((tokens, D), BF16),
            jax.ShapeDtypeStruct((tokens, D), F32),
        ]
        + shapes,
        in_specs=specs,
        out_specs=[whole, whole] + [anywhere()] * len(shapes),
        scratch_shapes=emit_scratch(geo, region)
        + [
            pltpu.VMEM((D, tokens), BF16),
            pltpu.VMEM((tokens, D), F32),
            pltpu.VMEM((tokens, width), BF16),
        ],
        input_output_aliases={key: value + 2 for key, value in aliases.items()},
        compiler_params=params_of(),
        cost_estimate=cost(8 * tokens * D * FF, 6 * D * FF + 6 * tokens * FF),
        name="mlp_down",
    )(*operands)
    return results[0], results[1], updated_slots(region, slots, results[2:])


def middle_back_kernel(s_ref, m_ref, g_ref, gain_ref, w_ref, mg_ref, bg_ref, cg_ref, vec_ref):
    @pl.when(pl.program_id(0) == 0)
    def _():
        vec_ref[...] = jnp.zeros(vec_ref.shape, F32)

    grad = s_ref[...]
    xhat, inverse = normalized(m_ref[...])
    middle_grad = g_ref[...].astype(F32) + normalized_back(grad * gain_ref[...], xhat, inverse)
    branch = middle_grad.astype(BF16)
    mg_ref[...] = middle_grad
    bg_ref[...] = branch
    cg_ref[...] = nt(branch, w_ref[...]).astype(BF16)
    vec_ref[0:1, :] += jnp.sum(branch.astype(F32), axis=0, keepdims=True)
    vec_ref[1:2, :] += jnp.sum(grad * xhat, axis=0, keepdims=True)
    vec_ref[2:3, :] += jnp.sum(grad, axis=0, keepdims=True)


def middle_back(second_grad, middle, grad_out, gain, weight):
    tokens = middle.shape[0]
    block = row_blocks(tokens)
    rows = pl.BlockSpec((block, D), lambda i: (i, 0))
    low = jax.ShapeDtypeStruct((tokens, D), BF16)
    return pl.pallas_call(
        middle_back_kernel,
        grid=(tokens // block,),
        out_shape=[
            jax.ShapeDtypeStruct((tokens, D), F32),
            low,
            low,
            jax.ShapeDtypeStruct((8, D), F32),
        ],
        in_specs=[
            rows,
            rows,
            rows,
            pl.BlockSpec((1, D), lambda i: (0, 0)),
            pl.BlockSpec((D, D), lambda i: (0, 0)),
        ],
        out_specs=[rows, rows, rows, pl.BlockSpec((8, D), lambda i: (0, 0))],
        compiler_params=params_of(),
        cost_estimate=cost(2 * tokens * D * D, 18 * tokens * D),
        name="middle_back",
    )(second_grad, middle, grad_out, gain, weight)


def first_back_kernel(mixed_ref, w_ref, x_ref, mg_ref, gain_ref, out_ref, vec_ref):
    @pl.when(pl.program_id(0) == 0)
    def _():
        vec_ref[...] = jnp.zeros(vec_ref.shape, F32)

    grad = nt(mixed_ref[...], w_ref[...])
    xhat, inverse = normalized(x_ref[...].astype(F32))
    inner = normalized_back(grad * gain_ref[...], xhat, inverse)
    out_ref[...] = (mg_ref[...] + inner).astype(BF16)
    vec_ref[0:1, :] += jnp.sum(grad * xhat, axis=0, keepdims=True)
    vec_ref[1:2, :] += jnp.sum(grad, axis=0, keepdims=True)


def first_back(mixed_grad, weight, x, middle_grad, gain):
    tokens = x.shape[0]
    block = row_blocks(tokens)
    rows = pl.BlockSpec((block, D), lambda i: (i, 0))
    return pl.pallas_call(
        first_back_kernel,
        grid=(tokens // block,),
        out_shape=[
            jax.ShapeDtypeStruct((tokens, D), BF16),
            jax.ShapeDtypeStruct((8, D), F32),
        ],
        in_specs=[
            pl.BlockSpec((block, 3 * D), lambda i: (i, 0)),
            pl.BlockSpec((D, 3 * D), lambda i: (0, 0), pipeline_mode=pl.Buffered(1)),
            rows,
            rows,
            pl.BlockSpec((1, D), lambda i: (0, 0)),
        ],
        out_specs=[rows, pl.BlockSpec((8, D), lambda i: (0, 0))],
        compiler_params=params_of(),
        cost_estimate=cost(6 * tokens * D * D, 6 * D * D + 14 * tokens * D),
        name="first_back",
    )(mixed_grad, weight, x, middle_grad, gain)


def split_span(geo, row, depth, cols, block):
    group = (row // geo.rows) // geo.fsdp
    edge = (group + 1) * geo.fsdp * geo.rows // 16 * 16
    inside = max(0, (edge - row) // cols) // block * block
    return min(depth, inside)


def local(
    patches,
    cotangent,
    window_rows,
    rel_index,
    params,
    first_moment,
    second_moment,
    learn_rate,
    step_count,
):
    arrivals = patches.shape[0]
    windows = arrivals // WT
    geo = Geometry(lax.axis_size("dp"), lax.axis_size("fsdp"), params.shape[0])
    dp_index = lax.axis_index("dp")
    fsdp_index = lax.axis_index("fsdp")
    me = jnp.stack(
        [lax.axis_index(AXES), dp_index // 2, dp_index % 2, fsdp_index // 2, fsdp_index % 2]
    ).astype(jnp.int32)

    shard = params.reshape(geo.rows, LANES)
    if geo.spill:
        spill = lax.ppermute(
            shard[: round_up(geo.spill, 8)], AXES, [(geo.spill_from, geo.spill_to)]
        )
    else:
        spill = jnp.zeros((8, LANES), F32)
    share = prepare(geo, me, shard, spill).reshape(4, geo.quarter, LANES)
    pieces = spread_quarters(geo, share, dp_index)
    gathered = {group: gather_group(geo, pieces[group]) for group in range(4)}

    mix_matrix = (MIX_ROW, D, 3 * D // LANES)
    out_matrix = (OUT_ROW, D, D // LANES)
    expand_matrix = (EXPAND_ROW, D, FF // LANES)
    shrink_matrix = (SHRINK_ROW, FF, D // LANES)
    out_end = p_row(STARTS[6])
    expand_end = p_row(STARTS[10])
    shrink_end = p_row(STARTS[12])
    mix_vectors = [(0, 8), (8, 8), (TAIL_ROW, TABLE_ROW - TAIL_ROW), (TABLE_ROW, SPLIT_ROW - TABLE_ROW)]
    out_vectors = [(out_end + 8 * i, 8) for i in range(3)]
    expand_vectors = [(expand_end, FF // LANES)]
    shrink_vectors = [(shrink_end, 8)]

    first = Region(
        geo, 0, OUT_ROW, mix_matrix, mix_vectors, high=geo.spill_to if geo.spill else None
    )
    mix_weight, attn_gain, attn_shift, mix_bias, table_rows = unpack(geo, first, me, gathered)
    out_weight, out_bias, mlp_gain, mlp_shift = unpack(
        geo, Region(geo, OUT_ROW, EXPAND_ROW, out_matrix, out_vectors), me, gathered
    )

    def in_two(matrix, vectors, end, block):
        row, depth, cols = matrix
        edge = split_span(geo, row, depth, cols, block)
        weight = None
        if 0 < edge < depth:
            part = Region(geo, row, row + edge * cols, matrix, [], span=(0, edge))
            (weight,) = unpack(geo, part, me, gathered)
            rest = Region(geo, row + edge * cols, end, matrix, vectors, span=(edge, depth))
            return unpack(geo, rest, me, gathered, weight)
        return unpack(geo, Region(geo, row, end, matrix, vectors), me, gathered)

    expand_weight, expand_bias = in_two(expand_matrix, expand_vectors, SHRINK_ROW, 16)
    shrink_weight, shrink_bias = in_two(shrink_matrix, shrink_vectors, END_ROW, 64)

    def line_of(rows):
        return rows.reshape(1, -1)

    entries = round_up(TABLE_ROWS, 16)
    table = table_rows.reshape(-1)[: TABLE_ROWS * HEADS].reshape(TABLE_ROWS, HEADS).T
    table = jnp.pad(table, ((0, 0), (0, entries - TABLE_ROWS))).astype(BF16)
    ids = jnp.pad(rel_index.T, ((0, WP - WT), (0, LANES - WT)), constant_values=-1)
    bias = score_bias(ids, table)

    row_ids = jnp.pad(
        window_rows.reshape(windows, WT), ((0, 0), (0, WP - WT)), constant_values=-1
    ).reshape(windows * WP)
    x, grad_out = permute_in(row_ids[:, None], patches, cotangent)
    normed, mixed = mix(x, line_of(attn_gain), line_of(attn_shift), mix_weight, line_of(mix_bias))
    attended, logs = attention(mixed, bias)
    middle, second = middle_rows(
        x, attended, out_weight, line_of(out_bias), line_of(mlp_gain), line_of(mlp_shift)
    )

    shrink_region = Region(
        geo, SHRINK_ROW, END_ROW, shrink_matrix, shrink_vectors, high=geo.devices - 1
    )
    expand_region = Region(geo, EXPAND_ROW, SHRINK_ROW, expand_matrix, expand_vectors)
    out_region = Region(geo, OUT_ROW, EXPAND_ROW, out_matrix, out_vectors)
    mix_region = Region(geo, 0, TAIL_ROW, mix_matrix, [])
    slots = {}
    shrink_bias_grad = jnp.sum(grad_out.astype(F32), axis=0).reshape(-1, LANES)
    hidden, slope, slots = mlp_up(
        geo,
        shrink_region,
        me,
        second,
        grad_out,
        expand_weight,
        line_of(expand_bias),
        shrink_bias_grad,
        slots,
        False,
    )
    result, second_grad, slots = mlp_down(
        geo,
        expand_region,
        me,
        hidden,
        slope,
        second,
        grad_out,
        expand_weight,
        shrink_weight,
        middle,
        line_of(shrink_bias),
        slots,
        expand_region.high == shrink_region.low,
    )
    middle_grad, branch_grad, context_grad, middle_vec = middle_back(
        second_grad, middle, grad_out, line_of(mlp_gain), out_weight
    )
    slots = pack(
        geo,
        out_region,
        me,
        attended,
        branch_grad,
        [middle_vec[i].reshape(8, LANES) for i in range(3)],
        slots,
        out_region.high == expand_region.low,
    )
    mixed_grad, score_sums, column_sums = attention_back(mixed, context_grad, bias, logs)
    slots = pack(
        geo, mix_region, me, normed, mixed_grad, [], slots, mix_region.high == out_region.low
    )
    sums = [reduce_group(geo, *slots[group]) for group in (3, 2, 1, 0)][::-1]
    input_rows, first_vec = first_back(
        mixed_grad, mix_weight, x, middle_grad, line_of(attn_gain)
    )
    activations = permute_out(row_ids[None], result, arrivals)
    input_grad = permute_out(row_ids[None], input_rows, arrivals)

    table_grad = score_bias_back(ids, score_sums, entries)[:TABLE_ROWS]
    table_pad = (SPLIT_ROW - TABLE_ROW) * LANES - TABLE_ROWS * HEADS
    late = jnp.concatenate(
        [
            first_vec[:2].reshape(HEAD_ROWS, LANES),
            column_sums[0].reshape(-1, LANES),
            jnp.pad(table_grad.reshape(-1), (0, table_pad)).reshape(-1, LANES),
        ],
        axis=0,
    )
    late = jnp.pad(late, ((0, LATE_ROWS - late.shape[0]), (0, 0)))
    late = sum_everywhere(geo, late)

    squares = sum_everywhere(geo, jnp.sum(square_sums(geo, me, sums), axis=1)[None])
    scale = 1.0 / jnp.sqrt(F32(arrivals * geo.devices))
    edges = [0, 8, HEAD_ROWS, HEAD_ROWS + TABLE_ROW - TAIL_ROW, LATE_ROWS]
    late_squares = [jnp.sum(late[a:b] * late[a:b]) for a, b in zip(edges, edges[1:])]
    totals = [squares[0, t] for t in range(len(SHAPES))]
    for number, t in enumerate((0, 1, 3, 4)):
        totals[t] = late_squares[number]
    entry_counts = jnp.array([math.prod(shape) for shape in SHAPES], F32)
    group_rms = jnp.sqrt(jnp.stack(totals) * (scale * scale) / entry_counts)

    step_float = step_count.astype(F32)
    coef = jnp.stack(
        [
            scale,
            1.0 - jnp.power(F32(0.9), step_float),
            1.0 - jnp.power(F32(0.999), step_float),
            learn_rate,
        ]
    )
    params_new, first_new, second_new = update_step(
        geo,
        me,
        coef,
        collect_quarters(geo, sums, dp_index),
        late,
        shard,
        first_moment.reshape(geo.rows, LANES),
        second_moment.reshape(geo.rows, LANES),
    )
    return (
        activations,
        input_grad,
        group_rms,
        params_new.reshape(-1),
        first_new.reshape(-1),
        second_new.reshape(-1),
    )


def solution(mesh):
    placed = (
        P(AXES, None),
        P(AXES, None),
        P(AXES),
        P(),
        P(AXES),
        P(AXES),
        P(AXES),
        P(),
        P(),
    )
    return jax.shard_map(
        local,
        mesh=mesh,
        in_specs=placed,
        out_specs=(P(AXES, None), P(AXES, None), P(), P(AXES), P(AXES), P(AXES)),
        check_vma=False,
    )
```

time: 2360 us -> 694 us (0.29); the launches traced: 2320 us -> 691 us
  waiting for transfers between devices: 983 us -> 186 us
  local copies, waits for them, and re-layouts: 790 us -> 34.6 us
  Pallas kernels: 0 us -> 322 us
  other arithmetic: 277 us -> 32 us
  matrix products: 214 us -> 0 us
  starting transfers between devices: 0.08 us -> 114 us
  blocking collectives: 39.5 us -> 0 us
    unnamed x3 -> x0, waiting for transfers between devices: 714 us -> none
    concatenate x4, local copies, waits for them, and re-layouts: 432 us -> 2.93 us  [gather_group(): near = jnp.concatenate([held, across], axis=0)]
    pallas_call x0 -> x24, Pallas kernels: none -> 322 us  [the longest x1 60.8 us: mlp_down(): pl.pallas_call(partial(mlp_down_kernel, geo, region, shared, steps, skip)...]
    all_gather x1 -> x0, waiting for transfers between devices: 269 us -> none  [gather_params(): return lax.all_gather(shard_low, ('dp', 'fsdp'), axis=0, tiled=True)]
    dot_general x20 -> x0, matrix products: 214 us -> none  [the longest x4 69.9 us: contract_last(): lax.dot_general(left_side, right_side, (((1,), (1,)), ((), ())), preferre...]
    ppermute x0 -> x73, waiting for transfers between devices: none -> 186 us  [the longest x72 186 us: permute(): return lax.ppermute(value, AXES, pairs)]
    all_gather x1 -> x0, other arithmetic: 155 us -> none  [gather_params(): return lax.all_gather(shard_low, ('dp', 'fsdp'), axis=0, tiled=True)]
    reshape x14 -> x4, local copies, waits for them, and re-layouts: 126 us -> 0.19 us  [the longest x1 0.1 us: local(): table_grad.reshape(-1)]
  transfers between devices with their start and end apart: 2 -> 73, of which waited for: 2 -> 25; matrix products, arithmetic and copies ran while one was open for 2% -> 9% of each run, Pallas kernels for 0% -> 44%
where the time goes in v2:
time: 694 us; the launch traced here: 691 us
  Pallas kernels  322 us (46%)
  waiting for transfers between devices  186 us (27%)
  starting transfers between devices  114 us (16%)
  local copies, waits for them, and re-layouts  34.6 us (5%)
  other arithmetic  32 us (5%)
    ppermute x72, waiting for transfers between devices, permute(): return lax.ppermute(value, AXES, pairs)  186 us
    ppermute x72, starting transfers between devices, permute(): return lax.ppermute(value, AXES, pairs)  113 us
    pallas_call x1, Pallas kernels, mlp_down(): pl.pallas_call(partial(mlp_down_kernel, geo, region, shared, steps, skip)...  60.8 us
    pallas_call x6, Pallas kernels, unpack(): pl.pallas_call(partial(unpack_kernel, geo, region, 64 if region.cols <= 8...  48 us
    pallas_call x1, Pallas kernels, mlp_up(): pl.pallas_call(partial(mlp_up_kernel, geo, region, shared, steps, skip),...  37.5 us
    pallas_call x2, Pallas kernels, pack(): pl.pallas_call(partial(pack_kernel, geo, region, shared, steps, height, s...  30.3 us
    pallas_call x1, Pallas kernels, attention_back(): pl.pallas_call(attention_back_kernel, grid=(windows,), out_shape=[jax.Sha...  27 us
    pallas_call x1, Pallas kernels, first_back(): pl.pallas_call(first_back_kernel, grid=(tokens // block,), out_shape=[jax...  14.7 us
  transfers between devices with their start and end apart: 73, of which 25 were waited for; matrix products, arithmetic and copies ran while one was open for 9% of the time, Pallas kernels for 44%

profile of v2, /device:TPU:0, one launch (start us, length us, event | category | flops | bytes accessed | tf_op | source)
XLA Modules:
  0.0 691.1 jit_solution(5486209447642456459)
XLA Ops:
  34.8 9.5 %collective-permute-done.5 = bf16[1,792,128]{2,1,0:T(8,128)(2,1)S(1)} collective-permute-done((bf16[1,792,128]{2,1,0:T(8,128)(2,1)S(1)}, bf16[1,792,128]{2,1,0:T(8,128)(2,1)S(1)}, u32[]{:S(2)}, u32[]{:S(2)}) %collective-permute-start.5) | collective-permute-done | bytes 202784 | tf_op jit(solution)/shard_map/ppermute | solution.py:126
  55.2 10.9 %collective-permute-done.12 = bf16[1,792,128]{2,1,0:T(8,128)(2,1)S(1)} collective-permute-done((bf16[1,792,128]{2,1,0:T(8,128)(2,1)S(1)}, bf16[1,792,128]{2,1,0:T(8,128)(2,1)S(1)}, u32[]{:S(2)}, u32[]{:S(2)}) %collective-permute-start.12) | collective-permute-done | bytes 202784 | tf_op jit(solution)/shard_map/ppermute | solution.py:126
  100.0 11.7 %collective-permute-done.26 = bf16[1,792,128]{2,1,0:T(8,128)(2,1)S(1)} collective-permute-done((bf16[1,792,128]{2,1,0:T(8,128)(2,1)S(1)}, bf16[1,792,128]{2,1,0:T(8,128)(2,1)S(1)}, u32[]{:S(2)}, u32[]{:S(2)}) %collective-permute-start.26) | collective-permute-done | bytes 202784 | tf_op jit(solution)/shard_map/ppermute | solution.py:126
  119.8 13.0 %collective-permute-done.28 = bf16[4,792,128]{2,1,0:T(8,128)(2,1)S(1)} collective-permute-done((bf16[4,792,128]{2,1,0:T(8,128)(2,1)S(1)}, bf16[4,792,128]{2,1,0:T(8,128)(2,1)S(1)}, u32[]{:S(2)}, u32[]{:S(2)}) %collective-permute-start.28) | collective-permute-done | bytes 811040 | tf_op jit(solution)/shard_map/ppermute | solution.py:126
  136.7 9.1 %window_order.1 = (bf16[832,1024]{1,0:T(8,128)(2,1)}, bf16[832,1024]{1,0:T(8,128)(2,1)}) custom-call(s32[832,1]{1,0:T(8,128)} %broadcast_in_dim_reshape.9.rows_ref, bf16[800,1024]{1,0:T(8,128)(2,1)} %patches_ref.1, bf16[800,1024]{1,0:T(8,128)(2,1)} %cot_ref.1), custom_call_target="tpu_custom_call" | custom-call | flops 2835349504 | bytes 6815744 | tf_op jit(solution)/shard_map/window_order/pallas_call | solution.py:751
  149.8 10.3 %unpack_weights.6 = (bf16[1024,3072]{1,0:T(8,128)(2,1)}, f32[8,128]{1,0:T(8,128)}, f32[8,128]{1,0:T(8,128)}, f32[24,128]{1,0:T(8,128)}, f32[91,128]{1,0:T(8,128)}) custom-call(s32[5]{0:T(128)} %stack.66.me_ref, bf16[8,792,128]{2,1,0:T(8,128)(2,1)} %constant_dynamic-update-slice_fusion.refs_0_, bf16[8,792,128]{2,1,0:T(8,128)(2,1)} %collective-permute-done.8.refs_1_, ...), custom_call_target="tpu_custom_call" | custom-call | bytes 25165824 | tf_op jit(solution)/shard_map/unpack_weights/pallas_call | solution.py:347
  169.4 13.0 %mix_rows.1 = (bf16[832,1024]{1,0:T(8,128)(2,1)}, bf16[832,3072]{1,0:T(8,128)(2,1)}) custom-call(bf16[832,1024]{1,0:T(8,128)(2,1)} %get-tuple-element.67.x_ref, f32[1,1024]{1,0:T(1,128)} %bitcast.101, f32[1,1024]{1,0:T(1,128)} %bitcast.104, bf16[1024,3072]{1,0:T(8,128)(2,1)} %get-tuple-element.70.w_ref, f32[1,3072]{1,0:T(1,128)} %bitcast.100), custom_call_target="tpu_custom_call" | custom-call | flops 5234491392 | bytes 13107200 | tf_op jit(solution)/shard_map/mix_rows/pallas_call | solution.py:825
  183.0 13.6 %attention.1 = (bf16[832,1024]{1,0:T(8,128)(2,1)}, f32[8,32,128]{2,1,0:T(8,128)}) custom-call(bf16[832,3072]{1,0:T(8,128)(2,1)} %get-tuple-element.72.q_ref.k_ref.v_ref, bf16[832,3072]{1,0:T(8,128)(2,1)} %get-tuple-element.72.q_ref.k_ref.v_ref, bf16[832,3072]{1,0:T(8,128)(2,1)} %get-tuple-element.72.q_ref.k_ref.v_ref, f32[32,104,128]{2,1,0:T(8,128)} %score_bias.1.bias_ref), custom_call_target="tpu_custom_call" | custom-call | flops 12000000000 | bytes 6815744 | tf_op jit(solution)/shard_map/attention/pallas_call | solution.py:946
  225.5 37.5 %mlp_up.1 = (bf16[832,4096]{1,0:T(8,128)(2,1)}, f32[832,4096]{1,0:T(8,128)}, bf16[8,792,128]{2,1,0:T(8,128)(2,1)}, bf16[8,792,128]{2,1,0:T(8,128)(2,1)}, bf16[8,...) custom-call(s32[5]{0:T(128)} %stack.66.me_ref, ...), custom_call_target="tpu_custom_call" | custom-call | flops 13958643712 | bytes 37224448 | tf_op jit(solution)/shard_map/mlp_up/pallas_call | solution.py:1121
  269.4 10.6 %unpack_weights.11 = (bf16[4096,1024]{1,0:T(8,128)(2,1)}, f32[8,128]{1,0:T(8,128)}) custom-call(s32[5]{0:T(128)} %stack.66.me_ref, bf16[8,792,128]{2,1,0:T(8,128)(2,1)} %constant_dynamic-update-slice_fusion.10.refs_4_.refs_0_, bf16[8,792,128]{2,1,0:T(8,128)(2,1)} %collective-permute-done.22.refs_5_.refs_1_, ...), custom_call_target="tpu_custom_call", output_to_operand_aliasing={{0}: (9, {})} | custom-call | bytes 25165824 | tf_op jit(solution)/shard_map/unpack_weights/pallas_call | solution.py:347
  280.0 60.8 %mlp_down.1 = (bf16[832,1024]{1,0:T(8,128)(2,1)}, f32[832,1024]{1,0:T(8,128)}, bf16[8,792,128]{2,1,0:T(8,128)(2,1)}, bf16[8,792,128]{2,1,0:T(8,128)(2,1)}, bf16[...) custom-call(s32[5]{0:T(128)} %stack.66.me_ref, ...), custom_call_target="tpu_custom_call", output_to_operand_aliasing={{6}: (9, {}), {7}: (10, {}), {8}: (11, {}), {9}: (12, {})} | custom-call | flops 27917287424 | bytes 45613056 | tf_op jit(solution)/shard_map/mlp_down/pallas_call | solution.py:1207
  340.8 9.1 %middle_back.1 = (f32[832,1024]{1,0:T(8,128)}, bf16[832,1024]{1,0:T(8,128)(2,1)}, bf16[832,1024]{1,0:T(8,128)(2,1)}, f32[8,1024]{1,0:T(8,128)}) custom-call(f32[832,1024]{1,0:T(8,128)} %get-tuple-element.93.s_ref, f32[832,1024]{1,0:T(8,128)} %get-tuple-element.86.refs_6_.m_ref, bf16[832,1024]{1,0:T(8,128)(2,1)} %get-tuple-element.80.g_ref.refs_3_, ...), custom_call_target="tpu_custom_call" | custom-call | flops 1744830464 | bytes 15335424 | tf_op jit(solution)/shard_map/middle_back/pallas_call | solution.py:1253
  349.9 27.0 %attention_back.1 = (bf16[832,3072]{1,0:T(8,128)(2,1)}, f32[32,104,128]{2,1,0:T(8,128)}, f32[8,3072]{1,0:T(8,128)}) custom-call(bf16[832,3072]{1,0:T(8,128)(2,1)} %get-tuple-element.72.q_ref.k_ref.v_ref, bf16[832,3072]{1,0:T(8,128)(2,1)} %get-tuple-element.72.q_ref.k_ref.v_ref, bf16[832,3072]{1,0:T(8,128)(2,1)} %get-tuple-element.72.q_ref.k_ref.v_ref, ...), custom_call_target="tpu_custom_call" | custom-call | flops 24999999488 | bytes 13631488 | tf_op jit(solution)/shard_map/attention_back/pallas_call | solution.py:1010
  376.9 13.2 %score_bias_back.1 = f32[368,96]{1,0:T(8,128)} custom-call(s32[104,128]{1,0:T(8,128)} %pad.22.ids_ref, f32[32,104,128]{2,1,0:T(8,128)} %get-tuple-element.101.sums_ref), custom_call_target="tpu_custom_call" | custom-call | flops 981467136 | bytes 1703936 | tf_op jit(solution)/shard_map/score_bias_back/pallas_call | solution.py:893
  391.4 14.7 %first_back.1 = (bf16[832,1024]{1,0:T(8,128)(2,1)}, f32[8,1024]{1,0:T(8,128)}) custom-call(bf16[832,3072]{1,0:T(8,128)(2,1)} %get-tuple-element.96.mixed_ref.b_ref, bf16[1024,3072]{1,0:T(8,128)(2,1)} %get-tuple-element.70.w_ref, bf16[832,1024]{1,0:T(8,128)(2,1)} %get-tuple-element.67.x_ref, f32[832,1024]{1,0:T(8,128)} %get-tuple-element.97.mg_ref, ...), custom_call_target="tpu_custom_call" | custom-call | flops 5234491392 | bytes 18219008 | tf_op jit(solution)/shard_map/first_back/pallas_call | solution.py:1293
  424.2 10.2 %weight_grad_pack.3 = (bf16[8,792,128]{2,1,0:T(8,128)(2,1)}, bf16[8,792,128]{2,1,0:T(8,128)(2,1)}, bf16[8,792,128]{2,1,0:T(8,128)(2,1)}, bf16[8,792,128]{2,1,0:T(8,128)(2,1)}) custom-call(s32[5]{0:T(128)} %stack.66.me_ref, bf16[832,1024]{1,0:T(8,128)(2,1)} %get-tuple-element.74.a_ref, ...), custom_call_target="tpu_custom_call", output_to_operand_aliasing={{0}: (6, {}), {1}: (7, {}), {2}: (8, {}), {3}: (9, {})} | custom-call | flops 1744830464 | bytes 2097152 | tf_op jit(solution)/shard_map/weight_grad_pack/pallas_call | solution.py:543
  435.8 20.2 %weight_grad_pack.2 = (bf16[8,792,128]{2,1,0:T(8,128)(2,1)}, bf16[8,792,128]{2,1,0:T(8,128)(2,1)}, bf16[8,792,128]{2,1,0:T(8,128)(2,1)}, bf16[8,792,128]{2,1,0:T(8,128)(2,1)}) custom-call(s32[5]{0:T(128)} %stack.66.me_ref, bf16[832,1024]{1,0:T(8,128)(2,1)} %get-tuple-element.102.a_ref, bf16[832,3072]{1,0:T(8,128)(2,1)} %get-tuple-element.96.mixed_ref.b_ref), custom_call_target="tpu_custom_call" | custom-call | flops 5234491392 | bytes 6291456 | tf_op jit(solution)/shard_map/weight_grad_pack/pallas_call | solution.py:543
  503.1 27.9 %collective-permute-done.46 = bf16[8,792,128]{2,1,0:T(8,128)(2,1)} collective-permute-done((bf16[8,792,128]{2,1,0:T(8,128)(2,1)}, bf16[8,792,128]{2,1,0:T(8,128)(2,1)}, u32[]{:S(2)}, u32[]{:S(2)}) %collective-permute-start.46) | collective-permute-done | bytes 1622048 | tf_op jit(solution)/shard_map/ppermute | solution.py:126
  535.0 24.2 %collective-permute-done.39 = bf16[8,792,128]{2,1,0:T(8,128)(2,1)} collective-permute-done((bf16[8,792,128]{2,1,0:T(8,128)(2,1)}, bf16[8,792,128]{2,1,0:T(8,128)(2,1)}, u32[]{:S(2)}, u32[]{:S(2)}) %collective-permute-start.39) | collective-permute-done | bytes 1622048 | tf_op jit(solution)/shard_map/ppermute | solution.py:126
  583.0 14.2 %collective-permute-start.49 = (bf16[1,792,128]{2,1,0:T(8,128)(2,1)S(1)}, bf16[1,792,128]{2,1,0:T(8,128)(2,1)S(1)}, u32[]{:S(2)}, u32[]{:S(2)}) collective-permute-start(bf16[1,792,128]{2,1,0:T(8,128)(2,1)S(1)} %get-tuple-element.158), channel_id=1, source_target_pairs={{0,4},{1,5},{2,6},{3,7},{4,0},{5,1},{6,2},{7,3},{8,12},{9,13},{10,... | collective-permute-start | bytes 608264 | tf_op jit(solution)/shard_map/ppermute | solution.py:126
  599.1 9.7 %collective-permute-done.56 = bf16[1,792,128]{2,1,0:T(8,128)(2,1)S(1)} collective-permute-done((bf16[1,792,128]{2,1,0:T(8,128)(2,1)S(1)}, bf16[1,792,128]{2,1,0:T(8,128)(2,1)S(1)}, u32[]{:S(2)}, u32[]{:S(2)}) %collective-permute-start.56) | collective-permute-done | bytes 202784 | tf_op jit(solution)/shard_map/ppermute | solution.py:126
  616.5 9.9 %collective-permute-done.49 = bf16[1,792,128]{2,1,0:T(8,128)(2,1)S(1)} collective-permute-done((bf16[1,792,128]{2,1,0:T(8,128)(2,1)S(1)}, bf16[1,792,128]{2,1,0:T(8,128)(2,1)S(1)}, u32[]{:S(2)}, u32[]{:S(2)}) %collective-permute-start.49) | collective-permute-done | bytes 202784 | tf_op jit(solution)/shard_map/ppermute | solution.py:126
  657.2 12.4 %collective-permute-done.69 = f32[1,16]{1,0:T(1,128)S(1)} collective-permute-done((f32[1,16]{1,0:T(1,128)S(1)}, f32[1,16]{1,0:T(1,128)S(1)}, u32[]{:S(2)}, u32[]{:S(2)}) %collective-permute-start.69) | collective-permute-done | bytes 96 | tf_op jit(solution)/shard_map/ppermute | solution.py:126
  680.0 11.0 %moments_update.1 = (f32[3081,128]{1,0:T(8,128)}, f32[3081,128]{1,0:T(8,128)}, f32[3081,128]{1,0:T(8,128)}) custom-call(s32[5]{0:T(128)} %stack.66.me_ref, f32[4]{0:T(128)} %pad_maximum_fusion.6.coef_ref, f32[792,128]{1,0:T(8,128)} %get-tuple-element.149.q0, f32[792,128]{1,0:T(8,128)} %copy-done.14, f32[792,128]{1,0:T(8,128)} %copy-done.15, ...), custom_call_target="tpu_custom_call" | custom-call | tf_op jit(solution)/shard_map/moments_update/pallas_call | solution.py:723
  (277 shorter events, 284.7 us)
Async XLA Ops:
  69.4 47.9 %collective-permute-start.8 = (bf16[8,792,128]{2,1,0:T(8,128)(2,1)}, bf16[8,792,128]{2,1,0:T(8,128)(2,1)}, u32[]{:S(2)}, u32[]{:S(2)}) collective-permute-start(bf16[8,792,128]{2,1,0:T(8,128)(2,1)} %constant_dynamic-update-slice_fusion.refs_0_), channel_id=1, source_target_pairs={{0,1},{1,0},{2,3},{3,2},{4,5},{5,4},{6,7},{7,6},{8,24},{9,25},{10,... | collective-permute-start | bytes 4866056 | tf_op jit(solution)/shard_map/ppermute | solution.py:126
  84.3 49.5 %collective-permute-start.15 = (bf16[8,792,128]{2,1,0:T(8,128)(2,1)S(1)}, bf16[8,792,128]{2,1,0:T(8,128)(2,1)}, u32[]{:S(2)}, u32[]{:S(2)}) collective-permute-start(bf16[8,792,128]{2,1,0:T(8,128)(2,1)S(1)} %constant_dynamic-update-slice_fusion.5.refs_0_), channel_id=1, source_target_pairs={{0,1},{1,0},{2,3},{3,2},{4,5},{5,4},{6,7},{7,6},{8,24},{9,25},{10,... | collective-permute-start | bytes 4866056 | tf_op jit(solution)/shard_map/ppermute | solution.py:126
  117.2 32.0 %collective-permute-start.9 = (bf16[8,792,128]{2,1,0:T(8,128)(2,1)}, bf16[8,792,128]{2,1,0:T(8,128)(2,1)}, u32[]{:S(2)}, u32[]{:S(2)}) collective-permute-start(bf16[8,792,128]{2,1,0:T(8,128)(2,1)} %constant_dynamic-update-slice_fusion.refs_0_), channel_id=1, source_target_pairs={{0,8},{1,9},{2,10},{3,11},{4,12},{5,13},{6,14},{7,15},{8,0},{9,1},... | collective-permute-start | bytes 4866056 | tf_op jit(solution)/shard_map/ppermute | solution.py:126
  117.3 32.1 %collective-permute-start.10 = (bf16[8,792,128]{2,1,0:T(8,128)(2,1)}, bf16[8,792,128]{2,1,0:T(8,128)(2,1)}, u32[]{:S(2)}, u32[]{:S(2)}) collective-permute-start(bf16[8,792,128]{2,1,0:T(8,128)(2,1)} %collective-permute-done.8.refs_1_), channel_id=1, source_target_pairs={{0,8},{1,9},{2,10},{3,11},{4,12},{5,13},{6,14},{7,15},{8,0},{9,1},... | collective-permute-start | bytes 4866056 | tf_op jit(solution)/shard_map/ppermute | solution.py:126
  132.9 49.6 %collective-permute-start.16 = (bf16[8,792,128]{2,1,0:T(8,128)(2,1)S(1)}, bf16[8,792,128]{2,1,0:T(8,128)(2,1)}, u32[]{:S(2)}, u32[]{:S(2)}) collective-permute-start(bf16[8,792,128]{2,1,0:T(8,128)(2,1)S(1)} %constant_dynamic-update-slice_fusion.5.refs_0_), channel_id=1, source_target_pairs={{0,8},{1,9},{2,10},{3,11},{4,12},{5,13},{6,14},{7,15},{8,0},{9,1},... | collective-permute-start | bytes 4866056 | tf_op jit(solution)/shard_map/ppermute | solution.py:126
  133.8 48.7 %collective-permute-start.29 = (bf16[8,792,128]{2,1,0:T(8,128)(2,1)}, bf16[8,792,128]{2,1,0:T(8,128)(2,1)}, u32[]{:S(2)}, u32[]{:S(2)}) collective-permute-start(bf16[8,792,128]{2,1,0:T(8,128)(2,1)} %constant_dynamic-update-slice_fusion.15.refs_4_), channel_id=1, source_target_pairs={{0,1},{1,0},{2,3},{3,2},{4,5},{5,4},{6,7},{7,6},{8,24},{9,25},{10,... | collective-permute-start | bytes 4866056 | tf_op jit(solution)/shard_map/ppermute | solution.py:126
  148.1 61.5 %collective-permute-start.23 = (bf16[8,792,128]{2,1,0:T(8,128)(2,1)}, bf16[8,792,128]{2,1,0:T(8,128)(2,1)}, u32[]{:S(2)}, u32[]{:S(2)}) collective-permute-start(bf16[8,792,128]{2,1,0:T(8,128)(2,1)} %constant_dynamic-update-slice_fusion.10.refs_4_.refs_0_), channel_id=1, source_target_pairs={{0,8},{1,9},{2,10},{3,11},{4,12},{5,13},{6,14},{7,15},{8,0},{9,1},... | collective-permute-start | bytes 4866056 | tf_op jit(solution)/shard_map/ppermute | solution.py:126
  149.3 47.3 %collective-permute-start.17 = (bf16[8,792,128]{2,1,0:T(8,128)(2,1)}, bf16[8,792,128]{2,1,0:T(8,128)(2,1)}, u32[]{:S(2)}, u32[]{:S(2)}) collective-permute-start(bf16[8,792,128]{2,1,0:T(8,128)(2,1)} %collective-permute-done.15.refs_1_), channel_id=1, source_target_pairs={{0,8},{1,9},{2,10},{3,11},{4,12},{5,13},{6,14},{7,15},{8,0},{9,1},... | collective-permute-start | bytes 4866056 | tf_op jit(solution)/shard_map/ppermute | solution.py:126
  149.3 60.3 %collective-permute-start.24 = (bf16[8,792,128]{2,1,0:T(8,128)(2,1)}, bf16[8,792,128]{2,1,0:T(8,128)(2,1)}, u32[]{:S(2)}, u32[]{:S(2)}) collective-permute-start(bf16[8,792,128]{2,1,0:T(8,128)(2,1)} %collective-permute-done.22.refs_5_.refs_1_), channel_id=1, source_target_pairs={{0,8},{1,9},{2,10},{3,11},{4,12},{5,13},{6,14},{7,15},{8,0},{9,1},... | collective-permute-start | bytes 4866056 | tf_op jit(solution)/shard_map/ppermute | solution.py:126
  182.5 85.7 %collective-permute-start.30 = (bf16[8,792,128]{2,1,0:T(8,128)(2,1)}, bf16[8,792,128]{2,1,0:T(8,128)(2,1)S(1)}, u32[]{:S(2)}, u32[]{:S(2)}) collective-permute-start(bf16[8,792,128]{2,1,0:T(8,128)(2,1)} %constant_dynamic-update-slice_fusion.15.refs_4_), channel_id=1, source_target_pairs={{0,8},{1,9},{2,10},{3,11},{4,12},{5,13},{6,14},{7,15},{8,0},{9,1},... | collective-permute-start | bytes 4866056 | tf_op jit(solution)/shard_map/ppermute | solution.py:126
  182.5 85.6 %collective-permute-start.31 = (bf16[8,792,128]{2,1,0:T(8,128)(2,1)}, bf16[8,792,128]{2,1,0:T(8,128)(2,1)}, u32[]{:S(2)}, u32[]{:S(2)}) collective-permute-start(bf16[8,792,128]{2,1,0:T(8,128)(2,1)} %collective-permute-done.29.refs_5_), channel_id=1, source_target_pairs={{0,8},{1,9},{2,10},{3,11},{4,12},{5,13},{6,14},{7,15},{8,0},{9,1},... | collective-permute-start | bytes 4866056 | tf_op jit(solution)/shard_map/ppermute | solution.py:126
  263.0 193.1 %collective-permute-start.59 = (bf16[8,792,128]{2,1,0:T(8,128)(2,1)}, bf16[8,792,128]{2,1,0:T(8,128)(2,1)}, u32[]{:S(2)}, u32[]{:S(2)}) collective-permute-start(bf16[8,792,128]{2,1,0:T(8,128)(2,1)} %get-tuple-element.124), channel_id=1, source_target_pairs={{0,8},{1,9},{2,10},{3,11},{4,12},{5,13},{6,14},{7,15},{8,0},{9,1},... | collective-permute-start | bytes 4866056 | tf_op jit(solution)/shard_map/ppermute | solution.py:126
  410.6 49.1 %collective-permute-start.52 = (bf16[8,792,128]{2,1,0:T(8,128)(2,1)}, bf16[8,792,128]{2,1,0:T(8,128)(2,1)}, u32[]{:S(2)}, u32[]{:S(2)}) collective-permute-start(bf16[8,792,128]{2,1,0:T(8,128)(2,1)} %get-tuple-element.120), channel_id=1, source_target_pairs={{0,8},{1,9},{2,10},{3,11},{4,12},{5,13},{6,14},{7,15},{8,0},{9,1},... | collective-permute-start | bytes 4866056 | tf_op jit(solution)/shard_map/ppermute | solution.py:126
  416.5 54.7 %collective-permute-start.58 = (bf16[8,792,128]{2,1,0:T(8,128)(2,1)}, bf16[8,792,128]{2,1,0:T(8,128)(2,1)}, u32[]{:S(2)}, u32[]{:S(2)}) collective-permute-start(bf16[8,792,128]{2,1,0:T(8,128)(2,1)} %get-tuple-element.122), channel_id=1, source_target_pairs={{0,8},{1,9},{2,10},{3,11},{4,12},{5,13},{6,14},{7,15},{8,0},{9,1},... | collective-permute-start | bytes 4866056 | tf_op jit(solution)/shard_map/ppermute | solution.py:126
  434.4 32.2 %collective-permute-start.45 = (bf16[8,792,128]{2,1,0:T(8,128)(2,1)}, bf16[8,792,128]{2,1,0:T(8,128)(2,1)}, u32[]{:S(2)}, u32[]{:S(2)}) collective-permute-start(bf16[8,792,128]{2,1,0:T(8,128)(2,1)} %get-tuple-element.116), channel_id=1, source_target_pairs={{0,8},{1,9},{2,10},{3,11},{4,12},{5,13},{6,14},{7,15},{8,0},{9,1},... | collective-permute-start | bytes 4866056 | tf_op jit(solution)/shard_map/ppermute | solution.py:126
  466.5 31.8 %collective-permute-start.53 = (bf16[8,792,128]{2,1,0:T(8,128)(2,1)}, bf16[8,792,128]{2,1,0:T(8,128)(2,1)}, u32[]{:S(2)}, u32[]{:S(2)}) collective-permute-start(bf16[8,792,128]{2,1,0:T(8,128)(2,1)} %add_convert_fusion.1), channel_id=1, source_target_pairs={{0,1},{1,0},{2,3},{3,2},{4,5},{5,4},{6,7},{7,6},{8,24},{9,25},{10,... | collective-permute-start | bytes 4866056 | tf_op jit(solution)/shard_map/ppermute | solution.py:126
  471.2 59.8 %collective-permute-start.46 = (bf16[8,792,128]{2,1,0:T(8,128)(2,1)}, bf16[8,792,128]{2,1,0:T(8,128)(2,1)}, u32[]{:S(2)}, u32[]{:S(2)}) collective-permute-start(bf16[8,792,128]{2,1,0:T(8,128)(2,1)} %add_convert_fusion.2), channel_id=1, source_target_pairs={{0,1},{1,0},{2,3},{3,2},{4,5},{5,4},{6,7},{7,6},{8,24},{9,25},{10,... | collective-permute-start | bytes 4866056 | tf_op jit(solution)/shard_map/ppermute | solution.py:126
  481.5 53.5 %collective-permute-start.37 = (bf16[8,792,128]{2,1,0:T(8,128)(2,1)}, bf16[8,792,128]{2,1,0:T(8,128)(2,1)}, u32[]{:S(2)}, u32[]{:S(2)}) collective-permute-start(bf16[8,792,128]{2,1,0:T(8,128)(2,1)} %get-tuple-element.104), channel_id=1, source_target_pairs={{0,8},{1,9},{2,10},{3,11},{4,12},{5,13},{6,14},{7,15},{8,0},{9,1},... | collective-permute-start | bytes 4866056 | tf_op jit(solution)/shard_map/ppermute | solution.py:126
  481.5 77.7 %collective-permute-start.39 = (bf16[8,792,128]{2,1,0:T(8,128)(2,1)}, bf16[8,792,128]{2,1,0:T(8,128)(2,1)}, u32[]{:S(2)}, u32[]{:S(2)}) collective-permute-start(bf16[8,792,128]{2,1,0:T(8,128)(2,1)} %add_convert_fusion.3), channel_id=1, source_target_pairs={{0,1},{1,0},{2,3},{3,2},{4,5},{5,4},{6,7},{7,6},{8,24},{9,25},{10,... | collective-permute-start | bytes 4866056 | tf_op jit(solution)/shard_map/ppermute | solution.py:126
  498.4 64.7 %collective-permute-start.61 = (bf16[4,792,128]{2,1,0:T(8,128)(2,1)S(1)}, bf16[4,792,128]{2,1,0:T(8,128)(2,1)S(1)}, u32[]{:S(2)}, u32[]{:S(2)}) collective-permute-start(bf16[4,792,128]{2,1,0:T(8,128)(2,1)S(1)} %slice.310), channel_id=1, source_target_pairs={{0,16},{1,17},{2,18},{3,19},{4,20},{5,21},{6,22},{7,23},{8,9},{9,8... | collective-permute-start | bytes 2433032 | tf_op jit(solution)/shard_map/ppermute | solution.py:126
  502.1 63.9 %collective-permute-start.54 = (bf16[4,792,128]{2,1,0:T(8,128)(2,1)S(1)}, bf16[4,792,128]{2,1,0:T(8,128)(2,1)S(1)}, u32[]{:S(2)}, u32[]{:S(2)}) collective-permute-start(bf16[4,792,128]{2,1,0:T(8,128)(2,1)S(1)} %slice.311), channel_id=1, source_target_pairs={{0,16},{1,17},{2,18},{3,19},{4,20},{5,21},{6,22},{7,23},{8,9},{9,8... | collective-permute-start | bytes 2433032 | tf_op jit(solution)/shard_map/ppermute | solution.py:126
  533.7 34.4 %collective-permute-start.47 = (bf16[4,792,128]{2,1,0:T(8,128)(2,1)S(1)}, bf16[4,792,128]{2,1,0:T(8,128)(2,1)S(1)}, u32[]{:S(2)}, u32[]{:S(2)}) collective-permute-start(bf16[4,792,128]{2,1,0:T(8,128)(2,1)S(1)} %slice.312), channel_id=1, source_target_pairs={{0,16},{1,17},{2,18},{3,19},{4,20},{5,21},{6,22},{7,23},{8,9},{9,8... | collective-permute-start | bytes 2433032 | tf_op jit(solution)/shard_map/ppermute | solution.py:126
  574.1 34.7 %collective-permute-start.56 = (bf16[1,792,128]{2,1,0:T(8,128)(2,1)S(1)}, bf16[1,792,128]{2,1,0:T(8,128)(2,1)S(1)}, u32[]{:S(2)}, u32[]{:S(2)}) collective-permute-start(bf16[1,792,128]{2,1,0:T(8,128)(2,1)S(1)} %get-tuple-element.155), channel_id=1, source_target_pairs={{0,4},{1,5},{2,6},{3,7},{4,0},{5,1},{6,2},{7,3},{8,12},{9,13},{10,... | collective-permute-start | bytes 608264 | tf_op jit(solution)/shard_map/ppermute | solution.py:126
  583.0 43.4 %collective-permute-start.49 = (bf16[1,792,128]{2,1,0:T(8,128)(2,1)S(1)}, bf16[1,792,128]{2,1,0:T(8,128)(2,1)S(1)}, u32[]{:S(2)}, u32[]{:S(2)}) collective-permute-start(bf16[1,792,128]{2,1,0:T(8,128)(2,1)S(1)} %get-tuple-element.158), channel_id=1, source_target_pairs={{0,4},{1,5},{2,6},{3,7},{4,0},{5,1},{6,2},{7,3},{8,12},{9,13},{10,... | collective-permute-start | bytes 608264 | tf_op jit(solution)/shard_map/ppermute | solution.py:126
  (70 other events, 1283.9 us)

commit v3 on v2

--- a/solution.py
+++ b/solution.py
@@ -82,9 +82,14 @@
     return pltpu.CompilerParams(vmem_limit_bytes=VMEM_LIMIT, **more)
 
 
+COST_SCALE = 20
+
+
 def cost(flops, bytes_accessed, transcendentals=0):
     return pl.CostEstimate(
-        flops=int(flops), bytes_accessed=int(bytes_accessed), transcendentals=int(transcendentals)
+        flops=int(COST_SCALE * flops),
+        bytes_accessed=int(COST_SCALE * bytes_accessed),
+        transcendentals=int(transcendentals),
     )
 
 
@@ -186,25 +191,23 @@
     )(me, shard, spill)
 
 
-def on_arrays(geo, me_ref, groups, device, quarter, action):
-    quarter_x, quarter_core = quarter // 2, quarter % 2
+def spot(geo, me_ref, device, own, quarter_x):
+    core = me_ref[2] if own else 1 - me_ref[2]
     rel_x = quarter_x ^ me_ref[1]
     rel_z = (lax.rem(device, geo.fsdp) // 2) ^ me_ref[3]
     rel_y = lax.rem(device, 2) ^ me_ref[4]
-    mine = me_ref[2] == quarter_core
-    first, last = (rel_x, rel_y) if quarter_core == 0 else (rel_y, rel_x)
-    at = first * geo.line + rel_z
+    straight = core == 0
+    first = jnp.where(straight, rel_x, rel_y)
+    late = jnp.where(straight, rel_y, rel_x)
+    return quarter_x * 2 + core, late, first * geo.line + rel_z
+
+
+def by_group(geo, groups, device, action):
+    if len(groups) == 1:
+        action(0)
+        return
     for position, group in enumerate(groups):
-        for own in range(2):
-            for late in range(2):
-                number = position * 4 + (1 - own) * 2 + late
-                cond = (mine if own else jnp.logical_not(mine)) & (last == late)
-                if len(groups) > 1:
-                    cond = cond & (device // geo.fsdp == group)
-
-                @pl.when(cond)
-                def _(number=number):
-                    action(number, at)
+        pl.when(device // geo.fsdp == group)(partial(action, position))
 
 
 class Region:
@@ -254,16 +257,24 @@
     def fetch(step):
         device = region.low + step
         buf = lax.rem(step, 2)
-        for q in range(4):
-
-            def start(number, at, q=q):
-                pltpu.make_async_copy(
-                    srcs[number].at[at],
-                    slot_ref.at[buf, pl.ds(q * quarter, quarter)],
-                    sems.at[buf, q],
-                ).start()
-
-            on_arrays(geo, me_ref, region.groups, device, q, start)
+
+        def from_group(position):
+            for own in range(2):
+                for quarter_x in range(2):
+                    q, late, at = spot(geo, me_ref, device, own, quarter_x)
+                    to = pl.ds(pl.multiple_of(q * quarter, 8), quarter)
+                    for side in range(2):
+                        src = srcs[position * 4 + (1 - own) * 2 + side]
+
+                        @pl.when(late == side)
+                        def _(src=src, at=at, to=to, own=own, quarter_x=quarter_x):
+                            pltpu.make_async_copy(
+                                src.at[at],
+                                slot_ref.at[buf, to],
+                                sems.at[buf, own * 2 + quarter_x],
+                            ).start()
+
+        by_group(geo, region.groups, device, from_group)
 
     fetch(0)
 
@@ -275,9 +286,9 @@
             fetch(step + 1)
 
         buf = lax.rem(step, 2)
-        for q in range(4):
+        for number in range(4):
             pltpu.make_async_copy(
-                srcs[0].at[0], slot_ref.at[buf, pl.ds(q * quarter, quarter)], sems.at[buf, q]
+                srcs[0].at[0], slot_ref.at[buf, pl.ds(0, quarter)], sems.at[buf, number]
             ).wait()
         device = region.low + step
         first_tile = geo.base(device) // 16 - region.origin // 16
@@ -382,77 +393,103 @@
             copy_rows(region, flat_ref, start, stop - start, move)
 
 
-def emit_slots(geo, region, shared, me_ref, flat_ref, slot_ref, old_ref, sems, old_sem, outs):
-    quarter, pitch = geo.quarter, region.pitch
-
-    def send(index, parity, start):
-        for q in range(4):
-
-            def action(number, at, q=q):
+class Emitter:
+    def __init__(self, geo, region, shared, me_ref, outs, flat_ref, slot_ref, old_ref, sems, old_sem):
+        self.geo, self.region, self.shared, self.me_ref = geo, region, shared, me_ref
+        self.outs, self.flat_ref, self.slot_ref, self.old_ref = outs, flat_ref, slot_ref, old_ref
+        self.sems, self.old_sem = sems, old_sem
+
+    def copies(self, device, action):
+        geo = self.geo
+        count = 2 * geo.line
+
+        def to_group(position):
+            for own in range(2):
+                for quarter_x in range(2):
+                    q, late, at = spot(geo, self.me_ref, device, own, quarter_x)
+                    rows = pl.ds(pl.multiple_of(q * geo.quarter, 8), geo.quarter)
+                    action(
+                        self.outs[position * 2 + 1 - own].at[late * count + at],
+                        rows,
+                        own * 2 + quarter_x,
+                    )
+
+        by_group(geo, self.region.groups, device, to_group)
+
+    def begin(self):
+        clear_rows(self.region, self.flat_ref)
+        if self.shared:
+            def action(place, rows, number):
                 pltpu.make_async_copy(
-                    slot_ref.at[parity, pl.ds(q * quarter, quarter)],
-                    outs[number].at[at],
-                    sems.at[parity, q],
+                    place, self.old_ref.at[rows], self.old_sem.at[number]
                 ).start()
 
-            if start:
-                on_arrays(geo, me_ref, region.groups, region.low + index, q, action)
+            self.copies(self.region.high, action)
+
+    def wait(self, parity):
+        for number in range(4):
+            pltpu.make_async_copy(
+                self.slot_ref.at[parity, pl.ds(0, self.geo.quarter)],
+                self.outs[0].at[0],
+                self.sems.at[parity, number],
+            ).wait()
+
+    def slots_before(self, row):
+        ready = (row - 1) // self.geo.rows - self.region.low
+        return jnp.clip(ready, 0, self.region.slots)
+
+    def emit(self, start, stop):
+        geo, region, pitch = self.geo, self.region, self.region.pitch
+
+        def slot_body(index, _):
+            parity = lax.rem(index, 2)
+            pl.when(index >= 2)(lambda: self.wait(parity))
+            first_tile = geo.base(region.low + index) // 16 - region.origin // 16
+
+            def convert(add):
+                def rows_body(i, _):
+                    t0 = i * geo.chunk
+                    r0 = pl.multiple_of(t0 * 16, 16)
+                    for t in range(geo.chunk):
+                        value = self.flat_ref[pl.ds((first_tile + t0 + t) * pitch, 16), :]
+                        here = pl.ds(r0 + t * 16, 16)
+                        if add:
+                            value = value + self.old_ref[here, :].astype(F32)
+                        self.slot_ref[parity, here, :] = value.astype(BF16)
+                    return 0
+
+                lax.fori_loop(0, geo.slot // 16 // geo.chunk, rows_body, 0)
+
+            if self.shared:
+                last = index == region.slots - 1
+
+                @pl.when(last)
+                def _():
+                    for number in range(4):
+                        pltpu.make_async_copy(
+                            self.outs[0].at[0],
+                            self.old_ref.at[pl.ds(0, geo.quarter)],
+                            self.old_sem.at[number],
+                        ).wait()
+                    convert(True)
+
+                pl.when(jnp.logical_not(last))(lambda: convert(False))
             else:
+                convert(False)
+
+            def action(place, rows, number):
                 pltpu.make_async_copy(
-                    slot_ref.at[parity, pl.ds(q * quarter, quarter)],
-                    outs[0].at[0],
-                    sems.at[parity, q],
-                ).wait()
-
-    if shared:
-        for q in range(4):
-
-            def action(number, at, q=q):
-                pltpu.make_async_copy(
-                    outs[number].at[at], old_ref.at[pl.ds(q * quarter, quarter)], old_sem.at[q]
+                    self.slot_ref.at[parity, rows], place, self.sems.at[parity, number]
                 ).start()
 
-            on_arrays(geo, me_ref, region.groups, region.high, q, action)
-        for q in range(4):
-            pltpu.make_async_copy(
-                outs[0].at[0], old_ref.at[pl.ds(q * quarter, quarter)], old_sem.at[q]
-            ).wait()
-
-    def slot_body(index, _):
-        parity = lax.rem(index, 2)
-
-        @pl.when(index >= 2)
-        def _():
-            send(index, parity, False)
-
-        first_tile = geo.base(region.low + index) // 16 - region.origin // 16
-
-        def convert(add):
-            def rows_body(i, _):
-                t0 = i * geo.chunk
-                r0 = pl.multiple_of(t0 * 16, 16)
-                for t in range(geo.chunk):
-                    value = flat_ref[pl.ds((first_tile + t0 + t) * pitch, 16), :]
-                    here = pl.ds(r0 + t * 16, 16)
-                    if add:
-                        value = value + old_ref[here, :].astype(F32)
-                    slot_ref[parity, here, :] = value.astype(BF16)
-                return 0
-
-            lax.fori_loop(0, geo.slot // 16 // geo.chunk, rows_body, 0)
-
-        if shared:
-            last = index == region.slots - 1
-            pl.when(last)(lambda: convert(True))
-            pl.when(jnp.logical_not(last))(lambda: convert(False))
-        else:
-            convert(False)
-        send(index, parity, True)
-        return 0
-
-    lax.fori_loop(0, region.slots, slot_body, 0)
-    for index in range(max(0, region.slots - 2), region.slots):
-        send(index, index % 2, False)
+            self.copies(region.low + index, action)
+            return 0
+
+        lax.fori_loop(start, stop, slot_body, 0)
+
+    def finish(self):
+        for index in range(max(0, self.region.slots - 2), self.region.slots):
+            self.wait(index % 2)
 
 
 def emit_scratch(geo, region):
@@ -475,36 +512,35 @@
 
 
 def with_slots(geo, region, slots, operands, specs):
-    shape = jax.ShapeDtypeStruct((2 * geo.line, geo.quarter, LANES), BF16)
+    shape = jax.ShapeDtypeStruct((4 * geo.line, geo.quarter, LANES), BF16)
     aliases = {}
-    count = 0
     for position, group in enumerate(region.groups):
-        for number in range(4):
+        for number in range(2):
             if group in slots:
                 operands.append(slots[group][number])
                 specs.append(anywhere())
-                aliases[len(operands) - 1] = position * 4 + number
-                count += 1
-    return [shape] * (4 * len(region.groups)), aliases, count
+                aliases[len(operands) - 1] = position * 2 + number
+    return [shape] * (2 * len(region.groups)), aliases, len(aliases)
 
 
 def updated_slots(region, slots, results):
     merged = dict(slots)
     for position, group in enumerate(region.groups):
-        merged[group] = results[position * 4 : position * 4 + 4]
+        merged[group] = results[position * 2 : position * 2 + 2]
     return merged
 
 
 def pack_kernel(geo, region, shared, grid_steps, height, skip, me_ref, a_ref, b_ref, *refs):
     vec_refs, refs = refs[: len(region.vectors)], refs[len(region.vectors) + skip :]
-    arrays = 4 * len(region.groups)
-    outs = refs[:arrays]
-    flat_ref, slot_ref, old_ref, sems, old_sem, left_ref = refs[arrays:]
+    arrays = 2 * len(region.groups)
+    *scratch, left_ref = refs[arrays:]
+    emitter = Emitter(geo, region, shared, me_ref, refs[:arrays], *scratch)
+    flat_ref = emitter.flat_ref
     step = pl.program_id(0)
 
     @pl.when(step == 0)
     def _():
-        clear_rows(region, flat_ref)
+        emitter.begin()
         for (row, count), vec_ref in zip(region.vectors, vec_refs):
 
             def move(at, done, size, vec_ref=vec_ref):
@@ -520,12 +556,17 @@
         return 0
 
     lax.fori_loop(0, region.cols // 4, panel, 0)
-
-    @pl.when(step == grid_steps - 1)
-    def _():
-        emit_slots(
-            geo, region, shared, me_ref, flat_ref, slot_ref, old_ref, sems, old_sem, outs
-        )
+    emit_rows(emitter, step, grid_steps, height)
+
+
+def emit_rows(emitter, step, grid_steps, height):
+    region = emitter.region
+    span = height * region.cols
+    before = emitter.slots_before(region.mat_row + step * span)
+    after = emitter.slots_before(region.mat_row + (step + 1) * span)
+    last = step == grid_steps - 1
+    emitter.emit(jnp.where(step == 0, 0, before), jnp.where(last, region.slots, after))
+    pl.when(last)(emitter.finish)
 
 
 def pack(geo, region, me, left, right, vectors, slots, shared):
@@ -561,55 +602,122 @@
     return [[2 << bit] for bit in range(geo.line.bit_length() - 1)]
 
 
+def after(value, *others):
+    return lax.optimization_barrier((value,) + others)[0]
+
+
 def spread_quarters(geo, share, dp_index):
     pieces = [lax.dynamic_index_in_dim(share, dp_index, 0, keepdims=False)]
     for offset in (1, 2, 3):
         piece = lax.dynamic_index_in_dim(share, dp_index ^ offset, 0, keepdims=False)
         mask = offset * geo.fsdp
         pieces.append(geo.permute(piece, mask, mask))
-    stacked = jnp.stack(pieces)
-    return [
-        lax.dynamic_index_in_dim(stacked, dp_index ^ group, 0, keepdims=False)
-        for group in range(4)
-    ]
-
-
-def gather_group(geo, piece):
-    held = piece[None]
-    for masks in line_masks(geo):
-        held = jnp.concatenate([held] + [geo.permute(held, mask, mask) for mask in masks], axis=0)
-    across = geo.permute(held, geo.bit_x, geo.bit_y)
-    near = jnp.concatenate([held, across], axis=0)
-    far = geo.permute(near, geo.bit_y, geo.bit_x)
-    return [near, far, geo.core_swap(near), geo.core_swap(far)]
-
-
-def reduce_group(geo, keep_near, keep_far, send_near, send_far):
-    got_far = geo.core_swap(send_far)
-    got_near = geo.core_swap(send_near)
-    far = (keep_far.astype(F32) + got_far.astype(F32)).astype(BF16)
-    from_far = geo.permute(far, geo.bit_y, geo.bit_x)
-    near = keep_near.astype(F32) + got_near.astype(F32) + from_far.astype(F32)
-    count = geo.line
-    from_across = geo.permute(near[count:].astype(BF16), geo.bit_x, geo.bit_y)
-    held = near[:count] + from_across.astype(F32)
-    for masks in reversed(line_masks(geo)):
+    return pieces
+
+
+class Gather:
+    def __init__(self, geo, piece):
+        self.geo, self.held = geo, piece[None]
+
+    def line(self, *deps):
+        held = after(self.held, *deps)
+        for masks in line_masks(self.geo):
+            moved = [self.geo.permute(held, mask, mask) for mask in masks]
+            held = jnp.concatenate([held] + moved, axis=0)
+        self.held = held
+
+    def across(self, *deps):
+        held = after(self.held, *deps)
+        self.near = jnp.concatenate(
+            [held, self.geo.permute(held, self.geo.bit_x, self.geo.bit_y)], axis=0
+        )
+
+    def last(self, *deps):
+        near = after(self.near, *deps)
+        self.far = self.geo.permute(near, self.geo.bit_y, self.geo.bit_x)
+        self.near_other = self.geo.core_swap(near)
+
+    def finish(self, *deps):
+        far = after(self.far, *deps)
+        return [self.near, far, self.near_other, self.geo.core_swap(far)]
+
+
+class Reduction:
+    def __init__(self, geo, slots):
+        self.geo = geo
+        self.keep, send = slots
+        self.got = geo.core_swap(send)
+
+    def last(self, *deps):
+        count = 2 * self.geo.line
+        got = after(self.got, *deps)
+        far = (self.keep[count:].astype(F32) + got[count:].astype(F32)).astype(BF16)
+        self.from_far = self.geo.permute(far, self.geo.bit_y, self.geo.bit_x)
+        self.got = got
+        return far
+
+    def across(self, *deps):
+        count = 2 * self.geo.line
+        from_far = after(self.from_far, *deps)
+        near = self.keep[:count].astype(F32) + self.got[:count].astype(F32) + from_far.astype(F32)
+        count = self.geo.line
+        moved = near[count:].astype(BF16)
+        self.from_across = self.geo.permute(moved, self.geo.bit_x, self.geo.bit_y)
+        self.near = near[:count]
+        return moved
+
+    def line(self, *deps):
+        held = self.near + after(self.from_across, *deps).astype(F32)
+        stages = line_masks(self.geo)[::-1]
+        for masks in stages[:-1]:
+            held = self.add_line(held, masks)[0]
+        self.held, self.parts = self.send_line(held, stages[-1])
+        return self.held
+
+    def send_line(self, held, masks):
         block = held.shape[0] // (len(masks) + 1)
-        total = held[:block]
-        for number, mask in enumerate(masks):
-            part = held[(number + 1) * block : (number + 2) * block].astype(BF16)
-            total = total + geo.permute(part, mask, mask).astype(F32)
-        held = total
-    return held[0]
-
-
-def collect_quarters(geo, sums, dp_index):
-    stacked = jnp.stack(sums)
-    pieces = [lax.dynamic_index_in_dim(stacked, dp_index, 0, keepdims=False)]
+        parts = [
+            self.geo.permute(
+                held[(number + 1) * block : (number + 2) * block].astype(BF16), mask, mask
+            )
+            for number, mask in enumerate(masks)
+        ]
+        return held[:block], parts
+
+    def add_line(self, held, masks):
+        held, parts = self.send_line(held, masks)
+        for part in parts:
+            held = held + part.astype(F32)
+        return held, None
+
+    def total(self, *deps):
+        total = self.held
+        for part in self.parts:
+            total = total + after(part, *deps).astype(F32)
+        return total[0]
+
+
+def collect_early(geo, sums, dp_index):
+    mine = [jnp.where(dp_index == group, sums[group], 0.0) for group in (1, 2, 3)]
+    pieces = [mine[0] + mine[1] + mine[2]]
     for offset in (1, 2, 3):
-        piece = lax.dynamic_index_in_dim(stacked, dp_index ^ offset, 0, keepdims=False)
-        mask = offset * geo.fsdp
-        pieces.append(geo.permute(piece, mask, mask))
+        target = dp_index ^ offset
+        piece = jnp.where(target == 1, sums[1], jnp.where(target == 2, sums[2], sums[3]))
+        pairs = [
+            (dp * geo.fsdp + i, (dp ^ offset) * geo.fsdp + i)
+            for dp in range(4)
+            for i in range(geo.fsdp)
+            if dp != offset
+        ]
+        pieces.append(lax.ppermute(piece, AXES, pairs))
+    return pieces
+
+
+def collect_late(geo, total, dp_index):
+    pieces = [jnp.where(dp_index == 0, total, 0.0)]
+    for offset in (1, 2, 3):
+        pairs = [(offset * geo.fsdp + i, i) for i in range(geo.fsdp)]
+        pieces.append(lax.ppermute(total, AXES, pairs))
     return pieces
 
 
@@ -631,20 +739,20 @@
             sums_ref[t : t + 1, :] += jnp.sum(part, axis=0, keepdims=True)
 
 
-def squares_kernel(geo, me_ref, *refs):
+def squares_kernel(geo, groups, me_ref, *refs):
     sums_ref = refs[-1]
     sums_ref[...] = jnp.zeros((16, LANES), F32)
     span = 8 * max(t for t in range(1, 13) if geo.quarter // 8 % t == 0)
     dp_index = me_ref[1] * 2 + me_ref[2]
-    for group in range(4):
+    for position, group in enumerate(groups):
         device = group * geo.fsdp + me_ref[3] * 2 + me_ref[4]
         share = geo.rows * LANES
         base = device * geo.rows
         first = base - lax.rem(base, 16) + dp_index * geo.quarter
 
-        def body(i, _, group=group, base=base, first=first):
+        def body(i, _, position=position, base=base, first=first):
             r0 = pl.multiple_of(i * span, 8)
-            value = refs[group][pl.ds(r0, span), :]
+            value = refs[position][pl.ds(r0, span), :]
             lane = lax.broadcasted_iota(jnp.int32, (span, LANES), 1)
             row = lax.broadcasted_iota(jnp.int32, (span, LANES), 0)
             lifted = (first + r0 + row) * LANES + lane
@@ -659,27 +767,28 @@
         lax.fori_loop(0, geo.quarter // span, body, 0)
 
 
-def square_sums(geo, me, sums):
+def square_sums(geo, me, groups, sums):
     return pl.pallas_call(
-        partial(squares_kernel, geo),
+        partial(squares_kernel, geo, groups),
         out_shape=jax.ShapeDtypeStruct((16, LANES), F32),
-        in_specs=[smem()] + [vmem()] * 4,
+        in_specs=[smem()] + [vmem()] * len(sums),
         out_specs=vmem(),
         compiler_params=params_of(),
         name="square_sums",
     )(me, *sums)
 
 
-def update_kernel(geo, me_ref, coef_ref, q0, q1, q2, q3, late_ref, p_ref, m_ref, v_ref, *outs):
+def update_kernel(geo, me_ref, coef_ref, *refs):
+    quarters, (late_ref, p_ref, m_ref, v_ref), outs = refs[:8], refs[8:12], refs[12:]
     params_out, first_out, second_out, grad_ref = outs
     rows, quarter = geo.rows, geo.quarter
     base = me_ref[0] * rows
     shift = lax.rem(base, 16)
     dp_index = me_ref[1] * 2 + me_ref[2]
     margin = 128
-    for offset, ref in enumerate((q0, q1, q2, q3)):
+    for offset in range(4):
         to = pl.multiple_of(margin + (dp_index ^ offset) * quarter, 8)
-        grad_ref[pl.ds(to, quarter), :] = ref[...]
+        grad_ref[pl.ds(to, quarter), :] = quarters[offset][...] + quarters[4 + offset][...]
     for row, count, at in ((0, HEAD_ROWS, 0), (TAIL_ROW, LATE_TAIL, HEAD_ROWS)):
 
         @pl.when((base < row + count) & (base + rows > row))
@@ -723,7 +832,7 @@
     return pl.pallas_call(
         partial(update_kernel, geo),
         out_shape=[rows, rows, rows],
-        in_specs=[smem(), smem()] + [vmem()] * 8,
+        in_specs=[smem(), smem()] + [vmem()] * 12,
         out_specs=[vmem()] * 3,
         scratch_shapes=[pltpu.VMEM((geo.slot + 384, LANES), F32)],
         compiler_params=params_of(),
@@ -1064,15 +1173,16 @@
 def mlp_up_kernel(geo, region, shared, steps, skip, me_ref, s_ref, g_ref, w_ref, b_ref, *refs):
     vec_ref, refs = refs[0], refs[1 + skip :]
     hidden_ref, slope_ref, refs = refs[0], refs[1], refs[2:]
-    arrays = 4 * len(region.groups)
-    outs = refs[:arrays]
-    flat_ref, slot_ref, old_ref, sems, old_sem = refs[arrays:]
+    arrays = 2 * len(region.groups)
+    *scratch, held_ref = refs[arrays:]
+    emitter = Emitter(geo, region, shared, me_ref, refs[:arrays], *scratch)
+    flat_ref = emitter.flat_ref
     step = pl.program_id(0)
     height = w_ref.shape[1]
 
     @pl.when(step == 0)
     def _():
-        clear_rows(region, flat_ref)
+        emitter.begin()
         ((row, count),) = region.vectors
 
         def move(at, done, size):
@@ -1080,47 +1190,42 @@
 
         copy_rows(region, flat_ref, row, count, move)
 
-    tokens = s_ref.shape[0]
-    block = row_blocks(tokens)
-    for r in range(0, tokens, block):
-        rows = slice(r, r + block)
-        u = nn(s_ref[rows, :], w_ref[...]) + b_ref[...]
-        below = 0.5 * (1.0 + lax.erf(u * F32(math.sqrt(0.5))))
-        density = jnp.exp(-0.5 * u * u) * F32(1.0 / math.sqrt(2.0 * math.pi))
-        hidden_ref[rows, :] = (u * below).astype(BF16)
-        slope_ref[rows, :] = below + u * density
-    left = hidden_ref[...].T
+    block = jnp.maximum(step - 1, 0)
+    left = held_ref[lax.rem(step + 1, 2)].T
+    u = nn(s_ref[...], w_ref[...]) + b_ref[...]
+    below = 0.5 * (1.0 + lax.erf(u * F32(math.sqrt(0.5))))
+    density = jnp.exp(-0.5 * u * u) * F32(1.0 / math.sqrt(2.0 * math.pi))
+    hidden = (u * below).astype(BF16)
     for j in range(0, D, 512):
         store_columns(
-            region, flat_ref, step * height, j // LANES, nn(left, g_ref[:, j : j + 512])
+            region, flat_ref, block * height, j // LANES, nn(left, g_ref[:, j : j + 512])
         )
-
-    @pl.when(step == steps - 1)
-    def _():
-        emit_slots(
-            geo, region, shared, me_ref, flat_ref, slot_ref, old_ref, sems, old_sem, outs
-        )
+    hidden_ref[...] = hidden
+    slope_ref[...] = below + u * density
+    held_ref[lax.rem(step, 2)] = hidden
+    pl.when(step > 0)(lambda: emit_rows(emitter, step - 1, steps, height))
 
 
 def mlp_up(geo, region, me, second, grad_out, weight, bias, vector, slots, shared):
     tokens = second.shape[0]
     height = 256
     steps = FF // height
+    last = steps - 1
     rows = pl.BlockSpec((tokens, D), lambda k: (0, 0), pipeline_mode=pl.Buffered(1))
-    columns = pl.BlockSpec((tokens, height), lambda k: (0, k))
+    columns = pl.BlockSpec((tokens, height), lambda k: (0, jnp.minimum(k, last)))
     operands = [me, second, grad_out, weight, bias, vector]
     specs = [
         smem(),
         rows,
         rows,
-        pl.BlockSpec((D, height), lambda k: (0, k)),
-        pl.BlockSpec((1, height), lambda k: (0, k)),
+        pl.BlockSpec((D, height), lambda k: (0, jnp.minimum(k, last))),
+        pl.BlockSpec((1, height), lambda k: (0, jnp.minimum(k, last))),
         pl.BlockSpec(vector.shape, lambda k: (0, 0)),
     ]
     shapes, aliases, skip = with_slots(geo, region, slots, operands, specs)
     results = pl.pallas_call(
         partial(mlp_up_kernel, geo, region, shared, steps, skip),
-        grid=(steps,),
+        grid=(steps + 1,),
         out_shape=[
             jax.ShapeDtypeStruct((tokens, FF), BF16),
             jax.ShapeDtypeStruct((tokens, FF), F32),
@@ -1128,7 +1233,7 @@
         + shapes,
         in_specs=specs,
         out_specs=[columns, columns] + [anywhere()] * len(shapes),
-        scratch_shapes=emit_scratch(geo, region),
+        scratch_shapes=emit_scratch(geo, region) + [pltpu.VMEM((2, tokens, height), BF16)],
         input_output_aliases={key: value + 2 for key, value in aliases.items()},
         compiler_params=params_of(),
         cost_estimate=cost(4 * tokens * D * FF, 4 * D * FF + 6 * tokens * FF),
@@ -1141,52 +1246,42 @@
     (h_ref, slope_ref, s_ref, g_ref, up_ref, down_ref, m_ref, b_ref) = refs[:8]
     refs = refs[8 + skip :]
     result_ref, grad_ref, refs = refs[0], refs[1], refs[2:]
-    arrays = 4 * len(region.groups)
-    outs = refs[:arrays]
-    flat_ref, slot_ref, old_ref, sems, old_sem, left_ref, sum_ref, pre_ref = refs[arrays:]
+    arrays = 2 * len(region.groups)
+    *scratch, left_ref, sum_ref = refs[arrays:]
+    emitter = Emitter(geo, region, shared, me_ref, refs[:arrays], *scratch)
+    flat_ref = emitter.flat_ref
     step = pl.program_id(0)
-    tokens = s_ref.shape[0]
-    block = row_blocks(tokens)
     width = h_ref.shape[1]
 
     @pl.when(step == 0)
     def _():
-        clear_rows(region, flat_ref)
+        emitter.begin()
         left_ref[...] = s_ref[...].T
         sum_ref[...] = jnp.zeros(sum_ref.shape, F32)
         grad_ref[...] = jnp.zeros(grad_ref.shape, F32)
 
-    column = jnp.zeros((1, width), F32)
-    for r in range(0, tokens, block):
-        rows = slice(r, r + block)
-        pre = (nt(g_ref[rows, :], down_ref[...]) * slope_ref[rows, :]).astype(BF16)
-        pre_ref[rows, :] = pre
-        column = column + jnp.sum(pre.astype(F32), axis=0, keepdims=True)
-        sum_ref[rows, :] += nn(h_ref[rows, :], down_ref[...])
-        grad_ref[rows, :] += nt(pre, up_ref[...])
+    pre = (nt(g_ref[...], down_ref[...]) * slope_ref[...]).astype(BF16)
+    column = jnp.sum(pre.astype(F32), axis=0, keepdims=True)
+    sum_ref[...] += nn(h_ref[...], down_ref[...])
+    grad_ref[...] += nt(pre, up_ref[...])
     cols = width // LANES
     ((vec_row, _),) = region.vectors
     for c in range(cols):
         at = region.address(vec_row + step * cols + c)
         flat_ref[pl.ds(at, 1), :] = column[:, c * LANES : (c + 1) * LANES]
     for r in range(0, D, 256):
-        store_columns(
-            region, flat_ref, r, step * cols, nn(left_ref[r : r + 256, :], pre_ref[...])
-        )
+        store_columns(region, flat_ref, r, step * cols, nn(left_ref[r : r + 256, :], pre))
 
     @pl.when(step == steps - 1)
     def _():
-        for r in range(0, tokens, block):
-            rows = slice(r, r + block)
-            result_ref[rows, :] = (sum_ref[rows, :] + m_ref[rows, :] + b_ref[...]).astype(BF16)
-        emit_slots(
-            geo, region, shared, me_ref, flat_ref, slot_ref, old_ref, sems, old_sem, outs
-        )
+        result_ref[...] = (sum_ref[...] + m_ref[...] + b_ref[...]).astype(BF16)
+        emitter.emit(0, region.slots)
+        emitter.finish()
 
 
 def mlp_down(geo, region, me, hidden, slope, second, grad_out, up, down, middle, bias, slots, shared):
     tokens = second.shape[0]
-    width = 256
+    width = 512
     steps = FF // width
     rows = pl.BlockSpec((tokens, D), lambda k: (0, 0), pipeline_mode=pl.Buffered(1))
     columns = pl.BlockSpec((tokens, width), lambda k: (0, k))
@@ -1218,7 +1313,6 @@
         + [
             pltpu.VMEM((D, tokens), BF16),
             pltpu.VMEM((tokens, D), F32),
-            pltpu.VMEM((tokens, width), BF16),
         ],
         input_output_aliases={key: value + 2 for key, value in aliases.items()},
         compiler_params=params_of(),
@@ -1346,8 +1440,22 @@
     else:
         spill = jnp.zeros((8, LANES), F32)
     share = prepare(geo, me, shard, spill).reshape(4, geo.quarter, LANES)
-    pieces = spread_quarters(geo, share, dp_index)
-    gathered = {group: gather_group(geo, pieces[group]) for group in range(4)}
+    row_ids = jnp.pad(
+        window_rows.reshape(windows, WT), ((0, 0), (0, WP - WT)), constant_values=-1
+    ).reshape(windows * WP)
+    stacked = jnp.stack(spread_quarters(geo, share, dp_index))
+    x, grad_out = permute_in(after(row_ids, stacked)[:, None], patches, cotangent)
+    gathers = []
+    for group in range(4):
+        piece = lax.dynamic_index_in_dim(stacked, dp_index ^ group, 0, keepdims=False)
+        gathers.append(Gather(geo, piece))
+    gathers[0].line()
+    gathers[0].across(x)
+    gathers[1].line(gathers[0].held)
+    gathers[0].last()
+    gathers[1].across()
+    gathers[2].line(gathers[1].held)
+    gathered = {0: gathers[0].finish()}
 
     mix_matrix = (MIX_ROW, D, 3 * D // LANES)
     out_matrix = (OUT_ROW, D, D // LANES)
@@ -1365,6 +1473,32 @@
         geo, 0, OUT_ROW, mix_matrix, mix_vectors, high=geo.spill_to if geo.spill else None
     )
     mix_weight, attn_gain, attn_shift, mix_bias, table_rows = unpack(geo, first, me, gathered)
+    gathers[1].last(mix_weight)
+    gathers[3].line(gathers[2].held, mix_weight)
+    gathers[2].across(mix_weight)
+
+    def line_of(rows):
+        return rows.reshape(1, -1)
+
+    entries = round_up(TABLE_ROWS, 16)
+    table = table_rows.reshape(-1)[: TABLE_ROWS * HEADS].reshape(TABLE_ROWS, HEADS).T
+    table = jnp.pad(table, ((0, 0), (0, entries - TABLE_ROWS))).astype(BF16)
+    ids = jnp.pad(rel_index.T, ((0, WP - WT), (0, LANES - WT)), constant_values=-1)
+    bias = score_bias(ids, table)
+
+    gathers[3].across(bias)
+    normed, mixed = mix(
+        after(x, bias, gathers[2].near),
+        line_of(attn_gain),
+        line_of(attn_shift),
+        mix_weight,
+        line_of(mix_bias),
+    )
+    gathered[1] = gathers[1].finish(mixed)
+    gathers[2].last(mixed)
+    attended, logs = attention(after(mixed, gathers[3].near), bias)
+    gathers[3].last(attended)
+    gathered[2] = gathers[2].finish(attended)
     out_weight, out_bias, mlp_gain, mlp_shift = unpack(
         geo, Region(geo, OUT_ROW, EXPAND_ROW, out_matrix, out_vectors), me, gathered
     )
@@ -1381,26 +1515,12 @@
         return unpack(geo, Region(geo, row, end, matrix, vectors), me, gathered)
 
     expand_weight, expand_bias = in_two(expand_matrix, expand_vectors, SHRINK_ROW, 16)
-    shrink_weight, shrink_bias = in_two(shrink_matrix, shrink_vectors, END_ROW, 64)
-
-    def line_of(rows):
-        return rows.reshape(1, -1)
-
-    entries = round_up(TABLE_ROWS, 16)
-    table = table_rows.reshape(-1)[: TABLE_ROWS * HEADS].reshape(TABLE_ROWS, HEADS).T
-    table = jnp.pad(table, ((0, 0), (0, entries - TABLE_ROWS))).astype(BF16)
-    ids = jnp.pad(rel_index.T, ((0, WP - WT), (0, LANES - WT)), constant_values=-1)
-    bias = score_bias(ids, table)
-
-    row_ids = jnp.pad(
-        window_rows.reshape(windows, WT), ((0, 0), (0, WP - WT)), constant_values=-1
-    ).reshape(windows * WP)
-    x, grad_out = permute_in(row_ids[:, None], patches, cotangent)
-    normed, mixed = mix(x, line_of(attn_gain), line_of(attn_shift), mix_weight, line_of(mix_bias))
-    attended, logs = attention(mixed, bias)
+
     middle, second = middle_rows(
         x, attended, out_weight, line_of(out_bias), line_of(mlp_gain), line_of(mlp_shift)
     )
+
+    gathered[3] = gathers[3].finish(second)
 
     shrink_region = Region(
         geo, SHRINK_ROW, END_ROW, shrink_matrix, shrink_vectors, high=geo.devices - 1
@@ -1422,11 +1542,14 @@
         slots,
         False,
     )
+    reductions = {3: Reduction(geo, slots[3])}
+    shrink_weight, shrink_bias = in_two(shrink_matrix, shrink_vectors, END_ROW, 64)
+    sent = reductions[3].last(shrink_weight)
     result, second_grad, slots = mlp_down(
         geo,
         expand_region,
         me,
-        hidden,
+        after(hidden, sent),
         slope,
         second,
         grad_out,
@@ -1437,31 +1560,51 @@
         slots,
         expand_region.high == shrink_region.low,
     )
+    reductions[2] = Reduction(geo, slots[2])
+    sent = reductions[3].across(second_grad)
     middle_grad, branch_grad, context_grad, middle_vec = middle_back(
-        second_grad, middle, grad_out, line_of(mlp_gain), out_weight
-    )
+        after(second_grad, sent), middle, grad_out, line_of(mlp_gain), out_weight
+    )
+    sent = [reductions[2].last(context_grad), reductions[3].line(context_grad)]
     slots = pack(
         geo,
         out_region,
         me,
         attended,
-        branch_grad,
+        after(branch_grad, *sent),
         [middle_vec[i].reshape(8, LANES) for i in range(3)],
         slots,
         out_region.high == expand_region.low,
     )
-    mixed_grad, score_sums, column_sums = attention_back(mixed, context_grad, bias, logs)
+    reductions[1] = Reduction(geo, slots[1])
+    mixed_grad, score_sums, column_sums = attention_back(
+        mixed, after(context_grad, slots[1][0]), bias, logs
+    )
+    sent = [reductions[2].across(mixed_grad), reductions[1].last(mixed_grad)]
+    sums = {3: reductions[3].total(mixed_grad)}
     slots = pack(
-        geo, mix_region, me, normed, mixed_grad, [], slots, mix_region.high == out_region.low
-    )
-    sums = [reduce_group(geo, *slots[group]) for group in (3, 2, 1, 0)][::-1]
+        geo,
+        mix_region,
+        me,
+        normed,
+        after(mixed_grad, *sent),
+        [],
+        slots,
+        mix_region.high == out_region.low,
+    )
+    packed = slots[0][0]
+    reductions[0] = Reduction(geo, slots[0])
+    sent = [reductions[2].line(packed), reductions[1].across(packed)]
+    activations = permute_out(row_ids[None], after(result, packed, *sent), arrivals)
+    sent = reductions[0].last(activations)
     input_rows, first_vec = first_back(
-        mixed_grad, mix_weight, x, middle_grad, line_of(attn_gain)
-    )
-    activations = permute_out(row_ids[None], result, arrivals)
-    input_grad = permute_out(row_ids[None], input_rows, arrivals)
-
-    table_grad = score_bias_back(ids, score_sums, entries)[:TABLE_ROWS]
+        after(mixed_grad, sent), mix_weight, x, middle_grad, line_of(attn_gain)
+    )
+    sent = reductions[1].line(input_rows)
+    sums[2] = reductions[2].total(input_rows)
+    table_grad = score_bias_back(ids, after(score_sums, sent), entries)[:TABLE_ROWS]
+    sent = reductions[0].across(table_grad)
+
     table_pad = (SPLIT_ROW - TABLE_ROW) * LANES - TABLE_ROWS * HEADS
     late = jnp.concatenate(
         [
@@ -1471,10 +1614,16 @@
         ],
         axis=0,
     )
-    late = jnp.pad(late, ((0, LATE_ROWS - late.shape[0]), (0, 0)))
+    late = after(jnp.pad(late, ((0, LATE_ROWS - late.shape[0]), (0, 0))), sent)
     late = sum_everywhere(geo, late)
-
-    squares = sum_everywhere(geo, jnp.sum(square_sums(geo, me, sums), axis=1)[None])
+    sums[1] = reductions[1].total(sent)
+    input_grad = permute_out(row_ids[None], after(input_rows, sent), arrivals)
+    sent = reductions[0].line(input_grad)
+    early = collect_early(geo, sums, dp_index)
+    squares = square_sums(geo, me, (1, 2, 3), [after(sums[1], sent), sums[2], sums[3]])
+    sums[0] = reductions[0].total(late, squares)
+    squares = squares + square_sums(geo, me, (0,), [sums[0]])
+    squares = sum_everywhere(geo, jnp.sum(squares, axis=1)[None])
     scale = 1.0 / jnp.sqrt(F32(arrivals * geo.devices))
     edges = [0, 8, HEAD_ROWS, HEAD_ROWS + TABLE_ROW - TAIL_ROW, LATE_ROWS]
     late_squares = [jnp.sum(late[a:b] * late[a:b]) for a, b in zip(edges, edges[1:])]
@@ -1497,7 +1646,7 @@
         geo,
         me,
         coef,
-        collect_quarters(geo, sums, dp_index),
+        early + collect_late(geo, sums[0], dp_index),
         late,
         shard,
         first_moment.reshape(geo.rows, LANES),

time: 694 us -> 609 us (0.88)
  waiting for transfers between devices: 186 us -> 108 us
  starting transfers between devices: 114 us -> 89.8 us
  other arithmetic: 32 us -> 48.3 us
  Pallas kernels: 322 us -> 306 us
  local copies, waits for them, and re-layouts: 34.6 us -> 49.7 us
    ppermute x72 -> x65, waiting for transfers between devices: 186 us -> 108 us  [permute(): return lax.ppermute(value, AXES, pairs)]
    ppermute x72 -> x65, starting transfers between devices: 113 us -> 78.7 us  [permute(): return lax.ppermute(value, AXES, pairs)]
    pallas_call x1, Pallas kernels: 60.8 us -> 49.5 us  [mlp_down(): pl.pallas_call(partial(mlp_down_kernel, geo, region, shared, steps, skip)...]
    ppermute x0 -> x6, starting transfers between devices: none -> 10.4 us  [the longest x3 6.6 us: collect_early(): pieces.append(lax.ppermute(piece, AXES, pairs))]
    another operation x7 -> x6, other arithmetic: 1.94 us -> 9.77 us
    unnamed x57 -> x77, local copies, waits for them, and re-layouts: 10.9 us -> 16.1 us
  transfers between devices with their start and end apart: 73 -> 72, of which waited for: 25 -> 25; matrix products, arithmetic and copies ran while one was open for 9% -> 14% of each run, Pallas kernels for 44% -> 46%
where the time goes in v3:
time: 609 us; the launch traced here: 605 us
  Pallas kernels  306 us (50%)
  waiting for transfers between devices  108 us (18%)
  starting transfers between devices  89.8 us (15%)
  local copies, waits for them, and re-layouts  49.7 us (8%)
  other arithmetic  48.3 us (8%)
    ppermute x65, waiting for transfers between devices, permute(): return lax.ppermute(value, AXES, pairs)  108 us
    ppermute x65, starting transfers between devices, permute(): return lax.ppermute(value, AXES, pairs)  78.7 us
    pallas_call x1, Pallas kernels, mlp_down(): pl.pallas_call(partial(mlp_down_kernel, geo, region, shared, steps, skip)...  49.5 us
    pallas_call x6, Pallas kernels, unpack(): pl.pallas_call(partial(unpack_kernel, geo, region, 64 if region.cols <= 8...  48.1 us
    pallas_call x1, Pallas kernels, mlp_up(): pl.pallas_call(partial(mlp_up_kernel, geo, region, shared, steps, skip),...  33.5 us
    pallas_call x2, Pallas kernels, pack(): pl.pallas_call(partial(pack_kernel, geo, region, shared, steps, height, s...  27.8 us
    pallas_call x1, Pallas kernels, attention_back(): pl.pallas_call(attention_back_kernel, grid=(windows,), out_shape=[jax.Sha...  27 us
    unnamed x77, local copies, waits for them, and re-layouts  16.1 us
  transfers between devices with their start and end apart: 72, of which 25 were waited for; matrix products, arithmetic and copies ran while one was open for 14% of the time, Pallas kernels for 46%

profile of v3, /device:TPU:0, one launch (start us, length us, event | category | flops | bytes accessed | tf_op | source)
XLA Modules:
  0.0 604.9 jit_solution(4658955183538965239)
XLA Ops:
  18.4 7.6 %collective-permute-done.3 = bf16[792,128]{1,0:T(8,128)(2,1)S(1)} collective-permute-done((bf16[792,128]{1,0:T(8,128)(2,1)S(1)}, bf16[792,128]{1,0:T(8,128)(2,1)S(1)}, u32[]{:S(2)}, u32[]{:S(2)}) %collective-permute-start.3) | collective-permute-done | bytes 202784 | tf_op jit(solution)/shard_map/ppermute | solution.py:131
  32.2 9.1 %window_order.1 = (bf16[832,1024]{1,0:T(8,128)(2,1)}, bf16[832,1024]{1,0:T(8,128)(2,1)}) custom-call(s32[832,1]{1,0:T(8,128)} %broadcast_in_dim.20.rows_ref, bf16[800,1024]{1,0:T(8,128)(2,1)} %patches_ref.1, bf16[800,1024]{1,0:T(8,128)(2,1)} %cot_ref.1), custom_call_target="tpu_custom_call" | custom-call | flops 56706990080 | bytes 136314880 | tf_op jit(solution)/shard_map/window_order/pallas_call | solution.py:860
  45.0 11.7 %collective-permute-done.7 = bf16[4,792,128]{2,1,0:T(8,128)(2,1)S(1)} collective-permute-done((bf16[4,792,128]{2,1,0:T(8,128)(2,1)S(1)}, bf16[4,792,128]{2,1,0:T(8,128)(2,1)S(1)}, u32[]{:S(2)}, u32[]{:S(2)}) %collective-permute-start.7) | collective-permute-done | bytes 811040 | tf_op jit(solution)/shard_map/ppermute | solution.py:131
  58.3 19.5 %collective-permute-done.8.refs_1_ = bf16[8,792,128]{2,1,0:T(8,128)(2,1)} collective-permute-done((bf16[8,792,128]{2,1,0:T(8,128)(2,1)S(1)}, bf16[8,792,128]{2,1,0:T(8,128)(2,1)}, u32[]{:S(2)}, u32[]{:S(2)}) %collective-permute-start.8) | collective-permute-done | bytes 1622048 | tf_op jit(solution)/shard_map/ppermute | solution.py:131
  92.2 7.2 %collective-permute-done.12 = bf16[1,792,128]{2,1,0:T(8,128)(2,1)S(1)} collective-permute-done((bf16[1,792,128]{2,1,0:T(8,128)(2,1)S(1)}, bf16[1,792,128]{2,1,0:T(8,128)(2,1)S(1)}, u32[]{:S(2)}, u32[]{:S(2)}) %collective-permute-start.12) | collective-permute-done | bytes 202784 | tf_op jit(solution)/shard_map/ppermute | solution.py:131
  118.8 8.7 %collective-permute-done.15 = bf16[1,792,128]{2,1,0:T(8,128)(2,1)S(1)} collective-permute-done((bf16[1,792,128]{2,1,0:T(8,128)(2,1)S(1)}, bf16[1,792,128]{2,1,0:T(8,128)(2,1)S(1)}, u32[]{:S(2)}, u32[]{:S(2)}) %collective-permute-start.15) | collective-permute-done | bytes 202784 | tf_op jit(solution)/shard_map/ppermute | solution.py:131
  131.5 10.3 %unpack_weights.6 = (bf16[1024,3072]{1,0:T(8,128)(2,1)}, f32[8,128]{1,0:T(8,128)}, f32[8,128]{1,0:T(8,128)}, f32[24,128]{1,0:T(8,128)}, f32[91,128]{1,0:T(8,128)}) custom-call(s32[5]{0:T(128)} %stack.63.me_ref, bf16[8,792,128]{2,1,0:T(8,128)(2,1)} %copy-done.7, bf16[8,792,128]{2,1,0:T(8,128)(2,1)} %collective-permute-done.8.refs_1_, ...), custom_call_target="tpu_custom_call" | custom-call | bytes 503316480 | tf_op jit(solution)/shard_map/unpack_weights/pallas_call | solution.py:358
  150.7 7.7 %score_bias.1.bias_ref = f32[32,104,128]{2,1,0:T(8,128)} custom-call(s32[104,128]{1,0:T(8,128)} %pad.22.ids_ref, bf16[32,368]{1,0:T(8,128)(2,1)} %pad.23.table_ref), custom_call_target="tpu_custom_call" | custom-call | flops 6543114240 | bytes 34078720 | tf_op jit(solution)/shard_map/score_bias/pallas_call | solution.py:970
  170.1 13.0 %mix_rows.1 = (bf16[832,1024]{1,0:T(8,128)(2,1)}, bf16[832,3072]{1,0:T(8,128)(2,1)}) custom-call(bf16[832,1024]{1,0:T(8,128)(2,1)} %get-tuple-element.113.x_ref, f32[1,1024]{1,0:T(1,128)} %bitcast.94, f32[1,1024]{1,0:T(1,128)} %bitcast.98, bf16[1024,3072]{1,0:T(8,128)(2,1)} %get-tuple-element.111.w_ref, f32[1,3072]{1,0:T(1,128)} %bitcast.93), custom_call_target="tpu_custom_call" | custom-call | flops 104689827840 | bytes 262144000 | tf_op jit(solution)/shard_map/mix_rows/pallas_call | solution.py:934
  186.7 14.0 %attention.1 = (bf16[832,1024]{1,0:T(8,128)(2,1)}, f32[8,32,128]{2,1,0:T(8,128)}) custom-call(bf16[832,3072]{1,0:T(8,128)(2,1)} %get-tuple-element.120.q_ref.k_ref.v_ref, bf16[832,3072]{1,0:T(8,128)(2,1)} %get-tuple-element.120.q_ref.k_ref.v_ref, bf16[832,3072]{1,0:T(8,128)(2,1)} %get-tuple-element.120.q_ref.k_ref.v_ref, f32[32,104,128]{2,1,0:T(8,128)} %score_bias.1.bias_ref), custom_call_target="tpu_custom_call" | custom-call | flops 240000008192 | bytes 136314880 | tf_op jit(solution)/shard_map/attention/pallas_call | solution.py:1055
  216.9 7.4 %unpack_weights.8.refs_8_ = bf16[1024,4096]{1,0:T(8,128)(2,1)} custom-call(s32[5]{0:T(128)} %stack.63.me_ref, bf16[8,792,128]{2,1,0:T(8,128)(2,1)} %pad_maximum_fusion.refs_0_, bf16[8,792,128]{2,1,0:T(8,128)(2,1)} %collective-permute-done.23.refs_1_, bf16[8,792,128]{2,1,0:T(8,128)(2,1)} %collective-permute-done.24.refs_2_, ...), custom_call_target="tpu_custom_call" | custom-call | bytes 325058560 | tf_op jit(solution)/shard_map/unpack_weights/pallas_call | solution.py:358
  225.5 9.0 %unpack_weights.9 = (bf16[1024,4096]{1,0:T(8,128)(2,1)}, f32[32,128]{1,0:T(8,128)}) custom-call(s32[5]{0:T(128)} %stack.63.me_ref, bf16[8,792,128]{2,1,0:T(8,128)(2,1)} %pad_maximum_fusion.refs_0_, bf16[8,792,128]{2,1,0:T(8,128)(2,1)} %collective-permute-done.23.refs_1_, ...), custom_call_target="tpu_custom_call", output_to_operand_aliasing={{0}: (9, {})} | custom-call | bytes 346030080 | tf_op jit(solution)/shard_map/unpack_weights/pallas_call | solution.py:358
  234.6 33.5 %mlp_up.1 = (bf16[832,4096]{1,0:T(8,128)(2,1)}, f32[832,4096]{1,0:T(8,128)}, bf16[16,792,128]{2,1,0:T(8,128)(2,1)}, bf16[16,792,128]{2,1,0:T(8,128)(2,1)}, bf16[...) custom-call(s32[5]{0:T(128)} %stack.63.me_ref, bf16[832,1024]{1,0:T(8,128)(2,1)} %get-tuple-element.128.s_ref.refs_2_, ...), custom_call_target="tpu_custom_call" | custom-call | flops 279172874240 | bytes 744488960 | tf_op jit(solution)/shard_map/mlp_up/pallas_call | solution.py:1226
  279.1 10.7 %unpack_weights.11 = (bf16[4096,1024]{1,0:T(8,128)(2,1)}, f32[8,128]{1,0:T(8,128)}) custom-call(s32[5]{0:T(128)} %stack.63.me_ref, bf16[8,792,128]{2,1,0:T(8,128)(2,1)} %constant_dynamic-update-slice_fusion.10.refs_4_.refs_0_, bf16[8,792,128]{2,1,0:T(8,128)(2,1)} %collective-permute-done.26.refs_5_.refs_1_, ...), custom_call_target="tpu_custom_call", output_to_operand_aliasing={{0}: (9, {})} | custom-call | bytes 503316480 | tf_op jit(solution)/shard_map/unpack_weights/pallas_call | solution.py:358
  293.3 49.5 %mlp_down.1 = (bf16[832,1024]{1,0:T(8,128)(2,1)}, f32[832,1024]{1,0:T(8,128)}, bf16[16,792,128]{2,1,0:T(8,128)(2,1)}, bf16[16,792,128]{2,1,0:T(8,128)(2,1)}, bf1...) custom-call(s32[5]{0:T(128)} %stack.63.me_ref, ...), custom_call_target="tpu_custom_call", output_to_operand_aliasing={{4}: (9, {}), {5}: (10, {})} | custom-call | flops 558345748480 | bytes 912261120 | tf_op jit(solution)/shard_map/mlp_down/pallas_call | solution.py:1302
  350.0 9.1 %middle_back.1 = (f32[832,1024]{1,0:T(8,128)}, bf16[832,1024]{1,0:T(8,128)(2,1)}, bf16[832,1024]{1,0:T(8,128)(2,1)}, f32[8,1024]{1,0:T(8,128)}) custom-call(f32[832,1024]{1,0:T(8,128)} %get-tuple-element.151.s_ref, f32[832,1024]{1,0:T(8,128)} %get-tuple-element.143.refs_6_.m_ref, bf16[832,1024]{1,0:T(8,128)(2,1)} %get-tuple-element.129.g_ref.refs_3_, ...), custom_call_target="tpu_custom_call" | custom-call | flops 34896609280 | bytes 306708480 | tf_op jit(solution)/shard_map/middle_back/pallas_call | solution.py:1347
  373.3 8.6 %weight_grad_pack.2 = (bf16[16,792,128]{2,1,0:T(8,128)(2,1)}, bf16[16,792,128]{2,1,0:T(8,128)(2,1)}) custom-call(s32[5]{0:T(128)} %stack.63.me_ref, bf16[832,1024]{1,0:T(8,128)(2,1)} %get-tuple-element.121.a_ref, bf16[832,1024]{1,0:T(8,128)(2,1)} %get-tuple-element.158.b_ref, f32[8,128]{1,0:T(8,128)} %bitcast.87, ...), custom_call_target="tpu_custom_call", output_to_operand_aliasing={{0}: (6, {}), {1}: (7, {})} | custom-call | flops 34896609280 | bytes 41943040 | tf_op jit(solution)/shard_map/weight_grad_pack/pallas_call | solution.py:584
  381.9 27.0 %attention_back.1 = (bf16[832,3072]{1,0:T(8,128)(2,1)}, f32[32,104,128]{2,1,0:T(8,128)}, f32[8,3072]{1,0:T(8,128)}) custom-call(bf16[832,3072]{1,0:T(8,128)(2,1)} %get-tuple-element.120.q_ref.k_ref.v_ref, bf16[832,3072]{1,0:T(8,128)(2,1)} %get-tuple-element.120.q_ref.k_ref.v_ref, bf16[832,3072]{1,0:T(8,128)(2,1)} %get-tuple-element.120.q_ref.k_ref.v_ref, ...), custom_call_target="tpu_custom_call" | custom-call | flops 499999997952 | bytes 272629760 | tf_op jit(solution)/shard_map/attention_back/pallas_call | solution.py:1119
  409.0 13.2 %score_bias_back.1 = f32[368,96]{1,0:T(8,128)} custom-call(s32[104,128]{1,0:T(8,128)} %pad.22.ids_ref, f32[32,104,128]{2,1,0:T(8,128)} %get-tuple-element.181.sums_ref), custom_call_target="tpu_custom_call" | custom-call | flops 19629342720 | bytes 34078720 | tf_op jit(solution)/shard_map/score_bias_back/pallas_call | solution.py:1002
  434.2 19.2 %weight_grad_pack.3 = (bf16[16,792,128]{2,1,0:T(8,128)(2,1)}, bf16[16,792,128]{2,1,0:T(8,128)(2,1)}) custom-call(s32[5]{0:T(128)} %stack.63.me_ref, bf16[832,1024]{1,0:T(8,128)(2,1)} %get-tuple-element.148.a_ref, bf16[832,3072]{1,0:T(8,128)(2,1)} %get-tuple-element.176.b_ref.mixed_ref), custom_call_target="tpu_custom_call" | custom-call | flops 104689827840 | bytes 125829120 | tf_op jit(solution)/shard_map/weight_grad_pack/pallas_call | solution.py:584
  476.5 14.7 %first_back.1 = (bf16[832,1024]{1,0:T(8,128)(2,1)}, f32[8,1024]{1,0:T(8,128)}) custom-call(bf16[832,3072]{1,0:T(8,128)(2,1)} %get-tuple-element.176.b_ref.mixed_ref, bf16[1024,3072]{1,0:T(8,128)(2,1)} %get-tuple-element.111.w_ref, bf16[832,1024]{1,0:T(8,128)(2,1)} %get-tuple-element.113.x_ref, f32[832,1024]{1,0:T(8,128)} %get-tuple-element.177.mg_ref, ...), custom_call_target="tpu_custom_call" | custom-call | flops 104689827840 | bytes 364380160 | tf_op jit(solution)/shard_map/first_back/pallas_call | solution.py:1387
  519.2 8.3 %collective-permute-done.49 = bf16[1,792,128]{2,1,0:T(8,128)(2,1)} collective-permute-done((bf16[1,792,128]{2,1,0:T(8,128)(2,1)}, bf16[1,792,128]{2,1,0:T(8,128)(2,1)}, u32[]{:S(2)}, u32[]{:S(2)}) %collective-permute-start.49) | collective-permute-done | bytes 202784 | tf_op jit(solution)/shard_map/ppermute | solution.py:131
  583.4 8.2 %stack.72 = f32[13]{0:T(128)S(1)} concatenate(f32[1]{0:T(128)} %bitcast.30, f32[1]{0:T(128)} %bitcast.31, f32[1]{0:T(128)} %bitcast.37, f32[1]{0:T(128)} %bitcast.38, f32[1]{0:T(128)} %bitcast.39, f32[1]{0:T(128)} %bitcast.40, f32[1]{0:T(128)} %bitcast.41, f32[1]{0:T(128)} %bitcast.42, f32[1]{0:T(128)} %bitcast.43, f32[1]{0:T(128)} %bitcast.44, f32[1]{0:T(128)} %bitcast.45, ...), dimensions={0} | concatenate | bytes 104 | tf_op jit(solution)/shard_map/stack | solution.py:1634
  593.4 11.6 %moments_update.1 = (f32[3081,128]{1,0:T(8,128)}, f32[3081,128]{1,0:T(8,128)}, f32[3081,128]{1,0:T(8,128)}) custom-call(s32[5]{0:T(128)} %stack.63.me_ref, f32[4]{0:T(128)} %pad_maximum_fusion.4.coef_ref, f32[792,128]{1,0:T(8,128)} %get-tuple-element.222.refs_0_, f32[792,128]{1,0:T(8,128)} %collective-permute-done.66.refs_1_, ...), custom_call_target="tpu_custom_call" | custom-call | tf_op jit(solution)/shard_map/moments_update/pallas_call | solution.py:832
  (295 shorter events, 263.3 us)
Async XLA Ops:
  58.3 73.2 %collective-permute-start.9 = (bf16[8,792,128]{2,1,0:T(8,128)(2,1)S(1)}, bf16[8,792,128]{2,1,0:T(8,128)(2,1)}, u32[]{:S(2)}, u32[]{:S(2)}) collective-permute-start(bf16[8,792,128]{2,1,0:T(8,128)(2,1)S(1)} %constant_dynamic-update-slice_fusion.refs_0_), channel_id=1, source_target_pairs={{0,8},{1,9},{2,10},{3,11},{4,12},{5,13},{6,14},{7,15},{8,0},{9,1},... | collective-permute-start | bytes 4866056 | tf_op jit(solution)/shard_map/ppermute | solution.py:131
  77.9 53.7 %collective-permute-start.10 = (bf16[8,792,128]{2,1,0:T(8,128)(2,1)}, bf16[8,792,128]{2,1,0:T(8,128)(2,1)}, u32[]{:S(2)}, u32[]{:S(2)}) collective-permute-start(bf16[8,792,128]{2,1,0:T(8,128)(2,1)} %collective-permute-done.8.refs_1_), channel_id=1, source_target_pairs={{0,8},{1,9},{2,10},{3,11},{4,12},{5,13},{6,14},{7,15},{8,0},{9,1},... | collective-permute-start | bytes 4866056 | tf_op jit(solution)/shard_map/ppermute | solution.py:131
  100.8 28.1 %collective-permute-start.22 = (bf16[4,792,128]{2,1,0:T(8,128)(2,1)}, bf16[4,792,128]{2,1,0:T(8,128)(2,1)}, u32[]{:S(2)}, u32[]{:S(2)}) collective-permute-start(bf16[4,792,128]{2,1,0:T(8,128)(2,1)} %constant_dynamic-update-slice_fusion.2), channel_id=1, source_target_pairs={{0,16},{1,17},{2,18},{3,19},{4,20},{5,21},{6,22},{7,23},{8,9},{9,8... | collective-permute-start | bytes 2433032 | tf_op jit(solution)/shard_map/ppermute | solution.py:131
  149.8 36.9 %collective-permute-start.23 = (bf16[8,792,128]{2,1,0:T(8,128)(2,1)}, bf16[8,792,128]{2,1,0:T(8,128)(2,1)}, u32[]{:S(2)}, u32[]{:S(2)}) collective-permute-start(bf16[8,792,128]{2,1,0:T(8,128)(2,1)} %pad_maximum_fusion.refs_0_), channel_id=1, source_target_pairs={{0,1},{1,0},{2,3},{3,2},{4,5},{5,4},{6,7},{7,6},{8,24},{9,25},{10,... | collective-permute-start | bytes 4866056 | tf_op jit(solution)/shard_map/ppermute | solution.py:131
  160.5 43.8 %collective-permute-start.24 = (bf16[8,792,128]{2,1,0:T(8,128)(2,1)}, bf16[8,792,128]{2,1,0:T(8,128)(2,1)}, u32[]{:S(2)}, u32[]{:S(2)}) collective-permute-start(bf16[8,792,128]{2,1,0:T(8,128)(2,1)} %pad_maximum_fusion.refs_0_), channel_id=1, source_target_pairs={{0,8},{1,9},{2,10},{3,11},{4,12},{5,13},{6,14},{7,15},{8,0},{9,1},... | collective-permute-start | bytes 4866056 | tf_op jit(solution)/shard_map/ppermute | solution.py:131
  183.1 41.2 %collective-permute-start.27 = (bf16[8,792,128]{2,1,0:T(8,128)(2,1)}, bf16[8,792,128]{2,1,0:T(8,128)(2,1)}, u32[]{:S(2)}, u32[]{:S(2)}) collective-permute-start(bf16[8,792,128]{2,1,0:T(8,128)(2,1)} %constant_dynamic-update-slice_fusion.10.refs_4_.refs_0_), channel_id=1, source_target_pairs={{0,8},{1,9},{2,10},{3,11},{4,12},{5,13},{6,14},{7,15},{8,0},{9,1},... | collective-permute-start | bytes 4866056 | tf_op jit(solution)/shard_map/ppermute | solution.py:131
  200.8 68.0 %collective-permute-start.30 = (bf16[8,792,128]{2,1,0:T(8,128)(2,1)}, bf16[8,792,128]{2,1,0:T(8,128)(2,1)}, u32[]{:S(2)}, u32[]{:S(2)}) collective-permute-start(bf16[8,792,128]{2,1,0:T(8,128)(2,1)} %copy-done.11), channel_id=1, source_target_pairs={{0,1},{1,0},{2,3},{3,2},{4,5},{5,4},{6,7},{7,6},{8,24},{9,25},{10,... | collective-permute-start | bytes 4866056 | tf_op jit(solution)/shard_map/ppermute | solution.py:131
  293.3 51.5 %collective-permute-start.33 = (bf16[8,792,128]{2,1,0:T(8,128)(2,1)}, bf16[8,792,128]{2,1,0:T(8,128)(2,1)}, u32[]{:S(2)}, u32[]{:S(2)}) collective-permute-start(bf16[8,792,128]{2,1,0:T(8,128)(2,1)} %add_convert_fusion.3), channel_id=1, source_target_pairs={{0,1},{1,0},{2,3},{3,2},{4,5},{5,4},{6,7},{7,6},{8,24},{9,25},{10,... | collective-permute-start | bytes 4866056 | tf_op jit(solution)/shard_map/ppermute | solution.py:131
  342.8 27.2 %collective-permute-start.34 = (bf16[16,792,128]{2,1,0:T(8,128)(2,1)}, bf16[16,792,128]{2,1,0:T(8,128)(2,1)}, u32[]{:S(2)}, u32[]{:S(2)}) collective-permute-start(bf16[16,792,128]{2,1,0:T(8,128)(2,1)} %get-tuple-element.155), channel_id=1, source_target_pairs={{0,8},{1,9},{2,10},{3,11},{4,12},{5,13},{6,14},{7,15},{8,0},{9,1},... | collective-permute-start | bytes 9732104 | tf_op jit(solution)/shard_map/ppermute | solution.py:131
  365.6 43.4 %collective-permute-start.55 = (bf16[1,792,128]{2,1,0:T(8,128)(2,1)}, bf16[1,792,128]{2,1,0:T(8,128)(2,1)}, u32[]{:S(2)}, u32[]{:S(2)}) collective-permute-start(bf16[1,792,128]{2,1,0:T(8,128)(2,1)} %get-tuple-element.232), channel_id=1, source_target_pairs={{0,2},{1,3},{2,0},{3,1},{4,6},{5,7},{6,4},{7,5},{8,10},{9,11},{10,... | collective-permute-start | bytes 608264 | tf_op jit(solution)/shard_map/ppermute | solution.py:131
  366.6 42.4 %collective-permute-start.56 = (bf16[1,792,128]{2,1,0:T(8,128)(2,1)}, bf16[1,792,128]{2,1,0:T(8,128)(2,1)}, u32[]{:S(2)}, u32[]{:S(2)}) collective-permute-start(bf16[1,792,128]{2,1,0:T(8,128)(2,1)} %get-tuple-element.234), channel_id=1, source_target_pairs={{0,4},{1,5},{2,6},{3,7},{4,0},{5,1},{6,2},{7,3},{8,12},{9,13},{10,... | collective-permute-start | bytes 608264 | tf_op jit(solution)/shard_map/ppermute | solution.py:131
  368.5 40.5 %collective-permute-start.57 = (bf16[1,792,128]{2,1,0:T(8,128)(2,1)}, bf16[1,792,128]{2,1,0:T(8,128)(2,1)}, u32[]{:S(2)}, u32[]{:S(2)}) collective-permute-start(bf16[1,792,128]{2,1,0:T(8,128)(2,1)} %get-tuple-element.233), channel_id=1, source_target_pairs={{0,6},{1,7},{2,4},{3,5},{4,2},{5,3},{6,0},{7,1},{8,14},{9,15},{10,... | collective-permute-start | bytes 608264 | tf_op jit(solution)/shard_map/ppermute | solution.py:131
  373.0 52.8 %collective-permute-start.36 = (bf16[8,792,128]{2,1,0:T(8,128)(2,1)}, bf16[8,792,128]{2,1,0:T(8,128)(2,1)}, u32[]{:S(2)}, u32[]{:S(2)}) collective-permute-start(bf16[8,792,128]{2,1,0:T(8,128)(2,1)} %add_convert_fusion.2), channel_id=1, source_target_pairs={{0,1},{1,0},{2,3},{3,2},{4,5},{5,4},{6,7},{7,6},{8,24},{9,25},{10,... | collective-permute-start | bytes 4866056 | tf_op jit(solution)/shard_map/ppermute | solution.py:131
  381.8 49.8 %collective-permute-start.37 = (bf16[16,792,128]{2,1,0:T(8,128)(2,1)}, bf16[16,792,128]{2,1,0:T(8,128)(2,1)}, u32[]{:S(2)}, u32[]{:S(2)}) collective-permute-start(bf16[16,792,128]{2,1,0:T(8,128)(2,1)} %get-tuple-element.167), channel_id=1, source_target_pairs={{0,8},{1,9},{2,10},{3,11},{4,12},{5,13},{6,14},{7,15},{8,0},{9,1},... | collective-permute-start | bytes 9732104 | tf_op jit(solution)/shard_map/ppermute | solution.py:131
  430.0 23.5 %collective-permute-start.38 = (bf16[4,792,128]{2,1,0:T(8,128)(2,1)}, bf16[4,792,128]{2,1,0:T(8,128)(2,1)}, u32[]{:S(2)}, u32[]{:S(2)}) collective-permute-start(bf16[4,792,128]{2,1,0:T(8,128)(2,1)} %slice.376), channel_id=1, source_target_pairs={{0,16},{1,17},{2,18},{3,19},{4,20},{5,21},{6,22},{7,23},{8,9},{9,8... | collective-permute-start | bytes 2433032 | tf_op jit(solution)/shard_map/ppermute | solution.py:131
  433.6 28.4 %collective-permute-start.39 = (bf16[8,792,128]{2,1,0:T(8,128)(2,1)S(1)}, bf16[8,792,128]{2,1,0:T(8,128)(2,1)}, u32[]{:S(2)}, u32[]{:S(2)}) collective-permute-start(bf16[8,792,128]{2,1,0:T(8,128)(2,1)S(1)} %add_convert_fusion.1), channel_id=1, source_target_pairs={{0,1},{1,0},{2,3},{3,2},{4,5},{5,4},{6,7},{7,6},{8,24},{9,25},{10,... | collective-permute-start | bytes 4866056 | tf_op jit(solution)/shard_map/ppermute | solution.py:131
  457.6 51.1 %collective-permute-start.52 = (bf16[1,792,128]{2,1,0:T(8,128)(2,1)}, bf16[1,792,128]{2,1,0:T(8,128)(2,1)S(1)}, u32[]{:S(2)}, u32[]{:S(2)}) collective-permute-start(bf16[1,792,128]{2,1,0:T(8,128)(2,1)} %get-tuple-element.229), channel_id=1, source_target_pairs={{0,2},{1,3},{2,0},{3,1},{4,6},{5,7},{6,4},{7,5},{8,10},{9,11},{10,... | collective-permute-start | bytes 608264 | tf_op jit(solution)/shard_map/ppermute | solution.py:131
  457.9 51.6 %collective-permute-start.53 = (bf16[1,792,128]{2,1,0:T(8,128)(2,1)}, bf16[1,792,128]{2,1,0:T(8,128)(2,1)}, u32[]{:S(2)}, u32[]{:S(2)}) collective-permute-start(bf16[1,792,128]{2,1,0:T(8,128)(2,1)} %get-tuple-element.231), channel_id=1, source_target_pairs={{0,4},{1,5},{2,6},{3,7},{4,0},{5,1},{6,2},{7,3},{8,12},{9,13},{10,... | collective-permute-start | bytes 608264 | tf_op jit(solution)/shard_map/ppermute | solution.py:131
  460.5 50.6 %collective-permute-start.54 = (bf16[1,792,128]{2,1,0:T(8,128)(2,1)}, bf16[1,792,128]{2,1,0:T(8,128)(2,1)}, u32[]{:S(2)}, u32[]{:S(2)}) collective-permute-start(bf16[1,792,128]{2,1,0:T(8,128)(2,1)} %get-tuple-element.230), channel_id=1, source_target_pairs={{0,6},{1,7},{2,4},{3,5},{4,2},{5,3},{6,0},{7,1},{8,14},{9,15},{10,... | collective-permute-start | bytes 608264 | tf_op jit(solution)/shard_map/ppermute | solution.py:131
  467.0 24.2 %collective-permute-start.42 = (bf16[4,792,128]{2,1,0:T(8,128)(2,1)}, bf16[4,792,128]{2,1,0:T(8,128)(2,1)}, u32[]{:S(2)}, u32[]{:S(2)}) collective-permute-start(bf16[4,792,128]{2,1,0:T(8,128)(2,1)} %slice.375), channel_id=1, source_target_pairs={{0,16},{1,17},{2,18},{3,19},{4,20},{5,21},{6,22},{7,23},{8,9},{9,8... | collective-permute-start | bytes 2433032 | tf_op jit(solution)/shard_map/ppermute | solution.py:131
  511.1 25.9 %collective-permute-start.51 = (bf16[4,792,128]{2,1,0:T(8,128)(2,1)}, bf16[4,792,128]{2,1,0:T(8,128)(2,1)}, u32[]{:S(2)}, u32[]{:S(2)}) collective-permute-start(bf16[4,792,128]{2,1,0:T(8,128)(2,1)} %slice.374), channel_id=1, source_target_pairs={{0,16},{1,17},{2,18},{3,19},{4,20},{5,21},{6,22},{7,23},{8,9},{9,8... | collective-permute-start | bytes 2433032 | tf_op jit(solution)/shard_map/ppermute | solution.py:131
  544.7 33.0 %collective-permute-start.66 = (f32[792,128]{1,0:T(8,128)}, f32[792,128]{1,0:T(8,128)}, u32[]{:S(2)}, u32[]{:S(2)}) collective-permute-start(f32[792,128]{1,0:T(8,128)} %get-tuple-element.221), channel_id=1, source_target_pairs={{0,8},{1,9},{2,10},{3,11},{4,12},{5,13},{6,14},{7,15},{16,24},{17,... | collective-permute-start | bytes 1216520 | tf_op jit(solution)/shard_map/ppermute | solution.py:712
  551.5 40.7 %collective-permute-start.67 = (f32[792,128]{1,0:T(8,128)}, f32[792,128]{1,0:T(8,128)}, u32[]{:S(2)}, u32[]{:S(2)}) collective-permute-start(f32[792,128]{1,0:T(8,128)} %get-tuple-element.220), channel_id=1, source_target_pairs={{0,16},{1,17},{2,18},{3,19},{4,20},{5,21},{6,22},{7,23},{8,24},{9,... | collective-permute-start | bytes 1216520 | tf_op jit(solution)/shard_map/ppermute | solution.py:712
  562.5 29.7 %collective-permute-start.68 = (f32[792,128]{1,0:T(8,128)}, f32[792,128]{1,0:T(8,128)S(1)}, u32[]{:S(2)}, u32[]{:S(2)}) collective-permute-start(f32[792,128]{1,0:T(8,128)} %get-tuple-element.208), channel_id=1, source_target_pairs={{0,24},{1,25},{2,26},{3,27},{4,28},{5,29},{6,30},{7,31},{8,16},{9,... | collective-permute-start | bytes 1216520 | tf_op jit(solution)/shard_map/ppermute | solution.py:712
  (81 other events, 1124.7 us)

commit v4 on v3

--- a/solution.py
+++ b/solution.py
@@ -82,7 +82,7 @@
     return pltpu.CompilerParams(vmem_limit_bytes=VMEM_LIMIT, **more)
 
 
-COST_SCALE = 20
+COST_SCALE = 200
 
 
 def cost(flops, bytes_accessed, transcendentals=0):
@@ -117,7 +117,7 @@
         self.slot = 4 * self.quarter
         assert self.slot % 16 == 0
         tiles = self.slot // 16
-        self.chunk = max(t for t in range(1, 13) if tiles % t == 0)
+        self.chunk = max(t for t in range(1, 34) if tiles % t == 0)
         self.bit_x, self.bit_core, self.bit_y = 2 * fsdp, fsdp, 1
 
     def base(self, device):
@@ -191,7 +191,15 @@
     )(me, shard, spill)
 
 
-def spot(geo, me_ref, device, own, quarter_x):
+GATHER_PHASES = ((0,), (1,), (2,), (3,))
+REDUCE_PHASES = ((0,), (1,), (2,), (3,))
+
+
+def phase_of(phases, group):
+    return [number for number, groups in enumerate(phases) if group in groups][0]
+
+
+def spot(geo, me_ref, device, own, quarter_x, groups):
     core = me_ref[2] if own else 1 - me_ref[2]
     rel_x = quarter_x ^ me_ref[1]
     rel_z = (lax.rem(device, geo.fsdp) // 2) ^ me_ref[3]
@@ -199,15 +207,18 @@
     straight = core == 0
     first = jnp.where(straight, rel_x, rel_y)
     late = jnp.where(straight, rel_y, rel_x)
-    return quarter_x * 2 + core, late, first * geo.line + rel_z
-
-
-def by_group(geo, groups, device, action):
-    if len(groups) == 1:
-        action(0)
+    at = (first * geo.line + rel_z) * len(groups) + device // geo.fsdp - groups[0]
+    return quarter_x * 2 + core, late, at
+
+
+def by_phase(geo, phases, numbers, device, action):
+    if len(numbers) == 1:
+        action(0, phases[numbers[0]])
         return
-    for position, group in enumerate(groups):
-        pl.when(device // geo.fsdp == group)(partial(action, position))
+    group = device // geo.fsdp
+    for position, number in enumerate(numbers):
+        groups = phases[number]
+        pl.when((group >= groups[0]) & (group <= groups[-1]))(partial(action, position, groups))
 
 
 class Region:
@@ -223,7 +234,9 @@
         self.pitch = 17 if self.cols % 32 == 0 else 16
         self.stride = self.cols * self.pitch // 16
         self.scratch_tiles = (geo.base(self.high) + geo.slot - self.origin) // 16
-        self.groups = sorted({d // geo.fsdp for d in range(self.low, self.high + 1)})
+        groups = {d // geo.fsdp for d in range(self.low, self.high + 1)}
+        self.gather = sorted({phase_of(GATHER_PHASES, group) for group in groups})
+        self.reduce = sorted({phase_of(REDUCE_PHASES, group) for group in groups})
 
     def address(self, row):
         rel = row - self.origin
@@ -244,7 +257,7 @@
 
 
 def unpack_kernel(geo, region, block, aliased, me_ref, *refs):
-    arrays = 4 * len(region.groups)
+    arrays = 4 * len(region.gather)
     srcs, refs = refs[:arrays], refs[arrays:]
     if aliased:
         refs = refs[1:]
@@ -258,10 +271,10 @@
         device = region.low + step
         buf = lax.rem(step, 2)
 
-        def from_group(position):
+        def from_phase(position, groups):
             for own in range(2):
                 for quarter_x in range(2):
-                    q, late, at = spot(geo, me_ref, device, own, quarter_x)
+                    q, late, at = spot(geo, me_ref, device, own, quarter_x, groups)
                     to = pl.ds(pl.multiple_of(q * quarter, 8), quarter)
                     for side in range(2):
                         src = srcs[position * 4 + (1 - own) * 2 + side]
@@ -274,7 +287,7 @@
                                 sems.at[buf, own * 2 + quarter_x],
                             ).start()
 
-        by_group(geo, region.groups, device, from_group)
+        by_phase(geo, GATHER_PHASES, region.gather, device, from_phase)
 
     fetch(0)
 
@@ -347,7 +360,7 @@
 
 
 def unpack(geo, region, me, gathered, weight=None):
-    operands = [me] + [array for group in region.groups for array in gathered[group]]
+    operands = [me] + [array for phase in region.gather for array in gathered[phase]]
     specs = [smem()] + [anywhere()] * (len(operands) - 1)
     aliases = {}
     if weight is not None:
@@ -401,12 +414,12 @@
 
     def copies(self, device, action):
         geo = self.geo
-        count = 2 * geo.line
-
-        def to_group(position):
+
+        def to_phase(position, groups):
+            count = 2 * geo.line * len(groups)
             for own in range(2):
                 for quarter_x in range(2):
-                    q, late, at = spot(geo, self.me_ref, device, own, quarter_x)
+                    q, late, at = spot(geo, self.me_ref, device, own, quarter_x, groups)
                     rows = pl.ds(pl.multiple_of(q * geo.quarter, 8), geo.quarter)
                     action(
                         self.outs[position * 2 + 1 - own].at[late * count + at],
@@ -414,7 +427,7 @@
                         own * 2 + quarter_x,
                     )
 
-        by_group(geo, self.region.groups, device, to_group)
+        by_phase(geo, REDUCE_PHASES, self.region.reduce, device, to_phase)
 
     def begin(self):
         clear_rows(self.region, self.flat_ref)
@@ -450,9 +463,12 @@
                 def rows_body(i, _):
                     t0 = i * geo.chunk
                     r0 = pl.multiple_of(t0 * 16, 16)
-                    for t in range(geo.chunk):
-                        value = self.flat_ref[pl.ds((first_tile + t0 + t) * pitch, 16), :]
-                        here = pl.ds(r0 + t * 16, 16)
+                    run = 1 if pitch > 16 else geo.chunk
+                    for t in range(0, geo.chunk, run):
+                        row = (first_tile + t0 + t) * pitch
+                        row = pl.multiple_of(row, 16) if pitch == 16 else row
+                        value = self.flat_ref[pl.ds(row, run * 16), :]
+                        here = pl.ds(r0 + t * 16, run * 16)
                         if add:
                             value = value + self.old_ref[here, :].astype(F32)
                         self.slot_ref[parity, here, :] = value.astype(BF16)
@@ -512,27 +528,29 @@
 
 
 def with_slots(geo, region, slots, operands, specs):
-    shape = jax.ShapeDtypeStruct((4 * geo.line, geo.quarter, LANES), BF16)
+    shapes = []
     aliases = {}
-    for position, group in enumerate(region.groups):
+    for position, phase in enumerate(region.reduce):
+        count = 4 * geo.line * len(REDUCE_PHASES[phase])
         for number in range(2):
-            if group in slots:
-                operands.append(slots[group][number])
+            shapes.append(jax.ShapeDtypeStruct((count, geo.quarter, LANES), BF16))
+            if phase in slots:
+                operands.append(slots[phase][number])
                 specs.append(anywhere())
                 aliases[len(operands) - 1] = position * 2 + number
-    return [shape] * (2 * len(region.groups)), aliases, len(aliases)
+    return shapes, aliases, len(aliases)
 
 
 def updated_slots(region, slots, results):
     merged = dict(slots)
-    for position, group in enumerate(region.groups):
-        merged[group] = results[position * 2 : position * 2 + 2]
+    for position, phase in enumerate(region.reduce):
+        merged[phase] = results[position * 2 : position * 2 + 2]
     return merged
 
 
-def pack_kernel(geo, region, shared, grid_steps, height, skip, me_ref, a_ref, b_ref, *refs):
+def pack_kernel(geo, region, shared, grid_steps, skip, me_ref, a_ref, b_ref, *refs):
     vec_refs, refs = refs[: len(region.vectors)], refs[len(region.vectors) + skip :]
-    arrays = 2 * len(region.groups)
+    arrays = 2 * len(region.reduce)
     *scratch, left_ref = refs[arrays:]
     emitter = Emitter(geo, region, shared, me_ref, refs[:arrays], *scratch)
     flat_ref = emitter.flat_ref
@@ -548,15 +566,18 @@
 
             copy_rows(region, flat_ref, row, count, move)
 
-    left_ref[...] = a_ref[...].T
-
-    def panel(j, _):
-        lanes = pl.ds(pl.multiple_of(j * 512, 512), 512)
-        store_columns(region, flat_ref, step * height, j * 4, nn(left_ref[...], b_ref[:, lanes]))
-        return 0
-
-    lax.fori_loop(0, region.cols // 4, panel, 0)
-    emit_rows(emitter, step, grid_steps, height)
+        for r in range(0, region.depth, 256):
+            left_ref[r : r + 256, :] = a_ref[:, r : r + 256].T
+
+    width = b_ref.shape[1]
+    store_columns(
+        region, flat_ref, 0, step * (width // LANES), nn(left_ref[...], b_ref[...])
+    )
+
+    @pl.when(step == grid_steps - 1)
+    def _():
+        emitter.emit(0, region.slots)
+        emitter.finish()
 
 
 def emit_rows(emitter, step, grid_steps, height):
@@ -571,26 +592,27 @@
 
 def pack(geo, region, me, left, right, vectors, slots, shared):
     tokens = left.shape[0]
-    height = 256
-    steps = region.depth // height
-    width = region.cols * LANES
+    width = 512
+    steps = region.cols * LANES // width
     operands = [me, left, right] + vectors
     specs = [
         smem(),
-        pl.BlockSpec((tokens, height), lambda k: (0, k)),
-        pl.BlockSpec((tokens, width), lambda k: (0, 0), pipeline_mode=pl.Buffered(1)),
+        pl.BlockSpec((tokens, region.depth), lambda k: (0, 0), pipeline_mode=pl.Buffered(1)),
+        pl.BlockSpec((tokens, width), lambda k: (0, k)),
     ] + [pl.BlockSpec(vector.shape, lambda k: (0, 0)) for vector in vectors]
     shapes, aliases, skip = with_slots(geo, region, slots, operands, specs)
     results = pl.pallas_call(
-        partial(pack_kernel, geo, region, shared, steps, height, skip),
+        partial(pack_kernel, geo, region, shared, steps, skip),
         grid=(steps,),
         out_shape=shapes,
         in_specs=specs,
         out_specs=[anywhere()] * len(shapes),
-        scratch_shapes=emit_scratch(geo, region) + [pltpu.VMEM((height, tokens), BF16)],
+        scratch_shapes=emit_scratch(geo, region) + [pltpu.VMEM((region.depth, tokens), BF16)],
         input_output_aliases=aliases,
         compiler_params=params_of(),
-        cost_estimate=cost(2 * tokens * region.depth * width, 2 * region.depth * width),
+        cost_estimate=cost(
+            2 * tokens * region.depth * width * steps, 2 * region.depth * width * steps
+        ),
         name="weight_grad_pack",
     )(*operands)
     return updated_slots(region, slots, results)
@@ -615,117 +637,182 @@
     return pieces
 
 
+def light():
+    return pl.CostEstimate(flops=1024, bytes_accessed=1024, transcendentals=0)
+
+
+def join_kernel(*refs):
+    out_ref = refs[-1]
+    start = 0
+    for ref in refs[:-1]:
+        out_ref[start : start + ref.shape[0]] = ref[...]
+        start += ref.shape[0]
+
+
+def join(parts):
+    count = sum(part.shape[0] for part in parts)
+    return pl.pallas_call(
+        join_kernel,
+        out_shape=jax.ShapeDtypeStruct((count,) + parts[0].shape[1:], parts[0].dtype),
+        in_specs=[vmem()] * len(parts),
+        out_specs=vmem(),
+        compiler_params=params_of(),
+        cost_estimate=light(),
+        name="join",
+    )(*parts)
+
+
 class Gather:
-    def __init__(self, geo, piece):
-        self.geo, self.held = geo, piece[None]
+    def __init__(self, geo, pieces):
+        self.geo, self.held = geo, pieces
 
     def line(self, *deps):
         held = after(self.held, *deps)
-        for masks in line_masks(self.geo):
+        stages = line_masks(self.geo)
+        for masks in stages[:-1]:
             moved = [self.geo.permute(held, mask, mask) for mask in masks]
             held = jnp.concatenate([held] + moved, axis=0)
         self.held = held
+        self.moved = [self.geo.permute(held, mask, mask) for mask in stages[-1]]
+
+    def joined(self, *deps):
+        self.held = join([self.held] + [after(part, *deps) for part in self.moved])
+        return self.held
 
     def across(self, *deps):
-        held = after(self.held, *deps)
-        self.near = jnp.concatenate(
-            [held, self.geo.permute(held, self.geo.bit_x, self.geo.bit_y)], axis=0
+        self.moved = self.geo.permute(
+            after(self.held, *deps), self.geo.bit_x, self.geo.bit_y
         )
 
     def last(self, *deps):
-        near = after(self.near, *deps)
-        self.far = self.geo.permute(near, self.geo.bit_y, self.geo.bit_x)
-        self.near_other = self.geo.core_swap(near)
+        self.near = join([self.held, after(self.moved, *deps)])
+        self.moved = self.geo.permute(self.near, self.geo.bit_y, self.geo.bit_x)
+        self.near_other = self.geo.core_swap(self.near)
+        return self.near
 
     def finish(self, *deps):
-        far = after(self.far, *deps)
-        return [self.near, far, self.near_other, self.geo.core_swap(far)]
+        far = after(self.moved, *deps)
+        return [self.near, far, after(self.near_other, *deps), self.geo.core_swap(far)]
+
+
+def add_far_kernel(keep_ref, got_ref, out_ref):
+    out_ref[...] = (keep_ref[...].astype(F32) + got_ref[...].astype(F32)).astype(BF16)
+
+
+def add_near_kernel(keep_ref, got_ref, far_ref, kept_ref, moved_ref):
+    total = keep_ref[...].astype(F32) + got_ref[...].astype(F32) + far_ref[...].astype(F32)
+    half = kept_ref.shape[0]
+    kept_ref[...] = total[:half]
+    moved_ref[...] = total[half:].astype(BF16)
+
+
+def add_line_kernel(near_ref, across_ref, own_ref, *moved_refs):
+    own = own_ref.shape[0]
+    own_ref[...] = near_ref[:own] + across_ref[:own].astype(F32)
+    for number, ref in enumerate(moved_refs):
+        rows = slice((number + 1) * own, (number + 2) * own)
+        ref[...] = (near_ref[rows] + across_ref[rows].astype(F32)).astype(BF16)
+
+
+def add_total_kernel(own_ref, *refs):
+    total = own_ref[...]
+    for ref in refs[:-1]:
+        total = total + ref[...].astype(F32)
+    refs[-1][...] = total
 
 
 class Reduction:
-    def __init__(self, geo, slots):
+    def __init__(self, geo, slots, phase):
         self.geo = geo
+        self.count = geo.line * len(REDUCE_PHASES[phase])
         self.keep, send = slots
         self.got = geo.core_swap(send)
+        self.block = (1, geo.quarter, LANES)
+
+    def call(self, kernel, out_shape, **more):
+        return pl.pallas_call(
+            kernel,
+            out_shape=out_shape,
+            compiler_params=params_of(),
+            cost_estimate=light(),
+            name="add_terms",
+            **more,
+        )
+
+    def shape(self, count, dtype):
+        return jax.ShapeDtypeStruct((count,) + self.block[1:], dtype)
 
     def last(self, *deps):
-        count = 2 * self.geo.line
+        count = 2 * self.count
         got = after(self.got, *deps)
-        far = (self.keep[count:].astype(F32) + got[count:].astype(F32)).astype(BF16)
+        later = pl.BlockSpec((count,) + self.block[1:], lambda i: (1, 0, 0))
+        far = self.call(
+            add_far_kernel,
+            self.shape(count, BF16),
+            grid=(1,),
+            in_specs=[later, later],
+            out_specs=vmem(),
+        )(self.keep, got)
         self.from_far = self.geo.permute(far, self.geo.bit_y, self.geo.bit_x)
         self.got = got
         return far
 
     def across(self, *deps):
-        count = 2 * self.geo.line
-        from_far = after(self.from_far, *deps)
-        near = self.keep[:count].astype(F32) + self.got[:count].astype(F32) + from_far.astype(F32)
-        count = self.geo.line
-        moved = near[count:].astype(BF16)
+        count = self.count
+        part = pl.BlockSpec((2 * count,) + self.block[1:], lambda i: (0, 0, 0))
+        self.near, moved = self.call(
+            add_near_kernel,
+            [self.shape(count, F32), self.shape(count, BF16)],
+            grid=(1,),
+            in_specs=[part, part, part],
+            out_specs=[vmem(), vmem()],
+        )(self.keep, self.got, after(self.from_far, *deps))
         self.from_across = self.geo.permute(moved, self.geo.bit_x, self.geo.bit_y)
-        self.near = near[:count]
         return moved
 
     def line(self, *deps):
-        held = self.near + after(self.from_across, *deps).astype(F32)
+        near, received = self.near, after(self.from_across, *deps)
         stages = line_masks(self.geo)[::-1]
-        for masks in stages[:-1]:
-            held = self.add_line(held, masks)[0]
-        self.held, self.parts = self.send_line(held, stages[-1])
-        return self.held
-
-    def send_line(self, held, masks):
-        block = held.shape[0] // (len(masks) + 1)
-        parts = [
-            self.geo.permute(
-                held[(number + 1) * block : (number + 2) * block].astype(BF16), mask, mask
-            )
-            for number, mask in enumerate(masks)
-        ]
-        return held[:block], parts
-
-    def add_line(self, held, masks):
-        held, parts = self.send_line(held, masks)
-        for part in parts:
-            held = held + part.astype(F32)
-        return held, None
+        for masks in stages:
+            own = near.shape[0] // (len(masks) + 1)
+            near, *parts = self.call(
+                add_line_kernel,
+                [self.shape(own, F32)] + [self.shape(own, BF16)] * len(masks),
+                in_specs=[vmem(), vmem()],
+                out_specs=[vmem()] * (len(masks) + 1),
+            )(near, received)
+            moved = [self.geo.permute(part, mask, mask) for part, mask in zip(parts, masks)]
+            if masks is not stages[-1]:
+                (received,) = moved
+        self.near, self.parts = near, moved
+        return near
 
     def total(self, *deps):
-        total = self.held
-        for part in self.parts:
-            total = total + after(part, *deps).astype(F32)
-        return total[0]
-
-
-def collect_early(geo, sums, dp_index):
-    mine = [jnp.where(dp_index == group, sums[group], 0.0) for group in (1, 2, 3)]
-    pieces = [mine[0] + mine[1] + mine[2]]
+        parts = [after(part, *deps) for part in self.parts]
+        return self.call(
+            add_total_kernel,
+            self.shape(self.near.shape[0], F32),
+            in_specs=[vmem()] * (1 + len(parts)),
+            out_specs=vmem(),
+        )(self.near, *parts)
+
+
+def collect_quarters(geo, sums, dp_index):
+    def of_group(group):
+        low = jnp.where(group == 0, sums[0], sums[1])
+        return jnp.where(group < 2, low, jnp.where(group == 2, sums[2], sums[3]))
+
+    pieces = [of_group(dp_index)]
     for offset in (1, 2, 3):
-        target = dp_index ^ offset
-        piece = jnp.where(target == 1, sums[1], jnp.where(target == 2, sums[2], sums[3]))
-        pairs = [
-            (dp * geo.fsdp + i, (dp ^ offset) * geo.fsdp + i)
-            for dp in range(4)
-            for i in range(geo.fsdp)
-            if dp != offset
-        ]
-        pieces.append(lax.ppermute(piece, AXES, pairs))
+        mask = offset * geo.fsdp
+        pieces.append(geo.permute(of_group(dp_index ^ offset).astype(BF16), mask, mask))
     return pieces
 
 
-def collect_late(geo, total, dp_index):
-    pieces = [jnp.where(dp_index == 0, total, 0.0)]
-    for offset in (1, 2, 3):
-        pairs = [(offset * geo.fsdp + i, i) for i in range(geo.fsdp)]
-        pieces.append(lax.ppermute(total, AXES, pairs))
-    return pieces
-
-
-def sum_everywhere(geo, value):
-    mask = 1
-    while mask < geo.devices:
-        value = value + geo.permute(value, mask, mask)
-        mask *= 2
+def sum_everywhere(geo, value, start=0, stop=None):
+    bits = geo.devices.bit_length() - 1
+    for bit in range(start, bits if stop is None else stop):
+        value = value + geo.permute(value, 1 << bit, 1 << bit)
     return value
 
 
@@ -744,15 +831,16 @@
     sums_ref[...] = jnp.zeros((16, LANES), F32)
     span = 8 * max(t for t in range(1, 13) if geo.quarter // 8 % t == 0)
     dp_index = me_ref[1] * 2 + me_ref[2]
-    for position, group in enumerate(groups):
+    places = [(number, at, g) for number, part in enumerate(groups) for at, g in enumerate(part)]
+    for number, at, group in places:
         device = group * geo.fsdp + me_ref[3] * 2 + me_ref[4]
         share = geo.rows * LANES
         base = device * geo.rows
         first = base - lax.rem(base, 16) + dp_index * geo.quarter
 
-        def body(i, _, position=position, base=base, first=first):
+        def body(i, _, number=number, at=at, base=base, first=first):
             r0 = pl.multiple_of(i * span, 8)
-            value = refs[position][pl.ds(r0, span), :]
+            value = refs[number][at, pl.ds(r0, span), :]
             lane = lax.broadcasted_iota(jnp.int32, (span, LANES), 1)
             row = lax.broadcasted_iota(jnp.int32, (span, LANES), 0)
             lifted = (first + r0 + row) * LANES + lane
@@ -774,12 +862,13 @@
         in_specs=[smem()] + [vmem()] * len(sums),
         out_specs=vmem(),
         compiler_params=params_of(),
+        cost_estimate=light(),
         name="square_sums",
     )(me, *sums)
 
 
 def update_kernel(geo, me_ref, coef_ref, *refs):
-    quarters, (late_ref, p_ref, m_ref, v_ref), outs = refs[:8], refs[8:12], refs[12:]
+    quarters, (late_ref, p_ref, m_ref, v_ref), outs = refs[:4], refs[4:8], refs[8:]
     params_out, first_out, second_out, grad_ref = outs
     rows, quarter = geo.rows, geo.quarter
     base = me_ref[0] * rows
@@ -788,7 +877,7 @@
     margin = 128
     for offset in range(4):
         to = pl.multiple_of(margin + (dp_index ^ offset) * quarter, 8)
-        grad_ref[pl.ds(to, quarter), :] = quarters[offset][...] + quarters[4 + offset][...]
+        grad_ref[pl.ds(to, quarter), :] = quarters[offset][...].astype(F32)
     for row, count, at in ((0, HEAD_ROWS, 0), (TAIL_ROW, LATE_TAIL, HEAD_ROWS)):
 
         @pl.when((base < row + count) & (base + rows > row))
@@ -832,7 +921,7 @@
     return pl.pallas_call(
         partial(update_kernel, geo),
         out_shape=[rows, rows, rows],
-        in_specs=[smem(), smem()] + [vmem()] * 12,
+        in_specs=[smem(), smem()] + [vmem()] * 8,
         out_specs=[vmem()] * 3,
         scratch_shapes=[pltpu.VMEM((geo.slot + 384, LANES), F32)],
         compiler_params=params_of(),
@@ -844,29 +933,34 @@
     return tokens // 4 if tokens % 64 == 0 else tokens
 
 
-def permute_in_kernel(rows_ref, patches_ref, cot_ref, x_ref, g_ref):
-    arrivals = patches_ref.shape[0]
+def permute_in_kernel(rows_ref, values_ref, *refs):
+    arrivals = values_ref.shape[0]
     lane = lax.broadcasted_iota(jnp.int32, (WP, arrivals), 1)
     pick = jnp.where(rows_ref[...] == lane, 1.0, 0.0).astype(BF16)
-    x_ref[...] = nn(pick, patches_ref[...]).astype(BF16)
-    g_ref[...] = nn(pick, cot_ref[...]).astype(BF16)
-
-
-def permute_in(row_ids, patches, cotangent):
+    refs[-1][...] = nn(pick, values_ref[...]).astype(BF16)
+
+
+def permute_in(row_ids, values, start, stop, before=None):
     tokens = row_ids.shape[0]
-    whole = pl.BlockSpec(patches.shape, lambda i: (0, 0))
-    part = pl.BlockSpec((WP, D), lambda i: (i, 0))
-    shape = jax.ShapeDtypeStruct((tokens, D), BF16)
+    operands = [row_ids, values]
+    specs = [
+        pl.BlockSpec((WP, 1), lambda i: (i + start, 0)),
+        pl.BlockSpec(values.shape, lambda i: (0, 0)),
+    ]
+    if before is not None:
+        operands.append(before)
+        specs.append(anywhere())
     return pl.pallas_call(
         permute_in_kernel,
-        grid=(tokens // WP,),
-        out_shape=[shape, shape],
-        in_specs=[pl.BlockSpec((WP, 1), lambda i: (i, 0)), whole, whole],
-        out_specs=[part, part],
+        grid=(stop - start,),
+        out_shape=jax.ShapeDtypeStruct((tokens, D), BF16),
+        in_specs=specs,
+        out_specs=pl.BlockSpec((WP, D), lambda i: (i + start, 0)),
+        input_output_aliases={} if before is None else {2: 0},
         compiler_params=params_of(),
-        cost_estimate=cost(4 * tokens * tokens * D, 8 * tokens * D),
+        cost_estimate=cost(tokens * tokens * D, 2 * tokens * D),
         name="window_order",
-    )(row_ids, patches, cotangent)
+    )(*operands)
 
 
 def permute_out_kernel(rows_ref, x_ref, out_ref):
@@ -981,21 +1075,27 @@
 def bias_back_kernel(ids_ref, sums_ref, out_ref):
     entries = out_ref.shape[0]
     out_ref[...] = jnp.zeros(out_ref.shape, F32)
-
-    def body(j, _):
-        lane = lax.broadcasted_iota(jnp.int32, (HEADS, LANES), 1)
-        row = jnp.where(lane < WT, sums_ref[:, pl.ds(j, 1), :].reshape(HEADS, LANES), 0.0)
+    lane = lax.broadcasted_iota(jnp.int32, (HEADS, LANES), 1)
+    entry = lax.broadcasted_iota(jnp.int32, (entries, LANES), 0)
+    together = 4
+
+    def body(i, _):
+        rows, picks = [], []
+        for number in range(together):
+            j = i * together + number
+            row = sums_ref[:, pl.ds(j, 1), :].reshape(HEADS, LANES)
+            rows.append(jnp.where(lane < WT, row, 0.0))
+            picks.append(jnp.where(ids_ref[pl.ds(j, 1), :] == entry, 1.0, 0.0).astype(BF16))
+        row = jnp.concatenate(rows, axis=1)
         high = row.astype(BF16)
         rest = row - high.astype(F32)
         middle = rest.astype(BF16)
         low = (rest - middle.astype(F32)).astype(BF16)
         parts = jnp.concatenate([high, middle, low], axis=0)
-        entry = lax.broadcasted_iota(jnp.int32, (entries, LANES), 0)
-        pick = jnp.where(ids_ref[pl.ds(j, 1), :] == entry, 1.0, 0.0).astype(BF16)
-        out_ref[...] += nt(pick, parts)
+        out_ref[...] += nt(jnp.concatenate(picks, axis=1), parts)
         return 0
 
-    lax.fori_loop(0, WT, body, 0, unroll=4)
+    lax.fori_loop(0, WT // together, body, 0)
 
 
 def score_bias_back(ids, sums, entries):
@@ -1068,12 +1168,18 @@
 
 
 def attention_back_kernel(
-    q_ref, k_ref, v_ref, g_ref, bias_ref, log_ref, out_ref, acc_ref, column_ref
+    more, q_ref, k_ref, v_ref, g_ref, bias_ref, log_ref, *refs
 ):
+    out_ref, acc_ref, column_ref = refs[-3:]
+
     @pl.when(pl.program_id(0) == 0)
     def _():
-        acc_ref[...] = jnp.zeros(acc_ref.shape, F32)
-        column_ref[...] = jnp.zeros(column_ref.shape, F32)
+        if more:
+            acc_ref[...] = refs[0][...]
+            column_ref[...] = refs[1][...]
+        else:
+            acc_ref[...] = jnp.zeros(acc_ref.shape, F32)
+            column_ref[...] = jnp.zeros(column_ref.shape, F32)
 
     def put(third, b, value):
         lanes = pl.ds(pl.multiple_of(third * D + b * LANES, LANES), LANES)
@@ -1109,38 +1215,45 @@
     lax.fori_loop(0, HEADS // QUAD, block, 0, unroll=4)
 
 
-def attention_back(mixed, grads, bias, logs):
-    windows = mixed.shape[0] // WP
+def attention_back(mixed, grads, bias, logs, start, stop, before=None):
+    rows = mixed.shape[0]
 
     def third(c):
-        return pl.BlockSpec((WP, D), lambda i, c=c: (i, c))
+        return pl.BlockSpec((WP, D), lambda i, c=c: (i + start, c))
 
     fixed = pl.BlockSpec(bias.shape, lambda i: (0, 0, 0))
+    columns = pl.BlockSpec((8, 3 * D), lambda i: (0, 0))
+    operands = [mixed, mixed, mixed, grads, bias, logs]
+    specs = [
+        third(0),
+        third(1),
+        third(2),
+        third(0),
+        fixed,
+        pl.BlockSpec((1, HEADS, LANES), lambda i: (i + start, 0, 0)),
+    ]
+    aliases = {}
+    if before is not None:
+        operands += [before[1], before[2], before[0]]
+        specs += [fixed, columns, anywhere()]
+        aliases = {8: 0}
     return pl.pallas_call(
-        attention_back_kernel,
-        grid=(windows,),
+        partial(attention_back_kernel, before is not None),
+        grid=(stop - start,),
         out_shape=[
-            jax.ShapeDtypeStruct((windows * WP, 3 * D), BF16),
+            jax.ShapeDtypeStruct((rows, 3 * D), BF16),
             jax.ShapeDtypeStruct(bias.shape, F32),
             jax.ShapeDtypeStruct((8, 3 * D), F32),
         ],
-        in_specs=[
-            third(0),
-            third(1),
-            third(2),
-            third(0),
-            fixed,
-            pl.BlockSpec((1, HEADS, LANES), lambda i: (i, 0, 0)),
-        ],
-        out_specs=[
-            pl.BlockSpec((WP, 3 * D), lambda i: (i, 0)),
-            fixed,
-            pl.BlockSpec((8, 3 * D), lambda i: (0, 0)),
-        ],
+        in_specs=specs,
+        out_specs=[pl.BlockSpec((WP, 3 * D), lambda i: (i + start, 0)), fixed, columns],
+        input_output_aliases=aliases,
         compiler_params=params_of(),
-        cost_estimate=cost(25e9, 16 * windows * WP * D, windows * HEADS * WP * LANES),
+        cost_estimate=cost(
+            3e9 * (stop - start), 16 * (stop - start) * WP * D, HEADS * WP * LANES
+        ),
         name="attention_back",
-    )(mixed, mixed, mixed, grads, bias, logs)
+    )(*operands)
 
 
 def middle_kernel(x_ref, a_ref, w_ref, b_ref, gain_ref, shift_ref, middle_ref, second_ref):
@@ -1173,7 +1286,7 @@
 def mlp_up_kernel(geo, region, shared, steps, skip, me_ref, s_ref, g_ref, w_ref, b_ref, *refs):
     vec_ref, refs = refs[0], refs[1 + skip :]
     hidden_ref, slope_ref, refs = refs[0], refs[1], refs[2:]
-    arrays = 2 * len(region.groups)
+    arrays = 2 * len(region.reduce)
     *scratch, held_ref = refs[arrays:]
     emitter = Emitter(geo, region, shared, me_ref, refs[:arrays], *scratch)
     flat_ref = emitter.flat_ref
@@ -1208,7 +1321,7 @@
 
 def mlp_up(geo, region, me, second, grad_out, weight, bias, vector, slots, shared):
     tokens = second.shape[0]
-    height = 256
+    height = 512
     steps = FF // height
     last = steps - 1
     rows = pl.BlockSpec((tokens, D), lambda k: (0, 0), pipeline_mode=pl.Buffered(1))
@@ -1246,7 +1359,7 @@
     (h_ref, slope_ref, s_ref, g_ref, up_ref, down_ref, m_ref, b_ref) = refs[:8]
     refs = refs[8 + skip :]
     result_ref, grad_ref, refs = refs[0], refs[1], refs[2:]
-    arrays = 2 * len(region.groups)
+    arrays = 2 * len(region.reduce)
     *scratch, left_ref, sum_ref = refs[arrays:]
     emitter = Emitter(geo, region, shared, me_ref, refs[:arrays], *scratch)
     flat_ref = emitter.flat_ref
@@ -1269,8 +1382,7 @@
     for c in range(cols):
         at = region.address(vec_row + step * cols + c)
         flat_ref[pl.ds(at, 1), :] = column[:, c * LANES : (c + 1) * LANES]
-    for r in range(0, D, 256):
-        store_columns(region, flat_ref, r, step * cols, nn(left_ref[r : r + 256, :], pre))
+    store_columns(region, flat_ref, 0, step * cols, nn(left_ref[...], pre))
 
     @pl.when(step == steps - 1)
     def _():
@@ -1367,49 +1479,64 @@
     )(second_grad, middle, grad_out, gain, weight)
 
 
-def first_back_kernel(mixed_ref, w_ref, x_ref, mg_ref, gain_ref, out_ref, vec_ref):
-    @pl.when(pl.program_id(0) == 0)
+def first_back_kernel(steps, mixed_ref, w_ref, x_ref, mg_ref, gain_ref, out_ref, vec_ref, sum_ref):
+    step = pl.program_id(0)
+    part = nt(mixed_ref[...], w_ref[...])
+
+    @pl.when(step == 0)
     def _():
+        sum_ref[...] = part
+
+    @pl.when(step > 0)
+    def _():
+        sum_ref[...] += part
+
+    @pl.when(step == steps - 1)
+    def _():
+        block = row_blocks(x_ref.shape[0])
         vec_ref[...] = jnp.zeros(vec_ref.shape, F32)
 
-    grad = nt(mixed_ref[...], w_ref[...])
-    xhat, inverse = normalized(x_ref[...].astype(F32))
-    inner = normalized_back(grad * gain_ref[...], xhat, inverse)
-    out_ref[...] = (mg_ref[...] + inner).astype(BF16)
-    vec_ref[0:1, :] += jnp.sum(grad * xhat, axis=0, keepdims=True)
-    vec_ref[1:2, :] += jnp.sum(grad, axis=0, keepdims=True)
+        def body(i, _):
+            rows = pl.ds(pl.multiple_of(i * block, 16), block)
+            grad = sum_ref[rows, :]
+            xhat, inverse = normalized(x_ref[rows, :].astype(F32))
+            inner = normalized_back(grad * gain_ref[...], xhat, inverse)
+            out_ref[rows, :] = (mg_ref[rows, :] + inner).astype(BF16)
+            vec_ref[0:1, :] += jnp.sum(grad * xhat, axis=0, keepdims=True)
+            vec_ref[1:2, :] += jnp.sum(grad, axis=0, keepdims=True)
+            return 0
+
+        lax.fori_loop(0, x_ref.shape[0] // block, body, 0)
 
 
 def first_back(mixed_grad, weight, x, middle_grad, gain):
     tokens = x.shape[0]
-    block = row_blocks(tokens)
-    rows = pl.BlockSpec((block, D), lambda i: (i, 0))
+    width = 768
+    steps = 3 * D // width
+    rows = pl.BlockSpec((tokens, D), lambda k: (0, 0), pipeline_mode=pl.Buffered(1))
     return pl.pallas_call(
-        first_back_kernel,
-        grid=(tokens // block,),
+        partial(first_back_kernel, steps),
+        grid=(steps,),
         out_shape=[
             jax.ShapeDtypeStruct((tokens, D), BF16),
             jax.ShapeDtypeStruct((8, D), F32),
         ],
         in_specs=[
-            pl.BlockSpec((block, 3 * D), lambda i: (i, 0)),
-            pl.BlockSpec((D, 3 * D), lambda i: (0, 0), pipeline_mode=pl.Buffered(1)),
+            pl.BlockSpec((tokens, width), lambda k: (0, k)),
+            pl.BlockSpec((D, width), lambda k: (0, k)),
             rows,
             rows,
-            pl.BlockSpec((1, D), lambda i: (0, 0)),
+            pl.BlockSpec((1, D), lambda k: (0, 0)),
         ],
-        out_specs=[rows, pl.BlockSpec((8, D), lambda i: (0, 0))],
+        out_specs=[
+            pl.BlockSpec((tokens, D), lambda k: (0, 0)),
+            pl.BlockSpec((8, D), lambda k: (0, 0)),
+        ],
+        scratch_shapes=[pltpu.VMEM((tokens, D), F32)],
         compiler_params=params_of(),
         cost_estimate=cost(6 * tokens * D * D, 6 * D * D + 14 * tokens * D),
         name="first_back",
     )(mixed_grad, weight, x, middle_grad, gain)
-
-
-def split_span(geo, row, depth, cols, block):
-    group = (row // geo.rows) // geo.fsdp
-    edge = (group + 1) * geo.fsdp * geo.rows // 16 * 16
-    inside = max(0, (edge - row) // cols) // block * block
-    return min(depth, inside)
 
 
 def local(
@@ -1444,18 +1571,32 @@
         window_rows.reshape(windows, WT), ((0, 0), (0, WP - WT)), constant_values=-1
     ).reshape(windows * WP)
     stacked = jnp.stack(spread_quarters(geo, share, dp_index))
-    x, grad_out = permute_in(after(row_ids, stacked)[:, None], patches, cotangent)
     gathers = []
-    for group in range(4):
-        piece = lax.dynamic_index_in_dim(stacked, dp_index ^ group, 0, keepdims=False)
-        gathers.append(Gather(geo, piece))
+    for groups in GATHER_PHASES:
+        pieces = [
+            lax.dynamic_index_in_dim(stacked, dp_index ^ group, 0, keepdims=True)
+            for group in groups
+        ]
+        gathers.append(Gather(geo, jnp.concatenate(pieces, axis=0)))
     gathers[0].line()
-    gathers[0].across(x)
-    gathers[1].line(gathers[0].held)
-    gathers[0].last()
-    gathers[1].across()
-    gathers[2].line(gathers[1].held)
-    gathered = {0: gathers[0].finish()}
+    half = windows // 2
+    ids_of = row_ids[:, None]
+    x = permute_in(after(ids_of, gathers[0].held), patches, 0, half)
+    held = gathers[0].joined(x)
+    gathers[0].across()
+    gathers[1].line(held)
+    x = permute_in(after(ids_of, held), patches, half, windows, x)
+    near = gathers[0].last(x)
+    held = gathers[1].joined(x)
+    gathers[2].line(held)
+    grad_out = permute_in(after(ids_of, near, held), cotangent, 0, half)
+    gathered = {0: gathers[0].finish(grad_out)}
+    far = gathered[0][1]
+    gathers[1].across(far)
+    grad_out = permute_in(after(ids_of, far), cotangent, half, windows, grad_out)
+    held = gathers[2].joined(grad_out)
+    gathers[3].line(held)
+    gathered[0] = gathered[0][:3] + [after(gathered[0][3], grad_out, held)]
 
     mix_matrix = (MIX_ROW, D, 3 * D // LANES)
     out_matrix = (OUT_ROW, D, D // LANES)
@@ -1473,9 +1614,10 @@
         geo, 0, OUT_ROW, mix_matrix, mix_vectors, high=geo.spill_to if geo.spill else None
     )
     mix_weight, attn_gain, attn_shift, mix_bias, table_rows = unpack(geo, first, me, gathered)
-    gathers[1].last(mix_weight)
-    gathers[3].line(gathers[2].held, mix_weight)
-    gathers[2].across(mix_weight)
+    near = gathers[1].last(mix_weight)
+    held = gathers[3].joined(mix_weight)
+    gathers[2].across(near)
+    table_rows = after(table_rows, near, held)
 
     def line_of(rows):
         return rows.reshape(1, -1)
@@ -1486,41 +1628,35 @@
     ids = jnp.pad(rel_index.T, ((0, WP - WT), (0, LANES - WT)), constant_values=-1)
     bias = score_bias(ids, table)
 
-    gathers[3].across(bias)
     normed, mixed = mix(
-        after(x, bias, gathers[2].near),
+        after(x, bias),
         line_of(attn_gain),
         line_of(attn_shift),
         mix_weight,
         line_of(mix_bias),
     )
     gathered[1] = gathers[1].finish(mixed)
-    gathers[2].last(mixed)
-    attended, logs = attention(after(mixed, gathers[3].near), bias)
-    gathers[3].last(attended)
-    gathered[2] = gathers[2].finish(attended)
+    near = gathers[2].last(mixed)
+    gathers[3].across(near)
+    attended, logs = attention(after(mixed, near, gathered[1][1]), bias)
     out_weight, out_bias, mlp_gain, mlp_shift = unpack(
         geo, Region(geo, OUT_ROW, EXPAND_ROW, out_matrix, out_vectors), me, gathered
     )
-
-    def in_two(matrix, vectors, end, block):
-        row, depth, cols = matrix
-        edge = split_span(geo, row, depth, cols, block)
-        weight = None
-        if 0 < edge < depth:
-            part = Region(geo, row, row + edge * cols, matrix, [], span=(0, edge))
-            (weight,) = unpack(geo, part, me, gathered)
-            rest = Region(geo, row + edge * cols, end, matrix, vectors, span=(edge, depth))
-            return unpack(geo, rest, me, gathered, weight)
-        return unpack(geo, Region(geo, row, end, matrix, vectors), me, gathered)
-
-    expand_weight, expand_bias = in_two(expand_matrix, expand_vectors, SHRINK_ROW, 16)
-
+    gathered[2] = gathers[2].finish(out_weight)
+    near = gathers[3].last(out_weight)
     middle, second = middle_rows(
-        x, attended, out_weight, line_of(out_bias), line_of(mlp_gain), line_of(mlp_shift)
-    )
-
-    gathered[3] = gathers[3].finish(second)
+        x,
+        after(attended, near, gathered[2][1]),
+        out_weight,
+        line_of(out_bias),
+        line_of(mlp_gain),
+        line_of(mlp_shift),
+    )
+    expand_weight, expand_bias = unpack(
+        geo, Region(geo, EXPAND_ROW, SHRINK_ROW, expand_matrix, expand_vectors), me, gathered
+    )
+    gathered[3] = gathers[3].finish(expand_weight)
+    second = after(second, gathered[3][1])
 
     shrink_region = Region(
         geo, SHRINK_ROW, END_ROW, shrink_matrix, shrink_vectors, high=geo.devices - 1
@@ -1542,9 +1678,11 @@
         slots,
         False,
     )
-    reductions = {3: Reduction(geo, slots[3])}
-    shrink_weight, shrink_bias = in_two(shrink_matrix, shrink_vectors, END_ROW, 64)
-    sent = reductions[3].last(shrink_weight)
+    phase3 = Reduction(geo, slots[3], 3)
+    shrink_weight, shrink_bias = unpack(
+        geo, Region(geo, SHRINK_ROW, END_ROW, shrink_matrix, shrink_vectors), me, gathered
+    )
+    sent = phase3.last(shrink_weight)
     result, second_grad, slots = mlp_down(
         geo,
         expand_region,
@@ -1560,12 +1698,12 @@
         slots,
         expand_region.high == shrink_region.low,
     )
-    reductions[2] = Reduction(geo, slots[2])
-    sent = reductions[3].across(second_grad)
+    phase2 = Reduction(geo, slots[2], 2)
+    sent = phase3.across(second_grad)
     middle_grad, branch_grad, context_grad, middle_vec = middle_back(
         after(second_grad, sent), middle, grad_out, line_of(mlp_gain), out_weight
     )
-    sent = [reductions[2].last(context_grad), reductions[3].line(context_grad)]
+    sent = [phase3.line(context_grad), phase2.last(context_grad)]
     slots = pack(
         geo,
         out_region,
@@ -1576,12 +1714,15 @@
         slots,
         out_region.high == expand_region.low,
     )
-    reductions[1] = Reduction(geo, slots[1])
+    phase1 = Reduction(geo, slots[1], 1)
+    context_grad = after(context_grad, slots[1][0])
+    parts = attention_back(mixed, context_grad, bias, logs, 0, half)
+    sums = {3: phase3.total(parts[1])}
+    sent = [phase2.across(parts[1]), phase1.last(parts[1]), sums[3]]
     mixed_grad, score_sums, column_sums = attention_back(
-        mixed, after(context_grad, slots[1][0]), bias, logs
-    )
-    sent = [reductions[2].across(mixed_grad), reductions[1].last(mixed_grad)]
-    sums = {3: reductions[3].total(mixed_grad)}
+        mixed, after(context_grad, *sent), bias, logs, half, windows, parts
+    )
+    sent = [phase2.line(score_sums), phase1.across(score_sums)]
     slots = pack(
         geo,
         mix_region,
@@ -1593,17 +1734,17 @@
         mix_region.high == out_region.low,
     )
     packed = slots[0][0]
-    reductions[0] = Reduction(geo, slots[0])
-    sent = [reductions[2].line(packed), reductions[1].across(packed)]
+    phase0 = Reduction(geo, slots[0], 0)
+    sums[2] = phase2.total(packed)
+    sent = [phase1.line(packed), sums[2]]
     activations = permute_out(row_ids[None], after(result, packed, *sent), arrivals)
-    sent = reductions[0].last(activations)
+    sent = phase0.last(activations)
     input_rows, first_vec = first_back(
         after(mixed_grad, sent), mix_weight, x, middle_grad, line_of(attn_gain)
     )
-    sent = reductions[1].line(input_rows)
-    sums[2] = reductions[2].total(input_rows)
-    table_grad = score_bias_back(ids, after(score_sums, sent), entries)[:TABLE_ROWS]
-    sent = reductions[0].across(table_grad)
+    sums[1] = phase1.total(input_rows)
+    sent = [phase0.across(input_rows), sums[1]]
+    table_grad = score_bias_back(ids, after(score_sums, *sent), entries)[:TABLE_ROWS]
 
     table_pad = (SPLIT_ROW - TABLE_ROW) * LANES - TABLE_ROWS * HEADS
     late = jnp.concatenate(
@@ -1614,25 +1755,19 @@
         ],
         axis=0,
     )
+    sent = phase0.line(table_grad)
     late = after(jnp.pad(late, ((0, LATE_ROWS - late.shape[0]), (0, 0))), sent)
     late = sum_everywhere(geo, late)
-    sums[1] = reductions[1].total(sent)
     input_grad = permute_out(row_ids[None], after(input_rows, sent), arrivals)
-    sent = reductions[0].line(input_grad)
-    early = collect_early(geo, sums, dp_index)
-    squares = square_sums(geo, me, (1, 2, 3), [after(sums[1], sent), sums[2], sums[3]])
-    sums[0] = reductions[0].total(late, squares)
-    squares = squares + square_sums(geo, me, (0,), [sums[0]])
-    squares = sum_everywhere(geo, jnp.sum(squares, axis=1)[None])
+    squares = square_sums(
+        geo, me, REDUCE_PHASES[1:], [after(sums[1], sent), sums[2], sums[3]]
+    )
+    sums[0] = phase0.total(squares, input_grad)
+    squares = squares + square_sums(geo, me, REDUCE_PHASES[:1], [sums[0]])
+    collected = collect_quarters(geo, [sums[group][0] for group in range(4)], dp_index)
     scale = 1.0 / jnp.sqrt(F32(arrivals * geo.devices))
-    edges = [0, 8, HEAD_ROWS, HEAD_ROWS + TABLE_ROW - TAIL_ROW, LATE_ROWS]
-    late_squares = [jnp.sum(late[a:b] * late[a:b]) for a, b in zip(edges, edges[1:])]
-    totals = [squares[0, t] for t in range(len(SHAPES))]
-    for number, t in enumerate((0, 1, 3, 4)):
-        totals[t] = late_squares[number]
-    entry_counts = jnp.array([math.prod(shape) for shape in SHAPES], F32)
-    group_rms = jnp.sqrt(jnp.stack(totals) * (scale * scale) / entry_counts)
-
+    squares = sum_everywhere(geo, jnp.sum(squares, axis=1)[None], 0, 3)
+    collected[0] = after(collected[0], squares)
     step_float = step_count.astype(F32)
     coef = jnp.stack(
         [
@@ -1646,12 +1781,24 @@
         geo,
         me,
         coef,
-        early + collect_late(geo, sums[0], dp_index),
+        collected,
         late,
         shard,
         first_moment.reshape(geo.rows, LANES),
         second_moment.reshape(geo.rows, LANES),
     )
+    squares = sum_everywhere(geo, after(squares, params_new), 3)
+    tensor = lax.broadcasted_iota(jnp.int32, (LATE_ROWS, 16), 1)
+    row = lax.broadcasted_iota(jnp.int32, (LATE_ROWS, 16), 0)
+    inside = tensor < 0
+    edges = [0, 8, HEAD_ROWS, HEAD_ROWS + TABLE_ROW - TAIL_ROW, LATE_ROWS]
+    for t, start, stop in zip((0, 1, 3, 4), edges, edges[1:]):
+        inside = inside | ((tensor == t) & (row >= start) & (row < stop))
+    late_rows = jnp.sum(late * late, axis=1, keepdims=True)
+    totals = squares[0] + jnp.sum(jnp.where(inside, late_rows, 0.0), axis=0)
+    entry_counts = jnp.array([math.prod(shape) for shape in SHAPES], F32)
+    group_rms = jnp.sqrt(totals[: len(SHAPES)] * (scale * scale) / entry_counts)
+
     return (
         activations,
         input_grad,

time: 609 us -> 570 us (0.936)
  Pallas kernels: 306 us -> 379 us
  waiting for transfers between devices: 108 us -> 64.3 us
  other arithmetic: 48.3 us -> 11.8 us
  local copies, waits for them, and re-layouts: 49.7 us -> 22.7 us
  starting transfers between devices: 89.8 us -> 81.7 us
    pallas_call x5 -> x33, Pallas kernels: 78.6 us -> 164 us  [the longest x2 40.6 us: attention_back(): pl.pallas_call(partial(attention_back_kernel, before is not None), grid=(...]
    ppermute x65 -> x68, waiting for transfers between devices: 108 us -> 64.3 us  [permute(): return lax.ppermute(value, AXES, pairs)]
    add x14 -> x9, other arithmetic: 13.3 us -> 1.61 us  [the longest x8 1.6 us: sum_everywhere(): value = value + geo.permute(value, 1 << bit, 1 << bit)]
    ppermute x6 -> x0, starting transfers between devices: 10.4 us -> none  [the longest x3 6.6 us: collect_early(): pieces.append(lax.ppermute(piece, AXES, pairs))]
    another operation x5 -> x1, other arithmetic: 9.67 us -> 0.01 us
    convert_element_type x4 -> x1, other arithmetic: 10.7 us -> 1.21 us  [collect_quarters(): of_group(dp_index ^ offset).astype(BF16)]
    unnamed x77 -> x78, local copies, waits for them, and re-layouts: 16.1 us -> 7.47 us
    another operation x1, local copies, waits for them, and re-layouts: 8.22 us -> 0.08 us  [local(): ids_of = row_ids[:, None]]
  transfers between devices with their start and end apart: 72 -> 69, of which waited for: 25 -> 20; matrix products, arithmetic and copies ran while one was open for 14% -> 4% of each run, Pallas kernels for 46% -> 57%
where the time goes in v4:
time: 570 us; the launch traced here: 563 us
  Pallas kernels  379 us (66%)
  starting transfers between devices  81.7 us (14%)
  waiting for transfers between devices  64.3 us (11%)
  local copies, waits for them, and re-layouts  22.7 us (4%)
  other arithmetic  11.8 us (2%)
    ppermute x68, starting transfers between devices, permute(): return lax.ppermute(value, AXES, pairs)  81 us
    ppermute x68, waiting for transfers between devices, permute(): return lax.ppermute(value, AXES, pairs)  64.3 us
    pallas_call x1, Pallas kernels, mlp_down(): pl.pallas_call(partial(mlp_down_kernel, geo, region, shared, steps, skip)...  49.2 us
    pallas_call x4, Pallas kernels, unpack(): pl.pallas_call(partial(unpack_kernel, geo, region, 64 if region.cols <= 8...  42.8 us
    pallas_call x2, Pallas kernels, attention_back(): pl.pallas_call(partial(attention_back_kernel, before is not None), grid=(...  40.6 us
    pallas_call x1, Pallas kernels, mlp_up(): pl.pallas_call(partial(mlp_up_kernel, geo, region, shared, steps, skip),...  32.3 us
    pallas_call x2, Pallas kernels, pack(): pl.pallas_call(partial(pack_kernel, geo, region, shared, steps, skip), gr...  22.5 us
    pallas_call x8, Pallas kernels, join(): pl.pallas_call(join_kernel, out_shape=jax.ShapeDtypeStruct((count,) + par...  19.3 us
  transfers between devices with their start and end apart: 69, of which 20 were waited for; matrix products, arithmetic and copies ran while one was open for 4% of the time, Pallas kernels for 57%

profile of v4, /device:TPU:0, one launch (start us, length us, event | category | flops | bytes accessed | tf_op | source)
XLA Modules:
  0.0 562.9 jit_solution(7467457322478779739)
XLA Ops:
  10.8 6.9 %collective-permute-start.2 = (bf16[792,128]{1,0:T(8,128)(2,1)S(1)}, bf16[792,128]{1,0:T(8,128)(2,1)S(1)}, u32[]{:S(2)}, u32[]{:S(2)}) collective-permute-start(bf16[792,128]{1,0:T(8,128)(2,1)S(1)} %get-tuple-element.321), channel_id=1, source_target_pairs={{0,16},{1,17},{2,18},{3,19},{4,20},{5,21},{6,22},{7,23},{8,24},{9,... | collective-permute-start | bytes 608264 | tf_op jit(solution)/shard_map/ppermute | solution.py:131
  17.9 7.4 %collective-permute-done.2 = bf16[792,128]{1,0:T(8,128)(2,1)S(1)} collective-permute-done((bf16[792,128]{1,0:T(8,128)(2,1)S(1)}, bf16[792,128]{1,0:T(8,128)(2,1)S(1)}, u32[]{:S(2)}, u32[]{:S(2)}) %collective-permute-start.2) | collective-permute-done | bytes 202784 | tf_op jit(solution)/shard_map/ppermute | solution.py:131
  36.2 6.5 %collective-permute-done.5.refs_2_ = bf16[1,792,128]{2,1,0:T(8,128)(2,1)S(1)} collective-permute-done((bf16[1,792,128]{2,1,0:T(8,128)(2,1)S(1)}, bf16[1,792,128]{2,1,0:T(8,128)(2,1)S(1)}, u32[]{:S(2)}, u32[]{:S(2)}) %collective-permute-start.5) | collective-permute-done | bytes 202784 | tf_op jit(solution)/shard_map/ppermute | solution.py:131
  58.6 5.9 %collective-permute-done.10.refs_2_ = bf16[1,792,128]{2,1,0:T(8,128)(2,1)S(1)} collective-permute-done((bf16[1,792,128]{2,1,0:T(8,128)(2,1)S(1)}, bf16[1,792,128]{2,1,0:T(8,128)(2,1)S(1)}, u32[]{:S(2)}, u32[]{:S(2)}) %collective-permute-start.10) | collective-permute-done | bytes 202784 | tf_op jit(solution)/shard_map/ppermute | solution.py:131
  76.9 6.2 %collective-permute-start.8 = (bf16[8,792,128]{2,1,0:T(8,128)(2,1)}, bf16[8,792,128]{2,1,0:T(8,128)(2,1)}, u32[]{:S(2)}, u32[]{:S(2)}) collective-permute-start(bf16[8,792,128]{2,1,0:T(8,128)(2,1)} %join.9.refs_0_), channel_id=1, source_target_pairs={{0,1},{1,0},{2,3},{3,2},{4,5},{5,4},{6,7},{7,6},{8,24},{9,25},{10,... | collective-permute-start | bytes 4866056 | tf_op jit(solution)/shard_map/ppermute | solution.py:131
  88.8 13.6 %collective-permute-done.8.refs_1_ = bf16[8,792,128]{2,1,0:T(8,128)(2,1)} collective-permute-done((bf16[8,792,128]{2,1,0:T(8,128)(2,1)}, bf16[8,792,128]{2,1,0:T(8,128)(2,1)}, u32[]{:S(2)}, u32[]{:S(2)}) %collective-permute-start.8) | collective-permute-done | bytes 1622048 | tf_op jit(solution)/shard_map/ppermute | solution.py:131
  118.5 10.4 %unpack_weights.4 = (bf16[1024,3072]{1,0:T(8,128)(2,1)}, f32[8,128]{1,0:T(8,128)}, f32[8,128]{1,0:T(8,128)}, f32[24,128]{1,0:T(8,128)}, f32[91,128]{1,0:T(8,128)}) custom-call(s32[5]{0:T(128)} %stack.48.me_ref, bf16[8,792,128]{2,1,0:T(8,128)(2,1)} %join.9.refs_0_, bf16[8,792,128]{2,1,0:T(8,128)(2,1)} %collective-permute-done.8.refs_1_, ...), custom_call_target="tpu_custom_call" | custom-call | bytes 5033164800 | tf_op jit(solution)/shard_map/unpack_weights/pallas_call | solution.py:371
  138.2 7.7 %score_bias.1.bias_ref = f32[32,104,128]{2,1,0:T(8,128)} custom-call(s32[104,128]{1,0:T(8,128)} %pad.22.ids_ref, bf16[32,368]{1,0:T(8,128)(2,1)} %pad.23.table_ref), custom_call_target="tpu_custom_call" | custom-call | flops 65431142400 | bytes 340787200 | tf_op jit(solution)/shard_map/score_bias/pallas_call | solution.py:1064
  147.9 13.0 %mix_rows.1 = (bf16[832,1024]{1,0:T(8,128)(2,1)}, bf16[832,3072]{1,0:T(8,128)(2,1)}) custom-call(bf16[832,1024]{1,0:T(8,128)(2,1)} %window_order.5.x_ref, f32[1,1024]{1,0:T(1,128)} %bitcast.79, f32[1,1024]{1,0:T(1,128)} %bitcast.83, bf16[1024,3072]{1,0:T(8,128)(2,1)} %get-tuple-element.179.w_ref, f32[1,3072]{1,0:T(1,128)} %bitcast.78), custom_call_target="tpu_custom_call" | custom-call | flops 1046898278400 | bytes 2621440000 | tf_op jit(solution)/shard_map/mix_rows/pallas_call | solution.py:1028
  168.3 13.6 %attention.1 = (bf16[832,1024]{1,0:T(8,128)(2,1)}, f32[8,32,128]{2,1,0:T(8,128)}) custom-call(bf16[832,3072]{1,0:T(8,128)(2,1)} %get-tuple-element.194.q_ref.k_ref.v_ref, bf16[832,3072]{1,0:T(8,128)(2,1)} %get-tuple-element.194.q_ref.k_ref.v_ref, bf16[832,3072]{1,0:T(8,128)(2,1)} %get-tuple-element.194.q_ref.k_ref.v_ref, f32[32,104,128]{2,1,0:T(8,128)} %score_bias.1.bias_ref), custom_call_target="tpu_custom_call" | custom-call | flops 2399999885312 | bytes 1363148800 | tf_op jit(solution)/shard_map/attention/pallas_call | solution.py:1155
  181.9 5.6 %unpack_weights.5 = (bf16[1024,1024]{1,0:T(8,128)(2,1)}, f32[8,128]{1,0:T(8,128)}, f32[8,128]{1,0:T(8,128)}, f32[8,128]{1,0:T(8,128)}) custom-call(s32[5]{0:T(128)} %stack.48.me_ref, bf16[8,792,128]{2,1,0:T(8,128)(2,1)} %join.12.refs_0_, bf16[8,792,128]{2,1,0:T(8,128)(2,1)} %collective-permute-done.22.refs_1_, ...), custom_call_target="tpu_custom_call" | custom-call | bytes 1677721600 | tf_op jit(solution)/shard_map/unpack_weights/pallas_call | solution.py:371
  195.7 6.8 %middle_rows.1 = (f32[832,1024]{1,0:T(8,128)}, bf16[832,1024]{1,0:T(8,128)(2,1)}) custom-call(bf16[832,1024]{1,0:T(8,128)(2,1)} %window_order.5.x_ref, bf16[832,1024]{1,0:T(8,128)(2,1)} %get-tuple-element.201.a_ref, bf16[1024,1024]{1,0:T(8,128)(2,1)} %get-tuple-element.198.w_ref, f32[1,1024]{1,0:T(1,128)} %bitcast.85, f32[1,1024]{1,0:T(1,128)} %bitcast.81, ...), custom_call_target="tpu_custom_call" | custom-call | flops 348966092800 | bytes 1703936000 | tf_op jit(solution)/shard_map/middle_rows/pallas_call | solution.py:1271
  202.5 13.0 %unpack_weights.6 = (bf16[1024,4096]{1,0:T(8,128)(2,1)}, f32[32,128]{1,0:T(8,128)}) custom-call(s32[5]{0:T(128)} %stack.48.me_ref, bf16[8,792,128]{2,1,0:T(8,128)(2,1)} %join.12.refs_0_, bf16[8,792,128]{2,1,0:T(8,128)(2,1)} %collective-permute-done.22.refs_1_, bf16[8,792,128]{2,1,0:T(8,128)(2,1)} %collective-permute-done.24.refs_2_, ...), custom_call_target="tpu_custom_call" | custom-call | bytes 6710886400 | tf_op jit(solution)/shard_map/unpack_weights/pallas_call | solution.py:371
  216.7 32.3 %mlp_up.1 = (bf16[832,4096]{1,0:T(8,128)(2,1)}, f32[832,4096]{1,0:T(8,128)}, bf16[16,792,128]{2,1,0:T(8,128)(2,1)}, bf16[16,792,128]{2,1,0:T(8,128)(2,1)}, bf16[...) custom-call(s32[5]{0:T(128)} %stack.48.me_ref, bf16[832,1024]{1,0:T(8,128)(2,1)} %get-tuple-element.209.s_ref.refs_2_, ...), custom_call_target="tpu_custom_call" | custom-call | flops 2791728742400 | bytes 7444889600 | tf_op jit(solution)/shard_map/mlp_up/pallas_call | solution.py:1339
  259.8 13.7 %unpack_weights.7 = (bf16[4096,1024]{1,0:T(8,128)(2,1)}, f32[8,128]{1,0:T(8,128)}) custom-call(s32[5]{0:T(128)} %stack.48.me_ref, bf16[8,792,128]{2,1,0:T(8,128)(2,1)} %join.14.refs_4_.refs_0_, bf16[8,792,128]{2,1,0:T(8,128)(2,1)} %collective-permute-done.26.refs_5_.refs_1_, bf16[8,792,128]{2,1,0:T(8,128)(2,1)} %collective-permute-done.28.refs_6_.refs_2_, ...), custom_call_target="tpu_custom_call" | custom-call | bytes 6710886400 | tf_op jit(solution)/shard_map/unpack_weights/pallas_call | solution.py:371
  277.7 49.2 %mlp_down.1 = (bf16[832,1024]{1,0:T(8,128)(2,1)}, f32[832,1024]{1,0:T(8,128)}, bf16[16,792,128]{2,1,0:T(8,128)(2,1)}, bf16[16,792,128]{2,1,0:T(8,128)(2,1)}, bf1...) custom-call(s32[5]{0:T(128)} %stack.48.me_ref, ...), custom_call_target="tpu_custom_call", output_to_operand_aliasing={{4}: (9, {}), {5}: (10, {})} | custom-call | flops 5583457484800 | bytes 9122611200 | tf_op jit(solution)/shard_map/mlp_down/pallas_call | solution.py:1414
  332.3 9.0 %middle_back.1 = (f32[832,1024]{1,0:T(8,128)}, bf16[832,1024]{1,0:T(8,128)(2,1)}, bf16[832,1024]{1,0:T(8,128)(2,1)}, f32[8,1024]{1,0:T(8,128)}) custom-call(f32[832,1024]{1,0:T(8,128)} %get-tuple-element.228.s_ref, f32[832,1024]{1,0:T(8,128)} %get-tuple-element.219.refs_6_.m_ref, bf16[832,1024]{1,0:T(8,128)(2,1)} %window_order.7.g_ref.refs_3_, ...), custom_call_target="tpu_custom_call" | custom-call | flops 348966092800 | bytes 3067084800 | tf_op jit(solution)/shard_map/middle_back/pallas_call | solution.py:1459
  355.5 7.3 %weight_grad_pack.2 = (bf16[16,792,128]{2,1,0:T(8,128)(2,1)}, bf16[16,792,128]{2,1,0:T(8,128)(2,1)}) custom-call(s32[5]{0:T(128)} %stack.48.me_ref, bf16[832,1024]{1,0:T(8,128)(2,1)} %get-tuple-element.201.a_ref, bf16[832,1024]{1,0:T(8,128)(2,1)} %get-tuple-element.237.b_ref, f32[8,128]{1,0:T(8,128)} %bitcast.72, ...), custom_call_target="tpu_custom_call", output_to_operand_aliasing={{0}: (6, {}), {1}: (7, {})} | custom-call | flops 348966092800 | bytes 419430400 | tf_op jit(solution)/shard_map/weight_grad_pack/pallas_call | solution.py:604
  362.9 24.8 %attention_back.2 = (bf16[832,3072]{1,0:T(8,128)(2,1)}, f32[32,104,128]{2,1,0:T(8,128)}, f32[8,3072]{1,0:T(8,128)}) custom-call(bf16[832,3072]{1,0:T(8,128)(2,1)} %get-tuple-element.194.q_ref.k_ref.v_ref, bf16[832,3072]{1,0:T(8,128)(2,1)} %get-tuple-element.194.q_ref.k_ref.v_ref, bf16[832,3072]{1,0:T(8,128)(2,1)} %get-tuple-element.194.q_ref.k_ref.v_ref, ...), custom_call_target="tpu_custom_call" | custom-call | flops 2399999885312 | bytes 1363148800 | tf_op jit(solution)/shard_map/attention_back/pallas_call | solution.py:1240
  399.2 15.7 %attention_back.3 = (bf16[832,3072]{1,0:T(8,128)(2,1)}, f32[32,104,128]{2,1,0:T(8,128)}, f32[8,3072]{1,0:T(8,128)}) custom-call(bf16[832,3072]{1,0:T(8,128)(2,1)} %get-tuple-element.194.q_ref.k_ref.v_ref, bf16[832,3072]{1,0:T(8,128)(2,1)} %get-tuple-element.194.q_ref.k_ref.v_ref, ...), custom_call_target="tpu_custom_call", output_to_operand_aliasing={{0}: (8, {})} | custom-call | flops 2399999885312 | bytes 1363148800 | tf_op jit(solution)/shard_map/attention_back/pallas_call | solution.py:1240
  428.5 15.1 %weight_grad_pack.3 = (bf16[16,792,128]{2,1,0:T(8,128)(2,1)}, bf16[16,792,128]{2,1,0:T(8,128)(2,1)}) custom-call(s32[5]{0:T(128)} %stack.48.me_ref, bf16[832,1024]{1,0:T(8,128)(2,1)} %get-tuple-element.224.a_ref, bf16[832,3072]{1,0:T(8,128)(2,1)} %get-tuple-element.279.b_ref.mixed_ref), custom_call_target="tpu_custom_call" | custom-call | flops 1046898278400 | bytes 1258291200 | tf_op jit(solution)/shard_map/weight_grad_pack/pallas_call | solution.py:604
  462.8 14.5 %first_back.1 = (bf16[832,1024]{1,0:T(8,128)(2,1)}, f32[8,1024]{1,0:T(8,128)}) custom-call(bf16[832,3072]{1,0:T(8,128)(2,1)} %get-tuple-element.279.b_ref.mixed_ref, bf16[1024,3072]{1,0:T(8,128)(2,1)} %get-tuple-element.179.w_ref, bf16[832,1024]{1,0:T(8,128)(2,1)} %window_order.5.x_ref, f32[832,1024]{1,0:T(8,128)} %get-tuple-element.280.mg_ref, ...), custom_call_target="tpu_custom_call" | custom-call | flops 1046898278400 | bytes 3643801600 | tf_op jit(solution)/shard_map/first_back/pallas_call | solution.py:1517
  488.0 9.5 %score_bias_back.1 = f32[368,96]{1,0:T(8,128)} custom-call(s32[104,128]{1,0:T(8,128)} %pad.22.ids_ref, f32[32,104,128]{2,1,0:T(8,128)} %get-tuple-element.291.sums_ref), custom_call_target="tpu_custom_call" | custom-call | flops 196293427200 | bytes 340787200 | tf_op jit(solution)/shard_map/score_bias_back/pallas_call | solution.py:1102
  546.6 10.9 %moments_update.1 = (f32[3081,128]{1,0:T(8,128)}, f32[3081,128]{1,0:T(8,128)}, f32[3081,128]{1,0:T(8,128)}) custom-call(s32[5]{0:T(128)} %stack.48.me_ref, f32[4]{0:T(128)} %pad_maximum_fusion.1.coef_ref, f32[792,128]{1,0:T(8,128)} %select_bitcast_fusion.refs_0_, bf16[792,128]{1,0:T(8,128)(2,1)} %copy-done.11, ...), custom_call_target="tpu_custom_call" | custom-call | tf_op jit(solution)/shard_map/moments_update/pallas_call | solution.py:921
  (292 shorter events, 241.1 us)
Async XLA Ops:
  68.0 40.0 %collective-permute-start.14 = (bf16[1,792,128]{2,1,0:T(8,128)(2,1)}, bf16[1,792,128]{2,1,0:T(8,128)(2,1)}, u32[]{:S(2)}, u32[]{:S(2)}) collective-permute-start(bf16[1,792,128]{2,1,0:T(8,128)(2,1)} %get-tuple-element.172.refs_0_), channel_id=1, source_target_pairs={{0,2},{1,3},{2,0},{3,1},{4,6},{5,7},{6,4},{7,5},{8,10},{9,11},{10,... | collective-permute-start | bytes 608264 | tf_op jit(solution)/shard_map/ppermute | solution.py:131
  70.1 38.0 %collective-permute-start.15 = (bf16[1,792,128]{2,1,0:T(8,128)(2,1)}, bf16[1,792,128]{2,1,0:T(8,128)(2,1)}, u32[]{:S(2)}, u32[]{:S(2)}) collective-permute-start(bf16[1,792,128]{2,1,0:T(8,128)(2,1)} %get-tuple-element.172.refs_0_), channel_id=1, source_target_pairs={{0,4},{1,5},{2,6},{3,7},{4,0},{5,1},{6,2},{7,3},{8,12},{9,13},{10,... | collective-permute-start | bytes 608264 | tf_op jit(solution)/shard_map/ppermute | solution.py:131
  71.9 36.1 %collective-permute-start.16 = (bf16[1,792,128]{2,1,0:T(8,128)(2,1)}, bf16[1,792,128]{2,1,0:T(8,128)(2,1)}, u32[]{:S(2)}, u32[]{:S(2)}) collective-permute-start(bf16[1,792,128]{2,1,0:T(8,128)(2,1)} %get-tuple-element.172.refs_0_), channel_id=1, source_target_pairs={{0,6},{1,7},{2,4},{3,5},{4,2},{5,3},{6,0},{7,1},{8,14},{9,15},{10,... | collective-permute-start | bytes 608264 | tf_op jit(solution)/shard_map/ppermute | solution.py:131
  76.9 25.5 %collective-permute-start.8 = (bf16[8,792,128]{2,1,0:T(8,128)(2,1)}, bf16[8,792,128]{2,1,0:T(8,128)(2,1)}, u32[]{:S(2)}, u32[]{:S(2)}) collective-permute-start(bf16[8,792,128]{2,1,0:T(8,128)(2,1)} %join.9.refs_0_), channel_id=1, source_target_pairs={{0,1},{1,0},{2,3},{3,2},{4,5},{5,4},{6,7},{7,6},{8,24},{9,25},{10,... | collective-permute-start | bytes 4866056 | tf_op jit(solution)/shard_map/ppermute | solution.py:131
  103.4 25.5 %collective-permute-start.17 = (bf16[4,792,128]{2,1,0:T(8,128)(2,1)S(1)}, bf16[4,792,128]{2,1,0:T(8,128)(2,1)S(1)}, u32[]{:S(2)}, u32[]{:S(2)}) collective-permute-start(bf16[4,792,128]{2,1,0:T(8,128)(2,1)S(1)} %copy-done.5), channel_id=1, source_target_pairs={{0,16},{1,17},{2,18},{3,19},{4,20},{5,21},{6,22},{7,23},{8,9},{9,8... | collective-permute-start | bytes 2433032 | tf_op jit(solution)/shard_map/ppermute | solution.py:131
  110.2 24.3 %collective-permute-start.18 = (bf16[1,792,128]{2,1,0:T(8,128)(2,1)S(1)}, bf16[1,792,128]{2,1,0:T(8,128)(2,1)S(1)}, u32[]{:S(2)}, u32[]{:S(2)}) collective-permute-start(bf16[1,792,128]{2,1,0:T(8,128)(2,1)S(1)} %copy-done.6), channel_id=1, source_target_pairs={{0,2},{1,3},{2,0},{3,1},{4,6},{5,7},{6,4},{7,5},{8,10},{9,11},{10,... | collective-permute-start | bytes 608264 | tf_op jit(solution)/shard_map/ppermute | solution.py:131
  132.5 34.5 %collective-permute-start.22 = (bf16[8,792,128]{2,1,0:T(8,128)(2,1)}, bf16[8,792,128]{2,1,0:T(8,128)(2,1)}, u32[]{:S(2)}, u32[]{:S(2)}) collective-permute-start(bf16[8,792,128]{2,1,0:T(8,128)(2,1)} %join.12.refs_0_), channel_id=1, source_target_pairs={{0,1},{1,0},{2,3},{3,2},{4,5},{5,4},{6,7},{7,6},{8,24},{9,25},{10,... | collective-permute-start | bytes 4866056 | tf_op jit(solution)/shard_map/ppermute | solution.py:131
  134.5 47.4 %collective-permute-start.24 = (bf16[8,792,128]{2,1,0:T(8,128)(2,1)}, bf16[8,792,128]{2,1,0:T(8,128)(2,1)}, u32[]{:S(2)}, u32[]{:S(2)}) collective-permute-start(bf16[8,792,128]{2,1,0:T(8,128)(2,1)} %join.12.refs_0_), channel_id=1, source_target_pairs={{0,8},{1,9},{2,10},{3,11},{4,12},{5,13},{6,14},{7,15},{8,0},{9,1},... | collective-permute-start | bytes 4866056 | tf_op jit(solution)/shard_map/ppermute | solution.py:131
  165.5 29.9 %collective-permute-start.26 = (bf16[8,792,128]{2,1,0:T(8,128)(2,1)}, bf16[8,792,128]{2,1,0:T(8,128)(2,1)}, u32[]{:S(2)}, u32[]{:S(2)}) collective-permute-start(bf16[8,792,128]{2,1,0:T(8,128)(2,1)} %join.14.refs_4_.refs_0_), channel_id=1, source_target_pairs={{0,1},{1,0},{2,3},{3,2},{4,5},{5,4},{6,7},{7,6},{8,24},{9,25},{10,... | collective-permute-start | bytes 4866056 | tf_op jit(solution)/shard_map/ppermute | solution.py:131
  165.8 36.7 %collective-permute-start.28 = (bf16[8,792,128]{2,1,0:T(8,128)(2,1)}, bf16[8,792,128]{2,1,0:T(8,128)(2,1)}, u32[]{:S(2)}, u32[]{:S(2)}) collective-permute-start(bf16[8,792,128]{2,1,0:T(8,128)(2,1)} %join.14.refs_4_.refs_0_), channel_id=1, source_target_pairs={{0,8},{1,9},{2,10},{3,11},{4,12},{5,13},{6,14},{7,15},{8,0},{9,1},... | collective-permute-start | bytes 4866056 | tf_op jit(solution)/shard_map/ppermute | solution.py:131
  249.0 24.6 %collective-permute-start.30 = (bf16[16,792,128]{2,1,0:T(8,128)(2,1)}, bf16[16,792,128]{2,1,0:T(8,128)(2,1)}, u32[]{:S(2)}, u32[]{:S(2)}) collective-permute-start(bf16[16,792,128]{2,1,0:T(8,128)(2,1)} %get-tuple-element.213), channel_id=1, source_target_pairs={{0,8},{1,9},{2,10},{3,11},{4,12},{5,13},{6,14},{7,15},{8,0},{9,1},... | collective-permute-start | bytes 9732104 | tf_op jit(solution)/shard_map/ppermute | solution.py:131
  277.0 50.1 %collective-permute-start.33 = (bf16[8,792,128]{2,1,0:T(8,128)(2,1)}, bf16[8,792,128]{2,1,0:T(8,128)(2,1)}, u32[]{:S(2)}, u32[]{:S(2)}) collective-permute-start(bf16[8,792,128]{2,1,0:T(8,128)(2,1)} %add_terms.16), channel_id=1, source_target_pairs={{0,1},{1,0},{2,3},{3,2},{4,5},{5,4},{6,7},{7,6},{8,24},{9,25},{10,... | collective-permute-start | bytes 4866056 | tf_op jit(solution)/shard_map/ppermute | solution.py:131
  327.0 23.8 %collective-permute-start.35 = (bf16[16,792,128]{2,1,0:T(8,128)(2,1)}, bf16[16,792,128]{2,1,0:T(8,128)(2,1)}, u32[]{:S(2)}, u32[]{:S(2)}) collective-permute-start(bf16[16,792,128]{2,1,0:T(8,128)(2,1)} %get-tuple-element.235), channel_id=1, source_target_pairs={{0,8},{1,9},{2,10},{3,11},{4,12},{5,13},{6,14},{7,15},{8,0},{9,1},... | collective-permute-start | bytes 9732104 | tf_op jit(solution)/shard_map/ppermute | solution.py:131
  346.3 41.4 %collective-permute-start.38 = (bf16[1,792,128]{2,1,0:T(8,128)(2,1)}, bf16[1,792,128]{2,1,0:T(8,128)(2,1)}, u32[]{:S(2)}, u32[]{:S(2)}) collective-permute-start(bf16[1,792,128]{2,1,0:T(8,128)(2,1)} %get-tuple-element.249), channel_id=1, source_target_pairs={{0,2},{1,3},{2,0},{3,1},{4,6},{5,7},{6,4},{7,5},{8,10},{9,11},{10,... | collective-permute-start | bytes 608264 | tf_op jit(solution)/shard_map/ppermute | solution.py:131
  346.5 41.2 %collective-permute-start.39 = (bf16[1,792,128]{2,1,0:T(8,128)(2,1)}, bf16[1,792,128]{2,1,0:T(8,128)(2,1)}, u32[]{:S(2)}, u32[]{:S(2)}) collective-permute-start(bf16[1,792,128]{2,1,0:T(8,128)(2,1)} %get-tuple-element.251), channel_id=1, source_target_pairs={{0,4},{1,5},{2,6},{3,7},{4,0},{5,1},{6,2},{7,3},{8,12},{9,13},{10,... | collective-permute-start | bytes 608264 | tf_op jit(solution)/shard_map/ppermute | solution.py:131
  349.3 38.5 %collective-permute-start.40 = (bf16[1,792,128]{2,1,0:T(8,128)(2,1)}, bf16[1,792,128]{2,1,0:T(8,128)(2,1)}, u32[]{:S(2)}, u32[]{:S(2)}) collective-permute-start(bf16[1,792,128]{2,1,0:T(8,128)(2,1)} %get-tuple-element.253), channel_id=1, source_target_pairs={{0,6},{1,7},{2,4},{3,5},{4,2},{5,3},{6,0},{7,1},{8,14},{9,15},{10,... | collective-permute-start | bytes 608264 | tf_op jit(solution)/shard_map/ppermute | solution.py:131
  354.2 35.7 %collective-permute-start.36 = (bf16[8,792,128]{2,1,0:T(8,128)(2,1)}, bf16[8,792,128]{2,1,0:T(8,128)(2,1)}, u32[]{:S(2)}, u32[]{:S(2)}) collective-permute-start(bf16[8,792,128]{2,1,0:T(8,128)(2,1)} %add_terms.19), channel_id=1, source_target_pairs={{0,1},{1,0},{2,3},{3,2},{4,5},{5,4},{6,7},{7,6},{8,24},{9,25},{10,... | collective-permute-start | bytes 4866056 | tf_op jit(solution)/shard_map/ppermute | solution.py:131
  362.8 31.9 %collective-permute-start.37 = (bf16[16,792,128]{2,1,0:T(8,128)(2,1)}, bf16[16,792,128]{2,1,0:T(8,128)(2,1)}, u32[]{:S(2)}, u32[]{:S(2)}) collective-permute-start(bf16[16,792,128]{2,1,0:T(8,128)(2,1)} %get-tuple-element.247), channel_id=1, source_target_pairs={{0,8},{1,9},{2,10},{3,11},{4,12},{5,13},{6,14},{7,15},{8,0},{9,1},... | collective-permute-start | bytes 9732104 | tf_op jit(solution)/shard_map/ppermute | solution.py:131
  398.2 25.3 %collective-permute-start.42 = (bf16[8,792,128]{2,1,0:T(8,128)(2,1)}, bf16[8,792,128]{2,1,0:T(8,128)(2,1)}, u32[]{:S(2)}, u32[]{:S(2)}) collective-permute-start(bf16[8,792,128]{2,1,0:T(8,128)(2,1)} %add_terms.21), channel_id=1, source_target_pairs={{0,1},{1,0},{2,3},{3,2},{4,5},{5,4},{6,7},{7,6},{8,24},{9,25},{10,... | collective-permute-start | bytes 4866056 | tf_op jit(solution)/shard_map/ppermute | solution.py:131
  417.6 26.1 %collective-permute-start.44 = (bf16[1,792,128]{2,1,0:T(8,128)(2,1)}, bf16[1,792,128]{2,1,0:T(8,128)(2,1)}, u32[]{:S(2)}, u32[]{:S(2)}) collective-permute-start(bf16[1,792,128]{2,1,0:T(8,128)(2,1)} %get-tuple-element.270), channel_id=1, source_target_pairs={{0,2},{1,3},{2,0},{3,1},{4,6},{5,7},{6,4},{7,5},{8,10},{9,11},{10,... | collective-permute-start | bytes 608264 | tf_op jit(solution)/shard_map/ppermute | solution.py:131
  417.6 26.1 %collective-permute-start.45 = (bf16[1,792,128]{2,1,0:T(8,128)(2,1)}, bf16[1,792,128]{2,1,0:T(8,128)(2,1)}, u32[]{:S(2)}, u32[]{:S(2)}) collective-permute-start(bf16[1,792,128]{2,1,0:T(8,128)(2,1)} %get-tuple-element.272), channel_id=1, source_target_pairs={{0,4},{1,5},{2,6},{3,7},{4,0},{5,1},{6,2},{7,3},{8,12},{9,13},{10,... | collective-permute-start | bytes 608264 | tf_op jit(solution)/shard_map/ppermute | solution.py:131
  448.5 28.8 %collective-permute-start.50 = (bf16[1,792,128]{2,1,0:T(8,128)(2,1)}, bf16[1,792,128]{2,1,0:T(8,128)(2,1)}, u32[]{:S(2)}, u32[]{:S(2)}) collective-permute-start(bf16[1,792,128]{2,1,0:T(8,128)(2,1)} %get-tuple-element.285), channel_id=1, source_target_pairs={{0,2},{1,3},{2,0},{3,1},{4,6},{5,7},{6,4},{7,5},{8,10},{9,11},{10,... | collective-permute-start | bytes 608264 | tf_op jit(solution)/shard_map/ppermute | solution.py:131
  448.5 28.8 %collective-permute-start.51 = (bf16[1,792,128]{2,1,0:T(8,128)(2,1)}, bf16[1,792,128]{2,1,0:T(8,128)(2,1)}, u32[]{:S(2)}, u32[]{:S(2)}) collective-permute-start(bf16[1,792,128]{2,1,0:T(8,128)(2,1)} %get-tuple-element.287), channel_id=1, source_target_pairs={{0,4},{1,5},{2,6},{3,7},{4,0},{5,1},{6,2},{7,3},{8,12},{9,13},{10,... | collective-permute-start | bytes 608264 | tf_op jit(solution)/shard_map/ppermute | solution.py:131
  451.4 25.9 %collective-permute-start.52 = (bf16[1,792,128]{2,1,0:T(8,128)(2,1)}, bf16[1,792,128]{2,1,0:T(8,128)(2,1)}, u32[]{:S(2)}, u32[]{:S(2)}) collective-permute-start(bf16[1,792,128]{2,1,0:T(8,128)(2,1)} %get-tuple-element.289), channel_id=1, source_target_pairs={{0,6},{1,7},{2,4},{3,5},{4,2},{5,3},{6,0},{7,1},{8,14},{9,15},{10,... | collective-permute-start | bytes 608264 | tf_op jit(solution)/shard_map/ppermute | solution.py:131
  (83 other events, 991.6 us)

commit v5 on v4

--- a/solution.py
+++ b/solution.py
@@ -22,6 +22,8 @@
 BF16 = jnp.bfloat16
 F32 = jnp.float32
 VMEM_LIMIT = 62 << 20
+BUFFERS = 4
+FETCHES = 6
 
 SHAPES = [
     (D,),
@@ -269,7 +271,7 @@
 
     def fetch(step):
         device = region.low + step
-        buf = lax.rem(step, 2)
+        buf = lax.rem(step, FETCHES)
 
         def from_phase(position, groups):
             for own in range(2):
@@ -289,16 +291,22 @@
 
         by_phase(geo, GATHER_PHASES, region.gather, device, from_phase)
 
-    fetch(0)
+    ahead = min(FETCHES - 1, region.slots)
+
+    def fetch_body(step, _):
+        fetch(step)
+        return 0
+
+    lax.fori_loop(0, ahead, fetch_body, 0)
 
     def slot_body(step, carry):
         tile_carry, done = carry
 
-        @pl.when(step + 1 < region.slots)
+        @pl.when(step + ahead < region.slots)
         def _():
-            fetch(step + 1)
-
-        buf = lax.rem(step, 2)
+            fetch(step + ahead)
+
+        buf = lax.rem(step, FETCHES)
         for number in range(4):
             pltpu.make_async_copy(
                 srcs[0].at[0], slot_ref.at[buf, pl.ds(0, quarter)], sems.at[buf, number]
@@ -376,9 +384,9 @@
         out_specs=[anywhere()] + [vmem()] * len(region.vectors),
         scratch_shapes=[
             region.scratch(),
-            pltpu.VMEM((2, geo.slot, LANES), BF16),
+            pltpu.VMEM((FETCHES, geo.slot, LANES), BF16),
             pltpu.VMEM((height, region.cols * LANES), BF16),
-            pltpu.SemaphoreType.DMA((2, 4)),
+            pltpu.SemaphoreType.DMA((FETCHES, 4)),
             pltpu.SemaphoreType.DMA(()),
         ],
         input_output_aliases=aliases,
@@ -455,8 +463,8 @@
         geo, region, pitch = self.geo, self.region, self.region.pitch
 
         def slot_body(index, _):
-            parity = lax.rem(index, 2)
-            pl.when(index >= 2)(lambda: self.wait(parity))
+            parity = lax.rem(index, BUFFERS)
+            pl.when(index >= BUFFERS)(lambda: self.wait(parity))
             first_tile = geo.base(region.low + index) // 16 - region.origin // 16
 
             def convert(add):
@@ -504,16 +512,16 @@
         lax.fori_loop(start, stop, slot_body, 0)
 
     def finish(self):
-        for index in range(max(0, self.region.slots - 2), self.region.slots):
-            self.wait(index % 2)
+        for index in range(max(0, self.region.slots - BUFFERS), self.region.slots):
+            self.wait(index % BUFFERS)
 
 
 def emit_scratch(geo, region):
     return [
         region.scratch(),
-        pltpu.VMEM((2, geo.slot, LANES), BF16),
+        pltpu.VMEM((BUFFERS, geo.slot, LANES), BF16),
         pltpu.VMEM((geo.slot, LANES), BF16),
-        pltpu.SemaphoreType.DMA((2, 4)),
+        pltpu.SemaphoreType.DMA((BUFFERS, 4)),
         pltpu.SemaphoreType.DMA((4,)),
     ]
 
@@ -875,31 +883,37 @@
     shift = lax.rem(base, 16)
     dp_index = me_ref[1] * 2 + me_ref[2]
     margin = 128
-    for offset in range(4):
-        to = pl.multiple_of(margin + (dp_index ^ offset) * quarter, 8)
-        grad_ref[pl.ds(to, quarter), :] = quarters[offset][...].astype(F32)
-    for row, count, at in ((0, HEAD_ROWS, 0), (TAIL_ROW, LATE_TAIL, HEAD_ROWS)):
-
-        @pl.when((base < row + count) & (base + rows > row))
-        def _(row=row, count=count, at=at):
-            lane = lax.broadcasted_iota(jnp.int32, (count, LANES), 1)
-            p_rows = lax.broadcasted_iota(jnp.int32, (count, LANES), 0) + row
-            before = p_rows * LANES + lane < SPLIT
-            to = jnp.clip(margin + shift + row - base, 0, margin + geo.slot)
-            here = pl.ds(to, count)
-            late = late_ref[at : at + count, :]
-            grad_ref[here, :] = jnp.where(before, late, grad_ref[here, :])
+    step = pl.program_id(0)
+
+    @pl.when(step == 0)
+    def _():
+        for offset in range(4):
+            to = pl.multiple_of(margin + (dp_index ^ offset) * quarter, 8)
+            grad_ref[pl.ds(to, quarter), :] = quarters[offset][...].astype(F32)
+        for row, count, at in ((0, HEAD_ROWS, 0), (TAIL_ROW, LATE_TAIL, HEAD_ROWS)):
+
+            @pl.when((base < row + count) & (base + rows > row))
+            def _(row=row, count=count, at=at):
+                lane = lax.broadcasted_iota(jnp.int32, (count, LANES), 1)
+                p_rows = lax.broadcasted_iota(jnp.int32, (count, LANES), 0) + row
+                before = p_rows * LANES + lane < SPLIT
+                to = jnp.clip(margin + shift + row - base, 0, margin + geo.slot)
+                here = pl.ds(to, count)
+                late = late_ref[at : at + count, :]
+                grad_ref[here, :] = jnp.where(before, late, grad_ref[here, :])
 
     span = 64
+    count = p_ref.shape[0]
     scale, first_fix, second_fix, rate = (coef_ref[i] for i in range(4))
 
     def body(i, _):
-        r0 = jnp.minimum(i * span, rows - span)
-        here = grad_ref[pl.ds(margin + shift + r0, span), :]
-        below = grad_ref[pl.ds(margin + shift + r0 + 1, span), :]
+        r0 = pl.multiple_of(i * span, span)
+        ahead = step * count + r0
+        here = grad_ref[pl.ds(margin + shift + ahead, span), :]
+        below = grad_ref[pl.ds(margin + shift + ahead + 1, span), :]
         lane = lax.broadcasted_iota(jnp.int32, (span, LANES), 1)
         row = lax.broadcasted_iota(jnp.int32, (span, LANES), 0)
-        flat = (base + r0 + row) * LANES + lane
+        flat = (base + ahead + row) * LANES + lane
         back = LANES - LIFT
         moved = jnp.where(lane < back, pltpu.roll(here, back, 1), pltpu.roll(below, back, 1))
         scaled = jnp.where(flat < SPLIT, here, moved) * scale
@@ -913,17 +927,20 @@
         second_out[at, :] = second_new
         return 0
 
-    lax.fori_loop(0, -(-rows // span), body, 0)
+    lax.fori_loop(0, count // span, body, 0)
 
 
 def update_step(geo, me, coef, quarters, late, params, first, second):
     rows = jax.ShapeDtypeStruct((geo.rows, LANES), F32)
+    block = round_up(-(-geo.rows // 4), 64)
+    part = pl.BlockSpec((block, LANES), lambda i: (i, 0))
     return pl.pallas_call(
         partial(update_kernel, geo),
+        grid=(-(-geo.rows // block),),
         out_shape=[rows, rows, rows],
-        in_specs=[smem(), smem()] + [vmem()] * 8,
-        out_specs=[vmem()] * 3,
-        scratch_shapes=[pltpu.VMEM((geo.slot + 384, LANES), F32)],
+        in_specs=[smem(), smem()] + [vmem()] * 5 + [part] * 3,
+        out_specs=[part] * 3,
+        scratch_shapes=[pltpu.VMEM((geo.slot + 704, LANES), F32)],
         compiler_params=params_of(),
         name="moments_update",
     )(me, coef, *quarters, late, params, first, second)
@@ -1143,7 +1160,7 @@
         out_ref[:, lanes] = context[:WP].astype(BF16)
         return 0
 
-    lax.fori_loop(0, HEADS // QUAD, block, 0, unroll=4)
+    lax.fori_loop(0, HEADS // QUAD, block, 0, unroll=8)
 
 
 def attention(mixed, bias):
@@ -1481,15 +1498,9 @@
 
 def first_back_kernel(steps, mixed_ref, w_ref, x_ref, mg_ref, gain_ref, out_ref, vec_ref, sum_ref):
     step = pl.program_id(0)
-    part = nt(mixed_ref[...], w_ref[...])
-
-    @pl.when(step == 0)
-    def _():
-        sum_ref[...] = part
-
-    @pl.when(step > 0)
-    def _():
-        sum_ref[...] += part
+    width = w_ref.shape[0]
+    lanes = pl.ds(pl.multiple_of(step * width, width), width)
+    sum_ref[:, lanes] = nt(mixed_ref[...], w_ref[...])
 
     @pl.when(step == steps - 1)
     def _():
@@ -1511,8 +1522,8 @@
 
 def first_back(mixed_grad, weight, x, middle_grad, gain):
     tokens = x.shape[0]
-    width = 768
-    steps = 3 * D // width
+    width = 256
+    steps = D // width
     rows = pl.BlockSpec((tokens, D), lambda k: (0, 0), pipeline_mode=pl.Buffered(1))
     return pl.pallas_call(
         partial(first_back_kernel, steps),
@@ -1522,8 +1533,8 @@
             jax.ShapeDtypeStruct((8, D), F32),
         ],
         in_specs=[
-            pl.BlockSpec((tokens, width), lambda k: (0, k)),
-            pl.BlockSpec((D, width), lambda k: (0, k)),
+            pl.BlockSpec((tokens, 3 * D), lambda k: (0, 0), pipeline_mode=pl.Buffered(1)),
+            pl.BlockSpec((width, 3 * D), lambda k: (k, 0)),
             rows,
             rows,
             pl.BlockSpec((1, D), lambda k: (0, 0)),
@@ -1587,16 +1598,14 @@
     gathers[1].line(held)
     x = permute_in(after(ids_of, held), patches, half, windows, x)
     near = gathers[0].last(x)
-    held = gathers[1].joined(x)
-    gathers[2].line(held)
-    grad_out = permute_in(after(ids_of, near, held), cotangent, 0, half)
+    grad_out = permute_in(after(ids_of, near), cotangent, 0, half)
     gathered = {0: gathers[0].finish(grad_out)}
     far = gathered[0][1]
-    gathers[1].across(far)
+    held = gathers[1].joined(far)
+    gathers[1].across()
+    gathers[2].line(held)
     grad_out = permute_in(after(ids_of, far), cotangent, half, windows, grad_out)
-    held = gathers[2].joined(grad_out)
-    gathers[3].line(held)
-    gathered[0] = gathered[0][:3] + [after(gathered[0][3], grad_out, held)]
+    gathered[0] = gathered[0][:3] + [after(gathered[0][3], grad_out)]
 
     mix_matrix = (MIX_ROW, D, 3 * D // LANES)
     out_matrix = (OUT_ROW, D, D // LANES)
@@ -1615,8 +1624,9 @@
     )
     mix_weight, attn_gain, attn_shift, mix_bias, table_rows = unpack(geo, first, me, gathered)
     near = gathers[1].last(mix_weight)
-    held = gathers[3].joined(mix_weight)
+    held = gathers[2].joined(mix_weight)
     gathers[2].across(near)
+    gathers[3].line(held)
     table_rows = after(table_rows, near, held)
 
     def line_of(rows):
@@ -1637,8 +1647,9 @@
     )
     gathered[1] = gathers[1].finish(mixed)
     near = gathers[2].last(mixed)
+    held = gathers[3].joined(mixed)
     gathers[3].across(near)
-    attended, logs = attention(after(mixed, near, gathered[1][1]), bias)
+    attended, logs = attention(after(mixed, near, held, gathered[1][1]), bias)
     out_weight, out_bias, mlp_gain, mlp_shift = unpack(
         geo, Region(geo, OUT_ROW, EXPAND_ROW, out_matrix, out_vectors), me, gathered
     )
@@ -1735,16 +1746,15 @@
     )
     packed = slots[0][0]
     phase0 = Reduction(geo, slots[0], 0)
-    sums[2] = phase2.total(packed)
-    sent = [phase1.line(packed), sums[2]]
-    activations = permute_out(row_ids[None], after(result, packed, *sent), arrivals)
-    sent = phase0.last(activations)
+    activations = permute_out(row_ids[None], after(result, packed), arrivals)
+    far = phase0.last(activations)
+    sums[2] = phase2.total(packed, far)
+    sent = [phase1.line(packed, far), sums[2]]
     input_rows, first_vec = first_back(
-        after(mixed_grad, sent), mix_weight, x, middle_grad, line_of(attn_gain)
-    )
-    sums[1] = phase1.total(input_rows)
-    sent = [phase0.across(input_rows), sums[1]]
-    table_grad = score_bias_back(ids, after(score_sums, *sent), entries)[:TABLE_ROWS]
+        after(mixed_grad, far, *sent), mix_weight, x, middle_grad, line_of(attn_gain)
+    )
+    sent = phase0.across(input_rows)
+    table_grad = score_bias_back(ids, after(score_sums, sent), entries)[:TABLE_ROWS]
 
     table_pad = (SPLIT_ROW - TABLE_ROW) * LANES - TABLE_ROWS * HEADS
     late = jnp.concatenate(
@@ -1756,6 +1766,7 @@
         axis=0,
     )
     sent = phase0.line(table_grad)
+    sums[1] = phase1.total(sent)
     late = after(jnp.pad(late, ((0, LATE_ROWS - late.shape[0]), (0, 0))), sent)
     late = sum_everywhere(geo, late)
     input_grad = permute_out(row_ids[None], after(input_rows, sent), arrivals)

time: 570 us -> 552 us (0.968)
  Pallas kernels: 379 us -> 361 us
  waiting for transfers between devices: 64.3 us -> 72.4 us
    pallas_call x4, Pallas kernels: 42.8 us -> 31.5 us  [unpack(): pl.pallas_call(partial(unpack_kernel, geo, region, 64 if region.cols <= 8...]
    ppermute x68, waiting for transfers between devices: 64.3 us -> 72.4 us  [permute(): return lax.ppermute(value, AXES, pairs)]
  transfers between devices with their start and end apart: 69 -> 69, of which waited for: 20 -> 21; matrix products, arithmetic and copies ran while one was open for 4% -> 4% of each run, Pallas kernels for 57% -> 57%
where the time goes in v5:
time: 552 us; the launch traced here: 545 us
  Pallas kernels  361 us (65%)
  starting transfers between devices  76.6 us (14%)
  waiting for transfers between devices  72.4 us (13%)
  local copies, waits for them, and re-layouts  20.4 us (4%)
  other arithmetic  11.7 us (2%)
    ppermute x68, starting transfers between devices, permute(): return lax.ppermute(value, AXES, pairs)  76 us
    ppermute x68, waiting for transfers between devices, permute(): return lax.ppermute(value, AXES, pairs)  72.4 us
    pallas_call x1, Pallas kernels, mlp_down(): pl.pallas_call(partial(mlp_down_kernel, geo, region, shared, steps, skip)...  46.9 us
    pallas_call x2, Pallas kernels, attention_back(): pl.pallas_call(partial(attention_back_kernel, before is not None), grid=(...  40.3 us
    pallas_call x1, Pallas kernels, mlp_up(): pl.pallas_call(partial(mlp_up_kernel, geo, region, shared, steps, skip),...  32.7 us
    pallas_call x4, Pallas kernels, unpack(): pl.pallas_call(partial(unpack_kernel, geo, region, 64 if region.cols <= 8...  31.5 us
    pallas_call x2, Pallas kernels, pack(): pl.pallas_call(partial(pack_kernel, geo, region, shared, steps, skip), gr...  20.8 us
    pallas_call x8, Pallas kernels, join(): pl.pallas_call(join_kernel, out_shape=jax.ShapeDtypeStruct((count,) + par...  19.9 us
  transfers between devices with their start and end apart: 69, of which 21 were waited for; matrix products, arithmetic and copies ran while one was open for 4% of the time, Pallas kernels for 57%

profile of v5, /device:TPU:0, one launch (start us, length us, event | category | flops | bytes accessed | tf_op | source)
XLA Modules:
  0.0 545.4 jit_solution(4608024537078051895)
XLA Ops:
  10.8 7.0 %collective-permute-start.2 = (bf16[792,128]{1,0:T(8,128)(2,1)S(1)}, bf16[792,128]{1,0:T(8,128)(2,1)S(1)}, u32[]{:S(2)}, u32[]{:S(2)}) collective-permute-start(bf16[792,128]{1,0:T(8,128)(2,1)S(1)} %get-tuple-element.319), channel_id=1, source_target_pairs={{0,16},{1,17},{2,18},{3,19},{4,20},{5,21},{6,22},{7,23},{8,24},{9,... | collective-permute-start | bytes 608264 | tf_op jit(solution)/shard_map/ppermute | solution.py:133
  18.6 6.6 %collective-permute-done.2 = bf16[792,128]{1,0:T(8,128)(2,1)S(1)} collective-permute-done((bf16[792,128]{1,0:T(8,128)(2,1)S(1)}, bf16[792,128]{1,0:T(8,128)(2,1)S(1)}, u32[]{:S(2)}, u32[]{:S(2)}) %collective-permute-start.2) | collective-permute-done | bytes 202784 | tf_op jit(solution)/shard_map/ppermute | solution.py:133
  36.2 6.5 %collective-permute-done.5.refs_2_ = bf16[1,792,128]{2,1,0:T(8,128)(2,1)S(1)} collective-permute-done((bf16[1,792,128]{2,1,0:T(8,128)(2,1)S(1)}, bf16[1,792,128]{2,1,0:T(8,128)(2,1)S(1)}, u32[]{:S(2)}, u32[]{:S(2)}) %collective-permute-start.5) | collective-permute-done | bytes 202784 | tf_op jit(solution)/shard_map/ppermute | solution.py:133
  58.7 5.8 %collective-permute-done.7.refs_1_ = bf16[4,792,128]{2,1,0:T(8,128)(2,1)S(1)} collective-permute-done((bf16[4,792,128]{2,1,0:T(8,128)(2,1)}, bf16[4,792,128]{2,1,0:T(8,128)(2,1)S(1)}, u32[]{:S(2)}, u32[]{:S(2)}) %collective-permute-start.7) | collective-permute-done | bytes 811040 | tf_op jit(solution)/shard_map/ppermute | solution.py:133
  78.1 13.5 %collective-permute-done.8.refs_1_ = bf16[8,792,128]{2,1,0:T(8,128)(2,1)S(1)} collective-permute-done((bf16[8,792,128]{2,1,0:T(8,128)(2,1)}, bf16[8,792,128]{2,1,0:T(8,128)(2,1)S(1)}, u32[]{:S(2)}, u32[]{:S(2)}) %collective-permute-start.8) | collective-permute-done | bytes 1622048 | tf_op jit(solution)/shard_map/ppermute | solution.py:133
  108.0 7.7 %unpack_weights.4 = (bf16[1024,3072]{1,0:T(8,128)(2,1)}, f32[8,128]{1,0:T(8,128)}, f32[8,128]{1,0:T(8,128)}, f32[24,128]{1,0:T(8,128)}, f32[91,128]{1,0:T(8,128)}) custom-call(s32[5]{0:T(128)} %stack.48.me_ref, bf16[8,792,128]{2,1,0:T(8,128)(2,1)} %join.9.refs_0_, bf16[8,792,128]{2,1,0:T(8,128)(2,1)} %copy-done.5, ...), custom_call_target="tpu_custom_call" | custom-call | bytes 5033164800 | tf_op jit(solution)/shard_map/unpack_weights/pallas_call | solution.py:379
  128.4 7.7 %score_bias.1.bias_ref = f32[32,104,128]{2,1,0:T(8,128)} custom-call(s32[104,128]{1,0:T(8,128)} %pad.22.ids_ref, bf16[32,368]{1,0:T(8,128)(2,1)} %pad.23.table_ref), custom_call_target="tpu_custom_call" | custom-call | flops 65431142400 | bytes 340787200 | tf_op jit(solution)/shard_map/score_bias/pallas_call | solution.py:1081
  137.5 13.0 %mix_rows.1 = (bf16[832,1024]{1,0:T(8,128)(2,1)}, bf16[832,3072]{1,0:T(8,128)(2,1)}) custom-call(bf16[832,1024]{1,0:T(8,128)(2,1)} %window_order.5.x_ref, f32[1,1024]{1,0:T(1,128)} %bitcast.79, f32[1,1024]{1,0:T(1,128)} %bitcast.83, bf16[1024,3072]{1,0:T(8,128)(2,1)} %get-tuple-element.173.w_ref, f32[1,3072]{1,0:T(1,128)} %bitcast.78), custom_call_target="tpu_custom_call" | custom-call | flops 1046898278400 | bytes 2621440000 | tf_op jit(solution)/shard_map/mix_rows/pallas_call | solution.py:1045
  158.8 12.2 %attention.1 = (bf16[832,1024]{1,0:T(8,128)(2,1)}, f32[8,32,128]{2,1,0:T(8,128)}) custom-call(bf16[832,3072]{1,0:T(8,128)(2,1)} %get-tuple-element.192.q_ref.k_ref.v_ref, bf16[832,3072]{1,0:T(8,128)(2,1)} %get-tuple-element.192.q_ref.k_ref.v_ref, bf16[832,3072]{1,0:T(8,128)(2,1)} %get-tuple-element.192.q_ref.k_ref.v_ref, f32[32,104,128]{2,1,0:T(8,128)} %score_bias.1.bias_ref), custom_call_target="tpu_custom_call" | custom-call | flops 2399999885312 | bytes 1363148800 | tf_op jit(solution)/shard_map/attention/pallas_call | solution.py:1172
  187.0 6.8 %middle_rows.1 = (f32[832,1024]{1,0:T(8,128)}, bf16[832,1024]{1,0:T(8,128)(2,1)}) custom-call(bf16[832,1024]{1,0:T(8,128)(2,1)} %window_order.5.x_ref, bf16[832,1024]{1,0:T(8,128)(2,1)} %get-tuple-element.199.a_ref, bf16[1024,1024]{1,0:T(8,128)(2,1)} %get-tuple-element.196.w_ref, f32[1,1024]{1,0:T(1,128)} %bitcast.85, f32[1,1024]{1,0:T(1,128)} %bitcast.81, ...), custom_call_target="tpu_custom_call" | custom-call | flops 348966092800 | bytes 1703936000 | tf_op jit(solution)/shard_map/middle_rows/pallas_call | solution.py:1288
  193.7 9.8 %unpack_weights.6 = (bf16[1024,4096]{1,0:T(8,128)(2,1)}, f32[32,128]{1,0:T(8,128)}) custom-call(s32[5]{0:T(128)} %stack.48.me_ref, bf16[8,792,128]{2,1,0:T(8,128)(2,1)} %join.11.refs_0_, bf16[8,792,128]{2,1,0:T(8,128)(2,1)} %collective-permute-done.22.refs_1_, bf16[8,792,128]{2,1,0:T(8,128)(2,1)} %collective-permute-done.24.refs_2_, ...), custom_call_target="tpu_custom_call" | custom-call | bytes 6710886400 | tf_op jit(solution)/shard_map/unpack_weights/pallas_call | solution.py:379
  207.7 32.7 %mlp_up.1 = (bf16[832,4096]{1,0:T(8,128)(2,1)}, f32[832,4096]{1,0:T(8,128)}, bf16[16,792,128]{2,1,0:T(8,128)(2,1)}, bf16[16,792,128]{2,1,0:T(8,128)(2,1)}, bf16[...) custom-call(s32[5]{0:T(128)} %stack.48.me_ref, bf16[832,1024]{1,0:T(8,128)(2,1)} %get-tuple-element.207.s_ref.refs_2_, ...), custom_call_target="tpu_custom_call" | custom-call | flops 2791728742400 | bytes 7444889600 | tf_op jit(solution)/shard_map/mlp_up/pallas_call | solution.py:1356
  251.2 9.3 %unpack_weights.7 = (bf16[4096,1024]{1,0:T(8,128)(2,1)}, f32[8,128]{1,0:T(8,128)}) custom-call(s32[5]{0:T(128)} %stack.48.me_ref, bf16[8,792,128]{2,1,0:T(8,128)(2,1)} %join.13.refs_4_.refs_0_, bf16[8,792,128]{2,1,0:T(8,128)(2,1)} %collective-permute-done.26.refs_5_.refs_1_, bf16[8,792,128]{2,1,0:T(8,128)(2,1)} %collective-permute-done.28.refs_6_.refs_2_, ...), custom_call_target="tpu_custom_call" | custom-call | bytes 6710886400 | tf_op jit(solution)/shard_map/unpack_weights/pallas_call | solution.py:379
  264.3 46.9 %mlp_down.1 = (bf16[832,1024]{1,0:T(8,128)(2,1)}, f32[832,1024]{1,0:T(8,128)}, bf16[16,792,128]{2,1,0:T(8,128)(2,1)}, bf16[16,792,128]{2,1,0:T(8,128)(2,1)}, bf1...) custom-call(s32[5]{0:T(128)} %stack.48.me_ref, ...), custom_call_target="tpu_custom_call", output_to_operand_aliasing={{4}: (9, {}), {5}: (10, {})} | custom-call | flops 5583457484800 | bytes 9122611200 | tf_op jit(solution)/shard_map/mlp_down/pallas_call | solution.py:1431
  316.9 9.1 %middle_back.1 = (f32[832,1024]{1,0:T(8,128)}, bf16[832,1024]{1,0:T(8,128)(2,1)}, bf16[832,1024]{1,0:T(8,128)(2,1)}, f32[8,1024]{1,0:T(8,128)}) custom-call(f32[832,1024]{1,0:T(8,128)} %get-tuple-element.226.s_ref, f32[832,1024]{1,0:T(8,128)} %get-tuple-element.217.refs_6_.m_ref, bf16[832,1024]{1,0:T(8,128)(2,1)} %window_order.7.g_ref.refs_3_, ...), custom_call_target="tpu_custom_call" | custom-call | flops 348966092800 | bytes 3067084800 | tf_op jit(solution)/shard_map/middle_back/pallas_call | solution.py:1476
  340.1 6.9 %weight_grad_pack.2 = (bf16[16,792,128]{2,1,0:T(8,128)(2,1)}, bf16[16,792,128]{2,1,0:T(8,128)(2,1)}) custom-call(s32[5]{0:T(128)} %stack.48.me_ref, bf16[832,1024]{1,0:T(8,128)(2,1)} %get-tuple-element.199.a_ref, bf16[832,1024]{1,0:T(8,128)(2,1)} %get-tuple-element.235.b_ref, f32[8,128]{1,0:T(8,128)} %bitcast.72, ...), custom_call_target="tpu_custom_call", output_to_operand_aliasing={{0}: (6, {}), {1}: (7, {})} | custom-call | flops 348966092800 | bytes 419430400 | tf_op jit(solution)/shard_map/weight_grad_pack/pallas_call | solution.py:612
  347.2 24.5 %attention_back.2 = (bf16[832,3072]{1,0:T(8,128)(2,1)}, f32[32,104,128]{2,1,0:T(8,128)}, f32[8,3072]{1,0:T(8,128)}) custom-call(bf16[832,3072]{1,0:T(8,128)(2,1)} %get-tuple-element.192.q_ref.k_ref.v_ref, bf16[832,3072]{1,0:T(8,128)(2,1)} %get-tuple-element.192.q_ref.k_ref.v_ref, bf16[832,3072]{1,0:T(8,128)(2,1)} %get-tuple-element.192.q_ref.k_ref.v_ref, ...), custom_call_target="tpu_custom_call" | custom-call | flops 2399999885312 | bytes 1363148800 | tf_op jit(solution)/shard_map/attention_back/pallas_call | solution.py:1257
  383.0 15.8 %attention_back.3 = (bf16[832,3072]{1,0:T(8,128)(2,1)}, f32[32,104,128]{2,1,0:T(8,128)}, f32[8,3072]{1,0:T(8,128)}) custom-call(bf16[832,3072]{1,0:T(8,128)(2,1)} %get-tuple-element.192.q_ref.k_ref.v_ref, bf16[832,3072]{1,0:T(8,128)(2,1)} %get-tuple-element.192.q_ref.k_ref.v_ref, ...), custom_call_target="tpu_custom_call", output_to_operand_aliasing={{0}: (8, {})} | custom-call | flops 2399999885312 | bytes 1363148800 | tf_op jit(solution)/shard_map/attention_back/pallas_call | solution.py:1257
  412.0 13.8 %weight_grad_pack.3 = (bf16[16,792,128]{2,1,0:T(8,128)(2,1)}, bf16[16,792,128]{2,1,0:T(8,128)(2,1)}) custom-call(s32[5]{0:T(128)} %stack.48.me_ref, bf16[832,1024]{1,0:T(8,128)(2,1)} %get-tuple-element.222.a_ref, bf16[832,3072]{1,0:T(8,128)(2,1)} %get-tuple-element.277.b_ref.mixed_ref), custom_call_target="tpu_custom_call" | custom-call | flops 1046898278400 | bytes 1258291200 | tf_op jit(solution)/shard_map/weight_grad_pack/pallas_call | solution.py:612
  425.9 5.2 arrival_order.2
  441.8 14.4 %first_back.1 = (bf16[832,1024]{1,0:T(8,128)(2,1)}, f32[8,1024]{1,0:T(8,128)}) custom-call(bf16[832,3072]{1,0:T(8,128)(2,1)} %get-tuple-element.277.b_ref.mixed_ref, bf16[1024,3072]{1,0:T(8,128)(2,1)} %get-tuple-element.173.w_ref, bf16[832,1024]{1,0:T(8,128)(2,1)} %window_order.5.x_ref, f32[832,1024]{1,0:T(8,128)} %get-tuple-element.278.mg_ref, ...), custom_call_target="tpu_custom_call" | custom-call | flops 1046898278400 | bytes 3643801600 | tf_op jit(solution)/shard_map/first_back/pallas_call | solution.py:1528
  465.1 9.5 %score_bias_back.1 = f32[368,96]{1,0:T(8,128)} custom-call(s32[104,128]{1,0:T(8,128)} %pad.22.ids_ref, f32[32,104,128]{2,1,0:T(8,128)} %get-tuple-element.283.sums_ref), custom_call_target="tpu_custom_call" | custom-call | flops 196293427200 | bytes 340787200 | tf_op jit(solution)/shard_map/score_bias_back/pallas_call | solution.py:1119
  488.1 5.2 arrival_order.3
  530.9 9.1 %moments_update.1 = (f32[3081,128]{1,0:T(8,128)}, f32[3081,128]{1,0:T(8,128)}, f32[3081,128]{1,0:T(8,128)}) custom-call(s32[5]{0:T(128)} %stack.48.me_ref, f32[4]{0:T(128)} %pad_maximum_fusion.1.coef_ref, f32[792,128]{1,0:T(8,128)} %select_bitcast_fusion.refs_0_, bf16[792,128]{1,0:T(8,128)(2,1)} %copy-done.9, ...), custom_call_target="tpu_custom_call" | custom-call | tf_op jit(solution)/shard_map/moments_update/pallas_call | solution.py:937
  (286 shorter events, 243.7 us)
Async XLA Ops:
  46.3 45.4 %collective-permute-start.11 = (bf16[1,792,128]{2,1,0:T(8,128)(2,1)}, bf16[1,792,128]{2,1,0:T(8,128)(2,1)}, u32[]{:S(2)}, u32[]{:S(2)}) collective-permute-start(bf16[1,792,128]{2,1,0:T(8,128)(2,1)} %get-tuple-element.169.refs_0_), channel_id=1, source_target_pairs={{0,2},{1,3},{2,0},{3,1},{4,6},{5,7},{6,4},{7,5},{8,10},{9,11},{10,... | collective-permute-start | bytes 608264 | tf_op jit(solution)/shard_map/ppermute | solution.py:133
  48.3 43.3 %collective-permute-start.12 = (bf16[1,792,128]{2,1,0:T(8,128)(2,1)}, bf16[1,792,128]{2,1,0:T(8,128)(2,1)}, u32[]{:S(2)}, u32[]{:S(2)}) collective-permute-start(bf16[1,792,128]{2,1,0:T(8,128)(2,1)} %get-tuple-element.169.refs_0_), channel_id=1, source_target_pairs={{0,4},{1,5},{2,6},{3,7},{4,0},{5,1},{6,2},{7,3},{8,12},{9,13},{10,... | collective-permute-start | bytes 608264 | tf_op jit(solution)/shard_map/ppermute | solution.py:133
  49.3 42.4 %collective-permute-start.13 = (bf16[1,792,128]{2,1,0:T(8,128)(2,1)}, bf16[1,792,128]{2,1,0:T(8,128)(2,1)}, u32[]{:S(2)}, u32[]{:S(2)}) collective-permute-start(bf16[1,792,128]{2,1,0:T(8,128)(2,1)} %get-tuple-element.169.refs_0_), channel_id=1, source_target_pairs={{0,6},{1,7},{2,4},{3,5},{4,2},{5,3},{6,0},{7,1},{8,14},{9,15},{10,... | collective-permute-start | bytes 608264 | tf_op jit(solution)/shard_map/ppermute | solution.py:133
  72.5 26.3 %collective-permute-start.9 = (bf16[8,792,128]{2,1,0:T(8,128)(2,1)}, bf16[8,792,128]{2,1,0:T(8,128)(2,1)}, u32[]{:S(2)}, u32[]{:S(2)}) collective-permute-start(bf16[8,792,128]{2,1,0:T(8,128)(2,1)} %join.9.refs_0_), channel_id=1, source_target_pairs={{0,8},{1,9},{2,10},{3,11},{4,12},{5,13},{6,14},{7,15},{8,0},{9,1},... | collective-permute-start | bytes 4866056 | tf_op jit(solution)/shard_map/ppermute | solution.py:133
  118.5 32.0 %collective-permute-start.19 = (bf16[1,792,128]{2,1,0:T(8,128)(2,1)}, bf16[1,792,128]{2,1,0:T(8,128)(2,1)}, u32[]{:S(2)}, u32[]{:S(2)}) collective-permute-start(bf16[1,792,128]{2,1,0:T(8,128)(2,1)} %get-tuple-element.187.refs_0_), channel_id=1, source_target_pairs={{0,2},{1,3},{2,0},{3,1},{4,6},{5,7},{6,4},{7,5},{8,10},{9,11},{10,... | collective-permute-start | bytes 608264 | tf_op jit(solution)/shard_map/ppermute | solution.py:133
  118.8 31.7 %collective-permute-start.20 = (bf16[1,792,128]{2,1,0:T(8,128)(2,1)}, bf16[1,792,128]{2,1,0:T(8,128)(2,1)}, u32[]{:S(2)}, u32[]{:S(2)}) collective-permute-start(bf16[1,792,128]{2,1,0:T(8,128)(2,1)} %get-tuple-element.187.refs_0_), channel_id=1, source_target_pairs={{0,4},{1,5},{2,6},{3,7},{4,0},{5,1},{6,2},{7,3},{8,12},{9,13},{10,... | collective-permute-start | bytes 608264 | tf_op jit(solution)/shard_map/ppermute | solution.py:133
  121.4 29.1 %collective-permute-start.21 = (bf16[1,792,128]{2,1,0:T(8,128)(2,1)}, bf16[1,792,128]{2,1,0:T(8,128)(2,1)}, u32[]{:S(2)}, u32[]{:S(2)}) collective-permute-start(bf16[1,792,128]{2,1,0:T(8,128)(2,1)} %get-tuple-element.187.refs_0_), channel_id=1, source_target_pairs={{0,6},{1,7},{2,4},{3,5},{4,2},{5,3},{6,0},{7,1},{8,14},{9,15},{10,... | collective-permute-start | bytes 608264 | tf_op jit(solution)/shard_map/ppermute | solution.py:133
  125.6 33.1 %collective-permute-start.22 = (bf16[8,792,128]{2,1,0:T(8,128)(2,1)}, bf16[8,792,128]{2,1,0:T(8,128)(2,1)}, u32[]{:S(2)}, u32[]{:S(2)}) collective-permute-start(bf16[8,792,128]{2,1,0:T(8,128)(2,1)} %join.11.refs_0_), channel_id=1, source_target_pairs={{0,1},{1,0},{2,3},{3,2},{4,5},{5,4},{6,7},{7,6},{8,24},{9,25},{10,... | collective-permute-start | bytes 4866056 | tf_op jit(solution)/shard_map/ppermute | solution.py:133
  156.5 29.9 %collective-permute-start.26 = (bf16[8,792,128]{2,1,0:T(8,128)(2,1)}, bf16[8,792,128]{2,1,0:T(8,128)(2,1)}, u32[]{:S(2)}, u32[]{:S(2)}) collective-permute-start(bf16[8,792,128]{2,1,0:T(8,128)(2,1)} %join.13.refs_4_.refs_0_), channel_id=1, source_target_pairs={{0,1},{1,0},{2,3},{3,2},{4,5},{5,4},{6,7},{7,6},{8,24},{9,25},{10,... | collective-permute-start | bytes 4866056 | tf_op jit(solution)/shard_map/ppermute | solution.py:133
  156.8 36.9 %collective-permute-start.28 = (bf16[8,792,128]{2,1,0:T(8,128)(2,1)}, bf16[8,792,128]{2,1,0:T(8,128)(2,1)}, u32[]{:S(2)}, u32[]{:S(2)}) collective-permute-start(bf16[8,792,128]{2,1,0:T(8,128)(2,1)} %join.13.refs_4_.refs_0_), channel_id=1, source_target_pairs={{0,8},{1,9},{2,10},{3,11},{4,12},{5,13},{6,14},{7,15},{8,0},{9,1},... | collective-permute-start | bytes 4866056 | tf_op jit(solution)/shard_map/ppermute | solution.py:133
  264.0 47.5 %collective-permute-start.33 = (bf16[8,792,128]{2,1,0:T(8,128)(2,1)}, bf16[8,792,128]{2,1,0:T(8,128)(2,1)}, u32[]{:S(2)}, u32[]{:S(2)}) collective-permute-start(bf16[8,792,128]{2,1,0:T(8,128)(2,1)} %add_terms.16), channel_id=1, source_target_pairs={{0,1},{1,0},{2,3},{3,2},{4,5},{5,4},{6,7},{7,6},{8,24},{9,25},{10,... | collective-permute-start | bytes 4866056 | tf_op jit(solution)/shard_map/ppermute | solution.py:133
  330.7 40.9 %collective-permute-start.38 = (bf16[1,792,128]{2,1,0:T(8,128)(2,1)}, bf16[1,792,128]{2,1,0:T(8,128)(2,1)}, u32[]{:S(2)}, u32[]{:S(2)}) collective-permute-start(bf16[1,792,128]{2,1,0:T(8,128)(2,1)} %get-tuple-element.247), channel_id=1, source_target_pairs={{0,2},{1,3},{2,0},{3,1},{4,6},{5,7},{6,4},{7,5},{8,10},{9,11},{10,... | collective-permute-start | bytes 608264 | tf_op jit(solution)/shard_map/ppermute | solution.py:133
  330.7 41.0 %collective-permute-start.39 = (bf16[1,792,128]{2,1,0:T(8,128)(2,1)}, bf16[1,792,128]{2,1,0:T(8,128)(2,1)}, u32[]{:S(2)}, u32[]{:S(2)}) collective-permute-start(bf16[1,792,128]{2,1,0:T(8,128)(2,1)} %get-tuple-element.249), channel_id=1, source_target_pairs={{0,4},{1,5},{2,6},{3,7},{4,0},{5,1},{6,2},{7,3},{8,12},{9,13},{10,... | collective-permute-start | bytes 608264 | tf_op jit(solution)/shard_map/ppermute | solution.py:133
  333.6 38.1 %collective-permute-start.40 = (bf16[1,792,128]{2,1,0:T(8,128)(2,1)}, bf16[1,792,128]{2,1,0:T(8,128)(2,1)}, u32[]{:S(2)}, u32[]{:S(2)}) collective-permute-start(bf16[1,792,128]{2,1,0:T(8,128)(2,1)} %get-tuple-element.251), channel_id=1, source_target_pairs={{0,6},{1,7},{2,4},{3,5},{4,2},{5,3},{6,0},{7,1},{8,14},{9,15},{10,... | collective-permute-start | bytes 608264 | tf_op jit(solution)/shard_map/ppermute | solution.py:133
  338.6 35.2 %collective-permute-start.36 = (bf16[8,792,128]{2,1,0:T(8,128)(2,1)}, bf16[8,792,128]{2,1,0:T(8,128)(2,1)}, u32[]{:S(2)}, u32[]{:S(2)}) collective-permute-start(bf16[8,792,128]{2,1,0:T(8,128)(2,1)} %add_terms.19), channel_id=1, source_target_pairs={{0,1},{1,0},{2,3},{3,2},{4,5},{5,4},{6,7},{7,6},{8,24},{9,25},{10,... | collective-permute-start | bytes 4866056 | tf_op jit(solution)/shard_map/ppermute | solution.py:133
  347.1 31.3 %collective-permute-start.37 = (bf16[16,792,128]{2,1,0:T(8,128)(2,1)}, bf16[16,792,128]{2,1,0:T(8,128)(2,1)}, u32[]{:S(2)}, u32[]{:S(2)}) collective-permute-start(bf16[16,792,128]{2,1,0:T(8,128)(2,1)} %get-tuple-element.245), channel_id=1, source_target_pairs={{0,8},{1,9},{2,10},{3,11},{4,12},{5,13},{6,14},{7,15},{8,0},{9,1},... | collective-permute-start | bytes 9732104 | tf_op jit(solution)/shard_map/ppermute | solution.py:133
  381.9 25.4 %collective-permute-start.42 = (bf16[8,792,128]{2,1,0:T(8,128)(2,1)}, bf16[8,792,128]{2,1,0:T(8,128)(2,1)}, u32[]{:S(2)}, u32[]{:S(2)}) collective-permute-start(bf16[8,792,128]{2,1,0:T(8,128)(2,1)} %add_terms.21), channel_id=1, source_target_pairs={{0,1},{1,0},{2,3},{3,2},{4,5},{5,4},{6,7},{7,6},{8,24},{9,25},{10,... | collective-permute-start | bytes 4866056 | tf_op jit(solution)/shard_map/ppermute | solution.py:133
  401.4 35.7 %collective-permute-start.45 = (bf16[1,792,128]{2,1,0:T(8,128)(2,1)}, bf16[1,792,128]{2,1,0:T(8,128)(2,1)}, u32[]{:S(2)}, u32[]{:S(2)}) collective-permute-start(bf16[1,792,128]{2,1,0:T(8,128)(2,1)} %get-tuple-element.271), channel_id=1, source_target_pairs={{0,2},{1,3},{2,0},{3,1},{4,6},{5,7},{6,4},{7,5},{8,10},{9,11},{10,... | collective-permute-start | bytes 608264 | tf_op jit(solution)/shard_map/ppermute | solution.py:133
  401.4 35.7 %collective-permute-start.46 = (bf16[1,792,128]{2,1,0:T(8,128)(2,1)}, bf16[1,792,128]{2,1,0:T(8,128)(2,1)}, u32[]{:S(2)}, u32[]{:S(2)}) collective-permute-start(bf16[1,792,128]{2,1,0:T(8,128)(2,1)} %get-tuple-element.273), channel_id=1, source_target_pairs={{0,4},{1,5},{2,6},{3,7},{4,0},{5,1},{6,2},{7,3},{8,12},{9,13},{10,... | collective-permute-start | bytes 608264 | tf_op jit(solution)/shard_map/ppermute | solution.py:133
  404.3 32.9 %collective-permute-start.47 = (bf16[1,792,128]{2,1,0:T(8,128)(2,1)}, bf16[1,792,128]{2,1,0:T(8,128)(2,1)}, u32[]{:S(2)}, u32[]{:S(2)}) collective-permute-start(bf16[1,792,128]{2,1,0:T(8,128)(2,1)} %get-tuple-element.275), channel_id=1, source_target_pairs={{0,6},{1,7},{2,4},{3,5},{4,2},{5,3},{6,0},{7,1},{8,14},{9,15},{10,... | collective-permute-start | bytes 608264 | tf_op jit(solution)/shard_map/ppermute | solution.py:133
  411.4 25.7 %collective-permute-start.44 = (bf16[4,792,128]{2,1,0:T(8,128)(2,1)}, bf16[4,792,128]{2,1,0:T(8,128)(2,1)}, u32[]{:S(2)}, u32[]{:S(2)}) collective-permute-start(bf16[4,792,128]{2,1,0:T(8,128)(2,1)} %get-tuple-element.262), channel_id=1, source_target_pairs={{0,16},{1,17},{2,18},{3,19},{4,20},{5,21},{6,22},{7,23},{8,9},{9,8... | collective-permute-start | bytes 2433032 | tf_op jit(solution)/shard_map/ppermute | solution.py:133
  435.5 24.9 %collective-permute-start.48 = (bf16[8,792,128]{2,1,0:T(8,128)(2,1)}, bf16[8,792,128]{2,1,0:T(8,128)(2,1)}, u32[]{:S(2)}, u32[]{:S(2)}) collective-permute-start(bf16[8,792,128]{2,1,0:T(8,128)(2,1)} %add_terms.25), channel_id=1, source_target_pairs={{0,1},{1,0},{2,3},{3,2},{4,5},{5,4},{6,7},{7,6},{8,24},{9,25},{10,... | collective-permute-start | bytes 4866056 | tf_op jit(solution)/shard_map/ppermute | solution.py:133
  457.6 28.2 %collective-permute-start.50 = (bf16[1,792,128]{2,1,0:T(8,128)(2,1)}, bf16[1,792,128]{2,1,0:T(8,128)(2,1)}, u32[]{:S(2)}, u32[]{:S(2)}) collective-permute-start(bf16[1,792,128]{2,1,0:T(8,128)(2,1)} %get-tuple-element.287), channel_id=1, source_target_pairs={{0,2},{1,3},{2,0},{3,1},{4,6},{5,7},{6,4},{7,5},{8,10},{9,11},{10,... | collective-permute-start | bytes 608264 | tf_op jit(solution)/shard_map/ppermute | solution.py:133
  457.6 29.7 %collective-permute-start.51 = (bf16[1,792,128]{2,1,0:T(8,128)(2,1)}, bf16[1,792,128]{2,1,0:T(8,128)(2,1)}, u32[]{:S(2)}, u32[]{:S(2)}) collective-permute-start(bf16[1,792,128]{2,1,0:T(8,128)(2,1)} %get-tuple-element.289), channel_id=1, source_target_pairs={{0,4},{1,5},{2,6},{3,7},{4,0},{5,1},{6,2},{7,3},{8,12},{9,13},{10,... | collective-permute-start | bytes 608264 | tf_op jit(solution)/shard_map/ppermute | solution.py:133
  (80 other events, 1047.7 us)

commit v6 on v5

--- a/solution.py
+++ b/solution.py
@@ -119,7 +119,7 @@
         self.slot = 4 * self.quarter
         assert self.slot % 16 == 0
         tiles = self.slot // 16
-        self.chunk = max(t for t in range(1, 34) if tiles % t == 0)
+        self.chunk = max(t for t in range(1, 19) if tiles % t == 0)
         self.bit_x, self.bit_core, self.bit_y = 2 * fsdp, fsdp, 1
 
     def base(self, device):
@@ -578,9 +578,18 @@
             left_ref[r : r + 256, :] = a_ref[:, r : r + 256].T
 
     width = b_ref.shape[1]
-    store_columns(
-        region, flat_ref, 0, step * (width // LANES), nn(left_ref[...], b_ref[...])
-    )
+    def rows_body(i, _):
+        r0 = pl.multiple_of(i * 512, 512)
+        store_columns(
+            region,
+            flat_ref,
+            r0,
+            step * (width // LANES),
+            nn(left_ref[pl.ds(r0, 512), :], b_ref[...]),
+        )
+        return 0
+
+    lax.fori_loop(0, region.depth // 512, rows_body, 0)
 
     @pl.when(step == grid_steps - 1)
     def _():
@@ -954,7 +963,14 @@
     arrivals = values_ref.shape[0]
     lane = lax.broadcasted_iota(jnp.int32, (WP, arrivals), 1)
     pick = jnp.where(rows_ref[...] == lane, 1.0, 0.0).astype(BF16)
-    refs[-1][...] = nn(pick, values_ref[...]).astype(BF16)
+    out_ref = refs[-1]
+
+    def body(i, _):
+        lanes = pl.ds(pl.multiple_of(i * 512, 512), 512)
+        out_ref[:, lanes] = nn(pick, values_ref[:, lanes]).astype(BF16)
+        return 0
+
+    lax.fori_loop(0, D // 512, body, 0)
 
 
 def permute_in(row_ids, values, start, stop, before=None):
@@ -984,7 +1000,13 @@
     count = out_ref.shape[0]
     arrival = lax.broadcasted_iota(jnp.int32, (count, rows_ref.shape[1]), 0)
     pick = jnp.where(rows_ref[...] == arrival + pl.program_id(0) * count, 1.0, 0.0).astype(BF16)
-    out_ref[...] = nn(pick, x_ref[...]).astype(BF16)
+
+    def body(i, _):
+        lanes = pl.ds(pl.multiple_of(i * 512, 512), 512)
+        out_ref[:, lanes] = nn(pick, x_ref[:, lanes]).astype(BF16)
+        return 0
+
+    lax.fori_loop(0, D // 512, body, 0)
 
 
 def permute_out(row_ids, values, arrivals):

time: 552 us -> 542 us (0.982)
    pallas_call x2, Pallas kernels: 40.3 us -> 31.1 us  [attention_back(): pl.pallas_call(partial(attention_back_kernel, before is not None), grid=(...]
  transfers between devices with their start and end apart: 69 -> 69, of which waited for: 21 -> 21; matrix products, arithmetic and copies ran while one was open for 4% -> 5% of each run, Pallas kernels for 57% -> 57%
where the time goes in v6:
time: 542 us; the launch traced here: 539 us
  Pallas kernels  358 us (66%)
  starting transfers between devices  76.6 us (14%)
  waiting for transfers between devices  69.2 us (13%)
  local copies, waits for them, and re-layouts  20.4 us (4%)
  other arithmetic  11.7 us (2%)
    ppermute x68, starting transfers between devices, permute(): return lax.ppermute(value, AXES, pairs)  76 us
    ppermute x68, waiting for transfers between devices, permute(): return lax.ppermute(value, AXES, pairs)  69.2 us
    pallas_call x1, Pallas kernels, mlp_down(): pl.pallas_call(partial(mlp_down_kernel, geo, region, shared, steps, skip)...  47.2 us
    pallas_call x1, Pallas kernels, mlp_up(): pl.pallas_call(partial(mlp_up_kernel, geo, region, shared, steps, skip),...  32.6 us
    pallas_call x4, Pallas kernels, unpack(): pl.pallas_call(partial(unpack_kernel, geo, region, 64 if region.cols <= 8...  32.5 us
    pallas_call x2, Pallas kernels, attention_back(): pl.pallas_call(partial(attention_back_kernel, before is not None), grid=(...  31.1 us
    pallas_call x2, Pallas kernels, pack(): pl.pallas_call(partial(pack_kernel, geo, region, shared, steps, skip), gr...  22.2 us
    pallas_call x4, Pallas kernels, permute_in(): pl.pallas_call(permute_in_kernel, grid=(stop - start,), out_shape=jax.Sha...  20.7 us
  transfers between devices with their start and end apart: 69, of which 21 were waited for; matrix products, arithmetic and copies ran while one was open for 5% of the time, Pallas kernels for 57%

profile of v6, /device:TPU:0, one launch (start us, length us, event | category | flops | bytes accessed | tf_op | source)
XLA Modules:
  0.0 539.1 jit_solution(14359698635691768015)
XLA Ops:
  11.1 7.0 %collective-permute-start.2 = (bf16[792,128]{1,0:T(8,128)(2,1)S(1)}, bf16[792,128]{1,0:T(8,128)(2,1)S(1)}, u32[]{:S(2)}, u32[]{:S(2)}) collective-permute-start(bf16[792,128]{1,0:T(8,128)(2,1)S(1)} %get-tuple-element.319), channel_id=1, source_target_pairs={{0,16},{1,17},{2,18},{3,19},{4,20},{5,21},{6,22},{7,23},{8,24},{9,... | collective-permute-start | bytes 608264 | tf_op jit(solution)/shard_map/ppermute | solution.py:133
  19.0 6.6 %collective-permute-done.2 = bf16[792,128]{1,0:T(8,128)(2,1)S(1)} collective-permute-done((bf16[792,128]{1,0:T(8,128)(2,1)S(1)}, bf16[792,128]{1,0:T(8,128)(2,1)S(1)}, u32[]{:S(2)}, u32[]{:S(2)}) %collective-permute-start.2) | collective-permute-done | bytes 202784 | tf_op jit(solution)/shard_map/ppermute | solution.py:133
  37.1 5.9 %collective-permute-done.5.refs_2_ = bf16[1,792,128]{2,1,0:T(8,128)(2,1)S(1)} collective-permute-done((bf16[1,792,128]{2,1,0:T(8,128)(2,1)S(1)}, bf16[1,792,128]{2,1,0:T(8,128)(2,1)S(1)}, u32[]{:S(2)}, u32[]{:S(2)}) %collective-permute-start.5) | collective-permute-done | bytes 202784 | tf_op jit(solution)/shard_map/ppermute | solution.py:133
  59.6 5.3 collective-permute-done.7.refs_1_
  79.0 13.0 %collective-permute-done.8.refs_1_ = bf16[8,792,128]{2,1,0:T(8,128)(2,1)S(1)} collective-permute-done((bf16[8,792,128]{2,1,0:T(8,128)(2,1)}, bf16[8,792,128]{2,1,0:T(8,128)(2,1)S(1)}, u32[]{:S(2)}, u32[]{:S(2)}) %collective-permute-start.8) | collective-permute-done | bytes 1622048 | tf_op jit(solution)/shard_map/ppermute | solution.py:133
  108.8 7.9 %unpack_weights.4 = (bf16[1024,3072]{1,0:T(8,128)(2,1)}, f32[8,128]{1,0:T(8,128)}, f32[8,128]{1,0:T(8,128)}, f32[24,128]{1,0:T(8,128)}, f32[91,128]{1,0:T(8,128)}) custom-call(s32[5]{0:T(128)} %stack.48.me_ref, bf16[8,792,128]{2,1,0:T(8,128)(2,1)} %join.9.refs_0_, bf16[8,792,128]{2,1,0:T(8,128)(2,1)} %copy-done.5, ...), custom_call_target="tpu_custom_call" | custom-call | bytes 5033164800 | tf_op jit(solution)/shard_map/unpack_weights/pallas_call | solution.py:379
  129.5 7.7 %score_bias.1.bias_ref = f32[32,104,128]{2,1,0:T(8,128)} custom-call(s32[104,128]{1,0:T(8,128)} %pad.22.ids_ref, bf16[32,368]{1,0:T(8,128)(2,1)} %pad.23.table_ref), custom_call_target="tpu_custom_call" | custom-call | flops 65431142400 | bytes 340787200 | tf_op jit(solution)/shard_map/score_bias/pallas_call | solution.py:1103
  138.6 13.0 %mix_rows.1 = (bf16[832,1024]{1,0:T(8,128)(2,1)}, bf16[832,3072]{1,0:T(8,128)(2,1)}) custom-call(bf16[832,1024]{1,0:T(8,128)(2,1)} %window_order.5.x_ref, f32[1,1024]{1,0:T(1,128)} %bitcast.79, f32[1,1024]{1,0:T(1,128)} %bitcast.83, bf16[1024,3072]{1,0:T(8,128)(2,1)} %get-tuple-element.173.w_ref, f32[1,3072]{1,0:T(1,128)} %bitcast.78), custom_call_target="tpu_custom_call" | custom-call | flops 1046898278400 | bytes 2621440000 | tf_op jit(solution)/shard_map/mix_rows/pallas_call | solution.py:1067
  159.9 12.2 %attention.1 = (bf16[832,1024]{1,0:T(8,128)(2,1)}, f32[8,32,128]{2,1,0:T(8,128)}) custom-call(bf16[832,3072]{1,0:T(8,128)(2,1)} %get-tuple-element.192.q_ref.k_ref.v_ref, bf16[832,3072]{1,0:T(8,128)(2,1)} %get-tuple-element.192.q_ref.k_ref.v_ref, bf16[832,3072]{1,0:T(8,128)(2,1)} %get-tuple-element.192.q_ref.k_ref.v_ref, f32[32,104,128]{2,1,0:T(8,128)} %score_bias.1.bias_ref), custom_call_target="tpu_custom_call" | custom-call | flops 2399999885312 | bytes 1363148800 | tf_op jit(solution)/shard_map/attention/pallas_call | solution.py:1194
  188.1 6.8 %middle_rows.1 = (f32[832,1024]{1,0:T(8,128)}, bf16[832,1024]{1,0:T(8,128)(2,1)}) custom-call(bf16[832,1024]{1,0:T(8,128)(2,1)} %window_order.5.x_ref, bf16[832,1024]{1,0:T(8,128)(2,1)} %get-tuple-element.199.a_ref, bf16[1024,1024]{1,0:T(8,128)(2,1)} %get-tuple-element.196.w_ref, f32[1,1024]{1,0:T(1,128)} %bitcast.85, f32[1,1024]{1,0:T(1,128)} %bitcast.81, ...), custom_call_target="tpu_custom_call" | custom-call | flops 348966092800 | bytes 1703936000 | tf_op jit(solution)/shard_map/middle_rows/pallas_call | solution.py:1310
  194.8 10.0 %unpack_weights.6 = (bf16[1024,4096]{1,0:T(8,128)(2,1)}, f32[32,128]{1,0:T(8,128)}) custom-call(s32[5]{0:T(128)} %stack.48.me_ref, bf16[8,792,128]{2,1,0:T(8,128)(2,1)} %join.11.refs_0_, bf16[8,792,128]{2,1,0:T(8,128)(2,1)} %collective-permute-done.22.refs_1_, bf16[8,792,128]{2,1,0:T(8,128)(2,1)} %collective-permute-done.24.refs_2_, ...), custom_call_target="tpu_custom_call" | custom-call | bytes 6710886400 | tf_op jit(solution)/shard_map/unpack_weights/pallas_call | solution.py:379
  208.8 32.6 %mlp_up.1 = (bf16[832,4096]{1,0:T(8,128)(2,1)}, f32[832,4096]{1,0:T(8,128)}, bf16[16,792,128]{2,1,0:T(8,128)(2,1)}, bf16[16,792,128]{2,1,0:T(8,128)(2,1)}, bf16[...) custom-call(s32[5]{0:T(128)} %stack.48.me_ref, bf16[832,1024]{1,0:T(8,128)(2,1)} %get-tuple-element.207.s_ref.refs_2_, ...), custom_call_target="tpu_custom_call" | custom-call | flops 2791728742400 | bytes 7444889600 | tf_op jit(solution)/shard_map/mlp_up/pallas_call | solution.py:1378
  252.3 9.6 %unpack_weights.7 = (bf16[4096,1024]{1,0:T(8,128)(2,1)}, f32[8,128]{1,0:T(8,128)}) custom-call(s32[5]{0:T(128)} %stack.48.me_ref, bf16[8,792,128]{2,1,0:T(8,128)(2,1)} %join.13.refs_4_.refs_0_, bf16[8,792,128]{2,1,0:T(8,128)(2,1)} %collective-permute-done.26.refs_5_.refs_1_, bf16[8,792,128]{2,1,0:T(8,128)(2,1)} %collective-permute-done.28.refs_6_.refs_2_, ...), custom_call_target="tpu_custom_call" | custom-call | bytes 6710886400 | tf_op jit(solution)/shard_map/unpack_weights/pallas_call | solution.py:379
  265.7 47.2 %mlp_down.1 = (bf16[832,1024]{1,0:T(8,128)(2,1)}, f32[832,1024]{1,0:T(8,128)}, bf16[16,792,128]{2,1,0:T(8,128)(2,1)}, bf16[16,792,128]{2,1,0:T(8,128)(2,1)}, bf1...) custom-call(s32[5]{0:T(128)} %stack.48.me_ref, ...), custom_call_target="tpu_custom_call", output_to_operand_aliasing={{4}: (9, {}), {5}: (10, {})} | custom-call | flops 5583457484800 | bytes 9122611200 | tf_op jit(solution)/shard_map/mlp_down/pallas_call | solution.py:1453
  318.6 9.0 %middle_back.1 = (f32[832,1024]{1,0:T(8,128)}, bf16[832,1024]{1,0:T(8,128)(2,1)}, bf16[832,1024]{1,0:T(8,128)(2,1)}, f32[8,1024]{1,0:T(8,128)}) custom-call(f32[832,1024]{1,0:T(8,128)} %get-tuple-element.226.s_ref, f32[832,1024]{1,0:T(8,128)} %get-tuple-element.217.refs_6_.m_ref, bf16[832,1024]{1,0:T(8,128)(2,1)} %window_order.7.g_ref.refs_3_, ...), custom_call_target="tpu_custom_call" | custom-call | flops 348966092800 | bytes 3067084800 | tf_op jit(solution)/shard_map/middle_back/pallas_call | solution.py:1498
  341.8 7.3 %weight_grad_pack.2 = (bf16[16,792,128]{2,1,0:T(8,128)(2,1)}, bf16[16,792,128]{2,1,0:T(8,128)(2,1)}) custom-call(s32[5]{0:T(128)} %stack.48.me_ref, bf16[832,1024]{1,0:T(8,128)(2,1)} %get-tuple-element.199.a_ref, bf16[832,1024]{1,0:T(8,128)(2,1)} %get-tuple-element.235.b_ref, f32[8,128]{1,0:T(8,128)} %bitcast.72, ...), custom_call_target="tpu_custom_call", output_to_operand_aliasing={{0}: (6, {}), {1}: (7, {})} | custom-call | flops 348966092800 | bytes 419430400 | tf_op jit(solution)/shard_map/weight_grad_pack/pallas_call | solution.py:621
  349.2 15.3 %attention_back.2 = (bf16[832,3072]{1,0:T(8,128)(2,1)}, f32[32,104,128]{2,1,0:T(8,128)}, f32[8,3072]{1,0:T(8,128)}) custom-call(bf16[832,3072]{1,0:T(8,128)(2,1)} %get-tuple-element.192.q_ref.k_ref.v_ref, bf16[832,3072]{1,0:T(8,128)(2,1)} %get-tuple-element.192.q_ref.k_ref.v_ref, bf16[832,3072]{1,0:T(8,128)(2,1)} %get-tuple-element.192.q_ref.k_ref.v_ref, ...), custom_call_target="tpu_custom_call" | custom-call | flops 2399999885312 | bytes 1363148800 | tf_op jit(solution)/shard_map/attention_back/pallas_call | solution.py:1279
  375.9 15.8 %attention_back.3 = (bf16[832,3072]{1,0:T(8,128)(2,1)}, f32[32,104,128]{2,1,0:T(8,128)}, f32[8,3072]{1,0:T(8,128)}) custom-call(bf16[832,3072]{1,0:T(8,128)(2,1)} %get-tuple-element.192.q_ref.k_ref.v_ref, bf16[832,3072]{1,0:T(8,128)(2,1)} %get-tuple-element.192.q_ref.k_ref.v_ref, ...), custom_call_target="tpu_custom_call", output_to_operand_aliasing={{0}: (8, {})} | custom-call | flops 2399999885312 | bytes 1363148800 | tf_op jit(solution)/shard_map/attention_back/pallas_call | solution.py:1279
  404.9 14.9 %weight_grad_pack.3 = (bf16[16,792,128]{2,1,0:T(8,128)(2,1)}, bf16[16,792,128]{2,1,0:T(8,128)(2,1)}) custom-call(s32[5]{0:T(128)} %stack.48.me_ref, bf16[832,1024]{1,0:T(8,128)(2,1)} %get-tuple-element.222.a_ref, bf16[832,3072]{1,0:T(8,128)(2,1)} %get-tuple-element.277.b_ref.mixed_ref), custom_call_target="tpu_custom_call" | custom-call | flops 1046898278400 | bytes 1258291200 | tf_op jit(solution)/shard_map/weight_grad_pack/pallas_call | solution.py:621
  419.9 5.8 %arrival_order.2 = bf16[800,1024]{1,0:T(8,128)(2,1)} custom-call(s32[1,832]{1,0:T(1,128)} %broadcast_in_dim_reshape.7.rows_ref, bf16[832,1024]{1,0:T(8,128)(2,1)} %get-tuple-element.265.x_ref), custom_call_target="tpu_custom_call" | custom-call | flops 272629760000 | bytes 681574400 | tf_op jit(solution)/shard_map/arrival_order/pallas_call | solution.py:1015
  435.7 14.4 %first_back.1 = (bf16[832,1024]{1,0:T(8,128)(2,1)}, f32[8,1024]{1,0:T(8,128)}) custom-call(bf16[832,3072]{1,0:T(8,128)(2,1)} %get-tuple-element.277.b_ref.mixed_ref, bf16[1024,3072]{1,0:T(8,128)(2,1)} %get-tuple-element.173.w_ref, bf16[832,1024]{1,0:T(8,128)(2,1)} %window_order.5.x_ref, f32[832,1024]{1,0:T(8,128)} %get-tuple-element.278.mg_ref, ...), custom_call_target="tpu_custom_call" | custom-call | flops 1046898278400 | bytes 3643801600 | tf_op jit(solution)/shard_map/first_back/pallas_call | solution.py:1550
  459.1 9.5 %score_bias_back.1 = f32[368,96]{1,0:T(8,128)} custom-call(s32[104,128]{1,0:T(8,128)} %pad.22.ids_ref, f32[32,104,128]{2,1,0:T(8,128)} %get-tuple-element.283.sums_ref), custom_call_target="tpu_custom_call" | custom-call | flops 196293427200 | bytes 340787200 | tf_op jit(solution)/shard_map/score_bias_back/pallas_call | solution.py:1141
  482.0 5.8 %arrival_order.3 = bf16[800,1024]{1,0:T(8,128)(2,1)} custom-call(s32[1,832]{1,0:T(1,128)} %broadcast_in_dim_reshape.7.rows_ref, bf16[832,1024]{1,0:T(8,128)(2,1)} %get-tuple-element.286.x_ref), custom_call_target="tpu_custom_call" | custom-call | flops 272629760000 | bytes 681574400 | tf_op jit(solution)/shard_map/arrival_order/pallas_call | solution.py:1015
  524.8 9.1 %moments_update.1 = (f32[3081,128]{1,0:T(8,128)}, f32[3081,128]{1,0:T(8,128)}, f32[3081,128]{1,0:T(8,128)}) custom-call(s32[5]{0:T(128)} %stack.48.me_ref, f32[4]{0:T(128)} %pad_maximum_fusion.1.coef_ref, f32[792,128]{1,0:T(8,128)} %select_bitcast_fusion.refs_0_, bf16[792,128]{1,0:T(8,128)(2,1)} %copy-done.9, ...), custom_call_target="tpu_custom_call" | custom-call | tf_op jit(solution)/shard_map/moments_update/pallas_call | solution.py:946
  (286 shorter events, 244.7 us)
Async XLA Ops:
  46.6 45.4 %collective-permute-start.11 = (bf16[1,792,128]{2,1,0:T(8,128)(2,1)}, bf16[1,792,128]{2,1,0:T(8,128)(2,1)}, u32[]{:S(2)}, u32[]{:S(2)}) collective-permute-start(bf16[1,792,128]{2,1,0:T(8,128)(2,1)} %get-tuple-element.169.refs_0_), channel_id=1, source_target_pairs={{0,2},{1,3},{2,0},{3,1},{4,6},{5,7},{6,4},{7,5},{8,10},{9,11},{10,... | collective-permute-start | bytes 608264 | tf_op jit(solution)/shard_map/ppermute | solution.py:133
  48.6 43.3 %collective-permute-start.12 = (bf16[1,792,128]{2,1,0:T(8,128)(2,1)}, bf16[1,792,128]{2,1,0:T(8,128)(2,1)}, u32[]{:S(2)}, u32[]{:S(2)}) collective-permute-start(bf16[1,792,128]{2,1,0:T(8,128)(2,1)} %get-tuple-element.169.refs_0_), channel_id=1, source_target_pairs={{0,4},{1,5},{2,6},{3,7},{4,0},{5,1},{6,2},{7,3},{8,12},{9,13},{10,... | collective-permute-start | bytes 608264 | tf_op jit(solution)/shard_map/ppermute | solution.py:133
  49.6 42.4 %collective-permute-start.13 = (bf16[1,792,128]{2,1,0:T(8,128)(2,1)}, bf16[1,792,128]{2,1,0:T(8,128)(2,1)}, u32[]{:S(2)}, u32[]{:S(2)}) collective-permute-start(bf16[1,792,128]{2,1,0:T(8,128)(2,1)} %get-tuple-element.169.refs_0_), channel_id=1, source_target_pairs={{0,6},{1,7},{2,4},{3,5},{4,2},{5,3},{6,0},{7,1},{8,14},{9,15},{10,... | collective-permute-start | bytes 608264 | tf_op jit(solution)/shard_map/ppermute | solution.py:133
  72.8 26.3 %collective-permute-start.9 = (bf16[8,792,128]{2,1,0:T(8,128)(2,1)}, bf16[8,792,128]{2,1,0:T(8,128)(2,1)}, u32[]{:S(2)}, u32[]{:S(2)}) collective-permute-start(bf16[8,792,128]{2,1,0:T(8,128)(2,1)} %join.9.refs_0_), channel_id=1, source_target_pairs={{0,8},{1,9},{2,10},{3,11},{4,12},{5,13},{6,14},{7,15},{8,0},{9,1},... | collective-permute-start | bytes 4866056 | tf_op jit(solution)/shard_map/ppermute | solution.py:133
  119.6 32.0 %collective-permute-start.19 = (bf16[1,792,128]{2,1,0:T(8,128)(2,1)}, bf16[1,792,128]{2,1,0:T(8,128)(2,1)}, u32[]{:S(2)}, u32[]{:S(2)}) collective-permute-start(bf16[1,792,128]{2,1,0:T(8,128)(2,1)} %get-tuple-element.187.refs_0_), channel_id=1, source_target_pairs={{0,2},{1,3},{2,0},{3,1},{4,6},{5,7},{6,4},{7,5},{8,10},{9,11},{10,... | collective-permute-start | bytes 608264 | tf_op jit(solution)/shard_map/ppermute | solution.py:133
  119.7 31.9 %collective-permute-start.20 = (bf16[1,792,128]{2,1,0:T(8,128)(2,1)}, bf16[1,792,128]{2,1,0:T(8,128)(2,1)}, u32[]{:S(2)}, u32[]{:S(2)}) collective-permute-start(bf16[1,792,128]{2,1,0:T(8,128)(2,1)} %get-tuple-element.187.refs_0_), channel_id=1, source_target_pairs={{0,4},{1,5},{2,6},{3,7},{4,0},{5,1},{6,2},{7,3},{8,12},{9,13},{10,... | collective-permute-start | bytes 608264 | tf_op jit(solution)/shard_map/ppermute | solution.py:133
  122.5 29.1 %collective-permute-start.21 = (bf16[1,792,128]{2,1,0:T(8,128)(2,1)}, bf16[1,792,128]{2,1,0:T(8,128)(2,1)}, u32[]{:S(2)}, u32[]{:S(2)}) collective-permute-start(bf16[1,792,128]{2,1,0:T(8,128)(2,1)} %get-tuple-element.187.refs_0_), channel_id=1, source_target_pairs={{0,6},{1,7},{2,4},{3,5},{4,2},{5,3},{6,0},{7,1},{8,14},{9,15},{10,... | collective-permute-start | bytes 608264 | tf_op jit(solution)/shard_map/ppermute | solution.py:133
  126.7 33.1 %collective-permute-start.22 = (bf16[8,792,128]{2,1,0:T(8,128)(2,1)}, bf16[8,792,128]{2,1,0:T(8,128)(2,1)}, u32[]{:S(2)}, u32[]{:S(2)}) collective-permute-start(bf16[8,792,128]{2,1,0:T(8,128)(2,1)} %join.11.refs_0_), channel_id=1, source_target_pairs={{0,1},{1,0},{2,3},{3,2},{4,5},{5,4},{6,7},{7,6},{8,24},{9,25},{10,... | collective-permute-start | bytes 4866056 | tf_op jit(solution)/shard_map/ppermute | solution.py:133
  157.6 29.9 %collective-permute-start.26 = (bf16[8,792,128]{2,1,0:T(8,128)(2,1)}, bf16[8,792,128]{2,1,0:T(8,128)(2,1)}, u32[]{:S(2)}, u32[]{:S(2)}) collective-permute-start(bf16[8,792,128]{2,1,0:T(8,128)(2,1)} %join.13.refs_4_.refs_0_), channel_id=1, source_target_pairs={{0,1},{1,0},{2,3},{3,2},{4,5},{5,4},{6,7},{7,6},{8,24},{9,25},{10,... | collective-permute-start | bytes 4866056 | tf_op jit(solution)/shard_map/ppermute | solution.py:133
  157.9 36.9 %collective-permute-start.28 = (bf16[8,792,128]{2,1,0:T(8,128)(2,1)}, bf16[8,792,128]{2,1,0:T(8,128)(2,1)}, u32[]{:S(2)}, u32[]{:S(2)}) collective-permute-start(bf16[8,792,128]{2,1,0:T(8,128)(2,1)} %join.13.refs_4_.refs_0_), channel_id=1, source_target_pairs={{0,8},{1,9},{2,10},{3,11},{4,12},{5,13},{6,14},{7,15},{8,0},{9,1},... | collective-permute-start | bytes 4866056 | tf_op jit(solution)/shard_map/ppermute | solution.py:133
  265.4 47.8 %collective-permute-start.33 = (bf16[8,792,128]{2,1,0:T(8,128)(2,1)}, bf16[8,792,128]{2,1,0:T(8,128)(2,1)}, u32[]{:S(2)}, u32[]{:S(2)}) collective-permute-start(bf16[8,792,128]{2,1,0:T(8,128)(2,1)} %add_terms.16), channel_id=1, source_target_pairs={{0,1},{1,0},{2,3},{3,2},{4,5},{5,4},{6,7},{7,6},{8,24},{9,25},{10,... | collective-permute-start | bytes 4866056 | tf_op jit(solution)/shard_map/ppermute | solution.py:133
  312.9 23.9 %collective-permute-start.35 = (bf16[16,792,128]{2,1,0:T(8,128)(2,1)}, bf16[16,792,128]{2,1,0:T(8,128)(2,1)}, u32[]{:S(2)}, u32[]{:S(2)}) collective-permute-start(bf16[16,792,128]{2,1,0:T(8,128)(2,1)} %get-tuple-element.233), channel_id=1, source_target_pairs={{0,8},{1,9},{2,10},{3,11},{4,12},{5,13},{6,14},{7,15},{8,0},{9,1},... | collective-permute-start | bytes 9732104 | tf_op jit(solution)/shard_map/ppermute | solution.py:133
  332.4 32.1 %collective-permute-start.38 = (bf16[1,792,128]{2,1,0:T(8,128)(2,1)}, bf16[1,792,128]{2,1,0:T(8,128)(2,1)}, u32[]{:S(2)}, u32[]{:S(2)}) collective-permute-start(bf16[1,792,128]{2,1,0:T(8,128)(2,1)} %get-tuple-element.247), channel_id=1, source_target_pairs={{0,2},{1,3},{2,0},{3,1},{4,6},{5,7},{6,4},{7,5},{8,10},{9,11},{10,... | collective-permute-start | bytes 608264 | tf_op jit(solution)/shard_map/ppermute | solution.py:133
  332.4 32.1 %collective-permute-start.39 = (bf16[1,792,128]{2,1,0:T(8,128)(2,1)}, bf16[1,792,128]{2,1,0:T(8,128)(2,1)}, u32[]{:S(2)}, u32[]{:S(2)}) collective-permute-start(bf16[1,792,128]{2,1,0:T(8,128)(2,1)} %get-tuple-element.249), channel_id=1, source_target_pairs={{0,4},{1,5},{2,6},{3,7},{4,0},{5,1},{6,2},{7,3},{8,12},{9,13},{10,... | collective-permute-start | bytes 608264 | tf_op jit(solution)/shard_map/ppermute | solution.py:133
  335.3 29.2 %collective-permute-start.40 = (bf16[1,792,128]{2,1,0:T(8,128)(2,1)}, bf16[1,792,128]{2,1,0:T(8,128)(2,1)}, u32[]{:S(2)}, u32[]{:S(2)}) collective-permute-start(bf16[1,792,128]{2,1,0:T(8,128)(2,1)} %get-tuple-element.251), channel_id=1, source_target_pairs={{0,6},{1,7},{2,4},{3,5},{4,2},{5,3},{6,0},{7,1},{8,14},{9,15},{10,... | collective-permute-start | bytes 608264 | tf_op jit(solution)/shard_map/ppermute | solution.py:133
  340.3 26.3 %collective-permute-start.36 = (bf16[8,792,128]{2,1,0:T(8,128)(2,1)}, bf16[8,792,128]{2,1,0:T(8,128)(2,1)}, u32[]{:S(2)}, u32[]{:S(2)}) collective-permute-start(bf16[8,792,128]{2,1,0:T(8,128)(2,1)} %add_terms.19), channel_id=1, source_target_pairs={{0,1},{1,0},{2,3},{3,2},{4,5},{5,4},{6,7},{7,6},{8,24},{9,25},{10,... | collective-permute-start | bytes 4866056 | tf_op jit(solution)/shard_map/ppermute | solution.py:133
  374.7 25.4 %collective-permute-start.42 = (bf16[8,792,128]{2,1,0:T(8,128)(2,1)}, bf16[8,792,128]{2,1,0:T(8,128)(2,1)}, u32[]{:S(2)}, u32[]{:S(2)}) collective-permute-start(bf16[8,792,128]{2,1,0:T(8,128)(2,1)} %add_terms.21), channel_id=1, source_target_pairs={{0,1},{1,0},{2,3},{3,2},{4,5},{5,4},{6,7},{7,6},{8,24},{9,25},{10,... | collective-permute-start | bytes 4866056 | tf_op jit(solution)/shard_map/ppermute | solution.py:133
  394.3 36.8 %collective-permute-start.45 = (bf16[1,792,128]{2,1,0:T(8,128)(2,1)}, bf16[1,792,128]{2,1,0:T(8,128)(2,1)}, u32[]{:S(2)}, u32[]{:S(2)}) collective-permute-start(bf16[1,792,128]{2,1,0:T(8,128)(2,1)} %get-tuple-element.271), channel_id=1, source_target_pairs={{0,2},{1,3},{2,0},{3,1},{4,6},{5,7},{6,4},{7,5},{8,10},{9,11},{10,... | collective-permute-start | bytes 608264 | tf_op jit(solution)/shard_map/ppermute | solution.py:133
  394.3 36.8 %collective-permute-start.46 = (bf16[1,792,128]{2,1,0:T(8,128)(2,1)}, bf16[1,792,128]{2,1,0:T(8,128)(2,1)}, u32[]{:S(2)}, u32[]{:S(2)}) collective-permute-start(bf16[1,792,128]{2,1,0:T(8,128)(2,1)} %get-tuple-element.273), channel_id=1, source_target_pairs={{0,4},{1,5},{2,6},{3,7},{4,0},{5,1},{6,2},{7,3},{8,12},{9,13},{10,... | collective-permute-start | bytes 608264 | tf_op jit(solution)/shard_map/ppermute | solution.py:133
  397.1 33.9 %collective-permute-start.47 = (bf16[1,792,128]{2,1,0:T(8,128)(2,1)}, bf16[1,792,128]{2,1,0:T(8,128)(2,1)}, u32[]{:S(2)}, u32[]{:S(2)}) collective-permute-start(bf16[1,792,128]{2,1,0:T(8,128)(2,1)} %get-tuple-element.275), channel_id=1, source_target_pairs={{0,6},{1,7},{2,4},{3,5},{4,2},{5,3},{6,0},{7,1},{8,14},{9,15},{10,... | collective-permute-start | bytes 608264 | tf_op jit(solution)/shard_map/ppermute | solution.py:133
  404.2 26.8 %collective-permute-start.44 = (bf16[4,792,128]{2,1,0:T(8,128)(2,1)}, bf16[4,792,128]{2,1,0:T(8,128)(2,1)}, u32[]{:S(2)}, u32[]{:S(2)}) collective-permute-start(bf16[4,792,128]{2,1,0:T(8,128)(2,1)} %get-tuple-element.262), channel_id=1, source_target_pairs={{0,16},{1,17},{2,18},{3,19},{4,20},{5,21},{6,22},{7,23},{8,9},{9,8... | collective-permute-start | bytes 2433032 | tf_op jit(solution)/shard_map/ppermute | solution.py:133
  429.4 24.9 %collective-permute-start.48 = (bf16[8,792,128]{2,1,0:T(8,128)(2,1)}, bf16[8,792,128]{2,1,0:T(8,128)(2,1)}, u32[]{:S(2)}, u32[]{:S(2)}) collective-permute-start(bf16[8,792,128]{2,1,0:T(8,128)(2,1)} %add_terms.25), channel_id=1, source_target_pairs={{0,1},{1,0},{2,3},{3,2},{4,5},{5,4},{6,7},{7,6},{8,24},{9,25},{10,... | collective-permute-start | bytes 4866056 | tf_op jit(solution)/shard_map/ppermute | solution.py:133
  451.5 28.1 %collective-permute-start.50 = (bf16[1,792,128]{2,1,0:T(8,128)(2,1)}, bf16[1,792,128]{2,1,0:T(8,128)(2,1)}, u32[]{:S(2)}, u32[]{:S(2)}) collective-permute-start(bf16[1,792,128]{2,1,0:T(8,128)(2,1)} %get-tuple-element.287), channel_id=1, source_target_pairs={{0,2},{1,3},{2,0},{3,1},{4,6},{5,7},{6,4},{7,5},{8,10},{9,11},{10,... | collective-permute-start | bytes 608264 | tf_op jit(solution)/shard_map/ppermute | solution.py:133
  451.5 29.7 %collective-permute-start.51 = (bf16[1,792,128]{2,1,0:T(8,128)(2,1)}, bf16[1,792,128]{2,1,0:T(8,128)(2,1)}, u32[]{:S(2)}, u32[]{:S(2)}) collective-permute-start(bf16[1,792,128]{2,1,0:T(8,128)(2,1)} %get-tuple-element.289), channel_id=1, source_target_pairs={{0,4},{1,5},{2,6},{3,7},{4,0},{5,1},{6,2},{7,3},{8,12},{9,13},{10,... | collective-permute-start | bytes 608264 | tf_op jit(solution)/shard_map/ppermute | solution.py:133
  (80 other events, 1050.2 us)

commit v7 on v6

--- a/solution.py
+++ b/solution.py
@@ -84,7 +84,7 @@
     return pltpu.CompilerParams(vmem_limit_bytes=VMEM_LIMIT, **more)
 
 
-COST_SCALE = 200
+COST_SCALE = 2000
 
 
 def cost(flops, bytes_accessed, transcendentals=0):
@@ -1799,7 +1799,7 @@
     squares = squares + square_sums(geo, me, REDUCE_PHASES[:1], [sums[0]])
     collected = collect_quarters(geo, [sums[group][0] for group in range(4)], dp_index)
     scale = 1.0 / jnp.sqrt(F32(arrivals * geo.devices))
-    squares = sum_everywhere(geo, jnp.sum(squares, axis=1)[None], 0, 3)
+    squares = sum_everywhere(geo, jnp.sum(squares, axis=1)[None], 0, 4)
     collected[0] = after(collected[0], squares)
     step_float = step_count.astype(F32)
     coef = jnp.stack(
@@ -1820,7 +1820,7 @@
         first_moment.reshape(geo.rows, LANES),
         second_moment.reshape(geo.rows, LANES),
     )
-    squares = sum_everywhere(geo, after(squares, params_new), 3)
+    squares = sum_everywhere(geo, after(squares, params_new), 4)
     tensor = lax.broadcasted_iota(jnp.int32, (LATE_ROWS, 16), 1)
     row = lax.broadcasted_iota(jnp.int32, (LATE_ROWS, 16), 0)
     inside = tensor < 0

time: 542 us -> 540 us (level)
  no operation moved by 1% of the time
where the time goes in v7:
time: 540 us; the launch traced here: 537 us
  Pallas kernels  358 us (66%)
  starting transfers between devices  76.8 us (14%)
  waiting for transfers between devices  69.7 us (13%)
  local copies, waits for them, and re-layouts  17 us (3%)
  other arithmetic  12.5 us (2%)
    ppermute x68, starting transfers between devices, permute(): return lax.ppermute(value, AXES, pairs)  76.1 us
    ppermute x68, waiting for transfers between devices, permute(): return lax.ppermute(value, AXES, pairs)  69.7 us
    pallas_call x1, Pallas kernels, mlp_down(): pl.pallas_call(partial(mlp_down_kernel, geo, region, shared, steps, skip)...  47.2 us
    pallas_call x1, Pallas kernels, mlp_up(): pl.pallas_call(partial(mlp_up_kernel, geo, region, shared, steps, skip),...  32.7 us
    pallas_call x4, Pallas kernels, unpack(): pl.pallas_call(partial(unpack_kernel, geo, region, 64 if region.cols <= 8...  32.5 us
    pallas_call x2, Pallas kernels, attention_back(): pl.pallas_call(partial(attention_back_kernel, before is not None), grid=(...  31.1 us
    pallas_call x2, Pallas kernels, pack(): pl.pallas_call(partial(pack_kernel, geo, region, shared, steps, skip), gr...  22.1 us
    pallas_call x4, Pallas kernels, permute_in(): pl.pallas_call(permute_in_kernel, grid=(stop - start,), out_shape=jax.Sha...  20.6 us
  transfers between devices with their start and end apart: 69, of which 21 were waited for; matrix products, arithmetic and copies ran while one was open for 5% of the time, Pallas kernels for 57%

profile of v7, /device:TPU:0, one launch (start us, length us, event | category | flops | bytes accessed | tf_op | source)
XLA Modules:
  0.0 536.9 jit_solution(7381558052147395899)
XLA Ops:
  11.1 6.9 %collective-permute-start.2 = (bf16[792,128]{1,0:T(8,128)(2,1)S(1)}, bf16[792,128]{1,0:T(8,128)(2,1)S(1)}, u32[]{:S(2)}, u32[]{:S(2)}) collective-permute-start(bf16[792,128]{1,0:T(8,128)(2,1)S(1)} %get-tuple-element.319), channel_id=1, source_target_pairs={{0,16},{1,17},{2,18},{3,19},{4,20},{5,21},{6,22},{7,23},{8,24},{9,... | collective-permute-start | bytes 608264 | tf_op jit(solution)/shard_map/ppermute | solution.py:133
  19.0 6.6 %collective-permute-done.2 = bf16[792,128]{1,0:T(8,128)(2,1)S(1)} collective-permute-done((bf16[792,128]{1,0:T(8,128)(2,1)S(1)}, bf16[792,128]{1,0:T(8,128)(2,1)S(1)}, u32[]{:S(2)}, u32[]{:S(2)}) %collective-permute-start.2) | collective-permute-done | bytes 202784 | tf_op jit(solution)/shard_map/ppermute | solution.py:133
  37.1 6.2 %collective-permute-done.5.refs_2_ = bf16[1,792,128]{2,1,0:T(8,128)(2,1)} collective-permute-done((bf16[1,792,128]{2,1,0:T(8,128)(2,1)}, bf16[1,792,128]{2,1,0:T(8,128)(2,1)}, u32[]{:S(2)}, u32[]{:S(2)}) %collective-permute-start.5) | collective-permute-done | bytes 202784 | tf_op jit(solution)/shard_map/ppermute | solution.py:133
  59.2 5.4 %collective-permute-done.7.refs_1_ = bf16[4,792,128]{2,1,0:T(8,128)(2,1)} collective-permute-done((bf16[4,792,128]{2,1,0:T(8,128)(2,1)}, bf16[4,792,128]{2,1,0:T(8,128)(2,1)}, u32[]{:S(2)}, u32[]{:S(2)}) %collective-permute-start.7) | collective-permute-done | bytes 811040 | tf_op jit(solution)/shard_map/ppermute | solution.py:133
  77.8 13.1 %collective-permute-done.8.refs_1_ = bf16[8,792,128]{2,1,0:T(8,128)(2,1)} collective-permute-done((bf16[8,792,128]{2,1,0:T(8,128)(2,1)}, bf16[8,792,128]{2,1,0:T(8,128)(2,1)}, u32[]{:S(2)}, u32[]{:S(2)}) %collective-permute-start.8) | collective-permute-done | bytes 1622048 | tf_op jit(solution)/shard_map/ppermute | solution.py:133
  106.5 7.9 %unpack_weights.4 = (bf16[1024,3072]{1,0:T(8,128)(2,1)}, f32[8,128]{1,0:T(8,128)}, f32[8,128]{1,0:T(8,128)}, f32[24,128]{1,0:T(8,128)}, f32[91,128]{1,0:T(8,128)}) custom-call(s32[5]{0:T(128)} %stack.48.me_ref, bf16[8,792,128]{2,1,0:T(8,128)(2,1)} %join.9.refs_0_, bf16[8,792,128]{2,1,0:T(8,128)(2,1)} %collective-permute-done.8.refs_1_, ...), custom_call_target="tpu_custom_call" | custom-call | bytes 50331648000 | tf_op jit(solution)/shard_map/unpack_weights/pallas_call | solution.py:379
  126.6 7.8 %score_bias.1.bias_ref = f32[32,104,128]{2,1,0:T(8,128)} custom-call(s32[104,128]{1,0:T(8,128)} %pad.22.ids_ref, bf16[32,368]{1,0:T(8,128)(2,1)} %pad.23.table_ref), custom_call_target="tpu_custom_call" | custom-call | flops 654311424000 | bytes 3407872000 | tf_op jit(solution)/shard_map/score_bias/pallas_call | solution.py:1103
  135.8 13.1 %mix_rows.1 = (bf16[832,1024]{1,0:T(8,128)(2,1)}, bf16[832,3072]{1,0:T(8,128)(2,1)}) custom-call(bf16[832,1024]{1,0:T(8,128)(2,1)} %window_order.5.x_ref, f32[1,1024]{1,0:T(1,128)} %bitcast.79, f32[1,1024]{1,0:T(1,128)} %bitcast.83, bf16[1024,3072]{1,0:T(8,128)(2,1)} %get-tuple-element.173.w_ref, f32[1,3072]{1,0:T(1,128)} %bitcast.78), custom_call_target="tpu_custom_call" | custom-call | flops 10468982784000 | bytes 26214400000 | tf_op jit(solution)/shard_map/mix_rows/pallas_call | solution.py:1067
  157.5 12.2 %attention.1 = (bf16[832,1024]{1,0:T(8,128)(2,1)}, f32[8,32,128]{2,1,0:T(8,128)}) custom-call(bf16[832,3072]{1,0:T(8,128)(2,1)} %get-tuple-element.192.q_ref.k_ref.v_ref, bf16[832,3072]{1,0:T(8,128)(2,1)} %get-tuple-element.192.q_ref.k_ref.v_ref, bf16[832,3072]{1,0:T(8,128)(2,1)} %get-tuple-element.192.q_ref.k_ref.v_ref, f32[32,104,128]{2,1,0:T(8,128)} %score_bias.1.bias_ref), custom_call_target="tpu_custom_call" | custom-call | flops 24000000425984 | bytes 13631488000 | tf_op jit(solution)/shard_map/attention/pallas_call | solution.py:1194
  185.9 6.8 %middle_rows.1 = (f32[832,1024]{1,0:T(8,128)}, bf16[832,1024]{1,0:T(8,128)(2,1)}) custom-call(bf16[832,1024]{1,0:T(8,128)(2,1)} %window_order.5.x_ref, bf16[832,1024]{1,0:T(8,128)(2,1)} %get-tuple-element.199.a_ref, bf16[1024,1024]{1,0:T(8,128)(2,1)} %get-tuple-element.196.w_ref, f32[1,1024]{1,0:T(1,128)} %bitcast.85, f32[1,1024]{1,0:T(1,128)} %bitcast.81, ...), custom_call_target="tpu_custom_call" | custom-call | flops 3489660928000 | bytes 17039360000 | tf_op jit(solution)/shard_map/middle_rows/pallas_call | solution.py:1310
  192.6 10.0 %unpack_weights.6 = (bf16[1024,4096]{1,0:T(8,128)(2,1)}, f32[32,128]{1,0:T(8,128)}) custom-call(s32[5]{0:T(128)} %stack.48.me_ref, bf16[8,792,128]{2,1,0:T(8,128)(2,1)} %join.11.refs_0_, bf16[8,792,128]{2,1,0:T(8,128)(2,1)} %collective-permute-done.22.refs_1_, bf16[8,792,128]{2,1,0:T(8,128)(2,1)} %collective-permute-done.24.refs_2_, ...), custom_call_target="tpu_custom_call" | custom-call | bytes 67108864000 | tf_op jit(solution)/shard_map/unpack_weights/pallas_call | solution.py:379
  206.5 32.7 %mlp_up.1 = (bf16[832,4096]{1,0:T(8,128)(2,1)}, f32[832,4096]{1,0:T(8,128)}, bf16[16,792,128]{2,1,0:T(8,128)(2,1)}, bf16[16,792,128]{2,1,0:T(8,128)(2,1)}, bf16[...) custom-call(s32[5]{0:T(128)} %stack.48.me_ref, bf16[832,1024]{1,0:T(8,128)(2,1)} %get-tuple-element.207.s_ref.refs_2_, ...), custom_call_target="tpu_custom_call" | custom-call | flops 27917287424000 | bytes 74448896000 | tf_op jit(solution)/shard_map/mlp_up/pallas_call | solution.py:1378
  250.0 9.6 %unpack_weights.7 = (bf16[4096,1024]{1,0:T(8,128)(2,1)}, f32[8,128]{1,0:T(8,128)}) custom-call(s32[5]{0:T(128)} %stack.48.me_ref, bf16[8,792,128]{2,1,0:T(8,128)(2,1)} %join.13.refs_4_.refs_0_, bf16[8,792,128]{2,1,0:T(8,128)(2,1)} %collective-permute-done.26.refs_5_.refs_1_, bf16[8,792,128]{2,1,0:T(8,128)(2,1)} %collective-permute-done.28.refs_6_.refs_2_, ...), custom_call_target="tpu_custom_call" | custom-call | bytes 67108864000 | tf_op jit(solution)/shard_map/unpack_weights/pallas_call | solution.py:379
  263.7 47.2 %mlp_down.1 = (bf16[832,1024]{1,0:T(8,128)(2,1)}, f32[832,1024]{1,0:T(8,128)}, bf16[16,792,128]{2,1,0:T(8,128)(2,1)}, bf16[16,792,128]{2,1,0:T(8,128)(2,1)}, bf1...) custom-call(s32[5]{0:T(128)} %stack.48.me_ref, ...), custom_call_target="tpu_custom_call", output_to_operand_aliasing={{4}: (9, {}), {5}: (10, {})} | custom-call | flops 55834574848000 | bytes 91226112000 | tf_op jit(solution)/shard_map/mlp_down/pallas_call | solution.py:1453
  316.3 9.1 %middle_back.1 = (f32[832,1024]{1,0:T(8,128)}, bf16[832,1024]{1,0:T(8,128)(2,1)}, bf16[832,1024]{1,0:T(8,128)(2,1)}, f32[8,1024]{1,0:T(8,128)}) custom-call(f32[832,1024]{1,0:T(8,128)} %get-tuple-element.226.s_ref, f32[832,1024]{1,0:T(8,128)} %get-tuple-element.217.refs_6_.m_ref, bf16[832,1024]{1,0:T(8,128)(2,1)} %window_order.7.g_ref.refs_3_, ...), custom_call_target="tpu_custom_call" | custom-call | flops 3489660928000 | bytes 30670848000 | tf_op jit(solution)/shard_map/middle_back/pallas_call | solution.py:1498
  339.5 7.3 %weight_grad_pack.2 = (bf16[16,792,128]{2,1,0:T(8,128)(2,1)}, bf16[16,792,128]{2,1,0:T(8,128)(2,1)}) custom-call(s32[5]{0:T(128)} %stack.48.me_ref, bf16[832,1024]{1,0:T(8,128)(2,1)} %get-tuple-element.199.a_ref, bf16[832,1024]{1,0:T(8,128)(2,1)} %get-tuple-element.235.b_ref, f32[8,128]{1,0:T(8,128)} %bitcast.72, ...), custom_call_target="tpu_custom_call", output_to_operand_aliasing={{0}: (6, {}), {1}: (7, {})} | custom-call | flops 3489660928000 | bytes 4194304000 | tf_op jit(solution)/shard_map/weight_grad_pack/pallas_call | solution.py:621
  346.9 15.3 %attention_back.2 = (bf16[832,3072]{1,0:T(8,128)(2,1)}, f32[32,104,128]{2,1,0:T(8,128)}, f32[8,3072]{1,0:T(8,128)}) custom-call(bf16[832,3072]{1,0:T(8,128)(2,1)} %get-tuple-element.192.q_ref.k_ref.v_ref, bf16[832,3072]{1,0:T(8,128)(2,1)} %get-tuple-element.192.q_ref.k_ref.v_ref, bf16[832,3072]{1,0:T(8,128)(2,1)} %get-tuple-element.192.q_ref.k_ref.v_ref, ...), custom_call_target="tpu_custom_call" | custom-call | flops 24000000425984 | bytes 13631488000 | tf_op jit(solution)/shard_map/attention_back/pallas_call | solution.py:1279
  373.7 15.8 %attention_back.3 = (bf16[832,3072]{1,0:T(8,128)(2,1)}, f32[32,104,128]{2,1,0:T(8,128)}, f32[8,3072]{1,0:T(8,128)}) custom-call(bf16[832,3072]{1,0:T(8,128)(2,1)} %get-tuple-element.192.q_ref.k_ref.v_ref, bf16[832,3072]{1,0:T(8,128)(2,1)} %get-tuple-element.192.q_ref.k_ref.v_ref, ...), custom_call_target="tpu_custom_call", output_to_operand_aliasing={{0}: (8, {})} | custom-call | flops 24000000425984 | bytes 13631488000 | tf_op jit(solution)/shard_map/attention_back/pallas_call | solution.py:1279
  402.9 14.8 %weight_grad_pack.3 = (bf16[16,792,128]{2,1,0:T(8,128)(2,1)}, bf16[16,792,128]{2,1,0:T(8,128)(2,1)}) custom-call(s32[5]{0:T(128)} %stack.48.me_ref, bf16[832,1024]{1,0:T(8,128)(2,1)} %get-tuple-element.222.a_ref, bf16[832,3072]{1,0:T(8,128)(2,1)} %get-tuple-element.277.b_ref.mixed_ref), custom_call_target="tpu_custom_call" | custom-call | flops 10468982784000 | bytes 12582912000 | tf_op jit(solution)/shard_map/weight_grad_pack/pallas_call | solution.py:621
  417.8 5.8 %arrival_order.2 = bf16[800,1024]{1,0:T(8,128)(2,1)} custom-call(s32[1,832]{1,0:T(1,128)} %broadcast_in_dim_reshape.7.rows_ref, bf16[832,1024]{1,0:T(8,128)(2,1)} %get-tuple-element.265.x_ref), custom_call_target="tpu_custom_call" | custom-call | flops 2726297600000 | bytes 6815744000 | tf_op jit(solution)/shard_map/arrival_order/pallas_call | solution.py:1015
  433.4 14.6 %first_back.1 = (bf16[832,1024]{1,0:T(8,128)(2,1)}, f32[8,1024]{1,0:T(8,128)}) custom-call(bf16[832,3072]{1,0:T(8,128)(2,1)} %get-tuple-element.277.b_ref.mixed_ref, bf16[1024,3072]{1,0:T(8,128)(2,1)} %get-tuple-element.173.w_ref, bf16[832,1024]{1,0:T(8,128)(2,1)} %window_order.5.x_ref, f32[832,1024]{1,0:T(8,128)} %get-tuple-element.278.mg_ref, ...), custom_call_target="tpu_custom_call" | custom-call | flops 10468982784000 | bytes 36438016000 | tf_op jit(solution)/shard_map/first_back/pallas_call | solution.py:1550
  457.0 9.5 %score_bias_back.1 = f32[368,96]{1,0:T(8,128)} custom-call(s32[104,128]{1,0:T(8,128)} %pad.22.ids_ref, f32[32,104,128]{2,1,0:T(8,128)} %get-tuple-element.283.sums_ref), custom_call_target="tpu_custom_call" | custom-call | flops 1962934272000 | bytes 3407872000 | tf_op jit(solution)/shard_map/score_bias_back/pallas_call | solution.py:1141
  480.0 5.8 %arrival_order.3 = bf16[800,1024]{1,0:T(8,128)(2,1)} custom-call(s32[1,832]{1,0:T(1,128)} %broadcast_in_dim_reshape.7.rows_ref, bf16[832,1024]{1,0:T(8,128)(2,1)} %get-tuple-element.286.x_ref), custom_call_target="tpu_custom_call" | custom-call | flops 2726297600000 | bytes 6815744000 | tf_op jit(solution)/shard_map/arrival_order/pallas_call | solution.py:1015
  523.7 9.1 %moments_update.1 = (f32[3081,128]{1,0:T(8,128)}, f32[3081,128]{1,0:T(8,128)}, f32[3081,128]{1,0:T(8,128)}) custom-call(s32[5]{0:T(128)} %stack.48.me_ref, f32[4]{0:T(128)} %pad_maximum_fusion.1.coef_ref, f32[792,128]{1,0:T(8,128)} %select_bitcast_fusion.refs_0_, bf16[792,128]{1,0:T(8,128)(2,1)} %copy-done.5, ...), custom_call_target="tpu_custom_call" | custom-call | tf_op jit(solution)/shard_map/moments_update/pallas_call | solution.py:946
  (278 shorter events, 241.7 us)
Async XLA Ops:
  45.5 45.3 %collective-permute-start.11 = (bf16[1,792,128]{2,1,0:T(8,128)(2,1)}, bf16[1,792,128]{2,1,0:T(8,128)(2,1)}, u32[]{:S(2)}, u32[]{:S(2)}) collective-permute-start(bf16[1,792,128]{2,1,0:T(8,128)(2,1)} %get-tuple-element.169.refs_0_), channel_id=1, source_target_pairs={{0,2},{1,3},{2,0},{3,1},{4,6},{5,7},{6,4},{7,5},{8,10},{9,11},{10,... | collective-permute-start | bytes 608264 | tf_op jit(solution)/shard_map/ppermute | solution.py:133
  48.3 42.6 %collective-permute-start.12 = (bf16[1,792,128]{2,1,0:T(8,128)(2,1)}, bf16[1,792,128]{2,1,0:T(8,128)(2,1)}, u32[]{:S(2)}, u32[]{:S(2)}) collective-permute-start(bf16[1,792,128]{2,1,0:T(8,128)(2,1)} %get-tuple-element.169.refs_0_), channel_id=1, source_target_pairs={{0,4},{1,5},{2,6},{3,7},{4,0},{5,1},{6,2},{7,3},{8,12},{9,13},{10,... | collective-permute-start | bytes 608264 | tf_op jit(solution)/shard_map/ppermute | solution.py:133
  49.3 41.6 %collective-permute-start.13 = (bf16[1,792,128]{2,1,0:T(8,128)(2,1)}, bf16[1,792,128]{2,1,0:T(8,128)(2,1)}, u32[]{:S(2)}, u32[]{:S(2)}) collective-permute-start(bf16[1,792,128]{2,1,0:T(8,128)(2,1)} %get-tuple-element.169.refs_0_), channel_id=1, source_target_pairs={{0,6},{1,7},{2,4},{3,5},{4,2},{5,3},{6,0},{7,1},{8,14},{9,15},{10,... | collective-permute-start | bytes 608264 | tf_op jit(solution)/shard_map/ppermute | solution.py:133
  71.6 25.8 %collective-permute-start.9 = (bf16[8,792,128]{2,1,0:T(8,128)(2,1)}, bf16[8,792,128]{2,1,0:T(8,128)(2,1)}, u32[]{:S(2)}, u32[]{:S(2)}) collective-permute-start(bf16[8,792,128]{2,1,0:T(8,128)(2,1)} %join.9.refs_0_), channel_id=1, source_target_pairs={{0,8},{1,9},{2,10},{3,11},{4,12},{5,13},{6,14},{7,15},{8,0},{9,1},... | collective-permute-start | bytes 4866056 | tf_op jit(solution)/shard_map/ppermute | solution.py:133
  116.7 32.1 %collective-permute-start.19 = (bf16[1,792,128]{2,1,0:T(8,128)(2,1)}, bf16[1,792,128]{2,1,0:T(8,128)(2,1)}, u32[]{:S(2)}, u32[]{:S(2)}) collective-permute-start(bf16[1,792,128]{2,1,0:T(8,128)(2,1)} %get-tuple-element.187.refs_0_), channel_id=1, source_target_pairs={{0,2},{1,3},{2,0},{3,1},{4,6},{5,7},{6,4},{7,5},{8,10},{9,11},{10,... | collective-permute-start | bytes 608264 | tf_op jit(solution)/shard_map/ppermute | solution.py:133
  118.3 30.5 %collective-permute-start.20 = (bf16[1,792,128]{2,1,0:T(8,128)(2,1)}, bf16[1,792,128]{2,1,0:T(8,128)(2,1)}, u32[]{:S(2)}, u32[]{:S(2)}) collective-permute-start(bf16[1,792,128]{2,1,0:T(8,128)(2,1)} %get-tuple-element.187.refs_0_), channel_id=1, source_target_pairs={{0,4},{1,5},{2,6},{3,7},{4,0},{5,1},{6,2},{7,3},{8,12},{9,13},{10,... | collective-permute-start | bytes 608264 | tf_op jit(solution)/shard_map/ppermute | solution.py:133
  119.6 29.2 %collective-permute-start.21 = (bf16[1,792,128]{2,1,0:T(8,128)(2,1)}, bf16[1,792,128]{2,1,0:T(8,128)(2,1)}, u32[]{:S(2)}, u32[]{:S(2)}) collective-permute-start(bf16[1,792,128]{2,1,0:T(8,128)(2,1)} %get-tuple-element.187.refs_0_), channel_id=1, source_target_pairs={{0,6},{1,7},{2,4},{3,5},{4,2},{5,3},{6,0},{7,1},{8,14},{9,15},{10,... | collective-permute-start | bytes 608264 | tf_op jit(solution)/shard_map/ppermute | solution.py:133
  123.7 33.8 %collective-permute-start.22 = (bf16[8,792,128]{2,1,0:T(8,128)(2,1)}, bf16[8,792,128]{2,1,0:T(8,128)(2,1)}, u32[]{:S(2)}, u32[]{:S(2)}) collective-permute-start(bf16[8,792,128]{2,1,0:T(8,128)(2,1)} %join.11.refs_0_), channel_id=1, source_target_pairs={{0,1},{1,0},{2,3},{3,2},{4,5},{5,4},{6,7},{7,6},{8,24},{9,25},{10,... | collective-permute-start | bytes 4866056 | tf_op jit(solution)/shard_map/ppermute | solution.py:133
  155.3 29.9 %collective-permute-start.26 = (bf16[8,792,128]{2,1,0:T(8,128)(2,1)}, bf16[8,792,128]{2,1,0:T(8,128)(2,1)}, u32[]{:S(2)}, u32[]{:S(2)}) collective-permute-start(bf16[8,792,128]{2,1,0:T(8,128)(2,1)} %join.13.refs_4_.refs_0_), channel_id=1, source_target_pairs={{0,1},{1,0},{2,3},{3,2},{4,5},{5,4},{6,7},{7,6},{8,24},{9,25},{10,... | collective-permute-start | bytes 4866056 | tf_op jit(solution)/shard_map/ppermute | solution.py:133
  155.9 36.7 %collective-permute-start.28 = (bf16[8,792,128]{2,1,0:T(8,128)(2,1)}, bf16[8,792,128]{2,1,0:T(8,128)(2,1)}, u32[]{:S(2)}, u32[]{:S(2)}) collective-permute-start(bf16[8,792,128]{2,1,0:T(8,128)(2,1)} %join.13.refs_4_.refs_0_), channel_id=1, source_target_pairs={{0,8},{1,9},{2,10},{3,11},{4,12},{5,13},{6,14},{7,15},{8,0},{9,1},... | collective-permute-start | bytes 4866056 | tf_op jit(solution)/shard_map/ppermute | solution.py:133
  263.1 47.9 %collective-permute-start.33 = (bf16[8,792,128]{2,1,0:T(8,128)(2,1)}, bf16[8,792,128]{2,1,0:T(8,128)(2,1)}, u32[]{:S(2)}, u32[]{:S(2)}) collective-permute-start(bf16[8,792,128]{2,1,0:T(8,128)(2,1)} %add_terms.16), channel_id=1, source_target_pairs={{0,1},{1,0},{2,3},{3,2},{4,5},{5,4},{6,7},{7,6},{8,24},{9,25},{10,... | collective-permute-start | bytes 4866056 | tf_op jit(solution)/shard_map/ppermute | solution.py:133
  310.9 23.8 %collective-permute-start.35 = (bf16[16,792,128]{2,1,0:T(8,128)(2,1)}, bf16[16,792,128]{2,1,0:T(8,128)(2,1)}, u32[]{:S(2)}, u32[]{:S(2)}) collective-permute-start(bf16[16,792,128]{2,1,0:T(8,128)(2,1)} %get-tuple-element.233), channel_id=1, source_target_pairs={{0,8},{1,9},{2,10},{3,11},{4,12},{5,13},{6,14},{7,15},{8,0},{9,1},... | collective-permute-start | bytes 9732104 | tf_op jit(solution)/shard_map/ppermute | solution.py:133
  330.3 31.9 %collective-permute-start.38 = (bf16[1,792,128]{2,1,0:T(8,128)(2,1)}, bf16[1,792,128]{2,1,0:T(8,128)(2,1)}, u32[]{:S(2)}, u32[]{:S(2)}) collective-permute-start(bf16[1,792,128]{2,1,0:T(8,128)(2,1)} %get-tuple-element.247), channel_id=1, source_target_pairs={{0,2},{1,3},{2,0},{3,1},{4,6},{5,7},{6,4},{7,5},{8,10},{9,11},{10,... | collective-permute-start | bytes 608264 | tf_op jit(solution)/shard_map/ppermute | solution.py:133
  331.1 31.1 %collective-permute-start.39 = (bf16[1,792,128]{2,1,0:T(8,128)(2,1)}, bf16[1,792,128]{2,1,0:T(8,128)(2,1)}, u32[]{:S(2)}, u32[]{:S(2)}) collective-permute-start(bf16[1,792,128]{2,1,0:T(8,128)(2,1)} %get-tuple-element.249), channel_id=1, source_target_pairs={{0,4},{1,5},{2,6},{3,7},{4,0},{5,1},{6,2},{7,3},{8,12},{9,13},{10,... | collective-permute-start | bytes 608264 | tf_op jit(solution)/shard_map/ppermute | solution.py:133
  333.3 28.9 %collective-permute-start.40 = (bf16[1,792,128]{2,1,0:T(8,128)(2,1)}, bf16[1,792,128]{2,1,0:T(8,128)(2,1)}, u32[]{:S(2)}, u32[]{:S(2)}) collective-permute-start(bf16[1,792,128]{2,1,0:T(8,128)(2,1)} %get-tuple-element.251), channel_id=1, source_target_pairs={{0,6},{1,7},{2,4},{3,5},{4,2},{5,3},{6,0},{7,1},{8,14},{9,15},{10,... | collective-permute-start | bytes 608264 | tf_op jit(solution)/shard_map/ppermute | solution.py:133
  338.1 26.1 %collective-permute-start.36 = (bf16[8,792,128]{2,1,0:T(8,128)(2,1)}, bf16[8,792,128]{2,1,0:T(8,128)(2,1)}, u32[]{:S(2)}, u32[]{:S(2)}) collective-permute-start(bf16[8,792,128]{2,1,0:T(8,128)(2,1)} %add_terms.19), channel_id=1, source_target_pairs={{0,1},{1,0},{2,3},{3,2},{4,5},{5,4},{6,7},{7,6},{8,24},{9,25},{10,... | collective-permute-start | bytes 4866056 | tf_op jit(solution)/shard_map/ppermute | solution.py:133
  372.5 25.5 %collective-permute-start.42 = (bf16[8,792,128]{2,1,0:T(8,128)(2,1)}, bf16[8,792,128]{2,1,0:T(8,128)(2,1)}, u32[]{:S(2)}, u32[]{:S(2)}) collective-permute-start(bf16[8,792,128]{2,1,0:T(8,128)(2,1)} %add_terms.21), channel_id=1, source_target_pairs={{0,1},{1,0},{2,3},{3,2},{4,5},{5,4},{6,7},{7,6},{8,24},{9,25},{10,... | collective-permute-start | bytes 4866056 | tf_op jit(solution)/shard_map/ppermute | solution.py:133
  392.1 36.6 %collective-permute-start.45 = (bf16[1,792,128]{2,1,0:T(8,128)(2,1)}, bf16[1,792,128]{2,1,0:T(8,128)(2,1)}, u32[]{:S(2)}, u32[]{:S(2)}) collective-permute-start(bf16[1,792,128]{2,1,0:T(8,128)(2,1)} %get-tuple-element.271), channel_id=1, source_target_pairs={{0,2},{1,3},{2,0},{3,1},{4,6},{5,7},{6,4},{7,5},{8,10},{9,11},{10,... | collective-permute-start | bytes 608264 | tf_op jit(solution)/shard_map/ppermute | solution.py:133
  392.1 36.6 %collective-permute-start.46 = (bf16[1,792,128]{2,1,0:T(8,128)(2,1)}, bf16[1,792,128]{2,1,0:T(8,128)(2,1)}, u32[]{:S(2)}, u32[]{:S(2)}) collective-permute-start(bf16[1,792,128]{2,1,0:T(8,128)(2,1)} %get-tuple-element.273), channel_id=1, source_target_pairs={{0,4},{1,5},{2,6},{3,7},{4,0},{5,1},{6,2},{7,3},{8,12},{9,13},{10,... | collective-permute-start | bytes 608264 | tf_op jit(solution)/shard_map/ppermute | solution.py:133
  395.0 33.7 %collective-permute-start.47 = (bf16[1,792,128]{2,1,0:T(8,128)(2,1)}, bf16[1,792,128]{2,1,0:T(8,128)(2,1)}, u32[]{:S(2)}, u32[]{:S(2)}) collective-permute-start(bf16[1,792,128]{2,1,0:T(8,128)(2,1)} %get-tuple-element.275), channel_id=1, source_target_pairs={{0,6},{1,7},{2,4},{3,5},{4,2},{5,3},{6,0},{7,1},{8,14},{9,15},{10,... | collective-permute-start | bytes 608264 | tf_op jit(solution)/shard_map/ppermute | solution.py:133
  402.1 26.7 %collective-permute-start.44 = (bf16[4,792,128]{2,1,0:T(8,128)(2,1)}, bf16[4,792,128]{2,1,0:T(8,128)(2,1)}, u32[]{:S(2)}, u32[]{:S(2)}) collective-permute-start(bf16[4,792,128]{2,1,0:T(8,128)(2,1)} %get-tuple-element.262), channel_id=1, source_target_pairs={{0,16},{1,17},{2,18},{3,19},{4,20},{5,21},{6,22},{7,23},{8,9},{9,8... | collective-permute-start | bytes 2433032 | tf_op jit(solution)/shard_map/ppermute | solution.py:133
  427.4 24.9 %collective-permute-start.48 = (bf16[8,792,128]{2,1,0:T(8,128)(2,1)}, bf16[8,792,128]{2,1,0:T(8,128)(2,1)}, u32[]{:S(2)}, u32[]{:S(2)}) collective-permute-start(bf16[8,792,128]{2,1,0:T(8,128)(2,1)} %add_terms.25), channel_id=1, source_target_pairs={{0,1},{1,0},{2,3},{3,2},{4,5},{5,4},{6,7},{7,6},{8,24},{9,25},{10,... | collective-permute-start | bytes 4866056 | tf_op jit(solution)/shard_map/ppermute | solution.py:133
  449.3 28.6 %collective-permute-start.50 = (bf16[1,792,128]{2,1,0:T(8,128)(2,1)}, bf16[1,792,128]{2,1,0:T(8,128)(2,1)}, u32[]{:S(2)}, u32[]{:S(2)}) collective-permute-start(bf16[1,792,128]{2,1,0:T(8,128)(2,1)} %get-tuple-element.287), channel_id=1, source_target_pairs={{0,2},{1,3},{2,0},{3,1},{4,6},{5,7},{6,4},{7,5},{8,10},{9,11},{10,... | collective-permute-start | bytes 608264 | tf_op jit(solution)/shard_map/ppermute | solution.py:133
  449.3 30.1 %collective-permute-start.51 = (bf16[1,792,128]{2,1,0:T(8,128)(2,1)}, bf16[1,792,128]{2,1,0:T(8,128)(2,1)}, u32[]{:S(2)}, u32[]{:S(2)}) collective-permute-start(bf16[1,792,128]{2,1,0:T(8,128)(2,1)} %get-tuple-element.289), channel_id=1, source_target_pairs={{0,4},{1,5},{2,6},{3,7},{4,0},{5,1},{6,2},{7,3},{8,12},{9,13},{10,... | collective-permute-start | bytes 608264 | tf_op jit(solution)/shard_map/ppermute | solution.py:133
  (76 other events, 1004.1 us)
